TPU v7x, 32 devices: a whole 2x2x4 slice. The times are simulated.
32 devices in a mesh: grp: 4 (over x, core), mem: 8 (over z, y).
Axes of the slice: x: 2, y: 2, z: 4, core: 2. Of those that a mesh axis runs over, the one named last changes fastest.
Arguments:
- leaf_fronts: float32 [4, 4096, 4096], P('grp', None, 'mem'), as said below
- block_owner: int32 [4, 32], P('grp', 'mem'), may hold values from 0 to 31, as said below
- root_front: float32 [4096, 4096], P('grp', 'mem'), as said below
Outputs:
- root_factor: float32 [4096, 4096], P('grp', 'mem')
- log_det: float32 [5], replicated
Inputs may be any that keep to these rules, and one draw needn't show every extreme that they name: Each row of block_owner is a permutation of 0 to 31. For each g, the matrix whose column block block_owner[g, t] is column block t of leaf_fronts[g] is symmetric positive definite. root_front is symmetric positive definite.
All inputs are finite; a program needn't handle non-finite values.
Results may differ from a plain program's by a relative error of at most 0.0021.
Values may be sent and summed in bfloat16 or wider, within the bound.
No kernel may reach another device: no remote copies, remote signals or barrier semaphores. Data moves between devices by JAX's collectives and lax.ppermute only.
A program may use at most 64 MiB of HBM per device.

v0:
```python
import jax
import jax.numpy as jnp
from jax import lax
from jax.sharding import PartitionSpec as P

PL = 3
PR = 2


def broadcast(value, axis, root):
    mine = lax.axis_index(axis) == root
    return lax.psum(jnp.where(mine, value, jnp.zeros_like(value)), axis)


def factor_panel(column, diagonal_block, holder, first_row, row_ids):
    eye_block = jnp.eye(diagonal_block.shape[0], dtype=jnp.float32)
    factor = jnp.linalg.cholesky(jnp.where(holder, diagonal_block, eye_block))
    panel_rows = lax.linalg.triangular_solve(
        factor, column, left_side=False, lower=True, transpose_a=True
    )
    panel_rows = jnp.where((row_ids >= first_row)[:, None], panel_rows, jnp.zeros_like(panel_rows))
    log_sum = 2.0 * jnp.sum(jnp.log(jnp.diagonal(factor)))
    return (panel_rows, log_sum)


def local(leaf_fronts, block_owner, root_front):
    members = lax.axis_size("mem")
    groups = lax.axis_size("grp")
    member = lax.axis_index("mem")
    my_group = lax.axis_index("grp")
    leaf_local = leaf_fronts[0]
    front_order = leaf_local.shape[0]
    owner_local = block_owner[0]
    per_member = owner_local.shape[0]
    block_width = front_order // (per_member * members)
    block_count = front_order // block_width
    cols_local = per_member * block_width
    owner_full = lax.all_gather(block_owner, "mem", axis=1, tiled=True)[0]
    slot_ids = jnp.arange(block_count, dtype=jnp.int32)
    row_ids = jnp.arange(front_order, dtype=jnp.int32)
    blocks = leaf_local.reshape(front_order, per_member, block_width)
    leaf_logs = jnp.zeros((), jnp.float32)
    for section_index in range(PL):
        holds_block = owner_local == section_index
        holder = jnp.any(holds_block)
        column = jnp.sum(jnp.where(holds_block[None, :, None], blocks, 0.0), axis=1)
        diagonal_block = column[section_index * block_width : (section_index + 1) * block_width]
        panel_rows, log_sum = factor_panel(
            column, diagonal_block, holder, section_index * block_width, row_ids
        )
        leaf_logs = leaf_logs + jnp.where(holder, log_sum, 0.0)
        source = jnp.sum(jnp.where(owner_full == section_index, slot_ids, 0)) // per_member
        shared = broadcast(panel_rows.astype(jnp.bfloat16), "mem", source)
        across = jnp.take(
            shared.reshape(block_count, block_width, block_width), owner_local, axis=0
        )
        blocks = blocks - jnp.einsum(
            "rc,jbc->rjb", shared, across, preferred_element_type=jnp.float32
        )
    keep_cols = owner_local >= PL
    masked = jnp.where(keep_cols[None, :, None], blocks, 0.0).reshape(
        block_count, block_width, cols_local
    )
    quarter_rows = root_front.shape[0]
    root_logs = jnp.zeros((), jnp.float32)
    placed_front = lax.dynamic_update_slice_in_dim(
        jnp.zeros((front_order, cols_local), jnp.float32), root_front, my_group * quarter_rows, 0
    )
    taken = jnp.take(masked, owner_full, axis=0)
    placed = jnp.where((owner_full >= PL)[:, None, None], taken, 0.0)
    root_full = lax.psum(placed.reshape(front_order, cols_local) + placed_front, "grp")
    panels_full = jnp.zeros_like(root_full)
    for section_index in range(PR):
        owner_member, local_slot = divmod(section_index, per_member)
        column = root_full[:, local_slot * block_width : (local_slot + 1) * block_width]
        diagonal_block = column[section_index * block_width : (section_index + 1) * block_width]
        holder = member == owner_member
        panel_rows, log_sum = factor_panel(
            column, diagonal_block, holder, section_index * block_width, row_ids
        )
        root_logs = root_logs + jnp.where(holder & (my_group == 0), log_sum, 0.0)
        full_panel = broadcast(panel_rows.astype(jnp.bfloat16), "mem", owner_member)
        col_rows = lax.dynamic_slice_in_dim(full_panel, member * cols_local, cols_local, 0)
        root_full = root_full - jnp.einsum(
            "rc,xc->rx", full_panel, col_rows, preferred_element_type=jnp.float32
        )
        kept_block = panels_full[:, local_slot * block_width : (local_slot + 1) * block_width]
        panels_full = panels_full.at[
            :, local_slot * block_width : (local_slot + 1) * block_width
        ].set(jnp.where(holder, panel_rows, kept_block))
    root_local = lax.dynamic_slice_in_dim(root_full, my_group * quarter_rows, quarter_rows, 0)
    panels_kept = lax.dynamic_slice_in_dim(panels_full, my_group * quarter_rows, quarter_rows, 0)
    global_rows = my_group * quarter_rows + jnp.arange(quarter_rows, dtype=jnp.int32)
    column_blocks = member * per_member + jnp.arange(per_member, dtype=jnp.int32)
    pivot_cols = jnp.repeat(column_blocks < PR, block_width, total_repeat_length=cols_local)
    trailing = jnp.where((global_rows >= PR * block_width)[:, None], root_local, 0.0)
    root_factor = jnp.where(pivot_cols[None, :], panels_kept, trailing)
    places = jnp.arange(groups + 1, dtype=jnp.int32)
    terms = jnp.where(places == my_group, leaf_logs / (PL * block_width), 0.0) + jnp.where(
        places == groups, root_logs / (PR * block_width), 0.0
    )
    log_det = lax.psum(terms, ("grp", "mem"))
    return (root_factor, log_det)


def solution(mesh):
    in_specs = (P("grp", None, "mem"), P("grp", "mem"), P("grp", "mem"))
    out_specs = (P("grp", "mem"), P())
    return jax.shard_map(local, mesh=mesh, in_specs=in_specs, out_specs=out_specs, check_vma=False)
```

profile of v0, /device:TPU:1, one launch (start us, length us, event | category | flops | bytes accessed | tf_op | source)
XLA Modules:
  0.0 840.9 jit_solution(10672149471551786729)
XLA Ops:
  9.9 9.5 %all-reduce.1 = s32[32]{0:T(128)S(1)} all-reduce(s32[32]{0:T(128)S(1)} %get-tuple-element.74), channel_id=1, replica_groups=mesh['grp'=4,'mem'=8] {'mem'}, use_global_device_ids=true, to_apply=%add.1 | all-reduce | flops 32 | bytes 256 | tf_op jit(solution)/shard_map/squeeze | solution.py:38
  24.1 8.9 %copy.38 = f32[1,4096,512]{1,2,0:T(8,128)} copy(f32[1,4096,512]{2,1,0:T(8,128)} %param.14) | data formatting | bytes 16777216 | tf_op args[0]
  33.1 8.9 %copy.44 = f32[4096,4,128]{2,0,1:T(8,128)} copy(f32[4096,4,128]{0,2,1:T(8,128)} %bitcast.141) | data formatting | bytes 16777216 | tf_op jit(solution)/shard_map/reshape;squeeze | solution.py:41
  42.0 4.3 select_reduce_fusion.2
  47.9 11.7 %cholesky.89 = f32[128,128]{1,0:T(8,128)S(1)} custom-call(f32[128,128]{1,0:T(8,128)S(1)} %fusion.34), custom_call_target="Cholesky" | custom-call | tf_op jit(solution)/shard_map/jit(cholesky)/cholesky | solution.py:17
  60.9 9.8 %custom-call.19 = f32[1,128,128]{1,2,0:T(8,128)S(1)} custom-call(f32[1,128,128]{2,1,0:T(8,128)S(1)} %get-tuple-element.61), custom_call_target="InvertDiagBlocksLowerTriangular" | custom-call | tf_op jit(solution)/shard_map/triangular_solve/custom-call.0 | solution.py:18
  70.8 2.9 fusion.6
  76.3 76.0 %all-reduce.9.cloned.1.call-done = bf16[4096,128]{0,1:T(8,128)(2,1)} async-done(((bf16[4096,128]{0,1:T(8,128)(2,1)}), bf16[4096,128]{0,1:T(8,128)(2,1)}) %all-reduce.9.cloned.1.call-update) | async-done | bytes 1048592 | tf_op jit(solution)/shard_map/psum | solution.py:12
  152.3 1.6 copy.68
  154.5 8.8 %select_reduce_fusion.1 = (f32[4096,128]{1,0:T(8,128)S(1)}, f32[4096,4,128]{2,0,1:T(8,128)}) fusion(pred[4]{0:T(512)(128)(4,1)S(1)} %get-tuple-element.71, f32[4096,4,128]{2,0,1:T(8,128)} %copy.44, bf16[4,128,128]{2,1,0:T(8,128)(2,1)S(1)} %gather_fusion.6, pred[4]{0:T(512)(128)(4,1)S(1)} %get-tuple-element.72, ...), kind=kOutput, calls=%fused_computation.12 | convolution fusion | flops 542703616 | bytes 20054024 | tf_op jit(solution)/shard_map/rc,jbc->rjb/dot_general | solution.py:57
  164.7 11.7 %cholesky.100 = f32[128,128]{1,0:T(8,128)S(1)} custom-call(f32[128,128]{1,0:T(8,128)S(1)} %fusion.32), custom_call_target="Cholesky" | custom-call | tf_op jit(solution)/shard_map/jit(cholesky)/cholesky | solution.py:17
  177.7 9.8 %custom-call.20 = f32[1,128,128]{1,2,0:T(8,128)S(1)} custom-call(f32[1,128,128]{2,1,0:T(8,128)S(1)} %get-tuple-element.59), custom_call_target="InvertDiagBlocksLowerTriangular" | custom-call | tf_op jit(solution)/shard_map/triangular_solve/custom-call.0 | solution.py:18
  187.5 3.0 fusion.8
  193.5 74.7 %all-reduce.11.cloned.1.call-done = bf16[4096,128]{0,1:T(8,128)(2,1)} async-done(((bf16[4096,128]{0,1:T(8,128)(2,1)}), bf16[4096,128]{0,1:T(8,128)(2,1)}) %all-reduce.11.cloned.1.call-update) | async-done | bytes 1048592 | tf_op jit(solution)/shard_map/psum | solution.py:12
  268.2 1.6 copy.70
  270.4 8.8 %select_reduce_fusion = (f32[4096,128]{1,0:T(8,128)S(1)}, f32[4096,4,128]{2,0,1:T(8,128)}) fusion(pred[4]{0:T(512)(128)(4,1)S(1)} %get-tuple-element.69, f32[4096,4,128]{2,0,1:T(8,128)} %get-tuple-element.77, bf16[4,128,128]{2,1,0:T(8,128)(2,1)S(1)} %gather_fusion.7, pred[4]{0:T(512)(128)(4,1)S(1)} %get-tuple-element.72, ...), kind=kOutput, calls=%fused_computation.11 | convolution fusion | flops 542703616 | bytes 20054024 | tf_op jit(solution)/shard_map/rc,jbc->rjb/dot_general | solution.py:57
  280.8 11.7 %cholesky.111 = f32[128,128]{1,0:T(8,128)S(1)} custom-call(f32[128,128]{1,0:T(8,128)S(1)} %fusion.30), custom_call_target="Cholesky" | custom-call | tf_op jit(solution)/shard_map/jit(cholesky)/cholesky | solution.py:17
  293.8 9.8 %custom-call.21 = f32[1,128,128]{1,2,0:T(8,128)S(1)} custom-call(f32[1,128,128]{2,1,0:T(8,128)S(1)} %get-tuple-element.57), custom_call_target="InvertDiagBlocksLowerTriangular" | custom-call | tf_op jit(solution)/shard_map/triangular_solve/custom-call.0 | solution.py:18
  303.6 3.0 fusion.7
  306.8 1.9 copy.56
  308.9 75.5 %all-reduce.13.cloned.1.call-done = bf16[4096,128]{0,1:T(8,128)(2,1)} async-done(((bf16[4096,128]{0,1:T(8,128)(2,1)}), bf16[4096,128]{0,1:T(8,128)(2,1)}) %all-reduce.13.cloned.1.call-update) | async-done | bytes 1048592 | tf_op jit(solution)/shard_map/psum | solution.py:12
  384.4 1.6 copy.72
  386.6 5.5 subtract_select_fusion
  392.2 18.6 %copy.73 = f32[4096,4,128]{2,1,0:T(4,128)} copy(f32[4096,4,128]{2,0,1:T(8,128)S(1)} %subtract_select_fusion) | data formatting | bytes 16777216 | tf_op jit(solution)/shard_map/reshape | solution.py:61
  410.8 10.3 %reshape.387 = f32[32,128,512]{2,1,0:T(8,128)} reshape(f32[4096,4,128]{2,1,0:T(4,128)} %copy.73) | data formatting | bytes 16777216 | tf_op jit(solution)/shard_map/reshape | solution.py:61
  421.1 7.7 gather_fusion
  428.8 8.9 %copy.74 = f32[4096,512]{0,1:T(8,128)} copy(f32[4096,512]{1,0:T(8,128)} %bitcast.140) | data formatting | bytes 16777216 | tf_op jit(solution)/shard_map/jit(_take)/gather | solution.py:69
  437.7 8.3 select_select_fusion
  445.9 3.3 add_dynamic-update-slice_fusion
  454.8 2.6 select_reduce_fusion.5
  463.7 138.7 %all-reduce.15.cloned.1.call-done = f32[4096,512]{0,1:T(8,128)} async-done(((f32[4096,512]{0,1:T(8,128)}), f32[4096,512]{0,1:T(8,128)}) %all-reduce.15.cloned.1.call-update) | async-done | bytes 8388624 | tf_op jit(solution)/shard_map/psum | solution.py:71
  604.2 11.7 %cholesky.122 = f32[128,128]{1,0:T(8,128)S(1)} custom-call(f32[128,128]{1,0:T(8,128)S(1)} %fusion.28), custom_call_target="Cholesky" | custom-call | tf_op jit(solution)/shard_map/jit(cholesky)/cholesky | solution.py:17
  617.2 9.8 %custom-call.22 = f32[1,128,128]{1,2,0:T(8,128)S(1)} custom-call(f32[1,128,128]{2,1,0:T(8,128)S(1)} %get-tuple-element.55), custom_call_target="InvertDiagBlocksLowerTriangular" | custom-call | tf_op jit(solution)/shard_map/triangular_solve/custom-call.0 | solution.py:18
  627.1 4.5 convert_select_fusion.1
  634.5 2.2 select_select_fusion.1
  636.7 72.8 %all-reduce.17.cloned.1.call-done = bf16[4096,128]{0,1:T(8,128)(2,1)} async-done(((bf16[4096,128]{0,1:T(8,128)(2,1)}), bf16[4096,128]{0,1:T(8,128)(2,1)}) %all-reduce.17.cloned.1.call-update) | async-done | bytes 1048592 | tf_op jit(solution)/shard_map/psum | solution.py:12
  709.5 5.1 convolution_subtract_fusion
  714.6 3.2 copy-done
  718.8 11.7 %cholesky.133 = f32[128,128]{1,0:T(8,128)S(1)} custom-call(f32[128,128]{1,0:T(8,128)S(1)} %fusion.26), custom_call_target="Cholesky" | custom-call | tf_op jit(solution)/shard_map/jit(cholesky)/cholesky | solution.py:17
  734.3 9.8 %custom-call.23 = f32[1,128,128]{1,2,0:T(8,128)S(1)} custom-call(f32[1,128,128]{2,1,0:T(8,128)S(1)} %get-tuple-element.53), custom_call_target="InvertDiagBlocksLowerTriangular" | custom-call | tf_op jit(solution)/shard_map/triangular_solve/custom-call.0 | solution.py:18
  744.1 4.6 convert_select_fusion
  748.8 5.8 scatter.6
  754.6 40.1 %psum.55 = f32[5]{0:T(128)} all-reduce(f32[5]{0:T(128)S(1)} %fusion.61), channel_id=1, replica_groups=mesh['grp'=4,'mem'=8] {'grp','mem'}, use_global_device_ids=true, to_apply=%region_24.28 | all-reduce | flops 5 | bytes 40 | tf_op jit(solution)/shard_map/psum | solution.py:102
  794.7 2.1 select_dynamic-update-slice_fusion
  796.8 29.9 %all-reduce.19.cloned.1.call-done = bf16[4096,128]{0,1:T(8,128)(2,1)} async-done(((bf16[4096,128]{0,1:T(8,128)(2,1)}), bf16[4096,128]{0,1:T(8,128)(2,1)}) %all-reduce.19.cloned.1.call-update) | async-done | bytes 1048592 | tf_op jit(solution)/shard_map/psum | solution.py:12
  826.7 2.5 fusion.19
  829.2 2.5 fusion.10
  831.8 1.8 copy.61
  (84 shorter events, 32.8 us)
Async XLA Ops:
  7.2 145.1 %all-reduce.9.cloned.1.call-start = ((), (), s32[]{:S(2)}) async-start(), calls=%async_computation | async-start | bytes 2097152 | tf_op jit(solution)/shard_map/psum | solution.py:12
  73.7 194.5 %all-reduce.11.cloned.1.call-start = ((), (), s32[]{:S(2)}) async-start(), calls=%async_computation.1 | async-start | bytes 2097152 | tf_op jit(solution)/shard_map/psum | solution.py:12
  190.5 193.9 %all-reduce.13.cloned.1.call-start = ((), (), s32[]{:S(2)}) async-start(), calls=%async_computation.2 | async-start | bytes 2097152 | tf_op jit(solution)/shard_map/psum | solution.py:12
  306.6 295.8 %all-reduce.15.cloned.1.call-start = ((), (), s32[]{:S(2)}) async-start(), calls=%async_computation.3 | async-start | bytes 16777216 | tf_op jit(solution)/shard_map/psum | solution.py:71
  449.2 260.3 %all-reduce.17.cloned.1.call-start = ((), (), s32[]{:S(2)}) async-start(), calls=%async_computation.4 | async-start | bytes 2097152 | tf_op jit(solution)/shard_map/psum | solution.py:12
  631.6 195.1 %all-reduce.19.cloned.1.call-start = ((), (), s32[]{:S(2)}) async-start(), calls=%async_computation.5 | async-start | bytes 2097152 | tf_op jit(solution)/shard_map/psum | solution.py:12
  714.6 3.2 copy-start
Sparse Core Ops, SparseCore 0:
  73.8 78.3 all-reduce.8
  190.6 77.5 all-reduce.10
  306.7 77.6 all-reduce.12
  449.4 152.9 all-reduce.14
  631.8 77.6 all-reduce.16
  748.9 77.7 all-reduce.18
where the time goes:
time: 851 us; the launch traced here: 841 us
  waiting for transfers between devices  468 us (55%)
  other arithmetic  153 us (18%)
  local copies, waits for them, and re-layouts  91.6 us (11%)
  blocking collectives  49.6 us (6%)
  matrix products  48.7 us (6%)
  between operations  28.3 us (3%)
    psum x5, waiting for transfers between devices, broadcast(): return lax.psum(jnp.where(mine, value, jnp.zeros_like(value)), axis)  329 us
    psum x1, waiting for transfers between devices, local(): lax.psum(placed.reshape(front_order, cols_local) + placed_front, 'grp')  139 us
    another operation x15, other arithmetic, factor_panel(): factor = jnp.linalg.cholesky(jnp.where(holder, diagonal_block, eye_block))  61.9 us
    another operation x10, other arithmetic, factor_panel(): lax.linalg.triangular_solve(factor, column, left_side=False, lower=True,...  52.3 us
    psum x1, blocking collectives, local(): log_det = lax.psum(terms, ('grp', 'mem'))  40.1 us
    reshape x2, local copies, waits for them, and re-layouts, local(): jnp.where(keep_cols[None, :, None], blocks, 0.0)  28.9 us
    dot_general x3, matrix products, local(): jnp.einsum('rc,jbc->rjb', shared, across, preferred_element_type=jnp.floa...  23.2 us
    another operation x5, matrix products, factor_panel(): lax.linalg.triangular_solve(factor, column, left_side=False, lower=True,...  18 us
  transfers between devices with their start and end apart: 6, of which 6 were waited for; matrix products, arithmetic and copies ran while one was open for 3% of the time, Pallas kernels for 0%

commit v1 on v0

v1 whole, which is shorter than its diff:
```python
import jax
import jax.numpy as jnp
from jax import lax
from jax.experimental import pallas as pl
from jax.experimental.pallas import tpu as pltpu
from jax.sharding import PartitionSpec as P

PL = 3
PR = 2
HIGHEST = lax.Precision.HIGHEST
ROWS = 64
SUB = 16
LOG_ROWS = 16
CORE, CHIP = 1, 2
f32, bf16 = jnp.float32, jnp.bfloat16


def mm(lhs, rhs):
    return jnp.dot(lhs, rhs, precision=HIGHEST, preferred_element_type=f32)


def mm_t(lhs, rhs):
    return lax.dot_general(
        lhs, rhs, (((1,), (1,)), ((), ())), precision=HIGHEST, preferred_element_type=f32
    )


def tdot(lhs, rhs):
    return lax.dot_general(lhs, rhs, (((0,), (0,)), ((), ())), preferred_element_type=f32)


def bits(size):
    out, bit = [], 1
    while bit < size:
        out.append(bit)
        bit *= 2
    return out


def flip(value, axis, bit):
    size = lax.axis_size(axis)
    return lax.ppermute(value, axis, [(i, i ^ bit) for i in range(size)])


def shape(dims, dtype):
    return jax.ShapeDtypeStruct(dims, dtype)


def cost(us):
    return pl.CostEstimate(flops=0, bytes_accessed=int(us * 3.0e6), transcendentals=0)


def invert_factor(block, work, inverse_ref):
    size = block.shape[0]
    rows = lax.broadcasted_iota(jnp.int32, (size, size), 0)
    cols = lax.broadcasted_iota(jnp.int32, (size, size), 1)
    work[:, :size] = block
    work[:, size:] = jnp.where(rows == cols, 1.0, 0.0)
    sub = lax.broadcasted_iota(jnp.int32, (ROWS, size), 0)
    lane = lax.broadcasted_iota(jnp.int32, (ROWS, size), 1)
    log_sum = jnp.zeros((1, 1), f32)
    for first in range(0, size, ROWS):
        left = work[first : first + ROWS, :size]
        right = work[first : first + ROWS, size:]
        for start in range(0, ROWS, SUB):
            at = first + start
            columns = [
                jnp.broadcast_to(left[:, at + j : at + j + 1], (ROWS, size)) for j in range(SUB)
            ]
            for j in range(SUB):
                i = start + j
                if i == ROWS - 1:
                    break
                factor = jnp.where(sub > i, columns[j], 0.0) * (1.0 / columns[j][i : i + 1, :])
                for k in range(j + 1, SUB):
                    columns[k] = columns[k] - factor * columns[k][i : i + 1, :]
                left = left - factor * left[i : i + 1, :]
                right = right - factor * right[i : i + 1, :]
        pivot = jnp.sum(jnp.where(lane == sub + first, left, 0.0), axis=1, keepdims=True)
        scale = lax.rsqrt(pivot)
        left, right = left * scale, right * scale
        inverse_ref[first : first + ROWS, :] = right
        log_sum = log_sum + jnp.sum(jnp.log(pivot), axis=0, keepdims=True)
        if first + ROWS < size:
            update = lax.dot_general(
                left, jnp.concatenate([left, right], axis=1), (((0,), (0,)), ((), ())),
                precision=HIGHEST, preferred_element_type=f32,
            )
            work[first + ROWS :, :] = work[first + ROWS :, :] - update[first + ROWS :, :]
    return log_sum


def pick_pivots(owner_ref, at_ref, front_ref, head_ref, rest_ref, mask_ref):
    b = head_ref.shape[1]
    per = front_ref.shape[1] // b
    for k in range(PL):
        total = jnp.zeros(((k + 1) * b, b), f32)
        for t in range(per):
            part = front_ref[: (k + 1) * b, t * b : (t + 1) * b]
            total = total + jnp.where(owner_ref[t] == k, part, 0.0)
        if k == 0:
            head_ref[:b, :] = total
        elif k == 1:
            rest_ref[: 2 * b, :] = total
        else:
            rest_ref[2 * b :, :] = total
    lane = lax.broadcasted_iota(jnp.int32, (8, b), 1)
    table = jnp.zeros((8, b), f32)
    for t in range(per):
        table = table + jnp.where(lane == at_ref[0] + t, owner_ref[t].astype(f32), 0.0)
        keep = jnp.where(owner_ref[t] >= PL, 1.0, 0.0).astype(f32)
        mask_ref[:, t * b : (t + 1) * b] = jnp.full((8, b), keep, f32)
    head_ref[b:, :] = table


def leaf_first(head_ref, w_ref, mask_ref, p_ref, inv_ref, log_ref, work):
    b = w_ref.shape[0]
    log_sum = invert_factor(head_ref[:b, :], work, inv_ref)
    log_ref[...] = jnp.broadcast_to(log_sum, log_ref.shape)
    panel = mm(inv_ref[...], w_ref[...])
    p_ref[...] = jnp.where(mask_ref[:1, :] > 0.0, panel, 0.0).astype(bf16)


def leaf_others(
    rest_ref, w1_ref, w2_ref, mask_ref, inv0_ref, p0_ref, log0_ref, p_ref, log_ref, inv, work
):
    b = w1_ref.shape[0]
    c01, c11, c02, c12, c22 = [rest_ref[i * b : (i + 1) * b, :] for i in range(5)]
    keep = mask_ref[:1, :] > 0.0
    p0 = p0_ref[...]
    x01 = mm(inv0_ref[...], c01).astype(bf16)
    log1 = invert_factor(c11 - tdot(x01, x01), work, inv)
    x02 = mm(inv0_ref[...], c02).astype(bf16)
    panel = mm(inv[...], w1_ref[...] - tdot(x01, p0))
    p1 = jnp.where(keep, panel, 0.0).astype(bf16)
    p_ref[:b, :] = p1
    x12 = mm(inv[...], c12 - tdot(x01, x02)).astype(bf16)
    log2 = invert_factor(c22 - tdot(x02, x02) - tdot(x12, x12), work, inv)
    panel = mm(inv[...], w2_ref[...] - tdot(x02, p0) - tdot(x12, p1))
    p_ref[b:, :] = jnp.where(keep, panel, 0.0).astype(bf16)
    log_ref[...] = log0_ref[...] + jnp.broadcast_to(log1 + log2, log_ref.shape)


def gather_rows(ways, near_steps, *refs):
    source_ref, keep_ref = refs[:2]
    fronts = refs[2 : 2 + ways]
    mask_ref, near_ref, far_ref = refs[2 + ways :]
    step = pl.program_id(0)
    b = fronts[0].shape[0]
    keep_cols = mask_ref[:1, :] > 0.0

    def store(out_ref):
        for i, front_ref in enumerate(fronts):
            keep = keep_cols & (keep_ref[step * ways + i] > 0)
            out_ref[i * b : (i + 1) * b, :] = jnp.where(keep, front_ref[...], 0.0)

    pl.when(step < near_steps)(lambda: store(near_ref))
    pl.when(step >= near_steps)(lambda: store(far_ref))


def add_rows(ways, with_near, *refs):
    source_ref, keep_ref, scale_ref = refs[:3]
    fronts = refs[3 : 3 + ways]
    mask_ref, root_ref = refs[3 + ways : 5 + ways]
    out_ref = refs[-1]
    step = pl.program_id(0)
    b = fronts[0].shape[0]
    keep_cols = mask_ref[:1, :] > 0.0
    for i, front_ref in enumerate(fronts):
        keep = keep_cols & (keep_ref[step * ways + i] > 0)
        at = slice(i * b, (i + 1) * b)
        total = jnp.where(scale_ref[0] > 0, root_ref[at, :], 0.0)
        total = total + jnp.where(keep, front_ref[...], 0.0)
        if with_near:
            total = total + refs[5 + ways][at, :]
        out_ref[at, :] = total


def root_step(
    corner_ref, lead_ref, first_ref, d0_ref, d12_ref,
    q_ref, inv0_ref, inv1_ref, x_ref, log_ref, work,
):
    b = inv0_ref.shape[0]
    groups = d0_ref.shape[0] // b
    pitch = lead_ref.shape[0] // groups
    corner = corner_ref[...]
    top = first_ref[...]
    for q in range(groups):
        lead = lead_ref[q * pitch : q * pitch + PL * b, :]
        corner = corner - tdot(lead, lead)
        top = top - tdot(lead[:b, :], d0_ref[q * b : (q + 1) * b, :])
        top = top - tdot(lead[b:, :], d12_ref[q * 2 * b : (q + 1) * 2 * b, :])
    log0 = invert_factor(corner[:b, :b], work, inv0_ref)
    x = mm(inv0_ref[...], corner[:b, b:]).astype(bf16)
    x_ref[...] = x
    log1 = invert_factor(corner[b:, b:] - tdot(x, x), work, inv1_ref)
    log_ref[...] = jnp.broadcast_to(log0 + log1, log_ref.shape)
    q0 = mm(inv0_ref[...], top[:b, :]).astype(bf16)
    q_ref[:b, :] = q0
    q_ref[b:, :] = mm(inv1_ref[...], top[b:, :] - tdot(x, q0)).astype(bf16)


def local(leaf_fronts, block_owner, root_front):
    members = lax.axis_size("mem")
    groups = lax.axis_size("grp")
    m = lax.axis_index("mem")
    g = lax.axis_index("grp")
    front = leaf_fronts[0]
    order, cols = front.shape
    owner = block_owner[0]
    per = owner.shape[0]
    b = cols // per
    count = order // b
    quarter = order // groups
    spread = members // groups
    quarter_blocks = quarter // b
    pr = PR * b
    lead_cols = min(pr, cols)
    leads = pr // lead_cols
    zone, inner = m // spread, m % spread
    smem = pl.BlockSpec(memory_space=pltpu.SMEM)
    vmem = pl.BlockSpec(memory_space=pltpu.VMEM)

    head, rest, mask = pl.pallas_call(
        pick_pivots,
        grid=(1,),
        in_specs=[smem, smem, pl.BlockSpec((PL * b, cols), lambda i: (0, 0))],
        out_specs=[vmem, vmem, vmem],
        out_shape=(shape((b + 8, b), f32), shape((5 * b, b), f32), shape((8, cols), f32)),
        name="pick_pivots",
    )(owner, (m * per).reshape(1), front)
    for bit in bits(members):
        head = head + flip(head, "mem", bit)
    for bit in bits(members):
        rest = rest + flip(rest, "mem", bit)
    table = head[b, :count].astype(jnp.int32)

    starts = [g ^ CORE, g ^ (CORE | CHIP), g ^ CHIP, g]
    places = jnp.concatenate(
        [s * quarter_blocks + jnp.arange(quarter_blocks) for s in starts] + [jnp.arange(PR)]
    )
    source = jnp.take(table, places)
    kept = (source >= PL).astype(jnp.int32)
    ways = 4
    sent = 3 * quarter_blocks
    near_steps = 2 * quarter_blocks // ways
    steps = sent // ways

    def front_spec(i, n):
        return pl.BlockSpec((b, cols), lambda s, *pre, i=i: (pre[0][s * n + i], 0))

    mask_spec = pl.BlockSpec((8, cols), lambda s, *pre: (0, 0))
    tall = (ways * b, cols)

    def gather_kernel(*refs):
        gather_rows(ways, near_steps, *refs)

    near, far = pl.pallas_call(
        gather_kernel,
        grid_spec=pltpu.PrefetchScalarGridSpec(
            num_scalar_prefetch=2,
            grid=(steps,),
            in_specs=[front_spec(i, ways) for i in range(ways)] + [mask_spec],
            out_specs=[
                pl.BlockSpec(tall, lambda s, *pre: (jnp.minimum(s, near_steps - 1), 0)),
                pl.BlockSpec(tall, lambda s, *pre: (jnp.maximum(s - near_steps, 0), 0)),
            ],
        ),
        out_shape=(shape((2 * quarter, cols), f32), shape((quarter, cols), f32)),
        cost_estimate=cost(6),
        name="gather_rows",
    )(source[:sent], kept[:sent], *([front] * ways), mask)
    near = flip(near, "grp", CORE)

    def first_kernel(*refs):
        add_rows(PR, False, *refs)

    first = pl.pallas_call(
        first_kernel,
        grid_spec=pltpu.PrefetchScalarGridSpec(
            num_scalar_prefetch=3,
            grid=(1,),
            in_specs=[front_spec(i, PR) for i in range(PR)]
            + [mask_spec, pl.BlockSpec((pr, cols), lambda s, *pre: (0, 0))],
            out_specs=pl.BlockSpec((pr, cols), lambda s, *pre: (0, 0)),
        ),
        out_shape=shape((pr, cols), f32),
        cost_estimate=cost(2),
        name="first_rows",
    )(
        source[sent + quarter_blocks :], kept[sent + quarter_blocks :],
        (g == 0).astype(jnp.int32).reshape(1), *([front] * PR), mask, root_front,
    )
    first = first + flip(first, "grp", CORE)
    first = first + flip(first, "grp", CHIP)

    work = [pltpu.VMEM((b, 2 * b), f32)]
    sq = shape((b, b), f32)
    sqh = shape((b, b), bf16)
    logs = shape((8, b), f32)

    def w_spec(k):
        return pl.BlockSpec((b, cols), lambda i: (k, 0))

    p0, inv0, log0 = pl.pallas_call(
        leaf_first,
        grid=(1,),
        in_specs=[vmem, w_spec(0), vmem],
        out_specs=[vmem, vmem, vmem],
        out_shape=(shape((b, cols), bf16), sq, logs),
        scratch_shapes=work,
        cost_estimate=cost(6),
        name="leaf_first",
    )(head, front, mask)

    far = far + near[quarter:]
    rest, far = lax.optimization_barrier((rest, far))
    far = flip(far, "grp", CHIP)

    p12, leaf_log = pl.pallas_call(
        leaf_others,
        grid=(1,),
        in_specs=[vmem, w_spec(1), w_spec(2), vmem, vmem, vmem, vmem],
        out_specs=[vmem, vmem],
        out_shape=(shape((2 * b, cols), bf16), logs),
        scratch_shapes=[pltpu.VMEM((b, b), f32)] + work,
        cost_estimate=cost(12),
        name="leaf_others",
    )(rest, front, front, mask, inv0, p0, log0)

    def base_kernel(*refs):
        add_rows(ways, True, *refs)

    base = pl.pallas_call(
        base_kernel,
        grid_spec=pltpu.PrefetchScalarGridSpec(
            num_scalar_prefetch=3,
            grid=(quarter_blocks // ways,),
            in_specs=[front_spec(i, ways) for i in range(ways)]
            + [mask_spec]
            + [pl.BlockSpec(tall, lambda s, *pre: (s, 0))] * 2,
            out_specs=pl.BlockSpec(tall, lambda s, *pre: (s, 0)),
        ),
        out_shape=shape((quarter, cols), f32),
        cost_estimate=cost(4),
        name="base_rows",
    )(
        source[sent : sent + quarter_blocks], kept[sent : sent + quarter_blocks],
        jnp.ones((1,), jnp.int32), *([front] * ways), mask, root_front, near,
    )

    def to_rows(value):
        stages = [([0], value)]
        held = value
        for bit in reversed(bits(groups)):
            have = [h for offsets, _ in stages for h in offsets]
            pairs = []
            for gi in range(groups):
                for h in have:
                    for j in range(spread):
                        src = (gi ^ h) * spread + j
                        dst = (gi ^ h ^ bit) * spread + j
                        pairs.append((gi * members + src, gi * members + dst))
            got = lax.ppermute(held, ("grp", "mem"), pairs)
            new = [h ^ bit for h in have]
            held = jnp.where(among(new), got, held)
            stages.append((new, got))
        slots = [held]
        for i in range(1, spread):
            part = None
            for offsets, sent_part in stages:
                pairs = []
                for gi in range(groups):
                    for h in offsets:
                        for j in range(spread):
                            at = gi * members + (gi ^ h) * spread
                            pairs.append((at + j, at + (j ^ i)))
                got = lax.ppermute(sent_part, ("grp", "mem"), pairs)
                part = got if part is None else jnp.where(among(offsets), got, part)
            slots.append(part)
        return slots

    def among(offsets):
        found = jnp.zeros((), jnp.bool_)
        for h in offsets:
            found = found | (zone == (g ^ h))
        return found

    def from_first(value):
        value = value[:, :lead_cols]
        parts = []
        for root in range(leads):
            held = value
            for bit in reversed(bits(members)):
                pairs = [(root ^ i, root ^ i ^ bit) for i in range(0, members, 2 * bit)]
                got = lax.ppermute(held, "mem", pairs)
                held = jnp.where((m ^ root) % (2 * bit) == bit, got, held)
            parts.append(held)
        return parts[0] if leads == 1 else jnp.concatenate(parts, axis=1)

    def across(value):
        far_value = flip(value, "grp", CHIP)
        both = jnp.concatenate([value, far_value], axis=0)
        return jnp.concatenate([both, flip(both, "grp", CORE)], axis=0)

    corner = from_first(first)
    d0 = across(p0)
    r0 = to_rows(d0)

    log_value = leaf_log[:1, :1]
    parts = []
    for _ in range(3):
        parts.append(log_value.astype(bf16))
        log_value = log_value - parts[-1].astype(f32)
    line = lax.broadcasted_iota(jnp.int32, (LOG_ROWS, lead_cols), 0)
    log_block = jnp.zeros((LOG_ROWS, lead_cols), bf16)
    for i, part in enumerate(parts):
        log_block = jnp.where(line == i, part, log_block)
    lead = jnp.concatenate([p0[:, :lead_cols], p12[:, :lead_cols], log_block], axis=0)
    lead = across(from_first(lead))
    d12 = across(p12)
    r12 = to_rows(d12)

    q, rinv0, rinv1, rx, root_log = pl.pallas_call(
        root_step,
        out_shape=(shape((pr, cols), bf16), sq, sq, sqh, logs),
        scratch_shapes=work,
        cost_estimate=cost(18),
        name="root_step",
    )(corner, lead, first, d0, d12)
    rq = to_rows(q)

    root_factor = jnp.zeros((quarter, cols), f32)
    for i in range(spread):
        start = (inner ^ i) * cols
        rows = g * quarter + start + jnp.arange(cols)
        part = lax.dynamic_slice_in_dim(base, start, cols, 0)
        part = part + lax.dynamic_slice_in_dim(far, start, cols, 0)
        part = part - tdot(r0[i], d0) - tdot(r12[i], d12)
        if leads == 1:
            q0 = mm_t(part[:, :b], rinv0)
            inside = part[:, b:pr] - jnp.dot(q0.astype(bf16), rx, preferred_element_type=f32)
            q1 = mm_t(inside, rinv1)
        else:
            q0, q1 = rq[i][:b].T.astype(f32), rq[i][b:].T.astype(f32)
        q1 = jnp.where((rows >= b)[:, None], q1, 0.0)
        panel = jnp.concatenate([q0, q1], axis=1)
        first_col = jnp.minimum(m, leads - 1) * lead_cols
        panel = lax.dynamic_slice_in_dim(panel, first_col, lead_cols, 1)
        part = jnp.where((rows >= pr)[:, None], part - tdot(rq[i], q), 0.0)
        head_cols = jnp.where(m < leads, panel, part[:, :lead_cols])
        part = jnp.concatenate([head_cols, part[:, lead_cols:]], axis=1)
        root_factor = lax.dynamic_update_slice_in_dim(root_factor, part, start, 0)

    pitch = lead.shape[0] // groups
    sums = [
        jnp.sum(lead[t * pitch + PL * b : t * pitch + PL * b + 3, 0].astype(f32))
        for t in range(groups)
    ]
    order_of = [0, CHIP, CORE, CORE | CHIP]
    log_list = []
    for leaf in range(groups):
        total = jnp.zeros((), f32)
        for at, bit in enumerate(order_of):
            total = total + jnp.where((g ^ bit) == leaf, sums[at], 0.0)
        log_list.append(total / (PL * b))
    log_det = jnp.stack(log_list + [root_log[0, 0] / pr])
    return root_factor, log_det


def solution(mesh):
    in_specs = (P("grp", None, "mem"), P("grp", "mem"), P("grp", "mem"))
    out_specs = (P("grp", "mem"), P())
    return jax.shard_map(local, mesh=mesh, in_specs=in_specs, out_specs=out_specs, check_vma=False)
```

time: 851 us -> 252 us (0.30)
  the two profiles are of different devices: /device:TPU:1 before, /device:TPU:3 now
where the time goes in v1:
time: 252 us; the launch traced here: 251 us
  waiting for transfers between devices  98.2 us (39%)
  starting transfers between devices  54.4 us (22%)
  Pallas kernels  43.7 us (17%)
  other arithmetic  16.7 us (7%)
  between operations  13.7 us (5%)
  matrix products  13.3 us (5%)
  local copies, waits for them, and re-layouts  11 us (4%)
    ppermute x16, waiting for transfers between devices, flip(): return lax.ppermute(value, axis, [(i, i ^ bit) for i in range(size)])  70.2 us
    ppermute x16, starting transfers between devices, flip(): return lax.ppermute(value, axis, [(i, i ^ bit) for i in range(size)])  22.1 us
    ppermute x9, waiting for transfers between devices, to_rows(): got = lax.ppermute(sent_part, ('grp', 'mem'), pairs)  20 us
    ppermute x9, starting transfers between devices, to_rows(): got = lax.ppermute(sent_part, ('grp', 'mem'), pairs)  14.4 us
    dot_general x6, matrix products, tdot(): lax.dot_general(lhs, rhs, (((0,), (0,)), ((), ())), preferred_element_typ...  11.4 us
    pallas_call x1, Pallas kernels, local(): pl.pallas_call(root_step, out_shape=(shape((pr, cols), bf16), sq, sq, sqh...  11 us
    ppermute x6, starting transfers between devices, from_first(): got = lax.ppermute(held, 'mem', pairs)  10.9 us
    pallas_call x1, Pallas kernels, local(): pl.pallas_call(leaf_others, grid=(1,), in_specs=[vmem, w_spec(1), w_spec(...  10.1 us
  transfers between devices with their start and end apart: 37, of which 13 were waited for; matrix products, arithmetic and copies ran while one was open for 14% of the time, Pallas kernels for 14%

profile of v1, /device:TPU:3, one launch (start us, length us, event | category | flops | bytes accessed | tf_op | source)
XLA Modules:
  0.0 251.0 jit_solution(855831781704831441)
XLA Ops:
  0.6 2.0 pick_pivots.1
  4.0 2.0 collective-permute-done
  6.9 1.4 collective-permute-start.1
  8.3 1.8 collective-permute-done.1
  10.1 2.4 collective-permute-start.2
  12.5 1.7 collective-permute-done.2
  15.6 7.7 %gather_rows.1 = (f32[2048,512]{1,0:T(8,128)}, f32[1024,512]{1,0:T(8,128)}) custom-call(s32[24]{0:T(128)} %bitcast.53, s32[24]{0:T(128)} %bitcast.52, f32[4096,512]{1,0:T(8,128)} %bitcast.39, f32[4096,512]{1,0:T(8,128)} %bitcast.40, f32[4096,512]{1,0:T(8,128)} %bitcast.41, f32[4096,512]{1,0:T(8,128)} %bitcast.42, ...), custom_call_target="tpu_custom_call" | custom-call | bytes 18000000 | tf_op jit(solution)/shard_map/gather_rows/pallas_call | solution.py:258
  23.3 4.2 %collective-permute-start.3 = (f32[2048,512]{1,0:T(8,128)}, f32[2048,512]{1,0:T(8,128)}, u32[]{:S(2)}, u32[]{:S(2)}) collective-permute-start(f32[2048,512]{1,0:T(8,128)} %get-tuple-element.21), channel_id=1, source_target_pairs={{0,8},{8,0},{16,24},{24,16},{1,9},{9,1},{17,25},{25,17},{2,10},{10... | collective-permute-start | bytes 12582920 | tf_op jit(solution)/shard_map/ppermute | solution.py:42
  27.5 5.3 %leaf_first.1 = (bf16[128,512]{1,0:T(8,128)(2,1)}, f32[128,128]{1,0:T(8,128)}, f32[8,128]{1,0:T(8,128)}) custom-call(f32[136,128]{1,0:T(8,128)} %copy-done.16, f32[4096,512]{1,0:T(8,128)} %bitcast.43, f32[8,512]{1,0:T(8,128)} %get-tuple-element.20.refs_6_.refs_7_.mask_ref.refs_5_), custom_call_target="tpu_custom_call" | custom-call | bytes 18000000 | tf_op jit(solution)/shard_map/leaf_first/pallas_call | solution.py:305
  32.8 1.5 collective-permute-start.4
  34.3 3.8 %collective-permute-done.8 = bf16[128,512]{1,0:T(8,128)(2,1)S(1)} collective-permute-done((bf16[128,512]{1,0:T(8,128)(2,1)}, bf16[128,512]{1,0:T(8,128)(2,1)S(1)}, u32[]{:S(2)}, u32[]{:S(2)}) %collective-permute-start.8) | collective-permute-done | bytes 131104 | tf_op jit(solution)/shard_map/ppermute | solution.py:42
  41.2 2.9 %first_rows.1 = f32[256,512]{1,0:T(8,128)} custom-call(s32[2]{0:T(128)} %slice.82.refs_0_, s32[2]{0:T(128)} %slice.83.refs_1_, s32[1]{0:T(128)} %bitcast.9.refs_2_, f32[4096,512]{1,0:T(8,128)} %bitcast.44, f32[4096,512]{1,0:T(8,128)} %bitcast.45, f32[8,512]{1,0:T(8,128)} %get-tuple-element.20.refs_6_.refs_7_.mask_ref.refs_5_, f32[1024,512]{1,0:T(8,128)} %refs_6_.1), custom_call_target="tpu_custom_call" | custom-call | bytes 6000000 | tf_op jit(solution)/shard_map/first_rows/pallas_call | solution.py:278
  44.2 1.4 collective-permute-start.5
  46.3 10.9 %collective-permute-done.5 = f32[640,128]{1,0:T(8,128)S(1)} collective-permute-done((f32[640,128]{1,0:T(8,128)S(1)}, f32[640,128]{1,0:T(8,128)S(1)}, u32[]{:S(2)}, u32[]{:S(2)}) %collective-permute-start.5) | collective-permute-done | bytes 327712 | tf_op jit(solution)/shard_map/ppermute | solution.py:42
  57.4 1.5 collective-permute-start.17
  60.2 1.6 collective-permute-start.30
  61.8 14.5 %collective-permute-done.6 = f32[640,128]{1,0:T(8,128)S(1)} collective-permute-done((f32[640,128]{1,0:T(8,128)S(1)}, f32[640,128]{1,0:T(8,128)S(1)}, u32[]{:S(2)}, u32[]{:S(2)}) %collective-permute-start.6) | collective-permute-done | bytes 327712 | tf_op jit(solution)/shard_map/ppermute | solution.py:42
  78.5 1.5 collective-permute-start.18
  80.0 3.4 %slice_add_fusion = f32[1024,512]{1,0:T(8,128)} fusion(f32[1024,512]{1,0:T(8,128)S(1)} %copy-done.8, f32[2048,512]{1,0:T(8,128)} %collective-permute-done.3.refs_9_), kind=kLoop, calls=%fused_computation.1 | loop fusion | flops 524288 | bytes 6291456 | tf_op jit(solution)/shard_map/add | solution.py:316
  83.4 10.1 %leaf_others.1 = (bf16[256,512]{1,0:T(8,128)(2,1)}, f32[8,128]{1,0:T(8,128)}) custom-call(f32[640,128]{1,0:T(8,128)} %add.240.rest_ref, f32[4096,512]{1,0:T(8,128)} %bitcast.46, f32[4096,512]{1,0:T(8,128)} %bitcast.47, f32[8,512]{1,0:T(8,128)} %get-tuple-element.20.refs_6_.refs_7_.mask_ref.refs_5_, f32[128,128]{1,0:T(8,128)} %get-tuple-element.27.inv0_ref, ...), custom_call_target="tpu_custom_call" | custom-call | bytes 36000000 | tf_op jit(solution)/shard_map/leaf_others/pallas_call | solution.py:320
  97.0 1.3 collective-permute-start.21
  98.3 3.1 %collective-permute-done.12 = bf16[256,512]{1,0:T(8,128)(2,1)S(1)} collective-permute-done((bf16[256,512]{1,0:T(8,128)(2,1)}, bf16[256,512]{1,0:T(8,128)(2,1)S(1)}, u32[]{:S(2)}, u32[]{:S(2)}) %collective-permute-start.12) | collective-permute-done | bytes 262176 | tf_op jit(solution)/shard_map/ppermute | solution.py:42
  102.4 3.9 %collective-permute-start.13 = (bf16[512,512]{1,0:T(8,128)(2,1)S(1)}, bf16[512,512]{1,0:T(8,128)(2,1)S(1)}, u32[]{:S(2)}, u32[]{:S(2)}) collective-permute-start(bf16[512,512]{1,0:T(8,128)(2,1)S(1)} %pad_maximum_fusion.1), channel_id=1, source_target_pairs={{0,8},{8,0},{16,24},{24,16},{1,9},{9,1},{17,25},{25,17},{2,10},{10... | collective-permute-start | bytes 1572872 | tf_op jit(solution)/shard_map/ppermute | solution.py:42
  106.3 1.3 collective-permute-start.19
  107.8 1.3 collective-permute-start.22
  109.1 1.7 collective-permute-start.7
  110.9 7.0 %collective-permute-done.22 = bf16[400,256]{1,0:T(8,128)(2,1)S(1)} collective-permute-done((bf16[400,256]{1,0:T(8,128)(2,1)S(1)}, bf16[400,256]{1,0:T(8,128)(2,1)S(1)}, u32[]{:S(2)}, u32[]{:S(2)}) %collective-permute-start.22) | collective-permute-done | bytes 204832 | tf_op jit(solution)/shard_map/ppermute | solution.py:396
  120.0 2.5 fusion.15
  124.7 4.2 %collective-permute-start.20 = (f32[256,256]{1,0:T(8,128)S(1)}, f32[256,256]{1,0:T(8,128)S(1)}, u32[]{:S(2)}, u32[]{:S(2)}) collective-permute-start(f32[256,256]{1,0:T(8,128)S(1)} %broadcast_select_fusion.7), channel_id=1, source_target_pairs={{0,1},{2,3},{4,5},{6,7},{8,9},{10,11},{12,13},{14,15},{16,17},{18,... | collective-permute-start | bytes 786440 | tf_op jit(solution)/shard_map/ppermute | solution.py:396
  128.9 32.4 %collective-permute-done.24 = bf16[400,256]{1,0:T(8,128)(2,1)S(1)} collective-permute-done((bf16[400,256]{1,0:T(8,128)(2,1)S(1)}, bf16[400,256]{1,0:T(8,128)(2,1)S(1)}, u32[]{:S(2)}, u32[]{:S(2)}) %collective-permute-start.24) | collective-permute-done | bytes 204832 | tf_op jit(solution)/shard_map/ppermute | solution.py:42
  163.8 1.5 collective-permute-start.15
  166.1 4.8 %base_rows.1 = f32[1024,512]{1,0:T(8,128)} custom-call(s32[8]{0:T(128)} %slice.76.refs_0_, s32[8]{0:T(128)} %slice.77.refs_1_, s32[1]{0:T(128)} %constant.98.clone.1.refs_2_, f32[4096,512]{1,0:T(8,128)} %bitcast.48, f32[4096,512]{1,0:T(8,128)} %bitcast.49, f32[4096,512]{1,0:T(8,128)} %bitcast.50, f32[4096,512]{1,0:T(8,128)} %bitcast.51, ...), custom_call_target="tpu_custom_call" | custom-call | bytes 12000000 | tf_op jit(solution)/shard_map/base_rows/pallas_call | solution.py:334
  171.9 11.0 %root_step.1 = (bf16[256,512]{1,0:T(8,128)(2,1)}, f32[128,128]{1,0:T(8,128)}, f32[128,128]{1,0:T(8,128)}, bf16[128,128]{1,0:T(8,128)(2,1)}, f32[8,128]{1,0:T(8,128)}) custom-call(f32[256,256]{1,0:T(8,128)} %broadcast_select_fusion.8.corner_ref, bf16[1600,256]{1,0:T(8,128)(2,1)} %pad_maximum_fusion.lead_ref, f32[256,512]{1,0:T(8,128)} %copy-done.5, ...), custom_call_target="tpu_custom_call" | custom-call | bytes 54000000 | tf_op jit(solution)/shard_map/root_step/pallas_call | solution.py:424
  182.9 1.4 collective-permute-start.26
  187.4 1.7 collective-permute-start.33
  200.7 1.7 broadcast_select_fusion.2
  202.4 1.4 collective-permute-start.27
  203.9 1.6 collective-permute-start.32
  205.5 1.9 collective-permute-start.31
  207.4 2.9 %subtract_subtract_fusion = f32[512,512]{1,0:T(8,128)S(1)} fusion(f32[512,512]{1,0:T(8,128)} %fusion.15, f32[1024,512]{1,0:T(8,128)} %collective-permute-done.7, s32[]{:T(128)S(6)} %select_n.256, f32[1024,512]{1,0:T(8,128)} %base_rows.1, bf16[1024,512]{1,0:T(8,128)(2,1)S(1)} %copy-done.1, bf16[1024,512]{1,0:T(8,128)(2,1)} %collective-permute-done.15, ...), kind=kOutput, calls=%fused_computation.17 | convolution fusion | flops 538181632 | bytes 7340037 | tf_op jit(solution)/shard_map/dot_general | solution.py:29
  214.3 3.4 %collective-permute-start.28 = (bf16[512,512]{1,0:T(8,128)(2,1)}, bf16[512,512]{1,0:T(8,128)(2,1)S(1)}, u32[]{:S(2)}, u32[]{:S(2)}) collective-permute-start(bf16[512,512]{1,0:T(8,128)(2,1)} %collective-permute-done.11), channel_id=1, source_target_pairs={{2,3},{3,2},{6,7},{7,6},{8,9},{9,8},{12,13},{13,12},{22,23},{23,22... | collective-permute-start | bytes 1572872 | tf_op jit(solution)/shard_map/ppermute | solution.py:378
  217.7 1.6 broadcast_in_dim.76
  221.3 11.4 %collective-permute-done.31 = bf16[1024,512]{1,0:T(8,128)(2,1)} collective-permute-done((bf16[1024,512]{1,0:T(8,128)(2,1)}, bf16[1024,512]{1,0:T(8,128)(2,1)}, u32[]{:S(2)}, u32[]{:S(2)}) %collective-permute-start.31) | collective-permute-done | bytes 1048608 | tf_op jit(solution)/shard_map/ppermute | solution.py:378
  233.3 2.3 fusion.3
  235.7 2.0 collective-permute-start.34
  237.7 6.0 %collective-permute-done.28 = bf16[512,512]{1,0:T(8,128)(2,1)S(1)} collective-permute-done((bf16[512,512]{1,0:T(8,128)(2,1)}, bf16[512,512]{1,0:T(8,128)(2,1)S(1)}, u32[]{:S(2)}, u32[]{:S(2)}) %collective-permute-start.28) | collective-permute-done | bytes 524320 | tf_op jit(solution)/shard_map/ppermute | solution.py:378
  243.8 2.0 fusion
  246.9 2.5 collective-permute-done.34
  (160 shorter events, 36.0 us)
Async XLA Ops:
  2.6 3.4 %collective-permute-start = (f32[136,128]{1,0:T(8,128)}, f32[136,128]{1,0:T(8,128)S(1)}, u32[]{:S(2)}, u32[]{:S(2)}) collective-permute-start(f32[136,128]{1,0:T(8,128)} %get-tuple-element.19), channel_id=1, source_target_pairs={{0,1},{1,0},{2,3},{3,2},{4,5},{5,4},{6,7},{7,6},{8,9},{9,8},{10,11... | collective-permute-start | bytes 208904 | tf_op jit(solution)/shard_map/ppermute | solution.py:42
  6.9 3.2 %collective-permute-start.1 = (f32[136,128]{1,0:T(8,128)S(1)}, f32[136,128]{1,0:T(8,128)S(1)}, u32[]{:S(2)}, u32[]{:S(2)}) collective-permute-start(f32[136,128]{1,0:T(8,128)S(1)} %add.231), channel_id=1, source_target_pairs={{0,2},{1,3},{2,0},{3,1},{4,6},{5,7},{6,4},{7,5},{8,10},{9,11},{10,... | collective-permute-start | bytes 208904 | tf_op jit(solution)/shard_map/ppermute | solution.py:42
  10.1 4.1 %collective-permute-start.2 = (f32[136,128]{1,0:T(8,128)S(1)}, f32[136,128]{1,0:T(8,128)S(1)}, u32[]{:S(2)}, u32[]{:S(2)}) collective-permute-start(f32[136,128]{1,0:T(8,128)S(1)} %add.232), channel_id=1, source_target_pairs={{0,4},{1,5},{2,6},{3,7},{4,0},{5,1},{6,2},{7,3},{8,12},{9,13},{10,... | collective-permute-start | bytes 208904 | tf_op jit(solution)/shard_map/ppermute | solution.py:42
  23.3 16.6 %copy-start.22 = (s32[34]{0:T(128)S(1)}, s32[34]{0:T(128)}, u32[]{:S(2)}) copy-start(s32[34]{0:T(128)} %get-tuple-element.39) | copy-start | bytes 412
  23.3 17.3 %copy-start.21 = (s32[34]{0:T(128)S(1)}, s32[34]{0:T(128)}, u32[]{:S(2)}) copy-start(s32[34]{0:T(128)} %get-tuple-element.38) | copy-start | bytes 412
  23.3 56.7 %collective-permute-start.3 = (f32[2048,512]{1,0:T(8,128)}, f32[2048,512]{1,0:T(8,128)}, u32[]{:S(2)}, u32[]{:S(2)}) collective-permute-start(f32[2048,512]{1,0:T(8,128)} %get-tuple-element.21), channel_id=1, source_target_pairs={{0,8},{8,0},{16,24},{24,16},{1,9},{9,1},{17,25},{25,17},{2,10},{10... | collective-permute-start | bytes 12582920 | tf_op jit(solution)/shard_map/ppermute | solution.py:42
  32.8 5.3 %collective-permute-start.8 = (bf16[128,512]{1,0:T(8,128)(2,1)}, bf16[128,512]{1,0:T(8,128)(2,1)S(1)}, u32[]{:S(2)}, u32[]{:S(2)}) collective-permute-start(bf16[128,512]{1,0:T(8,128)(2,1)} %get-tuple-element.25.p0_ref), channel_id=1, source_target_pairs={{0,16},{8,24},{16,0},{24,8},{1,17},{9,25},{17,1},{25,9},{2,18},{10... | collective-permute-start | bytes 393224 | tf_op jit(solution)/shard_map/ppermute | solution.py:42
  32.8 11.3 %collective-permute-start.4 = (f32[640,128]{1,0:T(8,128)S(1)}, f32[640,128]{1,0:T(8,128)S(1)}, u32[]{:S(2)}, u32[]{:S(2)}) collective-permute-start(f32[640,128]{1,0:T(8,128)S(1)} %copy-done.15), channel_id=1, source_target_pairs={{0,1},{1,0},{2,3},{3,2},{4,5},{5,4},{6,7},{7,6},{8,9},{9,8},{10,11... | collective-permute-start | bytes 983048 | tf_op jit(solution)/shard_map/ppermute | solution.py:42
  39.0 6.5 %collective-permute-start.9 = (bf16[256,512]{1,0:T(8,128)(2,1)S(1)}, bf16[256,512]{1,0:T(8,128)(2,1)S(1)}, u32[]{:S(2)}, u32[]{:S(2)}) collective-permute-start(bf16[256,512]{1,0:T(8,128)(2,1)S(1)} %pad_maximum_fusion.3), channel_id=1, source_target_pairs={{0,8},{8,0},{16,24},{24,16},{1,9},{9,1},{17,25},{25,17},{2,10},{10... | collective-permute-start | bytes 786440 | tf_op jit(solution)/shard_map/ppermute | solution.py:42
  44.1 13.3 %copy-start.9 = (f32[256,512]{1,0:T(8,128)S(1)}, f32[256,512]{1,0:T(8,128)}, u32[]{:S(2)}) copy-start(f32[256,512]{1,0:T(8,128)} %first_rows.1) | copy-start | bytes 1572868
  44.1 13.3 %collective-permute-start.16 = (f32[256,512]{1,0:T(8,128)}, f32[256,512]{1,0:T(8,128)S(1)}, u32[]{:S(2)}, u32[]{:S(2)}) collective-permute-start(f32[256,512]{1,0:T(8,128)} %first_rows.1), channel_id=1, source_target_pairs={{0,8},{8,0},{16,24},{24,16},{1,9},{9,1},{17,25},{25,17},{2,10},{10... | collective-permute-start | bytes 1572872 | tf_op jit(solution)/shard_map/ppermute | solution.py:42
  44.2 13.1 %collective-permute-start.5 = (f32[640,128]{1,0:T(8,128)S(1)}, f32[640,128]{1,0:T(8,128)S(1)}, u32[]{:S(2)}, u32[]{:S(2)}) collective-permute-start(f32[640,128]{1,0:T(8,128)S(1)} %add.238), channel_id=1, source_target_pairs={{0,2},{1,3},{2,0},{3,1},{4,6},{5,7},{6,4},{7,5},{8,10},{9,11},{10,... | collective-permute-start | bytes 983048 | tf_op jit(solution)/shard_map/ppermute | solution.py:42
  45.6 74.4 %copy-start.2 = (bf16[512,512]{1,0:T(8,128)(2,1)}, bf16[512,512]{1,0:T(8,128)(2,1)S(1)}, u32[]{:S(2)}) copy-start(bf16[512,512]{1,0:T(8,128)(2,1)S(1)} %constant_dynamic-update-slice_fusion.d0_ref) | copy-start | bytes 1572868
  45.6 31.4 %collective-permute-start.10 = (bf16[512,512]{1,0:T(8,128)(2,1)S(1)}, bf16[512,512]{1,0:T(8,128)(2,1)S(1)}, u32[]{:S(2)}, u32[]{:S(2)}) collective-permute-start(bf16[512,512]{1,0:T(8,128)(2,1)S(1)} %constant_dynamic-update-slice_fusion.d0_ref), channel_id=1, source_target_pairs={{0,4},{1,5},{10,14},{11,15},{20,16},{21,17},{30,26},{31,27}} | collective-permute-start | bytes 1572872 | tf_op jit(solution)/shard_map/ppermute | solution.py:364
  57.2 19.0 %collective-permute-start.6 = (f32[640,128]{1,0:T(8,128)S(1)}, f32[640,128]{1,0:T(8,128)S(1)}, u32[]{:S(2)}, u32[]{:S(2)}) collective-permute-start(f32[640,128]{1,0:T(8,128)S(1)} %add.239), channel_id=1, source_target_pairs={{0,4},{1,5},{2,6},{3,7},{4,0},{5,1},{6,2},{7,3},{8,12},{9,13},{10,... | collective-permute-start | bytes 983048 | tf_op jit(solution)/shard_map/ppermute | solution.py:42
  57.4 21.0 %collective-permute-start.17 = (f32[256,512]{1,0:T(8,128)S(1)}, f32[256,512]{1,0:T(8,128)S(1)}, u32[]{:S(2)}, u32[]{:S(2)}) collective-permute-start(f32[256,512]{1,0:T(8,128)S(1)} %add.245), channel_id=1, source_target_pairs={{0,16},{8,24},{16,0},{24,8},{1,17},{9,25},{17,1},{25,9},{2,18},{10... | collective-permute-start | bytes 1572872 | tf_op jit(solution)/shard_map/ppermute | solution.py:42
  60.2 19.9 %copy-start.8 = (f32[1024,512]{1,0:T(8,128)S(1)}, f32[1024,512]{1,0:T(8,128)}, u32[]{:S(2)}) copy-start(f32[1024,512]{1,0:T(8,128)} %get-tuple-element.23) | copy-start | bytes 6291460
  60.2 175.5 %collective-permute-start.30 = (bf16[512,512]{1,0:T(8,128)(2,1)S(1)}, bf16[512,512]{1,0:T(8,128)(2,1)}, u32[]{:S(2)}, u32[]{:S(2)}) collective-permute-start(bf16[512,512]{1,0:T(8,128)(2,1)S(1)} %constant_dynamic-update-slice_fusion.d0_ref), channel_id=1, source_target_pairs={{0,1},{1,0},{10,11},{11,10},{20,21},{21,20},{30,31},{31,30}} | collective-permute-start | bytes 1572872 | tf_op jit(solution)/shard_map/ppermute | solution.py:378
  77.1 41.6 %collective-permute-start.11 = (bf16[512,512]{1,0:T(8,128)(2,1)S(1)}, bf16[512,512]{1,0:T(8,128)(2,1)}, u32[]{:S(2)}, u32[]{:S(2)}) collective-permute-start(bf16[512,512]{1,0:T(8,128)(2,1)S(1)} %broadcast_select_fusion.1), channel_id=1, source_target_pairs={{0,2},{1,3},{4,6},{5,7},{10,8},{11,9},{14,12},{15,13},{20,22},{21,... | collective-permute-start | bytes 1572872 | tf_op jit(solution)/shard_map/ppermute | solution.py:364
  78.5 27.8 %copy-start.5 = (f32[256,512]{1,0:T(8,128)}, f32[256,512]{1,0:T(8,128)S(1)}, u32[]{:S(2)}) copy-start(f32[256,512]{1,0:T(8,128)S(1)} %add.246.first_ref) | copy-start | bytes 1572868
  78.5 27.8 %collective-permute-start.18 = (f32[256,256]{1,0:T(8,128)S(1)}, f32[256,256]{1,0:T(8,128)S(1)}, u32[]{:S(2)}, u32[]{:S(2)}) collective-permute-start(f32[256,256]{1,0:T(8,128)S(1)} %slice.105), channel_id=1, source_target_pairs={{0,4},{8,12},{16,20},{24,28}} | collective-permute-start | bytes 786440 | tf_op jit(solution)/shard_map/ppermute | solution.py:396
  93.5 14.1 %copy-start.10 = (bf16[256,512]{1,0:T(8,128)(2,1)S(1)}, bf16[256,512]{1,0:T(8,128)(2,1)}, u32[]{:S(2)}) copy-start(bf16[256,512]{1,0:T(8,128)(2,1)} %get-tuple-element.29) | copy-start | bytes 786436
  95.9 5.5 %collective-permute-start.12 = (bf16[256,512]{1,0:T(8,128)(2,1)}, bf16[256,512]{1,0:T(8,128)(2,1)S(1)}, u32[]{:S(2)}, u32[]{:S(2)}) collective-permute-start(bf16[256,512]{1,0:T(8,128)(2,1)} %get-tuple-element.29), channel_id=1, source_target_pairs={{0,16},{8,24},{16,0},{24,8},{1,17},{9,25},{17,1},{25,9},{2,18},{10... | collective-permute-start | bytes 786440 | tf_op jit(solution)/shard_map/ppermute | solution.py:42
  97.0 10.7 %collective-permute-start.21 = (bf16[400,256]{1,0:T(8,128)(2,1)S(1)}, bf16[400,256]{1,0:T(8,128)(2,1)S(1)}, u32[]{:S(2)}, u32[]{:S(2)}) collective-permute-start(bf16[400,256]{1,0:T(8,128)(2,1)S(1)} %pad_maximum_fusion.4), channel_id=1, source_target_pairs={{0,4},{8,12},{16,20},{24,28}} | collective-permute-start | bytes 614408 | tf_op jit(solution)/shard_map/ppermute | solution.py:396
  102.4 6.7 %collective-permute-start.13 = (bf16[512,512]{1,0:T(8,128)(2,1)S(1)}, bf16[512,512]{1,0:T(8,128)(2,1)S(1)}, u32[]{:S(2)}, u32[]{:S(2)}) collective-permute-start(bf16[512,512]{1,0:T(8,128)(2,1)S(1)} %pad_maximum_fusion.1), channel_id=1, source_target_pairs={{0,8},{8,0},{16,24},{24,16},{1,9},{9,1},{17,25},{25,17},{2,10},{10... | collective-permute-start | bytes 1572872 | tf_op jit(solution)/shard_map/ppermute | solution.py:42
  106.3 18.3 %collective-permute-start.19 = (f32[256,256]{1,0:T(8,128)S(1)}, f32[256,256]{1,0:T(8,128)S(1)}, u32[]{:S(2)}, u32[]{:S(2)}) collective-permute-start(f32[256,256]{1,0:T(8,128)S(1)} %broadcast_select_fusion.6), channel_id=1, source_target_pairs={{0,2},{4,6},{8,10},{12,14},{16,18},{20,22},{24,26},{28,30}} | collective-permute-start | bytes 786440 | tf_op jit(solution)/shard_map/ppermute | solution.py:396
  107.8 10.2 %collective-permute-start.22 = (bf16[400,256]{1,0:T(8,128)(2,1)S(1)}, bf16[400,256]{1,0:T(8,128)(2,1)S(1)}, u32[]{:S(2)}, u32[]{:S(2)}) collective-permute-start(bf16[400,256]{1,0:T(8,128)(2,1)S(1)} %broadcast_select_fusion.3), channel_id=1, source_target_pairs={{0,2},{4,6},{8,10},{12,14},{16,18},{20,22},{24,26},{28,30}} | collective-permute-start | bytes 614408 | tf_op jit(solution)/shard_map/ppermute | solution.py:396
  109.1 94.7 %collective-permute-start.7 = (f32[1024,512]{1,0:T(8,128)}, f32[1024,512]{1,0:T(8,128)}, u32[]{:S(2)}, u32[]{:S(2)}) collective-permute-start(f32[1024,512]{1,0:T(8,128)} %slice_add_fusion), channel_id=1, source_target_pairs={{0,16},{8,24},{16,0},{24,8},{1,17},{9,25},{17,1},{25,9},{2,18},{10... | collective-permute-start | bytes 6291464 | tf_op jit(solution)/shard_map/ppermute | solution.py:42
  110.9 51.9 %copy-start = (bf16[1024,512]{1,0:T(8,128)(2,1)}, bf16[1024,512]{1,0:T(8,128)(2,1)S(1)}, u32[]{:S(2)}) copy-start(bf16[1024,512]{1,0:T(8,128)(2,1)S(1)} %constant_dynamic-update-slice_fusion.3.d12_ref) | copy-start | bytes 3145732
  117.9 44.9 %collective-permute-start.14 = (bf16[1024,512]{1,0:T(8,128)(2,1)S(1)}, bf16[1024,512]{1,0:T(8,128)(2,1)S(1)}, u32[]{:S(2)}, u32[]{:S(2)}) collective-permute-start(bf16[1024,512]{1,0:T(8,128)(2,1)S(1)} %constant_dynamic-update-slice_fusion.3.d12_ref), channel_id=1, source_target_pairs={{0,4},{1,5},{10,14},{11,15},{20,16},{21,17},{30,26},{31,27}} | collective-permute-start | bytes 3145736 | tf_op jit(solution)/shard_map/ppermute | solution.py:364
  118.7 4.8 %collective-permute-start.23 = (bf16[400,256]{1,0:T(8,128)(2,1)S(1)}, bf16[400,256]{1,0:T(8,128)(2,1)S(1)}, u32[]{:S(2)}, u32[]{:S(2)}) collective-permute-start(bf16[400,256]{1,0:T(8,128)(2,1)S(1)} %broadcast_select_fusion.4), channel_id=1, source_target_pairs={{0,1},{2,3},{4,5},{6,7},{8,9},{10,11},{12,13},{14,15},{16,17},{18,... | collective-permute-start | bytes 614408 | tf_op jit(solution)/shard_map/ppermute | solution.py:396
  123.5 37.9 %collective-permute-start.24 = (bf16[400,256]{1,0:T(8,128)(2,1)S(1)}, bf16[400,256]{1,0:T(8,128)(2,1)S(1)}, u32[]{:S(2)}, u32[]{:S(2)}) collective-permute-start(bf16[400,256]{1,0:T(8,128)(2,1)S(1)} %broadcast_select_fusion.5), channel_id=1, source_target_pairs={{0,16},{8,24},{16,0},{24,8},{1,17},{9,25},{17,1},{25,9},{2,18},{10... | collective-permute-start | bytes 614408 | tf_op jit(solution)/shard_map/ppermute | solution.py:42
  124.7 40.6 %collective-permute-start.20 = (f32[256,256]{1,0:T(8,128)S(1)}, f32[256,256]{1,0:T(8,128)S(1)}, u32[]{:S(2)}, u32[]{:S(2)}) collective-permute-start(f32[256,256]{1,0:T(8,128)S(1)} %broadcast_select_fusion.7), channel_id=1, source_target_pairs={{0,1},{2,3},{4,5},{6,7},{8,9},{10,11},{12,13},{14,15},{16,17},{18,... | collective-permute-start | bytes 786440 | tf_op jit(solution)/shard_map/ppermute | solution.py:396
  162.1 8.7 %collective-permute-start.25 = (bf16[800,256]{1,0:T(8,128)(2,1)}, bf16[800,256]{1,0:T(8,128)(2,1)S(1)}, u32[]{:S(2)}, u32[]{:S(2)}) collective-permute-start(bf16[800,256]{1,0:T(8,128)(2,1)} %pad_maximum_fusion.2), channel_id=1, source_target_pairs={{0,8},{8,0},{16,24},{24,16},{1,9},{9,1},{17,25},{25,17},{2,10},{10... | collective-permute-start | bytes 1228808 | tf_op jit(solution)/shard_map/ppermute | solution.py:42
  163.8 41.7 %collective-permute-start.15 = (bf16[1024,512]{1,0:T(8,128)(2,1)S(1)}, bf16[1024,512]{1,0:T(8,128)(2,1)}, u32[]{:S(2)}, u32[]{:S(2)}) collective-permute-start(bf16[1024,512]{1,0:T(8,128)(2,1)S(1)} %broadcast_select_fusion), channel_id=1, source_target_pairs={{0,2},{1,3},{4,6},{5,7},{10,8},{11,9},{14,12},{15,13},{20,22},{21,... | collective-permute-start | bytes 3145736 | tf_op jit(solution)/shard_map/ppermute | solution.py:364
  170.8 16.5 %copy-start.1 = (bf16[1024,512]{1,0:T(8,128)(2,1)S(1)}, bf16[1024,512]{1,0:T(8,128)(2,1)}, u32[]{:S(2)}) copy-start(bf16[1024,512]{1,0:T(8,128)(2,1)} %copy-done) | copy-start | bytes 3145732
  182.9 17.9 %collective-permute-start.26 = (bf16[256,512]{1,0:T(8,128)(2,1)}, bf16[256,512]{1,0:T(8,128)(2,1)}, u32[]{:S(2)}, u32[]{:S(2)}) collective-permute-start(bf16[256,512]{1,0:T(8,128)(2,1)} %get-tuple-element.34), channel_id=1, source_target_pairs={{0,4},{1,5},{10,14},{11,15},{20,16},{21,17},{30,26},{31,27}} | collective-permute-start | bytes 786440 | tf_op jit(solution)/shard_map/ppermute | solution.py:364
  187.4 26.9 %collective-permute-start.33 = (bf16[1024,512]{1,0:T(8,128)(2,1)S(1)}, bf16[1024,512]{1,0:T(8,128)(2,1)}, u32[]{:S(2)}, u32[]{:S(2)}) collective-permute-start(bf16[1024,512]{1,0:T(8,128)(2,1)S(1)} %copy-done.1), channel_id=1, source_target_pairs={{0,1},{1,0},{10,11},{11,10},{20,21},{21,20},{30,31},{31,30}} | collective-permute-start | bytes 3145736 | tf_op jit(solution)/shard_map/ppermute | solution.py:378
  202.4 9.8 %collective-permute-start.27 = (bf16[256,512]{1,0:T(8,128)(2,1)}, bf16[256,512]{1,0:T(8,128)(2,1)}, u32[]{:S(2)}, u32[]{:S(2)}) collective-permute-start(bf16[256,512]{1,0:T(8,128)(2,1)} %broadcast_select_fusion.2), channel_id=1, source_target_pairs={{0,2},{1,3},{4,6},{5,7},{10,8},{11,9},{14,12},{15,13},{20,22},{21,... | collective-permute-start | bytes 786440 | tf_op jit(solution)/shard_map/ppermute | solution.py:364
  203.9 16.6 %collective-permute-start.32 = (bf16[1024,512]{1,0:T(8,128)(2,1)}, bf16[1024,512]{1,0:T(8,128)(2,1)}, u32[]{:S(2)}, u32[]{:S(2)}) collective-permute-start(bf16[1024,512]{1,0:T(8,128)(2,1)} %copy-done.12), channel_id=1, source_target_pairs={{4,5},{5,4},{14,15},{15,14},{16,17},{17,16},{26,27},{27,26}} | collective-permute-start | bytes 3145736 | tf_op jit(solution)/shard_map/ppermute | solution.py:378
  205.5 27.2 %collective-permute-start.31 = (bf16[1024,512]{1,0:T(8,128)(2,1)}, bf16[1024,512]{1,0:T(8,128)(2,1)}, u32[]{:S(2)}, u32[]{:S(2)}) collective-permute-start(bf16[1024,512]{1,0:T(8,128)(2,1)} %collective-permute-done.15), channel_id=1, source_target_pairs={{2,3},{3,2},{6,7},{7,6},{8,9},{9,8},{12,13},{13,12},{22,23},{23,22... | collective-permute-start | bytes 3145736 | tf_op jit(solution)/shard_map/ppermute | solution.py:378
  212.2 25.5 %collective-permute-start.29 = (bf16[512,512]{1,0:T(8,128)(2,1)}, bf16[512,512]{1,0:T(8,128)(2,1)S(1)}, u32[]{:S(2)}, u32[]{:S(2)}) collective-permute-start(bf16[512,512]{1,0:T(8,128)(2,1)} %copy-done.14), channel_id=1, source_target_pairs={{4,5},{5,4},{14,15},{15,14},{16,17},{17,16},{26,27},{27,26}} | collective-permute-start | bytes 1572872 | tf_op jit(solution)/shard_map/ppermute | solution.py:378
  214.3 29.5 %collective-permute-start.28 = (bf16[512,512]{1,0:T(8,128)(2,1)}, bf16[512,512]{1,0:T(8,128)(2,1)S(1)}, u32[]{:S(2)}, u32[]{:S(2)}) collective-permute-start(bf16[512,512]{1,0:T(8,128)(2,1)} %collective-permute-done.11), channel_id=1, source_target_pairs={{2,3},{3,2},{6,7},{7,6},{8,9},{9,8},{12,13},{13,12},{22,23},{23,22... | collective-permute-start | bytes 1572872 | tf_op jit(solution)/shard_map/ppermute | solution.py:378
  220.5 23.3 %copy-start.3 = (bf16[512,512]{1,0:T(8,128)(2,1)S(1)}, bf16[512,512]{1,0:T(8,128)(2,1)}, u32[]{:S(2)}) copy-start(bf16[512,512]{1,0:T(8,128)(2,1)} %copy-done.2) | copy-start | bytes 1572868
  220.5 23.3 %copy-start.4 = (f32[1024,512]{1,0:T(8,128)S(1)}, f32[1024,512]{1,0:T(8,128)}, u32[]{:S(2)}) copy-start(f32[1024,512]{1,0:T(8,128)} %base_rows.1) | copy-start | bytes 6291460
  220.5 26.5 %collective-permute-start.36 = (bf16[256,512]{1,0:T(8,128)(2,1)S(1)}, bf16[256,512]{1,0:T(8,128)(2,1)S(1)}, u32[]{:S(2)}, u32[]{:S(2)}) collective-permute-start(bf16[256,512]{1,0:T(8,128)(2,1)S(1)} %copy-done.7), channel_id=1, source_target_pairs={{0,1},{1,0},{10,11},{11,10},{20,21},{21,20},{30,31},{31,30}} | collective-permute-start | bytes 786440 | tf_op jit(solution)/shard_map/ppermute | solution.py:378
  232.7 14.3 %collective-permute-start.35 = (bf16[256,512]{1,0:T(8,128)(2,1)}, bf16[256,512]{1,0:T(8,128)(2,1)S(1)}, u32[]{:S(2)}, u32[]{:S(2)}) collective-permute-start(bf16[256,512]{1,0:T(8,128)(2,1)} %collective-permute-done.26), channel_id=1, source_target_pairs={{4,5},{5,4},{14,15},{15,14},{16,17},{17,16},{26,27},{27,26}} | collective-permute-start | bytes 786440 | tf_op jit(solution)/shard_map/ppermute | solution.py:378
  235.7 13.7 %collective-permute-start.34 = (bf16[256,512]{1,0:T(8,128)(2,1)}, bf16[256,512]{1,0:T(8,128)(2,1)S(1)}, u32[]{:S(2)}, u32[]{:S(2)}) collective-permute-start(bf16[256,512]{1,0:T(8,128)(2,1)} %collective-permute-done.27), channel_id=1, source_target_pairs={{2,3},{3,2},{6,7},{7,6},{8,9},{9,8},{12,13},{13,12},{22,23},{23,22... | collective-permute-start | bytes 786440 | tf_op jit(solution)/shard_map/ppermute | solution.py:378
  (12 other events, 80.5 us)

commit v2 on v1

--- a/solution.py
+++ b/solution.py
@@ -44,10 +44,6 @@
 
 def shape(dims, dtype):
     return jax.ShapeDtypeStruct(dims, dtype)
-
-
-def cost(us):
-    return pl.CostEstimate(flops=0, bytes_accessed=int(us * 3.0e6), transcendentals=0)
 
 
 def invert_factor(block, work, inverse_ref):
@@ -90,7 +86,7 @@
     return log_sum
 
 
-def pick_pivots(owner_ref, at_ref, front_ref, head_ref, rest_ref, mask_ref):
+def pick_pivots(owner_ref, at_ref, front_ref, table_ref, head_ref, rest_ref, mask_ref, lead_ref):
     b = head_ref.shape[1]
     per = front_ref.shape[1] // b
     for k in range(PL):
@@ -101,44 +97,69 @@
         if k == 0:
             head_ref[:b, :] = total
         elif k == 1:
-            rest_ref[: 2 * b, :] = total
+            head_ref[b:, :] = total
         else:
-            rest_ref[2 * b :, :] = total
+            rest_ref[...] = total
     lane = lax.broadcasted_iota(jnp.int32, (8, b), 1)
     table = jnp.zeros((8, b), f32)
     for t in range(per):
         table = table + jnp.where(lane == at_ref[0] + t, owner_ref[t].astype(f32), 0.0)
         keep = jnp.where(owner_ref[t] >= PL, 1.0, 0.0).astype(f32)
         mask_ref[:, t * b : (t + 1) * b] = jnp.full((8, b), keep, f32)
-    head_ref[b:, :] = table
-
-
-def leaf_first(head_ref, w_ref, mask_ref, p_ref, inv_ref, log_ref, work):
-    b = w_ref.shape[0]
-    log_sum = invert_factor(head_ref[:b, :], work, inv_ref)
-    log_ref[...] = jnp.broadcast_to(log_sum, log_ref.shape)
-    panel = mm(inv_ref[...], w_ref[...])
-    p_ref[...] = jnp.where(mask_ref[:1, :] > 0.0, panel, 0.0).astype(bf16)
-
-
-def leaf_others(
-    rest_ref, w1_ref, w2_ref, mask_ref, inv0_ref, p0_ref, log0_ref, p_ref, log_ref, inv, work
+    table_ref[...] = table
+    lead_ref[...] = front_ref[:, : lead_ref.shape[1]]
+
+
+def leaf_two(head_ref, w0_ref, w1_ref, mask_ref, p_ref, inv0_ref, inv1_ref, x_ref, log_ref, work):
+    b = w0_ref.shape[0]
+    c00, c01, c11 = [head_ref[i * b : (i + 1) * b, :] for i in range(3)]
+    keep = mask_ref[:1, :] > 0.0
+    log0 = invert_factor(c00, work, inv0_ref)
+    x01 = mm(inv0_ref[...], c01).astype(bf16)
+    x_ref[...] = x01
+    p0 = mm(inv0_ref[...], w0_ref[...]).astype(bf16)
+    log1 = invert_factor(c11 - tdot(x01, x01), work, inv1_ref)
+    p1 = mm(inv1_ref[...], w1_ref[...] - tdot(x01, p0)).astype(bf16)
+    p_ref[:b, :] = jnp.where(keep, p0, jnp.zeros_like(p0))
+    p_ref[b:, :] = jnp.where(keep, p1, jnp.zeros_like(p1))
+    log_ref[...] = jnp.broadcast_to(log0 + log1, log_ref.shape)
+
+
+def leaf_last(
+    rest_ref, w2_ref, w_lead_ref, table_ref, mask_ref, p_ref, inv0_ref, inv1_ref, x_ref, log_ref,
+    p2_ref, lead_ref, inv, work,
 ):
-    b = w1_ref.shape[0]
-    c01, c11, c02, c12, c22 = [rest_ref[i * b : (i + 1) * b, :] for i in range(5)]
+    b = w2_ref.shape[0]
+    wide = lead_ref.shape[1]
+    c02, c12, c22 = [rest_ref[i * b : (i + 1) * b, :] for i in range(3)]
+    inv0, inv1, x01 = inv0_ref[...], inv1_ref[...], x_ref[...]
+    x02 = mm(inv0, c02).astype(bf16)
+    x12 = mm(inv1, c12 - tdot(x01, x02)).astype(bf16)
+    log2 = invert_factor(c22 - tdot(x02, x02) - tdot(x12, x12), work, inv)
+    inv2 = inv[...]
     keep = mask_ref[:1, :] > 0.0
-    p0 = p0_ref[...]
-    x01 = mm(inv0_ref[...], c01).astype(bf16)
-    log1 = invert_factor(c11 - tdot(x01, x01), work, inv)
-    x02 = mm(inv0_ref[...], c02).astype(bf16)
-    panel = mm(inv[...], w1_ref[...] - tdot(x01, p0))
-    p1 = jnp.where(keep, panel, 0.0).astype(bf16)
-    p_ref[:b, :] = p1
-    x12 = mm(inv[...], c12 - tdot(x01, x02)).astype(bf16)
-    log2 = invert_factor(c22 - tdot(x02, x02) - tdot(x12, x12), work, inv)
-    panel = mm(inv[...], w2_ref[...] - tdot(x02, p0) - tdot(x12, p1))
-    p_ref[b:, :] = jnp.where(keep, panel, 0.0).astype(bf16)
-    log_ref[...] = log0_ref[...] + jnp.broadcast_to(log1 + log2, log_ref.shape)
+    panel = mm(inv2, w2_ref[...] - tdot(x02, p_ref[:b, :]) - tdot(x12, p_ref[b:, :])).astype(bf16)
+    p2_ref[...] = jnp.where(keep, panel, jnp.zeros_like(panel))
+    lane = lax.broadcasted_iota(jnp.int32, (1, wide), 1)
+    block = jnp.zeros((1, wide), f32)
+    for t in range(PR):
+        inside = (lane >= t * b) & (lane < (t + 1) * b)
+        block = jnp.where(inside, table_ref[:1, t : t + 1], block)
+    keep = block > PL - 0.5
+    lead0 = mm(inv0, w_lead_ref[:b, :]).astype(bf16)
+    lead1 = mm(inv1, w_lead_ref[b : 2 * b, :] - tdot(x01, lead0)).astype(bf16)
+    lead2 = w_lead_ref[2 * b :, :] - tdot(x02, lead0) - tdot(x12, lead1)
+    lead2 = mm(inv2, lead2).astype(bf16)
+    for i, lead in enumerate([lead0, lead1, lead2]):
+        lead_ref[i * b : (i + 1) * b, :] = jnp.where(keep, lead, jnp.zeros_like(lead))
+    value = log_ref[:1, :1] + log2
+    line = lax.broadcasted_iota(jnp.int32, (LOG_ROWS, wide), 0)
+    rows = jnp.zeros((LOG_ROWS, wide), f32)
+    for i in range(3):
+        part = value.astype(bf16).astype(f32)
+        rows = jnp.where(line == i, part, rows)
+        value = value - part
+    lead_ref[PL * b :, :] = rows.astype(bf16)
 
 
 def gather_rows(ways, near_steps, *refs):
@@ -177,19 +198,19 @@
 
 
 def root_step(
-    corner_ref, lead_ref, first_ref, d0_ref, d12_ref,
+    corner_ref, lead_ref, first_ref, d01_ref, d2_ref,
     q_ref, inv0_ref, inv1_ref, x_ref, log_ref, work,
 ):
     b = inv0_ref.shape[0]
-    groups = d0_ref.shape[0] // b
+    groups = d2_ref.shape[0] // b
     pitch = lead_ref.shape[0] // groups
     corner = corner_ref[...]
     top = first_ref[...]
     for q in range(groups):
         lead = lead_ref[q * pitch : q * pitch + PL * b, :]
         corner = corner - tdot(lead, lead)
-        top = top - tdot(lead[:b, :], d0_ref[q * b : (q + 1) * b, :])
-        top = top - tdot(lead[b:, :], d12_ref[q * 2 * b : (q + 1) * 2 * b, :])
+        top = top - tdot(lead[: 2 * b, :], d01_ref[q * 2 * b : (q + 1) * 2 * b, :])
+        top = top - tdot(lead[2 * b :, :], d2_ref[q * b : (q + 1) * b, :])
     log0 = invert_factor(corner[:b, :b], work, inv0_ref)
     x = mm(inv0_ref[...], corner[:b, b:]).astype(bf16)
     x_ref[...] = x
@@ -221,19 +242,42 @@
     smem = pl.BlockSpec(memory_space=pltpu.SMEM)
     vmem = pl.BlockSpec(memory_space=pltpu.VMEM)
 
-    head, rest, mask = pl.pallas_call(
+    def from_first(value):
+        value = value[:, :lead_cols]
+        parts = []
+        for root in range(leads):
+            held = value
+            for bit in reversed(bits(members)):
+                pairs = [(root ^ i, root ^ i ^ bit) for i in range(0, members, 2 * bit)]
+                got = lax.ppermute(held, "mem", pairs)
+                held = jnp.where((m ^ root) % (2 * bit) == bit, got, held)
+            parts.append(held)
+        return parts[0] if leads == 1 else jnp.concatenate(parts, axis=1)
+
+    table_rows, head, rest, mask, w_lead = pl.pallas_call(
         pick_pivots,
         grid=(1,),
         in_specs=[smem, smem, pl.BlockSpec((PL * b, cols), lambda i: (0, 0))],
-        out_specs=[vmem, vmem, vmem],
-        out_shape=(shape((b + 8, b), f32), shape((5 * b, b), f32), shape((8, cols), f32)),
+        out_specs=[vmem] * 5,
+        out_shape=(
+            shape((8, b), f32), shape((3 * b, b), f32), shape((3 * b, b), f32),
+            shape((8, cols), f32), shape((PL * b, lead_cols), f32),
+        ),
         name="pick_pivots",
     )(owner, (m * per).reshape(1), front)
-    for bit in bits(members):
+    hops = bits(members)
+    behind = 0
+    for at, bit in enumerate(hops):
+        table_rows = table_rows + flip(table_rows, "mem", bit)
+        if at >= len(hops) - 2:
+            head = head + flip(head, "mem", hops[behind])
+            behind += 1
+            table_rows, head = lax.optimization_barrier((table_rows, head))
+    for bit in hops[behind:]:
         head = head + flip(head, "mem", bit)
     for bit in bits(members):
         rest = rest + flip(rest, "mem", bit)
-    table = head[b, :count].astype(jnp.int32)
+    table = table_rows[0, :count].astype(jnp.int32)
 
     starts = [g ^ CORE, g ^ (CORE | CHIP), g ^ CHIP, g]
     places = jnp.concatenate(
@@ -267,7 +311,6 @@
             ],
         ),
         out_shape=(shape((2 * quarter, cols), f32), shape((quarter, cols), f32)),
-        cost_estimate=cost(6),
         name="gather_rows",
     )(source[:sent], kept[:sent], *([front] * ways), mask)
     near = flip(near, "grp", CORE)
@@ -285,7 +328,6 @@
             out_specs=pl.BlockSpec((pr, cols), lambda s, *pre: (0, 0)),
         ),
         out_shape=shape((pr, cols), f32),
-        cost_estimate=cost(2),
         name="first_rows",
     )(
         source[sent + quarter_blocks :], kept[sent + quarter_blocks :],
@@ -302,31 +344,29 @@
     def w_spec(k):
         return pl.BlockSpec((b, cols), lambda i: (k, 0))
 
-    p0, inv0, log0 = pl.pallas_call(
-        leaf_first,
+    p01, inv0, inv1, x01, log01 = pl.pallas_call(
+        leaf_two,
         grid=(1,),
-        in_specs=[vmem, w_spec(0), vmem],
-        out_specs=[vmem, vmem, vmem],
-        out_shape=(shape((b, cols), bf16), sq, logs),
+        in_specs=[vmem, w_spec(0), w_spec(1), vmem],
+        out_specs=[vmem] * 5,
+        out_shape=(shape((2 * b, cols), bf16), sq, sq, sqh, logs),
         scratch_shapes=work,
-        cost_estimate=cost(6),
-        name="leaf_first",
-    )(head, front, mask)
+        name="leaf_two",
+    )(head, front, front, mask)
 
     far = far + near[quarter:]
     rest, far = lax.optimization_barrier((rest, far))
     far = flip(far, "grp", CHIP)
 
-    p12, leaf_log = pl.pallas_call(
-        leaf_others,
+    p2, lead = pl.pallas_call(
+        leaf_last,
         grid=(1,),
-        in_specs=[vmem, w_spec(1), w_spec(2), vmem, vmem, vmem, vmem],
+        in_specs=[vmem, w_spec(2)] + [vmem] * 8,
         out_specs=[vmem, vmem],
-        out_shape=(shape((2 * b, cols), bf16), logs),
+        out_shape=(shape((b, cols), bf16), shape((PL * b + LOG_ROWS, pr), bf16)),
         scratch_shapes=[pltpu.VMEM((b, b), f32)] + work,
-        cost_estimate=cost(12),
-        name="leaf_others",
-    )(rest, front, front, mask, inv0, p0, log0)
+        name="leaf_last",
+    )(rest, front, from_first(w_lead), table_rows, mask, p01, inv0, inv1, x01, log01)
 
     def base_kernel(*refs):
         add_rows(ways, True, *refs)
@@ -342,7 +382,6 @@
             out_specs=pl.BlockSpec(tall, lambda s, *pre: (s, 0)),
         ),
         out_shape=shape((quarter, cols), f32),
-        cost_estimate=cost(4),
         name="base_rows",
     )(
         source[sent : sent + quarter_blocks], kept[sent : sent + quarter_blocks],
@@ -386,48 +425,25 @@
             found = found | (zone == (g ^ h))
         return found
 
-    def from_first(value):
-        value = value[:, :lead_cols]
-        parts = []
-        for root in range(leads):
-            held = value
-            for bit in reversed(bits(members)):
-                pairs = [(root ^ i, root ^ i ^ bit) for i in range(0, members, 2 * bit)]
-                got = lax.ppermute(held, "mem", pairs)
-                held = jnp.where((m ^ root) % (2 * bit) == bit, got, held)
-            parts.append(held)
-        return parts[0] if leads == 1 else jnp.concatenate(parts, axis=1)
-
     def across(value):
         far_value = flip(value, "grp", CHIP)
         both = jnp.concatenate([value, far_value], axis=0)
         return jnp.concatenate([both, flip(both, "grp", CORE)], axis=0)
 
     corner = from_first(first)
-    d0 = across(p0)
-    r0 = to_rows(d0)
-
-    log_value = leaf_log[:1, :1]
-    parts = []
-    for _ in range(3):
-        parts.append(log_value.astype(bf16))
-        log_value = log_value - parts[-1].astype(f32)
-    line = lax.broadcasted_iota(jnp.int32, (LOG_ROWS, lead_cols), 0)
-    log_block = jnp.zeros((LOG_ROWS, lead_cols), bf16)
-    for i, part in enumerate(parts):
-        log_block = jnp.where(line == i, part, log_block)
-    lead = jnp.concatenate([p0[:, :lead_cols], p12[:, :lead_cols], log_block], axis=0)
-    lead = across(from_first(lead))
-    d12 = across(p12)
-    r12 = to_rows(d12)
+    d01 = across(p01)
+    r01 = to_rows(d01)
+    lead = across(lead)
+    d2 = across(p2)
+    r2 = to_rows(d2)
+    lead, far = lax.optimization_barrier((lead, far))
 
     q, rinv0, rinv1, rx, root_log = pl.pallas_call(
         root_step,
         out_shape=(shape((pr, cols), bf16), sq, sq, sqh, logs),
         scratch_shapes=work,
-        cost_estimate=cost(18),
         name="root_step",
-    )(corner, lead, first, d0, d12)
+    )(corner, lead, first, d01, d2)
     rq = to_rows(q)
 
     root_factor = jnp.zeros((quarter, cols), f32)
@@ -436,7 +452,7 @@
         rows = g * quarter + start + jnp.arange(cols)
         part = lax.dynamic_slice_in_dim(base, start, cols, 0)
         part = part + lax.dynamic_slice_in_dim(far, start, cols, 0)
-        part = part - tdot(r0[i], d0) - tdot(r12[i], d12)
+        part = part - tdot(r01[i], d01) - tdot(r2[i], d2)
         if leads == 1:
             q0 = mm_t(part[:, :b], rinv0)
             inside = part[:, b:pr] - jnp.dot(q0.astype(bf16), rx, preferred_element_type=f32)

time: 252 us -> 277 us (1.099)
  the two profiles are of different devices: /device:TPU:3 before, /device:TPU:24 now
where the time goes in v2:
time: 277 us; the launch traced here: 275 us
  waiting for transfers between devices  104 us (38%)
  starting transfers between devices  63.1 us (23%)
  Pallas kernels  45.8 us (17%)
  other arithmetic  19.7 us (7%)
  matrix products  16.3 us (6%)
  local copies, waits for them, and re-layouts  13.8 us (5%)
  between operations  12.2 us (4%)
    ppermute x19, waiting for transfers between devices, flip(): return lax.ppermute(value, axis, [(i, i ^ bit) for i in range(size)])  56.2 us
    ppermute x19, starting transfers between devices, flip(): return lax.ppermute(value, axis, [(i, i ^ bit) for i in range(size)])  29.9 us
    ppermute x6, waiting for transfers between devices, from_first(): got = lax.ppermute(held, 'mem', pairs)  27.5 us
    ppermute x9, waiting for transfers between devices, to_rows(): got = lax.ppermute(sent_part, ('grp', 'mem'), pairs)  20.5 us
    ppermute x9, starting transfers between devices, to_rows(): got = lax.ppermute(sent_part, ('grp', 'mem'), pairs)  18 us
    dot_general x6, matrix products, tdot(): lax.dot_general(lhs, rhs, (((0,), (0,)), ((), ())), preferred_element_typ...  13.7 us
    pallas_call x1, Pallas kernels, local(): pl.pallas_call(root_step, out_shape=(shape((pr, cols), bf16), sq, sq, sqh...  11.2 us
    pallas_call x1, Pallas kernels, local(): pl.pallas_call(leaf_two, grid=(1,), in_specs=[vmem, w_spec(0), w_spec(1),...  9.4 us
  transfers between devices with their start and end apart: 40, of which 13 were waited for; matrix products, arithmetic and copies ran while one was open for 15% of the time, Pallas kernels for 13%

profile of v2, /device:TPU:24, one launch (start us, length us, event | category | flops | bytes accessed | tf_op | source)
XLA Modules:
  0.0 275.2 jit_solution(7611624948860232464)
XLA Ops:
  0.6 2.1 pick_pivots.1
  2.7 1.5 collective-permute-start
  4.9 1.7 collective-permute-done
  7.7 3.2 %collective-permute-done.1 = f32[8,128]{1,0:T(8,128)S(1)} collective-permute-done((f32[8,128]{1,0:T(8,128)S(1)}, f32[8,128]{1,0:T(8,128)S(1)}, u32[]{:S(2)}, u32[]{:S(2)}) %collective-permute-start.1) | collective-permute-done | bytes 4128 | tf_op jit(solution)/shard_map/ppermute | solution.py:42
  12.7 4.2 %collective-permute-done.3 = f32[8,128]{1,0:T(8,128)S(1)} collective-permute-done((f32[8,128]{1,0:T(8,128)S(1)}, f32[8,128]{1,0:T(8,128)S(1)}, u32[]{:S(2)}, u32[]{:S(2)}) %collective-permute-start.3) | collective-permute-done | bytes 4128 | tf_op jit(solution)/shard_map/ppermute | solution.py:42
  18.9 7.9 %gather_rows.1 = (f32[2048,512]{1,0:T(8,128)}, f32[1024,512]{1,0:T(8,128)}) custom-call(s32[24]{0:T(128)} %bitcast.50, s32[24]{0:T(128)} %bitcast.49, f32[4096,512]{1,0:T(8,128)} %bitcast.36, f32[4096,512]{1,0:T(8,128)} %bitcast.37, f32[4096,512]{1,0:T(8,128)} %bitcast.38, f32[4096,512]{1,0:T(8,128)} %bitcast.39, ...), custom_call_target="tpu_custom_call" | custom-call | tf_op jit(solution)/shard_map/gather_rows/pallas_call | solution.py:302
  27.6 1.4 collective-permute-start.12
  29.0 1.5 collective-permute-start.6
  30.6 17.9 %collective-permute-done.12 = f32[384,128]{1,0:T(8,128)S(1)} collective-permute-done((f32[384,128]{1,0:T(8,128)S(1)}, f32[384,128]{1,0:T(8,128)S(1)}, u32[]{:S(2)}, u32[]{:S(2)}) %collective-permute-start.12) | collective-permute-done | bytes 196640 | tf_op jit(solution)/shard_map/ppermute | solution.py:42
  49.2 9.4 %leaf_two.1 = (bf16[256,512]{1,0:T(8,128)(2,1)}, f32[128,128]{1,0:T(8,128)}, f32[128,128]{1,0:T(8,128)}, bf16[128,128]{1,0:T(8,128)(2,1)}, f32[8,128]{1,0:T(8,128)}) custom-call(f32[384,128]{1,0:T(8,128)} %add.255.head_ref, f32[4096,512]{1,0:T(8,128)} %bitcast.40, f32[4096,512]{1,0:T(8,128)} %bitcast.41, ...), custom_call_target="tpu_custom_call" | custom-call | tf_op jit(solution)/shard_map/leaf_two/pallas_call | solution.py:347
  58.6 1.6 collective-permute-start.16
  61.6 2.7 collective-permute-start.7
  64.3 2.5 collective-permute-done.16
  66.8 1.8 pad_maximum_fusion.1
  69.7 7.0 %collective-permute-done.7 = f32[384,128]{1,0:T(8,128)S(1)} collective-permute-done((f32[384,128]{1,0:T(8,128)S(1)}, f32[384,128]{1,0:T(8,128)S(1)}, u32[]{:S(2)}, u32[]{:S(2)}) %collective-permute-start.7) | collective-permute-done | bytes 196640 | tf_op jit(solution)/shard_map/ppermute | solution.py:42
  76.9 2.9 %first_rows.1 = f32[256,512]{1,0:T(8,128)} custom-call(s32[2]{0:T(128)} %slice.73.refs_0_, s32[2]{0:T(128)} %slice.74.refs_1_, s32[1]{0:T(128)} %bitcast.9.refs_2_, f32[4096,512]{1,0:T(8,128)} %bitcast.42, f32[4096,512]{1,0:T(8,128)} %bitcast.43, f32[8,512]{1,0:T(8,128)} %get-tuple-element.34.refs_6_.refs_7_.mask_ref.refs_5_, f32[1024,512]{1,0:T(8,128)} %refs_6_.1), custom_call_target="tpu_custom_call" | custom-call | tf_op jit(solution)/shard_map/first_rows/pallas_call | solution.py:321
  80.6 2.0 collective-permute-start.11
  83.4 2.0 constant_dynamic-update-slice_fusion.d01_ref
  85.4 1.6 collective-permute-start.18
  89.4 1.8 collective-permute-done.11
  92.0 3.4 %slice_add_fusion = f32[1024,512]{1,0:T(8,128)} fusion(f32[1024,512]{1,0:T(8,128)S(1)} %copy-done.8, f32[2048,512]{1,0:T(8,128)} %collective-permute-done.5.refs_9_), kind=kLoop, calls=%fused_computation.1 | loop fusion | flops 524288 | bytes 6291456 | tf_op jit(solution)/shard_map/add | solution.py:357
  95.4 7.5 %leaf_last.1 = (bf16[128,512]{1,0:T(8,128)(2,1)}, bf16[400,256]{1,0:T(8,128)(2,1)}) custom-call(f32[384,128]{1,0:T(8,128)} %add.251.rest_ref, f32[4096,512]{1,0:T(8,128)} %bitcast.44, f32[384,256]{1,0:T(8,128)} %broadcast_select_fusion.5.w_lead_ref, f32[8,128]{1,0:T(8,128)} %copy-done.25, f32[8,512]{1,0:T(8,128)} %get-tuple-element.34.refs_6_.refs_7_.mask_ref.refs_5_, ...), custom_call_target="tpu_custom_call" | custom-call | tf_op jit(solution)/shard_map/leaf_last/pallas_call | solution.py:361
  104.3 3.8 %collective-permute-done.20 = bf16[128,512]{1,0:T(8,128)(2,1)S(1)} collective-permute-done((bf16[128,512]{1,0:T(8,128)(2,1)}, bf16[128,512]{1,0:T(8,128)(2,1)S(1)}, u32[]{:S(2)}, u32[]{:S(2)}) %collective-permute-start.20) | collective-permute-done | bytes 131104 | tf_op jit(solution)/shard_map/ppermute | solution.py:42
  109.4 1.3 broadcast_select_fusion
  110.8 1.4 collective-permute-start.19
  112.3 1.5 collective-permute-start.22
  115.7 25.7 %collective-permute-done.27 = f32[256,256]{1,0:T(8,128)S(1)} collective-permute-done((f32[256,256]{1,0:T(8,128)S(1)}, f32[256,256]{1,0:T(8,128)S(1)}, u32[]{:S(2)}, u32[]{:S(2)}) %collective-permute-start.27) | collective-permute-done | bytes 262176 | tf_op jit(solution)/shard_map/ppermute | solution.py:252
  142.9 1.5 collective-permute-start.36
  144.5 15.3 %collective-permute-done.13 = bf16[400,256]{1,0:T(8,128)(2,1)S(1)} collective-permute-done((bf16[400,256]{1,0:T(8,128)(2,1)S(1)}, bf16[400,256]{1,0:T(8,128)(2,1)S(1)}, u32[]{:S(2)}, u32[]{:S(2)}) %collective-permute-start.13) | collective-permute-done | bytes 204832 | tf_op jit(solution)/shard_map/ppermute | solution.py:42
  161.8 16.1 %collective-permute-start.14 = (bf16[800,256]{1,0:T(8,128)(2,1)}, bf16[800,256]{1,0:T(8,128)(2,1)}, u32[]{:S(2)}, u32[]{:S(2)}) collective-permute-start(bf16[800,256]{1,0:T(8,128)(2,1)} %pad_maximum_fusion.2), channel_id=1, source_target_pairs={{0,8},{8,0},{16,24},{24,16},{1,9},{9,1},{17,25},{25,17},{2,10},{10... | collective-permute-start | bytes 1228808 | tf_op jit(solution)/shard_map/ppermute | solution.py:42
  178.9 1.5 collective-permute-start.35
  184.0 1.7 collective-permute-start.33
  185.7 1.7 collective-permute-start.32
  187.4 1.9 collective-permute-start.31
  190.0 4.1 %collective-permute-start.34 = (bf16[512,512]{1,0:T(8,128)(2,1)S(1)}, bf16[512,512]{1,0:T(8,128)(2,1)}, u32[]{:S(2)}, u32[]{:S(2)}) collective-permute-start(bf16[512,512]{1,0:T(8,128)(2,1)S(1)} %collective-permute-done.23), channel_id=1, source_target_pairs={{2,3},{3,2},{6,7},{7,6},{8,9},{9,8},{12,13},{13,12},{22,23},{23,22... | collective-permute-start | bytes 1572872 | tf_op jit(solution)/shard_map/ppermute | solution.py:417
  194.1 3.3 %fusion.5 = f32[512,512]{1,0:T(8,128)} fusion(bf16[1024,512]{1,0:T(8,128)(2,1)} %constant_dynamic-update-slice_fusion.d01_ref, bf16[1024,512]{1,0:T(8,128)(2,1)} %copy-done.32, bf16[1024,512]{1,0:T(8,128)(2,1)S(1)} %broadcast_select_fusion, pred[]{:T(512)S(6)} %or.2), kind=kOutput, calls=%fused_computation.15 | convolution fusion | flops 537395200 | bytes 4194305 | tf_op jit(solution)/shard_map/dot_general | solution.py:29
  197.4 4.8 %base_rows.1 = f32[1024,512]{1,0:T(8,128)} custom-call(s32[8]{0:T(128)} %slice.67.refs_0_, s32[8]{0:T(128)} %slice.68.refs_1_, s32[1]{0:T(128)} %constant.94.clone.1.refs_2_, f32[4096,512]{1,0:T(8,128)} %bitcast.45, f32[4096,512]{1,0:T(8,128)} %bitcast.46, f32[4096,512]{1,0:T(8,128)} %bitcast.47, f32[4096,512]{1,0:T(8,128)} %bitcast.48, ...), custom_call_target="tpu_custom_call" | custom-call | tf_op jit(solution)/shard_map/base_rows/pallas_call | solution.py:374
  202.2 2.0 pad_maximum_fusion.lead_ref
  204.2 14.9 %collective-permute-done.34 = bf16[512,512]{1,0:T(8,128)(2,1)} collective-permute-done((bf16[512,512]{1,0:T(8,128)(2,1)S(1)}, bf16[512,512]{1,0:T(8,128)(2,1)}, u32[]{:S(2)}, u32[]{:S(2)}) %collective-permute-start.34) | collective-permute-done | bytes 524320 | tf_op jit(solution)/shard_map/ppermute | solution.py:417
  219.1 2.7 fusion.10
  221.9 11.2 %root_step.1 = (bf16[256,512]{1,0:T(8,128)(2,1)}, f32[128,128]{1,0:T(8,128)}, f32[128,128]{1,0:T(8,128)}, bf16[128,128]{1,0:T(8,128)(2,1)}, f32[8,128]{1,0:T(8,128)}) custom-call(f32[256,256]{1,0:T(8,128)} %broadcast_select_fusion.8.corner_ref, bf16[1600,256]{1,0:T(8,128)(2,1)} %pad_maximum_fusion.lead_ref, f32[256,512]{1,0:T(8,128)} %copy-done.5, ...), custom_call_target="tpu_custom_call" | custom-call | tf_op jit(solution)/shard_map/root_step/pallas_call | solution.py:441
  233.9 1.4 collective-permute-start.39
  235.3 3.3 %fusion = f32[512,512]{1,0:T(8,128)S(1)} fusion(f32[512,512]{1,0:T(8,128)} %fusion.10, bf16[1024,512]{1,0:T(8,128)(2,1)} %constant_dynamic-update-slice_fusion.d01_ref, bf16[1024,512]{1,0:T(8,128)(2,1)} %collective-permute-done.31, bf16[1024,512]{1,0:T(8,128)(2,1)} %collective-permute-done.32, bf16[1024,512]{1,0:T(8,128)(2,1)} %collective-permute-done.33, ...), kind=kOutput, calls=%fused_computation.3 | convolution fusion | flops 538705920 | bytes 8388614 | tf_op jit(solution)/shard_map/dot_general | solution.py:29
  239.0 1.7 subtract_subtract_fusion
  245.8 1.4 convert_reduce_fusion
  261.2 3.6 %collective-permute-start.37 = (bf16[256,512]{1,0:T(8,128)(2,1)}, bf16[256,512]{1,0:T(8,128)(2,1)S(1)}, u32[]{:S(2)}, u32[]{:S(2)}) collective-permute-start(bf16[256,512]{1,0:T(8,128)(2,1)} %collective-permute-done.30), channel_id=1, source_target_pairs={{2,3},{3,2},{6,7},{7,6},{8,9},{9,8},{12,13},{13,12},{22,23},{23,22... | collective-permute-start | bytes 786440 | tf_op jit(solution)/shard_map/ppermute | solution.py:417
  264.9 1.3 fusion.2
  266.7 5.5 %collective-permute-done.37 = bf16[256,512]{1,0:T(8,128)(2,1)S(1)} collective-permute-done((bf16[256,512]{1,0:T(8,128)(2,1)}, bf16[256,512]{1,0:T(8,128)(2,1)S(1)}, u32[]{:S(2)}, u32[]{:S(2)}) %collective-permute-start.37) | collective-permute-done | bytes 262176 | tf_op jit(solution)/shard_map/ppermute | solution.py:417
  (180 shorter events, 40.7 us)
Async XLA Ops:
  2.7 3.8 %collective-permute-start = (f32[8,128]{1,0:T(8,128)}, f32[8,128]{1,0:T(8,128)S(1)}, u32[]{:S(2)}, u32[]{:S(2)}) collective-permute-start(f32[8,128]{1,0:T(8,128)} %get-tuple-element.29), channel_id=1, source_target_pairs={{0,1},{1,0},{2,3},{3,2},{4,5},{5,4},{6,7},{7,6},{8,9},{9,8},{10,11... | collective-permute-start | bytes 12296 | tf_op jit(solution)/shard_map/ppermute | solution.py:42
  4.3 6.6 %collective-permute-start.2 = (f32[384,128]{1,0:T(8,128)}, f32[384,128]{1,0:T(8,128)S(1)}, u32[]{:S(2)}, u32[]{:S(2)}) collective-permute-start(f32[384,128]{1,0:T(8,128)} %get-tuple-element.30), channel_id=1, source_target_pairs={{0,1},{1,0},{2,3},{3,2},{4,5},{5,4},{6,7},{7,6},{8,9},{9,8},{10,11... | collective-permute-start | bytes 589832 | tf_op jit(solution)/shard_map/ppermute | solution.py:42
  7.2 3.6 %collective-permute-start.1 = (f32[8,128]{1,0:T(8,128)S(1)}, f32[8,128]{1,0:T(8,128)S(1)}, u32[]{:S(2)}, u32[]{:S(2)}) collective-permute-start(f32[8,128]{1,0:T(8,128)S(1)} %add.240), channel_id=1, source_target_pairs={{0,2},{1,3},{2,0},{3,1},{4,6},{5,7},{6,4},{7,5},{8,10},{9,11},{10,... | collective-permute-start | bytes 12296 | tf_op jit(solution)/shard_map/ppermute | solution.py:42
  11.8 5.8 %collective-permute-start.4 = (f32[384,128]{1,0:T(8,128)S(1)}, f32[384,128]{1,0:T(8,128)S(1)}, u32[]{:S(2)}, u32[]{:S(2)}) collective-permute-start(f32[384,128]{1,0:T(8,128)S(1)} %add.242), channel_id=1, source_target_pairs={{0,2},{1,3},{2,0},{3,1},{4,6},{5,7},{6,4},{7,5},{8,10},{9,11},{10,... | collective-permute-start | bytes 589832 | tf_op jit(solution)/shard_map/ppermute | solution.py:42
  12.3 4.6 %collective-permute-start.3 = (f32[8,128]{1,0:T(8,128)S(1)}, f32[8,128]{1,0:T(8,128)S(1)}, u32[]{:S(2)}, u32[]{:S(2)}) collective-permute-start(f32[8,128]{1,0:T(8,128)S(1)} %add.241), channel_id=1, source_target_pairs={{0,4},{1,5},{2,6},{3,7},{4,0},{5,1},{6,2},{7,3},{8,12},{9,13},{10,... | collective-permute-start | bytes 12296 | tf_op jit(solution)/shard_map/ppermute | solution.py:42
  26.8 65.2 %collective-permute-start.5 = (f32[2048,512]{1,0:T(8,128)}, f32[2048,512]{1,0:T(8,128)}, u32[]{:S(2)}, u32[]{:S(2)}) collective-permute-start(f32[2048,512]{1,0:T(8,128)} %get-tuple-element.35), channel_id=1, source_target_pairs={{0,8},{8,0},{16,24},{24,16},{1,9},{9,1},{17,25},{25,17},{2,10},{10... | collective-permute-start | bytes 12582920 | tf_op jit(solution)/shard_map/ppermute | solution.py:42
  26.9 33.2 %collective-permute-start.9 = (f32[384,256]{1,0:T(8,128)S(1)}, f32[384,256]{1,0:T(8,128)S(1)}, u32[]{:S(2)}, u32[]{:S(2)}) collective-permute-start(f32[384,256]{1,0:T(8,128)S(1)} %copy-done.19), channel_id=1, source_target_pairs={{0,4},{8,12},{16,20},{24,28}} | collective-permute-start | bytes 1179656 | tf_op jit(solution)/shard_map/ppermute | solution.py:252
  27.6 20.9 %collective-permute-start.12 = (f32[384,128]{1,0:T(8,128)S(1)}, f32[384,128]{1,0:T(8,128)S(1)}, u32[]{:S(2)}, u32[]{:S(2)}) collective-permute-start(f32[384,128]{1,0:T(8,128)S(1)} %add.244), channel_id=1, source_target_pairs={{0,4},{1,5},{2,6},{3,7},{4,0},{5,1},{6,2},{7,3},{8,12},{9,13},{10,... | collective-permute-start | bytes 589832 | tf_op jit(solution)/shard_map/ppermute | solution.py:42
  29.0 32.5 %collective-permute-start.6 = (f32[384,128]{1,0:T(8,128)S(1)}, f32[384,128]{1,0:T(8,128)S(1)}, u32[]{:S(2)}, u32[]{:S(2)}) collective-permute-start(f32[384,128]{1,0:T(8,128)S(1)} %copy-done.23), channel_id=1, source_target_pairs={{0,1},{1,0},{2,3},{3,2},{4,5},{5,4},{6,7},{7,6},{8,9},{9,8},{10,11... | collective-permute-start | bytes 589832 | tf_op jit(solution)/shard_map/ppermute | solution.py:42
  58.6 10.6 %copy-start.26 = (s32[34]{0:T(128)S(1)}, s32[34]{0:T(128)}, u32[]{:S(2)}) copy-start(s32[34]{0:T(128)} %get-tuple-element.60) | copy-start | bytes 412
  58.6 8.2 %collective-permute-start.16 = (bf16[256,512]{1,0:T(8,128)(2,1)}, bf16[256,512]{1,0:T(8,128)(2,1)S(1)}, u32[]{:S(2)}, u32[]{:S(2)}) collective-permute-start(bf16[256,512]{1,0:T(8,128)(2,1)} %get-tuple-element.41.p_ref), channel_id=1, source_target_pairs={{0,16},{8,24},{16,0},{24,8},{1,17},{9,25},{17,1},{25,9},{2,18},{10... | collective-permute-start | bytes 786440 | tf_op jit(solution)/shard_map/ppermute | solution.py:42
  60.2 20.3 %collective-permute-start.10 = (f32[384,256]{1,0:T(8,128)S(1)}, f32[384,256]{1,0:T(8,128)S(1)}, u32[]{:S(2)}, u32[]{:S(2)}) collective-permute-start(f32[384,256]{1,0:T(8,128)S(1)} %broadcast_select_fusion.3), channel_id=1, source_target_pairs={{0,2},{4,6},{8,10},{12,14},{16,18},{20,22},{24,26},{28,30}} | collective-permute-start | bytes 1179656 | tf_op jit(solution)/shard_map/ppermute | solution.py:252
  61.6 15.2 %collective-permute-start.7 = (f32[384,128]{1,0:T(8,128)S(1)}, f32[384,128]{1,0:T(8,128)S(1)}, u32[]{:S(2)}, u32[]{:S(2)}) collective-permute-start(f32[384,128]{1,0:T(8,128)S(1)} %add.249), channel_id=1, source_target_pairs={{0,2},{1,3},{2,0},{3,1},{4,6},{5,7},{6,4},{7,5},{8,10},{9,11},{10,... | collective-permute-start | bytes 589832 | tf_op jit(solution)/shard_map/ppermute | solution.py:42
  68.6 14.8 %collective-permute-start.17 = (bf16[512,512]{1,0:T(8,128)(2,1)}, bf16[512,512]{1,0:T(8,128)(2,1)}, u32[]{:S(2)}, u32[]{:S(2)}) collective-permute-start(bf16[512,512]{1,0:T(8,128)(2,1)} %pad_maximum_fusion.1), channel_id=1, source_target_pairs={{0,8},{8,0},{16,24},{24,16},{1,9},{9,1},{17,25},{25,17},{2,10},{10... | collective-permute-start | bytes 1572872 | tf_op jit(solution)/shard_map/ppermute | solution.py:42
  76.8 10.2 %collective-permute-start.8 = (f32[384,128]{1,0:T(8,128)S(1)}, f32[384,128]{1,0:T(8,128)S(1)}, u32[]{:S(2)}, u32[]{:S(2)}) collective-permute-start(f32[384,128]{1,0:T(8,128)S(1)} %add.250), channel_id=1, source_target_pairs={{0,4},{1,5},{2,6},{3,7},{4,0},{5,1},{6,2},{7,3},{8,12},{9,13},{10,... | collective-permute-start | bytes 589832 | tf_op jit(solution)/shard_map/ppermute | solution.py:42
  79.8 7.9 %collective-permute-start.24 = (f32[256,512]{1,0:T(8,128)}, f32[256,512]{1,0:T(8,128)}, u32[]{:S(2)}, u32[]{:S(2)}) collective-permute-start(f32[256,512]{1,0:T(8,128)} %first_rows.1), channel_id=1, source_target_pairs={{0,8},{8,0},{16,24},{24,16},{1,9},{9,1},{17,25},{25,17},{2,10},{10... | collective-permute-start | bytes 1572872 | tf_op jit(solution)/shard_map/ppermute | solution.py:42
  80.6 10.6 %collective-permute-start.11 = (f32[384,256]{1,0:T(8,128)S(1)}, f32[384,256]{1,0:T(8,128)}, u32[]{:S(2)}, u32[]{:S(2)}) collective-permute-start(f32[384,256]{1,0:T(8,128)S(1)} %broadcast_select_fusion.4), channel_id=1, source_target_pairs={{0,1},{2,3},{4,5},{6,7},{8,9},{10,11},{12,13},{14,15},{16,17},{18,... | collective-permute-start | bytes 1179656 | tf_op jit(solution)/shard_map/ppermute | solution.py:252
  85.4 24.1 %collective-permute-start.18 = (bf16[1024,512]{1,0:T(8,128)(2,1)}, bf16[1024,512]{1,0:T(8,128)(2,1)}, u32[]{:S(2)}, u32[]{:S(2)}) collective-permute-start(bf16[1024,512]{1,0:T(8,128)(2,1)} %constant_dynamic-update-slice_fusion.d01_ref), channel_id=1, source_target_pairs={{0,4},{1,5},{10,14},{11,15},{20,16},{21,17},{30,26},{31,27}} | collective-permute-start | bytes 3145736 | tf_op jit(solution)/shard_map/ppermute | solution.py:403
  88.8 14.7 %collective-permute-start.25 = (f32[256,512]{1,0:T(8,128)S(1)}, f32[256,512]{1,0:T(8,128)S(1)}, u32[]{:S(2)}, u32[]{:S(2)}) collective-permute-start(f32[256,512]{1,0:T(8,128)S(1)} %add.257), channel_id=1, source_target_pairs={{0,16},{8,24},{16,0},{24,8},{1,17},{9,25},{17,1},{25,9},{2,18},{10... | collective-permute-start | bytes 1572872 | tf_op jit(solution)/shard_map/ppermute | solution.py:42
  103.0 5.2 %collective-permute-start.20 = (bf16[128,512]{1,0:T(8,128)(2,1)}, bf16[128,512]{1,0:T(8,128)(2,1)S(1)}, u32[]{:S(2)}, u32[]{:S(2)}) collective-permute-start(bf16[128,512]{1,0:T(8,128)(2,1)} %get-tuple-element.49), channel_id=1, source_target_pairs={{0,16},{8,24},{16,0},{24,8},{1,17},{9,25},{17,1},{25,9},{2,18},{10... | collective-permute-start | bytes 393224 | tf_op jit(solution)/shard_map/ppermute | solution.py:42
  103.6 10.2 %collective-permute-start.26 = (f32[256,256]{1,0:T(8,128)S(1)}, f32[256,256]{1,0:T(8,128)S(1)}, u32[]{:S(2)}, u32[]{:S(2)}) collective-permute-start(f32[256,256]{1,0:T(8,128)S(1)} %slice.92), channel_id=1, source_target_pairs={{0,4},{8,12},{16,20},{24,28}} | collective-permute-start | bytes 786440 | tf_op jit(solution)/shard_map/ppermute | solution.py:252
  108.2 4.1 %collective-permute-start.21 = (bf16[256,512]{1,0:T(8,128)(2,1)S(1)}, bf16[256,512]{1,0:T(8,128)(2,1)S(1)}, u32[]{:S(2)}, u32[]{:S(2)}) collective-permute-start(bf16[256,512]{1,0:T(8,128)(2,1)S(1)} %pad_maximum_fusion.3), channel_id=1, source_target_pairs={{0,8},{8,0},{16,24},{24,16},{1,9},{9,1},{17,25},{25,17},{2,10},{10... | collective-permute-start | bytes 786440 | tf_op jit(solution)/shard_map/ppermute | solution.py:42
  110.8 32.0 %copy-start.15 = (bf16[400,256]{1,0:T(8,128)(2,1)S(1)}, bf16[400,256]{1,0:T(8,128)(2,1)}, u32[]{:S(2)}) copy-start(bf16[400,256]{1,0:T(8,128)(2,1)} %get-tuple-element.46) | copy-start | bytes 614404
  110.8 67.1 %collective-permute-start.19 = (bf16[1024,512]{1,0:T(8,128)(2,1)S(1)}, bf16[1024,512]{1,0:T(8,128)(2,1)S(1)}, u32[]{:S(2)}, u32[]{:S(2)}) collective-permute-start(bf16[1024,512]{1,0:T(8,128)(2,1)S(1)} %broadcast_select_fusion), channel_id=1, source_target_pairs={{0,2},{1,3},{4,6},{5,7},{10,8},{11,9},{14,12},{15,13},{20,22},{21,... | collective-permute-start | bytes 3145736 | tf_op jit(solution)/shard_map/ppermute | solution.py:403
  112.3 106.8 %copy-start = (bf16[512,512]{1,0:T(8,128)(2,1)}, bf16[512,512]{1,0:T(8,128)(2,1)S(1)}, u32[]{:S(2)}) copy-start(bf16[512,512]{1,0:T(8,128)(2,1)S(1)} %constant_dynamic-update-slice_fusion.3.d2_ref) | copy-start | bytes 1572868
  112.3 30.6 %collective-permute-start.22 = (bf16[512,512]{1,0:T(8,128)(2,1)S(1)}, bf16[512,512]{1,0:T(8,128)(2,1)}, u32[]{:S(2)}, u32[]{:S(2)}) collective-permute-start(bf16[512,512]{1,0:T(8,128)(2,1)S(1)} %constant_dynamic-update-slice_fusion.3.d2_ref), channel_id=1, source_target_pairs={{0,4},{1,5},{10,14},{11,15},{20,16},{21,17},{30,26},{31,27}} | collective-permute-start | bytes 1572872 | tf_op jit(solution)/shard_map/ppermute | solution.py:403
  113.8 27.6 %collective-permute-start.27 = (f32[256,256]{1,0:T(8,128)S(1)}, f32[256,256]{1,0:T(8,128)S(1)}, u32[]{:S(2)}, u32[]{:S(2)}) collective-permute-start(f32[256,256]{1,0:T(8,128)S(1)} %broadcast_select_fusion.6), channel_id=1, source_target_pairs={{0,2},{4,6},{8,10},{12,14},{16,18},{20,22},{24,26},{28,30}} | collective-permute-start | bytes 786440 | tf_op jit(solution)/shard_map/ppermute | solution.py:252
  115.1 106.7 %collective-permute-start.15 = (f32[1024,512]{1,0:T(8,128)}, f32[1024,512]{1,0:T(8,128)}, u32[]{:S(2)}, u32[]{:S(2)}) collective-permute-start(f32[1024,512]{1,0:T(8,128)} %slice_add_fusion), channel_id=1, source_target_pairs={{0,16},{8,24},{16,0},{24,8},{1,17},{9,25},{17,1},{25,9},{2,18},{10... | collective-permute-start | bytes 6291464 | tf_op jit(solution)/shard_map/ppermute | solution.py:42
  141.5 20.3 %collective-permute-start.28 = (f32[256,256]{1,0:T(8,128)S(1)}, f32[256,256]{1,0:T(8,128)S(1)}, u32[]{:S(2)}, u32[]{:S(2)}) collective-permute-start(f32[256,256]{1,0:T(8,128)S(1)} %broadcast_select_fusion.7), channel_id=1, source_target_pairs={{0,1},{2,3},{4,5},{6,7},{8,9},{10,11},{12,13},{14,15},{16,17},{18,... | collective-permute-start | bytes 786440 | tf_op jit(solution)/shard_map/ppermute | solution.py:252
  142.8 16.9 %collective-permute-start.13 = (bf16[400,256]{1,0:T(8,128)(2,1)S(1)}, bf16[400,256]{1,0:T(8,128)(2,1)S(1)}, u32[]{:S(2)}, u32[]{:S(2)}) collective-permute-start(bf16[400,256]{1,0:T(8,128)(2,1)S(1)} %copy-done.15), channel_id=1, source_target_pairs={{0,16},{8,24},{16,0},{24,8},{1,17},{9,25},{17,1},{25,9},{2,18},{10... | collective-permute-start | bytes 614408 | tf_op jit(solution)/shard_map/ppermute | solution.py:42
  142.9 42.8 %collective-permute-start.36 = (bf16[512,512]{1,0:T(8,128)(2,1)S(1)}, bf16[512,512]{1,0:T(8,128)(2,1)}, u32[]{:S(2)}, u32[]{:S(2)}) collective-permute-start(bf16[512,512]{1,0:T(8,128)(2,1)S(1)} %constant_dynamic-update-slice_fusion.3.d2_ref), channel_id=1, source_target_pairs={{0,1},{1,0},{10,11},{11,10},{20,21},{21,20},{30,31},{31,30}} | collective-permute-start | bytes 1572872 | tf_op jit(solution)/shard_map/ppermute | solution.py:417
  144.5 53.0 %copy-start.10 = (bf16[512,512]{1,0:T(8,128)(2,1)}, bf16[512,512]{1,0:T(8,128)(2,1)S(1)}, u32[]{:S(2)}) copy-start(bf16[512,512]{1,0:T(8,128)(2,1)S(1)} %broadcast_select_fusion.1) | copy-start | bytes 1572868
  159.7 27.6 %collective-permute-start.23 = (bf16[512,512]{1,0:T(8,128)(2,1)S(1)}, bf16[512,512]{1,0:T(8,128)(2,1)S(1)}, u32[]{:S(2)}, u32[]{:S(2)}) collective-permute-start(bf16[512,512]{1,0:T(8,128)(2,1)S(1)} %broadcast_select_fusion.1), channel_id=1, source_target_pairs={{0,2},{1,3},{4,6},{5,7},{10,8},{11,9},{14,12},{15,13},{20,22},{21,... | collective-permute-start | bytes 1572872 | tf_op jit(solution)/shard_map/ppermute | solution.py:403
  161.8 22.2 %collective-permute-start.14 = (bf16[800,256]{1,0:T(8,128)(2,1)}, bf16[800,256]{1,0:T(8,128)(2,1)}, u32[]{:S(2)}, u32[]{:S(2)}) collective-permute-start(bf16[800,256]{1,0:T(8,128)(2,1)} %pad_maximum_fusion.2), channel_id=1, source_target_pairs={{0,8},{8,0},{16,24},{24,16},{1,9},{9,1},{17,25},{25,17},{2,10},{10... | collective-permute-start | bytes 1228808 | tf_op jit(solution)/shard_map/ppermute | solution.py:42
  178.9 11.1 %collective-permute-start.35 = (bf16[512,512]{1,0:T(8,128)(2,1)}, bf16[512,512]{1,0:T(8,128)(2,1)}, u32[]{:S(2)}, u32[]{:S(2)}) collective-permute-start(bf16[512,512]{1,0:T(8,128)(2,1)} %collective-permute-done.22), channel_id=1, source_target_pairs={{4,5},{5,4},{14,15},{15,14},{16,17},{17,16},{26,27},{27,26}} | collective-permute-start | bytes 1572872 | tf_op jit(solution)/shard_map/ppermute | solution.py:417
  184.0 51.3 %collective-permute-start.33 = (bf16[1024,512]{1,0:T(8,128)(2,1)}, bf16[1024,512]{1,0:T(8,128)(2,1)}, u32[]{:S(2)}, u32[]{:S(2)}) collective-permute-start(bf16[1024,512]{1,0:T(8,128)(2,1)} %constant_dynamic-update-slice_fusion.d01_ref), channel_id=1, source_target_pairs={{0,1},{1,0},{10,11},{11,10},{20,21},{21,20},{30,31},{31,30}} | collective-permute-start | bytes 3145736 | tf_op jit(solution)/shard_map/ppermute | solution.py:417
  185.7 49.6 %collective-permute-start.32 = (bf16[1024,512]{1,0:T(8,128)(2,1)}, bf16[1024,512]{1,0:T(8,128)(2,1)}, u32[]{:S(2)}, u32[]{:S(2)}) collective-permute-start(bf16[1024,512]{1,0:T(8,128)(2,1)} %collective-permute-done.18), channel_id=1, source_target_pairs={{4,5},{5,4},{14,15},{15,14},{16,17},{17,16},{26,27},{27,26}} | collective-permute-start | bytes 3145736 | tf_op jit(solution)/shard_map/ppermute | solution.py:417
  187.4 47.9 %collective-permute-start.31 = (bf16[1024,512]{1,0:T(8,128)(2,1)}, bf16[1024,512]{1,0:T(8,128)(2,1)}, u32[]{:S(2)}, u32[]{:S(2)}) collective-permute-start(bf16[1024,512]{1,0:T(8,128)(2,1)} %copy-done.32), channel_id=1, source_target_pairs={{2,3},{3,2},{6,7},{7,6},{8,9},{9,8},{12,13},{13,12},{22,23},{23,22... | collective-permute-start | bytes 3145736 | tf_op jit(solution)/shard_map/ppermute | solution.py:417
  190.0 29.1 %collective-permute-start.34 = (bf16[512,512]{1,0:T(8,128)(2,1)S(1)}, bf16[512,512]{1,0:T(8,128)(2,1)}, u32[]{:S(2)}, u32[]{:S(2)}) collective-permute-start(bf16[512,512]{1,0:T(8,128)(2,1)S(1)} %collective-permute-done.23), channel_id=1, source_target_pairs={{2,3},{3,2},{6,7},{7,6},{8,9},{9,8},{12,13},{13,12},{22,23},{23,22... | collective-permute-start | bytes 1572872 | tf_op jit(solution)/shard_map/ppermute | solution.py:417
  221.9 13.4 %copy-start.2 = (f32[1024,512]{1,0:T(8,128)S(1)}, f32[1024,512]{1,0:T(8,128)}, u32[]{:S(2)}) copy-start(f32[1024,512]{1,0:T(8,128)} %base_rows.1) | copy-start | bytes 6291460
  233.1 10.7 %collective-permute-start.29 = (bf16[256,512]{1,0:T(8,128)(2,1)}, bf16[256,512]{1,0:T(8,128)(2,1)S(1)}, u32[]{:S(2)}, u32[]{:S(2)}) collective-permute-start(bf16[256,512]{1,0:T(8,128)(2,1)} %get-tuple-element.54), channel_id=1, source_target_pairs={{0,4},{1,5},{10,14},{11,15},{20,16},{21,17},{30,26},{31,27}} | collective-permute-start | bytes 786440 | tf_op jit(solution)/shard_map/ppermute | solution.py:403
  233.9 32.8 %collective-permute-start.39 = (bf16[256,512]{1,0:T(8,128)(2,1)}, bf16[256,512]{1,0:T(8,128)(2,1)}, u32[]{:S(2)}, u32[]{:S(2)}) collective-permute-start(bf16[256,512]{1,0:T(8,128)(2,1)} %get-tuple-element.54), channel_id=1, source_target_pairs={{0,1},{1,0},{10,11},{11,10},{20,21},{21,20},{30,31},{31,30}} | collective-permute-start | bytes 786440 | tf_op jit(solution)/shard_map/ppermute | solution.py:417
  242.2 18.0 %copy-start.4 = (f32[512,512]{1,0:T(8,128)S(1)}, f32[512,512]{1,0:T(8,128)}, u32[]{:S(2)}) copy-start(f32[512,512]{1,0:T(8,128)} %copy-done.3) | copy-start | bytes 3145732
  242.2 18.0 %copy-start.29 = (pred[512]{0:T(512)(128)(4,1)S(1)}, pred[512]{0:T(512)(128)(4,1)}, u32[]{:S(2)}) copy-start(pred[512]{0:T(512)(128)(4,1)} %get-tuple-element.71) | copy-start | bytes 1540
  242.4 22.5 %copy-start.31 = (pred[512]{0:T(512)(128)(4,1)S(1)}, pred[512]{0:T(512)(128)(4,1)}, u32[]{:S(2)}) copy-start(pred[512]{0:T(512)(128)(4,1)} %get-tuple-element.70) | copy-start | bytes 1540
  244.5 16.7 %collective-permute-start.30 = (bf16[256,512]{1,0:T(8,128)(2,1)}, bf16[256,512]{1,0:T(8,128)(2,1)}, u32[]{:S(2)}, u32[]{:S(2)}) collective-permute-start(bf16[256,512]{1,0:T(8,128)(2,1)} %broadcast_select_fusion.2), channel_id=1, source_target_pairs={{0,2},{1,3},{4,6},{5,7},{10,8},{11,9},{14,12},{15,13},{20,22},{21,... | collective-permute-start | bytes 786440 | tf_op jit(solution)/shard_map/ppermute | solution.py:403
  260.5 6.2 %collective-permute-start.38 = (bf16[256,512]{1,0:T(8,128)(2,1)}, bf16[256,512]{1,0:T(8,128)(2,1)S(1)}, u32[]{:S(2)}, u32[]{:S(2)}) collective-permute-start(bf16[256,512]{1,0:T(8,128)(2,1)} %copy-done.22), channel_id=1, source_target_pairs={{4,5},{5,4},{14,15},{15,14},{16,17},{17,16},{26,27},{27,26}} | collective-permute-start | bytes 786440 | tf_op jit(solution)/shard_map/ppermute | solution.py:417
  261.2 11.1 %collective-permute-start.37 = (bf16[256,512]{1,0:T(8,128)(2,1)}, bf16[256,512]{1,0:T(8,128)(2,1)S(1)}, u32[]{:S(2)}, u32[]{:S(2)}) collective-permute-start(bf16[256,512]{1,0:T(8,128)(2,1)} %collective-permute-done.30), channel_id=1, source_target_pairs={{2,3},{3,2},{6,7},{7,6},{8,9},{9,8},{12,13},{13,12},{22,23},{23,22... | collective-permute-start | bytes 786440 | tf_op jit(solution)/shard_map/ppermute | solution.py:417
  (25 other events, 142.9 us)

commit v3 on v2

v3 whole, which is shorter than its diff:
```python
import jax
import jax.numpy as jnp
from jax import lax
from jax.experimental import pallas as pl
from jax.experimental.pallas import tpu as pltpu
from jax.sharding import PartitionSpec as P

PL = 3
PR = 2
HIGHEST = lax.Precision.HIGHEST
ROWS = 64
SUB = 16
LOG_ROWS = 32
B_ROWS = 128
CORE, CHIP = 1, 2
f32, bf16 = jnp.float32, jnp.bfloat16


def mm(lhs, rhs):
    return jnp.dot(lhs, rhs, precision=HIGHEST, preferred_element_type=f32)


def mm_t(lhs, rhs):
    return lax.dot_general(
        lhs, rhs, (((1,), (1,)), ((), ())), precision=HIGHEST, preferred_element_type=f32
    )


def tdot(lhs, rhs):
    return lax.dot_general(lhs, rhs, (((0,), (0,)), ((), ())), preferred_element_type=f32)


def bits(size):
    out, bit = [], 1
    while bit < size:
        out.append(bit)
        bit *= 2
    return out


def flip(value, axis, bit):
    size = lax.axis_size(axis)
    return lax.ppermute(value, axis, [(i, i ^ bit) for i in range(size)])


def shape(dims, dtype):
    return jax.ShapeDtypeStruct(dims, dtype)


def invert_factor(block, work, inverse_ref):
    size = block.shape[0]
    rows = lax.broadcasted_iota(jnp.int32, (size, size), 0)
    cols = lax.broadcasted_iota(jnp.int32, (size, size), 1)
    work[:, :size] = block
    work[:, size:] = jnp.where(rows == cols, 1.0, 0.0)
    sub = lax.broadcasted_iota(jnp.int32, (ROWS, size), 0)
    lane = lax.broadcasted_iota(jnp.int32, (ROWS, size), 1)
    log_sum = jnp.zeros((1, 1), f32)
    for first in range(0, size, ROWS):
        left = work[first : first + ROWS, :size]
        right = work[first : first + ROWS, size:]
        for start in range(0, ROWS, SUB):
            at = first + start
            columns = [
                jnp.broadcast_to(left[:, at + j : at + j + 1], (ROWS, size)) for j in range(SUB)
            ]
            for j in range(SUB):
                i = start + j
                if i == ROWS - 1:
                    break
                factor = jnp.where(sub > i, columns[j], 0.0) * (1.0 / columns[j][i : i + 1, :])
                for k in range(j + 1, SUB):
                    columns[k] = columns[k] - factor * columns[k][i : i + 1, :]
                left = left - factor * left[i : i + 1, :]
                right = right - factor * right[i : i + 1, :]
        pivot = jnp.sum(jnp.where(lane == sub + first, left, 0.0), axis=1, keepdims=True)
        scale = lax.rsqrt(pivot)
        left, right = left * scale, right * scale
        inverse_ref[first : first + ROWS, :] = right
        log_sum = log_sum + jnp.sum(jnp.log(pivot), axis=0, keepdims=True)
        if first + ROWS < size:
            update = lax.dot_general(
                left, jnp.concatenate([left, right], axis=1), (((0,), (0,)), ((), ())),
                precision=HIGHEST, preferred_element_type=f32,
            )
            work[first + ROWS :, :] = work[first + ROWS :, :] - update[first + ROWS :, :]
    return log_sum


def pick_pivots(owner_ref, at_ref, front_ref, table_ref, head_ref, rest_ref, mask_ref, lead_ref):
    b = head_ref.shape[1]
    per = front_ref.shape[1] // b
    for k in range(PL):
        total = jnp.zeros(((k + 1) * b, b), f32)
        for t in range(per):
            part = front_ref[: (k + 1) * b, t * b : (t + 1) * b]
            total = total + jnp.where(owner_ref[t] == k, part, 0.0)
        if k == 0:
            head_ref[:b, :] = total
        elif k == 1:
            head_ref[b:, :] = total
        else:
            rest_ref[...] = total
    lane = lax.broadcasted_iota(jnp.int32, (8, b), 1)
    table = jnp.zeros((8, b), f32)
    for t in range(per):
        table = table + jnp.where(lane == at_ref[0] + t, owner_ref[t].astype(f32), 0.0)
        keep = jnp.where(owner_ref[t] >= PL, 1.0, 0.0).astype(f32)
        mask_ref[:, t * b : (t + 1) * b] = jnp.full((8, b), keep, f32)
    table_ref[...] = table
    lead_ref[...] = front_ref[:, : lead_ref.shape[1]]


def leaf_two(head_ref, w0_ref, w1_ref, mask_ref, p_ref, inv0_ref, inv1_ref, x_ref, log_ref, work):
    b = w0_ref.shape[0]
    c00, c01, c11 = [head_ref[i * b : (i + 1) * b, :] for i in range(3)]
    keep = mask_ref[:1, :] > 0.0
    log0 = invert_factor(c00, work, inv0_ref)
    x01 = mm(inv0_ref[...], c01).astype(bf16)
    x_ref[...] = x01
    p0 = mm(inv0_ref[...], w0_ref[...]).astype(bf16)
    log1 = invert_factor(c11 - tdot(x01, x01), work, inv1_ref)
    p1 = mm(inv1_ref[...], w1_ref[...] - tdot(x01, p0)).astype(bf16)
    p_ref[:b, :] = jnp.where(keep, p0, jnp.zeros_like(p0))
    p_ref[b:, :] = jnp.where(keep, p1, jnp.zeros_like(p1))
    log_ref[...] = jnp.broadcast_to(log0 + log1, log_ref.shape)


def leaf_last(
    rest_ref, w2_ref, w_lead_ref, table_ref, mask_ref, p_ref, inv0_ref, inv1_ref, x_ref, log_ref,
    out_ref, inv, work,
):
    b, cols = w2_ref.shape
    wide = w_lead_ref.shape[1] if w_lead_ref.shape[1] > cols else PR * b
    c02, c12, c22 = [rest_ref[i * b : (i + 1) * b, :] for i in range(3)]
    inv0, inv1, x01 = inv0_ref[...], inv1_ref[...], x_ref[...]
    x02 = mm(inv0, c02).astype(bf16)
    x12 = mm(inv1, c12 - tdot(x01, x02)).astype(bf16)
    log2 = invert_factor(c22 - tdot(x02, x02) - tdot(x12, x12), work, inv)
    inv2 = inv[...]
    keep = mask_ref[:1, :] > 0.0
    panel = mm(inv2, w2_ref[...] - tdot(x02, p_ref[:b, :]) - tdot(x12, p_ref[b:, :])).astype(bf16)
    out_ref[:b, :] = jnp.where(keep, panel, jnp.zeros_like(panel))
    lane = lax.broadcasted_iota(jnp.int32, (1, wide), 1)
    block = jnp.zeros((1, wide), f32)
    for t in range(PR):
        inside = (lane >= t * b) & (lane < (t + 1) * b)
        block = jnp.where(inside, table_ref[:1, t : t + 1], block)
    keep = block > PL - 0.5
    lead0 = mm(inv0, w_lead_ref[:b, :]).astype(bf16)
    lead1 = mm(inv1, w_lead_ref[b : 2 * b, :] - tdot(x01, lead0)).astype(bf16)
    lead2 = w_lead_ref[2 * b :, :] - tdot(x02, lead0) - tdot(x12, lead1)
    lead2 = mm(inv2, lead2).astype(bf16)
    value = log_ref[:1, :1] + log2
    line = lax.broadcasted_iota(jnp.int32, (LOG_ROWS, wide), 0)
    rows = jnp.zeros((LOG_ROWS, wide), f32)
    for i in range(3):
        part = value.astype(bf16).astype(f32)
        rows = jnp.where(line == i, part, rows)
        value = value - part
    leads = [jnp.where(keep, lead, jnp.zeros_like(lead)) for lead in (lead0, lead1, lead2)]
    whole = jnp.concatenate(leads + [rows.astype(bf16)], axis=0)
    if cols >= wide:
        split = cols // wide
        tall = whole.shape[0] // split
        for i in range(split):
            out_ref[b:, i * wide : (i + 1) * wide] = whole[i * tall : (i + 1) * tall, :]
    else:
        tall = whole.shape[0]
        for i in range(wide // cols):
            out_ref[b + i * tall : b + (i + 1) * tall, :] = whole[:, i * cols : (i + 1) * cols]


def rows_kernel(ways, spans, *refs):
    keep_ref, scale_ref = refs[1:3]
    fronts = refs[3 : 3 + ways]
    mask_ref = refs[3 + ways]
    adds = refs[4 + ways : -1]
    out_ref = refs[-1]
    step = pl.program_id(0)
    b = fronts[0].shape[0]
    keep_cols = mask_ref[:1, :] > 0.0
    for i, front_ref in enumerate(fronts):
        at = slice(i * b, (i + 1) * b)
        keep = keep_cols & (keep_ref[step * ways + i] > 0)
        total = jnp.where(keep, front_ref[...], 0.0)
        for add_ref, (first, last) in zip(adds, spans):
            use = (step >= first) & (step < last) & (scale_ref[0] > 0)
            total = total + jnp.where(use, add_ref[at, :], 0.0)
        out_ref[at, :] = total


def take_rows(front, mask, source, kept, scale, ways, adds, name):
    b = B_ROWS
    cols = front.shape[1]
    steps = source.shape[0] // ways
    spans, add_specs = [], []
    for array, first, tile in adds:
        tiles = array.shape[0] // (ways * b) - tile
        last = min(steps, first + tiles)
        spans.append((first, last))

        def index(s, *pre, first=first, last=last, tile=tile):
            return (jnp.clip(s, first, last - 1) - first + tile, 0)

        add_specs.append(pl.BlockSpec((ways * b, cols), index))
    front_specs = [
        pl.BlockSpec((b, cols), lambda s, *pre, i=i: (pre[0][s * ways + i], 0)) for i in range(ways)
    ]

    def body(*refs):
        rows_kernel(ways, spans, *refs)

    return pl.pallas_call(
        body,
        grid_spec=pltpu.PrefetchScalarGridSpec(
            num_scalar_prefetch=3,
            grid=(steps,),
            in_specs=front_specs + [pl.BlockSpec((8, cols), lambda s, *pre: (0, 0))] + add_specs,
            out_specs=pl.BlockSpec((ways * b, cols), lambda s, *pre: (s, 0)),
        ),
        out_shape=shape((source.shape[0] * b, cols), f32),
        compiler_params=pltpu.CompilerParams(vmem_limit_bytes=32 << 20),
        name=name,
    )(source, kept, scale, *([front] * ways), mask, *[array for array, _, _ in adds])


def root_step(
    leaf_ref, corner_ref, first_ref, d01_ref, pack_ref,
    q_ref, inv0_ref, inv1_ref, x_ref, log_ref, work,
):
    b = inv0_ref.shape[0]
    cols = first_ref.shape[1]
    wide = corner_ref.shape[1]
    groups = d01_ref.shape[0] // (2 * b)
    pitch = pack_ref.shape[0] // groups
    corner = corner_ref[...]
    top = first_ref[...]
    lane = lax.broadcasted_iota(jnp.int32, (8, b), 1)
    logs = jnp.zeros((8, b), f32)
    for i in range(groups):
        at = i * pitch
        d2 = pack_ref[at : at + b, :]
        packed = pack_ref[at + b : at + pitch, :]
        if cols >= wide:
            parts = [packed[:, j * wide : (j + 1) * wide] for j in range(cols // wide)]
            whole = jnp.concatenate(parts, axis=0)
        else:
            tall = (pitch - b) // (wide // cols)
            parts = [packed[j * tall : (j + 1) * tall, :] for j in range(wide // cols)]
            whole = jnp.concatenate(parts, axis=1)
        lead = whole[: PL * b, :]
        corner = corner - tdot(lead, lead)
        top = top - tdot(lead[: 2 * b, :], d01_ref[i * 2 * b : (i + 1) * 2 * b, :])
        top = top - tdot(lead[2 * b :, :], d2)
        log_sum = jnp.sum(whole[PL * b : PL * b + 16, :b].astype(f32), axis=0, keepdims=True)
        logs = jnp.where(lane == leaf_ref[i], log_sum * (1.0 / (PL * b)), logs)
    log0 = invert_factor(corner[:b, :b], work, inv0_ref)
    x = mm(inv0_ref[...], corner[:b, b:]).astype(bf16)
    x_ref[...] = x
    log1 = invert_factor(corner[b:, b:] - tdot(x, x), work, inv1_ref)
    log_ref[...] = jnp.where(lane == groups, (log0 + log1) * (1.0 / wide), logs)
    q0 = mm(inv0_ref[...], top[:b, :]).astype(bf16)
    q_ref[:b, :] = q0
    q_ref[b:, :] = mm(inv1_ref[...], top[b:, :] - tdot(x, q0)).astype(bf16)


def update_kernel(slots, *refs):
    place_ref, base_ref, d01_ref, d2_ref = refs[:4]
    r01, r2 = refs[4 : 4 + slots], refs[4 + slots : 4 + 2 * slots]
    inv0_ref, inv1_ref, x_ref, out_ref, panel_ref = refs[4 + 2 * slots :]
    b = inv0_ref.shape[0]
    cols = out_ref.shape[1]

    def at_slot(i):
        total = base_ref[...] - tdot(r01[i][...], d01_ref[...]) - tdot(r2[i][...], d2_ref[...])
        out_ref[...] = total
        if cols >= PR * b:
            q0 = mm_t(total[:, :b], inv0_ref[...])
            inside = jnp.dot(q0.astype(bf16), x_ref[...], preferred_element_type=f32)
            panel_ref[:, :b] = q0
            panel_ref[:, b:] = mm_t(total[:, b : PR * b] - inside, inv1_ref[...])
        else:
            panel_ref[...] = jnp.zeros_like(panel_ref)

    for i in range(slots):
        pl.when(pl.program_id(0) == i)(lambda i=i: at_slot(i))


def finish_kernel(slots, *refs):
    place_ref, info_ref, part_ref, panel_ref, q_ref = refs[:5]
    rq, out_ref = refs[5 : 5 + slots], refs[5 + slots]
    rows, cols = out_ref.shape
    wide = q_ref.shape[0]
    b = wide // PR

    def at_slot(i):
        row = info_ref[i] + lax.broadcasted_iota(jnp.int32, (rows, cols), 0)
        total = part_ref[...] - tdot(rq[i][...], q_ref[...])
        total = jnp.where(row >= wide, total, 0.0)
        width = min(wide, cols)
        col = info_ref[slots] + lax.broadcasted_iota(jnp.int32, (rows, width), 1)
        panel = panel_ref[...]
        panel = jnp.where((row[:, :width] >= b) | (col < b), panel, 0.0)
        out_ref[:, :width] = jnp.where(col < wide, panel, total[:, :width])
        if width < cols:
            out_ref[:, width:] = total[:, width:]

    for i in range(slots):
        pl.when(pl.program_id(0) == i)(lambda i=i: at_slot(i))


def local(leaf_fronts, block_owner, root_front):
    members = lax.axis_size("mem")
    groups = lax.axis_size("grp")
    m = lax.axis_index("mem")
    g = lax.axis_index("grp")
    front = leaf_fronts[0]
    order, cols = front.shape
    owner = block_owner[0]
    per = owner.shape[0]
    b = cols // per
    count = order // b
    quarter = order // groups
    spread = members // groups
    quarter_blocks = quarter // b
    pr = PR * b
    lead_cols = min(pr, cols)
    leads = pr // lead_cols
    zone, inner = m // spread, m % spread
    smem = pl.BlockSpec(memory_space=pltpu.SMEM)
    vmem = pl.BlockSpec(memory_space=pltpu.VMEM)

    def lead_hop(value, at):
        bit = bits(members)[-1 - at]
        parts = []
        for root in range(leads):
            held = value[root]
            pairs = [(root ^ i, root ^ i ^ bit) for i in range(0, members, 2 * bit)]
            got = lax.ppermute(held, "mem", pairs)
            parts.append(jnp.where((m ^ root) % (2 * bit) == bit, got, held))
        return parts

    table_rows, head, rest, mask, w_lead = pl.pallas_call(
        pick_pivots,
        grid=(1,),
        in_specs=[smem, smem, pl.BlockSpec((PL * b, cols), lambda i: (0, 0))],
        out_specs=[vmem] * 5,
        out_shape=(
            shape((8, b), f32), shape((3 * b, b), f32), shape((3 * b, b), f32),
            shape((8, cols), f32), shape((PL * b, lead_cols), f32),
        ),
        name="pick_pivots",
    )(owner, (m * per).reshape(1), front)
    hops = bits(members)
    last = len(hops) - 1
    w_lead = [w_lead] * leads

    def table_hop(value, at):
        return value + flip(value, "mem", hops[at])

    table_rows = table_hop(table_hop(table_rows, 0), 1)
    head = table_hop(head, 0)
    table_rows, head, w_lead, rest = lax.optimization_barrier((table_rows, head, w_lead, rest))
    for at in range(2, last + 1):
        table_rows = table_hop(table_rows, at)
        head = table_hop(head, at - 1)
        rest = table_hop(rest, at - 2)
        w_lead = lead_hop(w_lead, at - 2)
        table_rows, head, rest, w_lead = lax.optimization_barrier((table_rows, head, rest, w_lead))
    table = table_rows[0, :count].astype(jnp.int32)

    starts = [g ^ (CORE | CHIP), g ^ CHIP, g ^ CORE, g]
    places = jnp.concatenate(
        [s * quarter_blocks + jnp.arange(quarter_blocks) for s in starts] + [jnp.arange(PR)]
    )
    source = jnp.take(table, places)
    kept = (source >= PL).astype(jnp.int32)
    one = jnp.ones((1,), jnp.int32)
    ways = quarter_blocks // 2
    n = quarter_blocks

    def rows_at(first, size, adds, name, scale=one, ways=ways):
        return take_rows(
            front, mask, source[first : first + size], kept[first : first + size], scale, ways,
            adds, name,
        )

    diagonal = flip(rows_at(0, n, [], "far_rows"), "grp", CORE)
    first = rows_at(
        4 * n, PR, [(root_front, 0, 0)], "first_rows", (g == 0).astype(jnp.int32).reshape(1), PR
    )
    first = first + flip(first, "grp", CORE)
    head = table_hop(head, last)
    rest = table_hop(rest, last - 1)
    head, rest, diagonal, first = lax.optimization_barrier((head, rest, diagonal, first))
    first = first + flip(first, "grp", CHIP)
    far = [rows_at(n + i * ways, ways, [(diagonal, 0, i)], "far_sum") for i in range(2)]
    head, far = lax.optimization_barrier((head, far))
    far = [flip(part, "grp", CHIP) for part in far]
    rest = table_hop(rest, last)
    w_lead = lead_hop(w_lead, last - 1)

    work = [pltpu.VMEM((b, 2 * b), f32)]
    sq = shape((b, b), f32)
    sqh = shape((b, b), bf16)
    logs = shape((8, b), f32)

    def w_spec(k):
        return pl.BlockSpec((b, cols), lambda i: (k, 0))

    p01, inv0, inv1, x01, log01 = pl.pallas_call(
        leaf_two,
        grid=(1,),
        in_specs=[vmem, w_spec(0), w_spec(1), vmem],
        out_specs=[vmem] * 5,
        out_shape=(shape((2 * b, cols), bf16), sq, sq, sqh, logs),
        scratch_shapes=work,
        name="leaf_two",
    )(head, front, front, mask)

    w_lead = lead_hop(w_lead, last)
    w_lead = w_lead[0] if leads == 1 else jnp.concatenate(w_lead, axis=1)
    lead_rows = (PL * b + LOG_ROWS) * pr // cols
    pack = pl.pallas_call(
        leaf_last,
        grid=(1,),
        in_specs=[vmem, w_spec(2)] + [vmem] * 8,
        out_specs=vmem,
        out_shape=shape((b + lead_rows, cols), bf16),
        scratch_shapes=[pltpu.VMEM((b, b), f32)] + work,
        name="leaf_last",
    )(rest, front, w_lead, table_rows, mask, p01, inv0, inv1, x01, log01)
    near = flip(rows_at(2 * n, n, [], "near_rows"), "grp", CORE)

    def among(offsets):
        found = jnp.zeros((), jnp.bool_)
        for h in offsets:
            found = found | (zone == (g ^ h))
        return found

    def to_rows(value, staged):
        have, held, ready = [0], value, None
        order = list(reversed(bits(groups)))
        for at, bit in enumerate(order):
            if at == len(order) - 1:
                ready = (list(have), held)
            pairs = []
            for gi in range(groups):
                for h in have:
                    for j in range(spread):
                        src = (gi ^ h) * spread + j
                        dst = (gi ^ h ^ bit) * spread + j
                        pairs.append((gi * members + src, gi * members + dst))
            got = lax.ppermute(held, ("grp", "mem"), pairs)
            new = [h ^ bit for h in have]
            held = jnp.where(among(new), got, held)
            have = have + new
        slots = [held]
        stages = [(have, held)]
        if staged:
            stages = [ready, (new, got)]
        for i in range(1, spread):
            part = None
            for offsets, sent_part in stages:
                pairs = []
                for gi in range(groups):
                    for h in offsets:
                        for j in range(spread):
                            at = gi * members + (gi ^ h) * spread
                            pairs.append((at + j, at + (j ^ i)))
                got = lax.ppermute(sent_part, ("grp", "mem"), pairs)
                part = got if part is None else jnp.where(among(offsets), got, part)
            slots.append(part)
        return slots

    def across(value):
        far_value = flip(value, "grp", CHIP)
        both = jnp.concatenate([value, far_value], axis=0)
        return jnp.concatenate([both, flip(both, "grp", CORE)], axis=0)

    corner = [first[:, :lead_cols]] * leads
    for at in range(last + 1):
        corner = lead_hop(corner, at)
    corner = corner[0] if leads == 1 else jnp.concatenate(corner, axis=1)
    d01 = across(p01)
    r01 = to_rows(d01, True)
    pack = across(pack)
    pack, far[0] = lax.optimization_barrier((pack, far[0]))
    d2 = pack.reshape(groups, b + lead_rows, cols)[:, :b].reshape(groups * b, cols)
    r2 = to_rows(d2, True)
    leaves = jnp.stack([g, g ^ CHIP, g ^ CORE, g ^ (CORE | CHIP)])
    q, rinv0, rinv1, rx, logs_out = pl.pallas_call(
        root_step,
        in_specs=[smem] + [vmem] * 4,
        out_shape=(shape((pr, cols), bf16), sq, sq, sqh, logs),
        scratch_shapes=work,
        compiler_params=pltpu.CompilerParams(vmem_limit_bytes=32 << 20),
        name="root_step",
    )(leaves, corner, first, d01, pack)
    rq = to_rows(q, False)

    base = rows_at(
        3 * n, n, [(root_front, 0, 0), (near, 0, 0), (far[0], 0, 0), (far[1], 1, 0)], "base_rows"
    )
    slot_of = inner ^ jnp.arange(spread, dtype=jnp.int32)

    def update_body(*refs):
        update_kernel(spread, *refs)

    def whole_spec(array):
        return pl.BlockSpec(array.shape, lambda s, *pre: (0, 0))

    fixed = [d01, d2] + r01 + r2 + [rinv0, rinv1, rx]
    part, panel = pl.pallas_call(
        update_body,
        grid_spec=pltpu.PrefetchScalarGridSpec(
            num_scalar_prefetch=1,
            grid=(spread,),
            in_specs=[pl.BlockSpec((cols, cols), lambda s, place: (place[s], 0))]
            + [whole_spec(array) for array in fixed],
            out_specs=[
                pl.BlockSpec((cols, cols), lambda s, place: (s, 0)),
                pl.BlockSpec((cols, lead_cols if leads > 1 else pr), lambda s, place: (s, 0)),
            ],
        ),
        out_shape=(shape((quarter, cols), f32), shape((quarter, lead_cols), f32)),
        compiler_params=pltpu.CompilerParams(vmem_limit_bytes=48 << 20),
        name="update",
    )(slot_of, base, *fixed)
    if leads > 1:
        first_col = jnp.minimum(m, leads - 1) * lead_cols
        panel = jnp.concatenate([rows.astype(f32).T for rows in rq], axis=0)
        panel = lax.dynamic_slice_in_dim(panel, first_col, lead_cols, 1)
    info = jnp.concatenate([g * quarter + slot_of * cols, (m * cols).reshape(1)])

    def finish_body(*refs):
        finish_kernel(spread, *refs)

    root_factor = pl.pallas_call(
        finish_body,
        grid_spec=pltpu.PrefetchScalarGridSpec(
            num_scalar_prefetch=2,
            grid=(spread,),
            in_specs=[
                pl.BlockSpec((cols, cols), lambda s, place, info: (s, 0)),
                pl.BlockSpec((cols, lead_cols), lambda s, place, info: (s, 0)),
                whole_spec(q),
            ]
            + [whole_spec(rows) for rows in rq],
            out_specs=pl.BlockSpec((cols, cols), lambda s, place, info: (place[s], 0)),
        ),
        out_shape=shape((quarter, cols), f32),
        compiler_params=pltpu.CompilerParams(vmem_limit_bytes=32 << 20),
        name="finish",
    )(slot_of, info, part, panel, q, *rq)
    return root_factor, logs_out[0, : groups + 1]


def solution(mesh):
    in_specs = (P("grp", None, "mem"), P("grp", "mem"), P("grp", "mem"))
    out_specs = (P("grp", "mem"), P())
    return jax.shard_map(local, mesh=mesh, in_specs=in_specs, out_specs=out_specs, check_vma=False)
```

time: 277 us -> 221 us (0.80)
  the two profiles are of different devices: /device:TPU:24 before, /device:TPU:1 now
where the time goes in v3:
time: 221 us; the launch traced here: 218 us
  waiting for transfers between devices  68.9 us (31%)
  starting transfers between devices  54 us (24%)
  Pallas kernels  49.6 us (22%)
  local copies, waits for them, and re-layouts  23.3 us (11%)
  other arithmetic  20.6 us (9%)
    ppermute x19, waiting for transfers between devices, flip(): return lax.ppermute(value, axis, [(i, i ^ bit) for i in range(size)])  27.6 us
    ppermute x5, waiting for transfers between devices, to_rows(): got = lax.ppermute(sent_part, ('grp', 'mem'), pairs)  25.7 us
    ppermute x6, starting transfers between devices, lead_hop(): got = lax.ppermute(held, 'mem', pairs)  20.3 us
    unnamed x56, local copies, waits for them, and re-layouts  18.5 us
    ppermute x19, starting transfers between devices, flip(): return lax.ppermute(value, axis, [(i, i ^ bit) for i in range(size)])  16.9 us
    pallas_call x6, Pallas kernels, take_rows(): pl.pallas_call(body, grid_spec=pltpu.PrefetchScalarGridSpec(num_scalar_pr...  12.3 us
    ppermute x6, waiting for transfers between devices, to_rows(): got = lax.ppermute(held, ('grp', 'mem'), pairs)  11.2 us
    pallas_call x1, Pallas kernels, local(): pl.pallas_call(leaf_two, grid=(1,), in_specs=[vmem, w_spec(0), w_spec(1),...  9.42 us
  transfers between devices with their start and end apart: 36, of which 15 were waited for; matrix products, arithmetic and copies ran while one was open for 11% of the time, Pallas kernels for 20%

profile of v3, /device:TPU:1, one launch (start us, length us, event | category | flops | bytes accessed | tf_op | source)
XLA Modules:
  0.0 217.7 jit_solution(9499538819563577203)
XLA Ops:
  0.6 2.1 pick_pivots.1
  2.7 2.1 collective-permute-start
  6.7 1.5 collective-permute-start.1
  11.5 4.2 %collective-permute-start.6 = (f32[384,256]{1,0:T(8,128)}, f32[384,256]{1,0:T(8,128)S(1)}, u32[]{:S(2)}, u32[]{:S(2)}) collective-permute-start(f32[384,256]{1,0:T(8,128)} %get-tuple-element.43), channel_id=1, source_target_pairs={{0,4},{8,12},{16,20},{24,28}} | collective-permute-start | bytes 1179656 | tf_op jit(solution)/shard_map/ppermute | solution.py:340
  16.4 10.3 %collective-permute-done.3 = f32[8,128]{1,0:T(8,128)S(1)} collective-permute-done((f32[8,128]{1,0:T(8,128)S(1)}, f32[8,128]{1,0:T(8,128)S(1)}, u32[]{:S(2)}, u32[]{:S(2)}) %collective-permute-start.3) | collective-permute-done | bytes 4128 | tf_op jit(solution)/shard_map/ppermute | solution.py:43
  29.9 3.4 %copy-done = f32[1,4096,512]{2,1,0:T(8,128)S(1)} copy-done((f32[1,4096,512]{2,1,0:T(8,128)S(1)}, f32[1,4096,512]{2,1,0:T(8,128)}, u32[]{:S(2)}) %copy-start) | copy-done | bytes 8388632
  33.3 2.0 far_rows.1
  35.2 2.8 %collective-permute-start.10 = (f32[1024,512]{1,0:T(8,128)}, f32[1024,512]{1,0:T(8,128)}, u32[]{:S(2)}, u32[]{:S(2)}) collective-permute-start(f32[1024,512]{1,0:T(8,128)} %far_rows.1), channel_id=1, source_target_pairs={{0,8},{8,0},{16,24},{24,16},{1,9},{9,1},{17,25},{25,17},{2,10},{10... | collective-permute-start | bytes 6291464 | tf_op jit(solution)/shard_map/ppermute | solution.py:43
  38.1 4.8 %collective-permute-start.13 = (f32[384,256]{1,0:T(8,128)S(1)}, f32[384,256]{1,0:T(8,128)}, u32[]{:S(2)}, u32[]{:S(2)}) collective-permute-start(f32[384,256]{1,0:T(8,128)S(1)} %broadcast_select_fusion.10), channel_id=1, source_target_pairs={{0,2},{4,6},{8,10},{12,14},{16,18},{20,22},{24,26},{28,30}} | collective-permute-start | bytes 1179656 | tf_op jit(solution)/shard_map/ppermute | solution.py:340
  43.0 3.4 %copy-done.1 = f32[1,4096,512]{2,1,0:T(8,128)S(1)} copy-done((f32[1,4096,512]{2,1,0:T(8,128)S(1)}, f32[1,4096,512]{2,1,0:T(8,128)}, u32[]{:S(2)}) %copy-start.1) | copy-done | bytes 8388632
  47.5 3.1 %collective-permute-done.13 = f32[384,256]{1,0:T(8,128)} collective-permute-done((f32[384,256]{1,0:T(8,128)S(1)}, f32[384,256]{1,0:T(8,128)}, u32[]{:S(2)}, u32[]{:S(2)}) %collective-permute-start.13) | collective-permute-done | bytes 393248 | tf_op jit(solution)/shard_map/ppermute | solution.py:340
  50.7 2.1 collective-permute-start.14
  52.8 4.7 %collective-permute-done.8 = f32[384,128]{1,0:T(8,128)S(1)} collective-permute-done((f32[384,128]{1,0:T(8,128)S(1)}, f32[384,128]{1,0:T(8,128)S(1)}, u32[]{:S(2)}, u32[]{:S(2)}) %collective-permute-start.8) | collective-permute-done | bytes 196640 | tf_op jit(solution)/shard_map/ppermute | solution.py:43
  60.0 2.8 %far_sum.2 = f32[512,512]{1,0:T(8,128)} custom-call(s32[4]{0:T(128)S(1)} %get-tuple-element.75.refs_0_, s32[4]{0:T(128)S(1)} %get-tuple-element.73.refs_1_, s32[1]{0:T(128)} %constant.84.clone.1.refs_2_, f32[4096,512]{1,0:T(8,128)S(1)} %bitcast.36, f32[4096,512]{1,0:T(8,128)S(1)} %bitcast.37, f32[4096,512]{1,0:T(8,128)S(1)} %bitcast.38, ...), custom_call_target="tpu_custom_call" | custom-call | tf_op jit(solution)/shard_map/far_sum/pallas_call | solution.py:214
  62.8 1.9 far_sum.3
  65.7 9.4 %leaf_two.1 = (bf16[256,512]{1,0:T(8,128)(2,1)}, f32[128,128]{1,0:T(8,128)}, f32[128,128]{1,0:T(8,128)}, bf16[128,128]{1,0:T(8,128)(2,1)}, f32[8,128]{1,0:T(8,128)}) custom-call(f32[384,128]{1,0:T(8,128)} %add.169.head_ref, f32[4096,512]{1,0:T(8,128)} %bitcast.27, f32[4096,512]{1,0:T(8,128)} %bitcast.28, f32[8,512]{1,0:T(8,128)} %get-tuple-element.45.refs_7_.refs_5_.mask_ref), custom_call_target="tpu_custom_call" | custom-call | tf_op jit(solution)/shard_map/leaf_two/pallas_call | solution.py:412
  77.2 5.2 %collective-permute-done.19 = bf16[256,512]{1,0:T(8,128)(2,1)S(1)} collective-permute-done((bf16[256,512]{1,0:T(8,128)(2,1)}, bf16[256,512]{1,0:T(8,128)(2,1)S(1)}, u32[]{:S(2)}, u32[]{:S(2)}) %collective-permute-start.19) | collective-permute-done | bytes 262176 | tf_op jit(solution)/shard_map/ppermute | solution.py:43
  82.4 1.9 pad_maximum_fusion.2
  84.3 2.9 %collective-permute-start.20 = (bf16[512,512]{1,0:T(8,128)(2,1)}, bf16[512,512]{1,0:T(8,128)(2,1)}, u32[]{:S(2)}, u32[]{:S(2)}) collective-permute-start(bf16[512,512]{1,0:T(8,128)(2,1)} %pad_maximum_fusion.2), channel_id=1, source_target_pairs={{0,8},{8,0},{16,24},{24,16},{1,9},{9,1},{17,25},{25,17},{2,10},{10... | collective-permute-start | bytes 1572872 | tf_op jit(solution)/shard_map/ppermute | solution.py:43
  88.7 7.6 %leaf_last.1 = bf16[336,512]{1,0:T(8,128)(2,1)} custom-call(f32[384,128]{1,0:T(8,128)} %add.172.rest_ref, f32[4096,512]{1,0:T(8,128)} %bitcast.29, f32[384,256]{1,0:T(8,128)} %broadcast_select_fusion.9.w_lead_ref, f32[8,128]{1,0:T(8,128)} %copy-done.26, f32[8,512]{1,0:T(8,128)} %get-tuple-element.45.refs_7_.refs_5_.mask_ref, ...), custom_call_target="tpu_custom_call" | custom-call | tf_op jit(solution)/shard_map/leaf_last/pallas_call | solution.py:425
  96.3 1.3 collective-permute-start.15
  98.9 1.3 add.174.first_ref
  100.2 2.2 %collective-permute-start.30 = (f32[256,256]{1,0:T(8,128)S(1)}, f32[256,256]{1,0:T(8,128)S(1)}, u32[]{:S(2)}, u32[]{:S(2)}) collective-permute-start(f32[256,256]{1,0:T(8,128)S(1)} %slice.67), channel_id=1, source_target_pairs={{0,4},{8,12},{16,20},{24,28}} | collective-permute-start | bytes 786440 | tf_op jit(solution)/shard_map/ppermute | solution.py:340
  102.5 3.0 %collective-permute-done.15 = bf16[336,512]{1,0:T(8,128)(2,1)S(1)} collective-permute-done((bf16[336,512]{1,0:T(8,128)(2,1)}, bf16[336,512]{1,0:T(8,128)(2,1)S(1)}, u32[]{:S(2)}, u32[]{:S(2)}) %collective-permute-start.15) | collective-permute-done | bytes 344096 | tf_op jit(solution)/shard_map/ppermute | solution.py:43
  106.4 2.9 %collective-permute-start.16 = (bf16[672,512]{1,0:T(8,128)(2,1)}, bf16[672,512]{1,0:T(8,128)(2,1)}, u32[]{:S(2)}, u32[]{:S(2)}) collective-permute-start(bf16[672,512]{1,0:T(8,128)(2,1)} %pad_maximum_fusion.1), channel_id=1, source_target_pairs={{0,8},{8,0},{16,24},{24,16},{1,9},{9,1},{17,25},{25,17},{2,10},{10... | collective-permute-start | bytes 2064392 | tf_op jit(solution)/shard_map/ppermute | solution.py:43
  110.4 1.7 collective-permute-start.21
  112.8 5.5 %collective-permute-start.31 = (f32[256,256]{1,0:T(8,128)}, f32[256,256]{1,0:T(8,128)}, u32[]{:S(2)}, u32[]{:S(2)}) collective-permute-start(f32[256,256]{1,0:T(8,128)} %broadcast_select_fusion.11), channel_id=1, source_target_pairs={{0,2},{4,6},{8,10},{12,14},{16,18},{20,22},{24,26},{28,30}} | collective-permute-start | bytes 786440 | tf_op jit(solution)/shard_map/ppermute | solution.py:340
  118.3 3.4 %copy-done.2 = f32[1,4096,512]{2,1,0:T(8,128)S(1)} copy-done((f32[1,4096,512]{2,1,0:T(8,128)S(1)}, f32[1,4096,512]{2,1,0:T(8,128)}, u32[]{:S(2)}) %copy-start.2) | copy-done | bytes 8388632
  121.7 2.0 near_rows.1
  125.1 1.4 collective-permute-start.32
  126.6 1.3 pad_maximum_fusion.pack_ref
  129.9 8.9 %root_step.1 = (bf16[256,512]{1,0:T(8,128)(2,1)S(1)}, f32[128,128]{1,0:T(8,128)S(1)}, f32[128,128]{1,0:T(8,128)S(1)}, bf16[128,128]{1,0:T(8,128)(2,1)S(1)}, f32[8,128]{1,0:T(8,128)S(1)}) custom-call(s32[4]{0:T(128)S(1)} %pad_add_fusion.1.leaf_ref, f32[256,256]{1,0:T(8,128)S(1)} %broadcast_select_fusion.13.corner_ref, f32[256,512]{1,0:T(8,128)S(1)} %copy-done.7, ...), custom_call_target="tpu_custom_call" | custom-call | tf_op jit(solution)/shard_map/root_step/pallas_call | solution.py:493
  138.9 1.4 collective-permute-start.33
  141.3 1.3 collective-permute-start.22
  143.6 1.3 collective-permute-start.26
  146.2 1.3 collective-permute-start.34
  148.1 3.4 %copy-done.3 = f32[1,4096,512]{2,1,0:T(8,128)S(1)} copy-done((f32[1,4096,512]{2,1,0:T(8,128)S(1)}, f32[1,4096,512]{2,1,0:T(8,128)}, u32[]{:S(2)}) %copy-start.3) | copy-done | bytes 8388632
  152.8 3.0 %base_rows.1.refs_1_ = f32[1024,512]{1,0:T(8,128)S(1)} custom-call(s32[8]{0:T(128)S(1)} %copy-done.17, s32[8]{0:T(128)S(1)} %copy-done.18, s32[1]{0:T(128)} %constant.84.clone.1.refs_2_, f32[4096,512]{1,0:T(8,128)S(1)} %bitcast.48, f32[4096,512]{1,0:T(8,128)S(1)} %bitcast.49, f32[4096,512]{1,0:T(8,128)S(1)} %bitcast.50, f32[4096,512]{1,0:T(8,128)S(1)} %bitcast.51, ...), custom_call_target="tpu_custom_call" | custom-call | tf_op jit(solution)/shard_map/base_rows/pallas_call | solution.py:214
  156.5 11.2 %collective-permute-done.26 = bf16[512,512]{1,0:T(8,128)(2,1)} collective-permute-done((bf16[512,512]{1,0:T(8,128)(2,1)}, bf16[512,512]{1,0:T(8,128)(2,1)}, u32[]{:S(2)}, u32[]{:S(2)}) %collective-permute-start.26) | collective-permute-done | bytes 524320 | tf_op jit(solution)/shard_map/ppermute | solution.py:455
  167.7 4.2 %collective-permute-start.27 = (bf16[512,512]{1,0:T(8,128)(2,1)}, bf16[512,512]{1,0:T(8,128)(2,1)S(1)}, u32[]{:S(2)}, u32[]{:S(2)}) collective-permute-start(bf16[512,512]{1,0:T(8,128)(2,1)} %collective-permute-done.26), channel_id=1, source_target_pairs={{2,3},{3,2},{6,7},{7,6},{8,9},{9,8},{12,13},{13,12},{22,23},{23,22... | collective-permute-start | bytes 1572872 | tf_op jit(solution)/shard_map/ppermute | solution.py:472
  173.8 2.1 collective-permute-start.23
  177.0 1.5 collective-permute-start.35
  179.6 4.6 %collective-permute-done.27 = bf16[512,512]{1,0:T(8,128)(2,1)S(1)} collective-permute-done((bf16[512,512]{1,0:T(8,128)(2,1)}, bf16[512,512]{1,0:T(8,128)(2,1)S(1)}, u32[]{:S(2)}, u32[]{:S(2)}) %collective-permute-start.27) | collective-permute-done | bytes 524320 | tf_op jit(solution)/shard_map/ppermute | solution.py:472
  184.3 1.3 broadcast_select_fusion.2.refs_4_
  185.7 21.0 %collective-permute-done.23 = bf16[1024,512]{1,0:T(8,128)(2,1)S(1)} collective-permute-done((bf16[1024,512]{1,0:T(8,128)(2,1)}, bf16[1024,512]{1,0:T(8,128)(2,1)S(1)}, u32[]{:S(2)}, u32[]{:S(2)}) %collective-permute-start.23) | collective-permute-done | bytes 1048608 | tf_op jit(solution)/shard_map/ppermute | solution.py:472
  206.9 7.0 %update.1 = (f32[1024,512]{1,0:T(8,128)}, f32[1024,256]{1,0:T(8,128)S(1)}) custom-call(s32[2]{0:T(128)S(1)} %copy-done.16, f32[1024,512]{1,0:T(8,128)} %copy-done.5, bf16[1024,512]{1,0:T(8,128)(2,1)S(1)} %constant_dynamic-update-slice_fusion.d01_ref.refs_2_, bf16[512,512]{1,0:T(8,128)(2,1)S(1)} %bitcast.54, ...), custom_call_target="tpu_custom_call" | custom-call | tf_op jit(solution)/shard_map/update/pallas_call | solution.py:515
  213.8 1.6 copy-done.10
  215.4 2.2 %finish.1 = f32[1024,512]{1,0:T(8,128)} custom-call(s32[2]{0:T(128)S(1)} %copy-done.16, s32[3]{0:T(128)S(1)} %copy-done.19, f32[1024,512]{1,0:T(8,128)S(1)} %copy-done.10, f32[1024,256]{1,0:T(8,128)S(1)} %get-tuple-element.67.refs_3_, bf16[256,512]{1,0:T(8,128)(2,1)S(1)} %get-tuple-element.68.refs_4_, bf16[256,512]{1,0:T(8,128)(2,1)S(1)} %broadcast_select_fusion.7.refs_5_, ...), custom_call_target="tpu_custom_call" | custom-call | tf_op jit(solution)/shard_map/finish/pallas_call | solution.py:540
  (147 shorter events, 34.8 us)
Async XLA Ops:
  2.7 25.0 %copy-start.25 = (f32[384,256]{1,0:T(8,128)S(1)}, f32[384,256]{1,0:T(8,128)}, u32[]{:S(2)}) copy-start(f32[384,256]{1,0:T(8,128)} %get-tuple-element.43) | copy-start | bytes 1179652
  2.7 27.2 %copy-start.11 = (f32[8,512]{1,0:T(8,128)S(1)}, f32[8,512]{1,0:T(8,128)}, u32[]{:S(2)}) copy-start(f32[8,512]{1,0:T(8,128)} %get-tuple-element.45.refs_7_.refs_5_.mask_ref) | copy-start | bytes 49156
  2.7 3.3 %collective-permute-start = (f32[8,128]{1,0:T(8,128)}, f32[8,128]{1,0:T(8,128)S(1)}, u32[]{:S(2)}, u32[]{:S(2)}) collective-permute-start(f32[8,128]{1,0:T(8,128)} %get-tuple-element.36), channel_id=1, source_target_pairs={{0,1},{1,0},{2,3},{3,2},{4,5},{5,4},{6,7},{7,6},{8,9},{9,8},{10,11... | collective-permute-start | bytes 12296 | tf_op jit(solution)/shard_map/ppermute | solution.py:43
  4.9 5.7 %collective-permute-start.2 = (f32[384,128]{1,0:T(8,128)}, f32[384,128]{1,0:T(8,128)S(1)}, u32[]{:S(2)}, u32[]{:S(2)}) collective-permute-start(f32[384,128]{1,0:T(8,128)} %get-tuple-element.37), channel_id=1, source_target_pairs={{0,1},{1,0},{2,3},{3,2},{4,5},{5,4},{6,7},{7,6},{8,9},{9,8},{10,11... | collective-permute-start | bytes 589832 | tf_op jit(solution)/shard_map/ppermute | solution.py:43
  6.7 2.8 %collective-permute-start.1 = (f32[8,128]{1,0:T(8,128)S(1)}, f32[8,128]{1,0:T(8,128)S(1)}, u32[]{:S(2)}, u32[]{:S(2)}) collective-permute-start(f32[8,128]{1,0:T(8,128)S(1)} %add.160), channel_id=1, source_target_pairs={{0,2},{1,3},{2,0},{3,1},{4,6},{5,7},{6,4},{7,5},{8,10},{9,11},{10,... | collective-permute-start | bytes 12296 | tf_op jit(solution)/shard_map/ppermute | solution.py:43
  11.5 16.3 %collective-permute-start.6 = (f32[384,256]{1,0:T(8,128)}, f32[384,256]{1,0:T(8,128)S(1)}, u32[]{:S(2)}, u32[]{:S(2)}) collective-permute-start(f32[384,256]{1,0:T(8,128)} %get-tuple-element.43), channel_id=1, source_target_pairs={{0,4},{8,12},{16,20},{24,28}} | collective-permute-start | bytes 1179656 | tf_op jit(solution)/shard_map/ppermute | solution.py:340
  15.7 11.0 %collective-permute-start.4 = (f32[384,128]{1,0:T(8,128)S(1)}, f32[384,128]{1,0:T(8,128)S(1)}, u32[]{:S(2)}, u32[]{:S(2)}) collective-permute-start(f32[384,128]{1,0:T(8,128)S(1)} %add.162), channel_id=1, source_target_pairs={{0,2},{1,3},{2,0},{3,1},{4,6},{5,7},{6,4},{7,5},{8,10},{9,11},{10,... | collective-permute-start | bytes 589832 | tf_op jit(solution)/shard_map/ppermute | solution.py:43
  15.8 11.0 %collective-permute-start.5 = (f32[384,128]{1,0:T(8,128)}, f32[384,128]{1,0:T(8,128)S(1)}, u32[]{:S(2)}, u32[]{:S(2)}) collective-permute-start(f32[384,128]{1,0:T(8,128)} %get-tuple-element.42), channel_id=1, source_target_pairs={{0,1},{1,0},{2,3},{3,2},{4,5},{5,4},{6,7},{7,6},{8,9},{9,8},{10,11... | collective-permute-start | bytes 589832 | tf_op jit(solution)/shard_map/ppermute | solution.py:43
  15.9 10.8 %collective-permute-start.3 = (f32[8,128]{1,0:T(8,128)S(1)}, f32[8,128]{1,0:T(8,128)S(1)}, u32[]{:S(2)}, u32[]{:S(2)}) collective-permute-start(f32[8,128]{1,0:T(8,128)S(1)} %add.161), channel_id=1, source_target_pairs={{0,4},{1,5},{2,6},{3,7},{4,0},{5,1},{6,2},{7,3},{8,12},{9,13},{10,... | collective-permute-start | bytes 12296 | tf_op jit(solution)/shard_map/ppermute | solution.py:43
  33.3 9.7 %copy-start.4 = (f32[1024,512]{1,0:T(8,128)S(1)}, f32[1024,512]{1,0:T(8,128)}, u32[]{:S(2)}) copy-start(f32[1024,512]{1,0:T(8,128)} %refs_8_.1) | copy-start | bytes 6291460
  35.2 24.7 %collective-permute-start.10 = (f32[1024,512]{1,0:T(8,128)}, f32[1024,512]{1,0:T(8,128)}, u32[]{:S(2)}, u32[]{:S(2)}) collective-permute-start(f32[1024,512]{1,0:T(8,128)} %far_rows.1), channel_id=1, source_target_pairs={{0,8},{8,0},{16,24},{24,16},{1,9},{9,1},{17,25},{25,17},{2,10},{10... | collective-permute-start | bytes 6291464 | tf_op jit(solution)/shard_map/ppermute | solution.py:43
  38.1 12.6 %collective-permute-start.13 = (f32[384,256]{1,0:T(8,128)S(1)}, f32[384,256]{1,0:T(8,128)}, u32[]{:S(2)}, u32[]{:S(2)}) collective-permute-start(f32[384,256]{1,0:T(8,128)S(1)} %broadcast_select_fusion.10), channel_id=1, source_target_pairs={{0,2},{4,6},{8,10},{12,14},{16,18},{20,22},{24,26},{28,30}} | collective-permute-start | bytes 1179656 | tf_op jit(solution)/shard_map/ppermute | solution.py:340
  47.0 12.1 %collective-permute-start.11 = (f32[256,512]{1,0:T(8,128)S(1)}, f32[256,512]{1,0:T(8,128)S(1)}, u32[]{:S(2)}, u32[]{:S(2)}) collective-permute-start(f32[256,512]{1,0:T(8,128)S(1)} %first_rows.1), channel_id=1, source_target_pairs={{0,8},{8,0},{16,24},{24,16},{1,9},{9,1},{17,25},{25,17},{2,10},{10... | collective-permute-start | bytes 1572872 | tf_op jit(solution)/shard_map/ppermute | solution.py:43
  47.4 10.1 %collective-permute-start.8 = (f32[384,128]{1,0:T(8,128)S(1)}, f32[384,128]{1,0:T(8,128)S(1)}, u32[]{:S(2)}, u32[]{:S(2)}) collective-permute-start(f32[384,128]{1,0:T(8,128)S(1)} %add.164), channel_id=1, source_target_pairs={{0,4},{1,5},{2,6},{3,7},{4,0},{5,1},{6,2},{7,3},{8,12},{9,13},{10,... | collective-permute-start | bytes 589832 | tf_op jit(solution)/shard_map/ppermute | solution.py:43
  47.5 11.5 %collective-permute-start.9 = (f32[384,128]{1,0:T(8,128)S(1)}, f32[384,128]{1,0:T(8,128)S(1)}, u32[]{:S(2)}, u32[]{:S(2)}) collective-permute-start(f32[384,128]{1,0:T(8,128)S(1)} %add.165), channel_id=1, source_target_pairs={{0,2},{1,3},{2,0},{3,1},{4,6},{5,7},{6,4},{7,5},{8,10},{9,11},{10,... | collective-permute-start | bytes 589832 | tf_op jit(solution)/shard_map/ppermute | solution.py:43
  50.7 36.5 %collective-permute-start.14 = (f32[384,256]{1,0:T(8,128)S(1)}, f32[384,256]{1,0:T(8,128)}, u32[]{:S(2)}, u32[]{:S(2)}) collective-permute-start(f32[384,256]{1,0:T(8,128)S(1)} %broadcast_select_fusion.8), channel_id=1, source_target_pairs={{0,1},{2,3},{4,5},{6,7},{8,9},{10,11},{12,13},{14,15},{16,17},{18,... | collective-permute-start | bytes 1179656 | tf_op jit(solution)/shard_map/ppermute | solution.py:340
  75.2 7.3 %collective-permute-start.19 = (bf16[256,512]{1,0:T(8,128)(2,1)}, bf16[256,512]{1,0:T(8,128)(2,1)S(1)}, u32[]{:S(2)}, u32[]{:S(2)}) collective-permute-start(bf16[256,512]{1,0:T(8,128)(2,1)} %get-tuple-element.53.p_ref), channel_id=1, source_target_pairs={{0,16},{8,24},{16,0},{24,8},{1,17},{9,25},{17,1},{25,9},{2,18},{10... | collective-permute-start | bytes 786440 | tf_op jit(solution)/shard_map/ppermute | solution.py:43
  76.4 11.7 %collective-permute-start.12 = (f32[384,128]{1,0:T(8,128)S(1)}, f32[384,128]{1,0:T(8,128)S(1)}, u32[]{:S(2)}, u32[]{:S(2)}) collective-permute-start(f32[384,128]{1,0:T(8,128)S(1)} %add.170), channel_id=1, source_target_pairs={{0,4},{1,5},{2,6},{3,7},{4,0},{5,1},{6,2},{7,3},{8,12},{9,13},{10,... | collective-permute-start | bytes 589832 | tf_op jit(solution)/shard_map/ppermute | solution.py:43
  76.9 21.9 %collective-permute-start.29 = (f32[256,512]{1,0:T(8,128)}, f32[256,512]{1,0:T(8,128)}, u32[]{:S(2)}, u32[]{:S(2)}) collective-permute-start(f32[256,512]{1,0:T(8,128)} %add.171), channel_id=1, source_target_pairs={{0,16},{8,24},{16,0},{24,8},{1,17},{9,25},{17,1},{25,9},{2,18},{10... | collective-permute-start | bytes 1572872 | tf_op jit(solution)/shard_map/ppermute | solution.py:43
  82.4 13.9 %copy-start.23 = (bf16[256,512]{1,0:T(8,128)(2,1)}, bf16[256,512]{1,0:T(8,128)(2,1)S(1)}, u32[]{:S(2)}) copy-start(bf16[256,512]{1,0:T(8,128)(2,1)S(1)} %collective-permute-done.19) | copy-start | bytes 786436
  84.3 25.0 %collective-permute-start.20 = (bf16[512,512]{1,0:T(8,128)(2,1)}, bf16[512,512]{1,0:T(8,128)(2,1)}, u32[]{:S(2)}, u32[]{:S(2)}) collective-permute-start(bf16[512,512]{1,0:T(8,128)(2,1)} %pad_maximum_fusion.2), channel_id=1, source_target_pairs={{0,8},{8,0},{16,24},{24,16},{1,9},{9,1},{17,25},{25,17},{2,10},{10... | collective-permute-start | bytes 1572872 | tf_op jit(solution)/shard_map/ppermute | solution.py:43
  96.3 9.1 %collective-permute-start.15 = (bf16[336,512]{1,0:T(8,128)(2,1)}, bf16[336,512]{1,0:T(8,128)(2,1)S(1)}, u32[]{:S(2)}, u32[]{:S(2)}) collective-permute-start(bf16[336,512]{1,0:T(8,128)(2,1)} %leaf_last.1), channel_id=1, source_target_pairs={{0,16},{8,24},{16,0},{24,8},{1,17},{9,25},{17,1},{25,9},{2,18},{10... | collective-permute-start | bytes 1032200 | tf_op jit(solution)/shard_map/ppermute | solution.py:43
  97.6 30.4 %collective-permute-start.17 = (f32[512,512]{1,0:T(8,128)}, f32[512,512]{1,0:T(8,128)}, u32[]{:S(2)}, u32[]{:S(2)}) collective-permute-start(f32[512,512]{1,0:T(8,128)} %far_sum.2), channel_id=1, source_target_pairs={{0,16},{8,24},{16,0},{24,8},{1,17},{9,25},{17,1},{25,9},{2,18},{10... | collective-permute-start | bytes 3145736 | tf_op jit(solution)/shard_map/ppermute | solution.py:43
  100.1 12.7 %copy-start.6 = (f32[256,512]{1,0:T(8,128)}, f32[256,512]{1,0:T(8,128)S(1)}, u32[]{:S(2)}) copy-start(f32[256,512]{1,0:T(8,128)S(1)} %add.174.first_ref) | copy-start | bytes 1572868
  100.2 18.2 %copy-start.12 = (f32[8,512]{1,0:T(8,128)S(1)}, f32[8,512]{1,0:T(8,128)}, u32[]{:S(2)}) copy-start(f32[8,512]{1,0:T(8,128)} %get-tuple-element.45.refs_7_.refs_5_.mask_ref) | copy-start | bytes 49156
  100.2 11.9 %collective-permute-start.30 = (f32[256,256]{1,0:T(8,128)S(1)}, f32[256,256]{1,0:T(8,128)S(1)}, u32[]{:S(2)}, u32[]{:S(2)}) collective-permute-start(f32[256,256]{1,0:T(8,128)S(1)} %slice.67), channel_id=1, source_target_pairs={{0,4},{8,12},{16,20},{24,28}} | collective-permute-start | bytes 786440 | tf_op jit(solution)/shard_map/ppermute | solution.py:340
  105.5 12.9 %copy-start.22 = (bf16[336,512]{1,0:T(8,128)(2,1)}, bf16[336,512]{1,0:T(8,128)(2,1)S(1)}, u32[]{:S(2)}) copy-start(bf16[336,512]{1,0:T(8,128)(2,1)S(1)} %collective-permute-done.15) | copy-start | bytes 1032196
  106.4 18.7 %collective-permute-start.16 = (bf16[672,512]{1,0:T(8,128)(2,1)}, bf16[672,512]{1,0:T(8,128)(2,1)}, u32[]{:S(2)}, u32[]{:S(2)}) collective-permute-start(bf16[672,512]{1,0:T(8,128)(2,1)} %pad_maximum_fusion.1), channel_id=1, source_target_pairs={{0,8},{8,0},{16,24},{24,16},{1,9},{9,1},{17,25},{25,17},{2,10},{10... | collective-permute-start | bytes 2064392 | tf_op jit(solution)/shard_map/ppermute | solution.py:43
  110.4 29.9 %collective-permute-start.21 = (bf16[1024,512]{1,0:T(8,128)(2,1)S(1)}, bf16[1024,512]{1,0:T(8,128)(2,1)}, u32[]{:S(2)}, u32[]{:S(2)}) collective-permute-start(bf16[1024,512]{1,0:T(8,128)(2,1)S(1)} %constant_dynamic-update-slice_fusion.d01_ref.refs_2_), channel_id=1, source_target_pairs={{0,4},{1,5},{10,14},{11,15},{20,16},{21,17},{30,26},{31,27}} | collective-permute-start | bytes 3145736 | tf_op jit(solution)/shard_map/ppermute | solution.py:455
  112.8 11.3 %collective-permute-start.31 = (f32[256,256]{1,0:T(8,128)}, f32[256,256]{1,0:T(8,128)}, u32[]{:S(2)}, u32[]{:S(2)}) collective-permute-start(f32[256,256]{1,0:T(8,128)} %broadcast_select_fusion.11), channel_id=1, source_target_pairs={{0,2},{4,6},{8,10},{12,14},{16,18},{20,22},{24,26},{28,30}} | collective-permute-start | bytes 786440 | tf_op jit(solution)/shard_map/ppermute | solution.py:340
  123.7 24.4 %collective-permute-start.7 = (f32[1024,512]{1,0:T(8,128)}, f32[1024,512]{1,0:T(8,128)}, u32[]{:S(2)}, u32[]{:S(2)}) collective-permute-start(f32[1024,512]{1,0:T(8,128)} %near_rows.1), channel_id=1, source_target_pairs={{0,8},{8,0},{16,24},{24,16},{1,9},{9,1},{17,25},{25,17},{2,10},{10... | collective-permute-start | bytes 6291464 | tf_op jit(solution)/shard_map/ppermute | solution.py:43
  124.1 24.0 %collective-permute-start.18 = (f32[512,512]{1,0:T(8,128)}, f32[512,512]{1,0:T(8,128)}, u32[]{:S(2)}, u32[]{:S(2)}) collective-permute-start(f32[512,512]{1,0:T(8,128)} %copy-done.13), channel_id=1, source_target_pairs={{0,16},{8,24},{16,0},{24,8},{1,17},{9,25},{17,1},{25,9},{2,18},{10... | collective-permute-start | bytes 3145736 | tf_op jit(solution)/shard_map/ppermute | solution.py:43
  125.1 4.7 %collective-permute-start.32 = (f32[256,256]{1,0:T(8,128)S(1)}, f32[256,256]{1,0:T(8,128)S(1)}, u32[]{:S(2)}, u32[]{:S(2)}) collective-permute-start(f32[256,256]{1,0:T(8,128)S(1)} %broadcast_select_fusion.12), channel_id=1, source_target_pairs={{0,1},{2,3},{4,5},{6,7},{8,9},{10,11},{12,13},{14,15},{16,17},{18,... | collective-permute-start | bytes 786440 | tf_op jit(solution)/shard_map/ppermute | solution.py:340
  128.1 14.6 %copy-start.8 = (bf16[4,128,512]{2,1,0:T(8,128)(2,1)}, bf16[4,128,512]{2,1,0:T(8,128)(2,1)S(1)}, u32[]{:S(2)}) copy-start(bf16[4,128,512]{2,1,0:T(8,128)(2,1)S(1)} %slice.66) | copy-start | bytes 1572868
  128.1 14.5 %collective-permute-start.25 = (bf16[512,512]{1,0:T(8,128)(2,1)S(1)}, bf16[512,512]{1,0:T(8,128)(2,1)S(1)}, u32[]{:S(2)}, u32[]{:S(2)}) collective-permute-start(bf16[512,512]{1,0:T(8,128)(2,1)S(1)} %bitcast.53), channel_id=1, source_target_pairs={{0,4},{1,5},{10,14},{11,15},{20,16},{21,17},{30,26},{31,27}} | collective-permute-start | bytes 1572872 | tf_op jit(solution)/shard_map/ppermute | solution.py:455
  138.9 6.5 %collective-permute-start.33 = (bf16[256,512]{1,0:T(8,128)(2,1)S(1)}, bf16[256,512]{1,0:T(8,128)(2,1)}, u32[]{:S(2)}, u32[]{:S(2)}) collective-permute-start(bf16[256,512]{1,0:T(8,128)(2,1)S(1)} %get-tuple-element.68.refs_4_), channel_id=1, source_target_pairs={{0,4},{1,5},{10,14},{11,15},{20,16},{21,17},{30,26},{31,27}} | collective-permute-start | bytes 786440 | tf_op jit(solution)/shard_map/ppermute | solution.py:455
  141.3 32.5 %collective-permute-start.22 = (bf16[1024,512]{1,0:T(8,128)(2,1)}, bf16[1024,512]{1,0:T(8,128)(2,1)}, u32[]{:S(2)}, u32[]{:S(2)}) collective-permute-start(bf16[1024,512]{1,0:T(8,128)(2,1)} %broadcast_select_fusion), channel_id=1, source_target_pairs={{0,2},{1,3},{4,6},{5,7},{10,8},{11,9},{14,12},{15,13},{20,22},{21,... | collective-permute-start | bytes 3145736 | tf_op jit(solution)/shard_map/ppermute | solution.py:455
  143.6 24.1 %collective-permute-start.26 = (bf16[512,512]{1,0:T(8,128)(2,1)}, bf16[512,512]{1,0:T(8,128)(2,1)}, u32[]{:S(2)}, u32[]{:S(2)}) collective-permute-start(bf16[512,512]{1,0:T(8,128)(2,1)} %broadcast_select_fusion.3), channel_id=1, source_target_pairs={{0,2},{1,3},{4,6},{5,7},{10,8},{11,9},{14,12},{15,13},{20,22},{21,... | collective-permute-start | bytes 1572872 | tf_op jit(solution)/shard_map/ppermute | solution.py:455
  146.2 29.8 %collective-permute-start.34 = (bf16[256,512]{1,0:T(8,128)(2,1)}, bf16[256,512]{1,0:T(8,128)(2,1)}, u32[]{:S(2)}, u32[]{:S(2)}) collective-permute-start(bf16[256,512]{1,0:T(8,128)(2,1)} %broadcast_select_fusion.6), channel_id=1, source_target_pairs={{0,2},{1,3},{4,6},{5,7},{10,8},{11,9},{14,12},{15,13},{20,22},{21,... | collective-permute-start | bytes 786440 | tf_op jit(solution)/shard_map/ppermute | solution.py:455
  155.8 29.8 %copy-start.5 = (f32[1024,512]{1,0:T(8,128)}, f32[1024,512]{1,0:T(8,128)S(1)}, u32[]{:S(2)}) copy-start(f32[1024,512]{1,0:T(8,128)S(1)} %base_rows.1.refs_1_) | copy-start | bytes 6291460
  155.8 23.8 %collective-permute-start.28 = (bf16[512,512]{1,0:T(8,128)(2,1)}, bf16[512,512]{1,0:T(8,128)(2,1)S(1)}, u32[]{:S(2)}, u32[]{:S(2)}) collective-permute-start(bf16[512,512]{1,0:T(8,128)(2,1)} %broadcast_select_fusion.3), channel_id=1, source_target_pairs={{0,1},{1,0},{4,5},{5,4},{10,11},{11,10},{14,15},{15,14},{20,21},{2... | collective-permute-start | bytes 1572872 | tf_op jit(solution)/shard_map/ppermute | solution.py:472
  167.7 16.6 %collective-permute-start.27 = (bf16[512,512]{1,0:T(8,128)(2,1)}, bf16[512,512]{1,0:T(8,128)(2,1)S(1)}, u32[]{:S(2)}, u32[]{:S(2)}) collective-permute-start(bf16[512,512]{1,0:T(8,128)(2,1)} %collective-permute-done.26), channel_id=1, source_target_pairs={{2,3},{3,2},{6,7},{7,6},{8,9},{9,8},{12,13},{13,12},{22,23},{23,22... | collective-permute-start | bytes 1572872 | tf_op jit(solution)/shard_map/ppermute | solution.py:472
  173.1 12.6 %collective-permute-start.24 = (bf16[1024,512]{1,0:T(8,128)(2,1)}, bf16[1024,512]{1,0:T(8,128)(2,1)S(1)}, u32[]{:S(2)}, u32[]{:S(2)}) collective-permute-start(bf16[1024,512]{1,0:T(8,128)(2,1)} %broadcast_select_fusion), channel_id=1, source_target_pairs={{0,1},{1,0},{4,5},{5,4},{10,11},{11,10},{14,15},{15,14},{20,21},{2... | collective-permute-start | bytes 3145736 | tf_op jit(solution)/shard_map/ppermute | solution.py:472
  173.8 32.9 %collective-permute-start.23 = (bf16[1024,512]{1,0:T(8,128)(2,1)}, bf16[1024,512]{1,0:T(8,128)(2,1)S(1)}, u32[]{:S(2)}, u32[]{:S(2)}) collective-permute-start(bf16[1024,512]{1,0:T(8,128)(2,1)} %collective-permute-done.22), channel_id=1, source_target_pairs={{2,3},{3,2},{6,7},{7,6},{8,9},{9,8},{12,13},{13,12},{22,23},{23,22... | collective-permute-start | bytes 3145736 | tf_op jit(solution)/shard_map/ppermute | solution.py:472
  177.0 36.9 %collective-permute-start.35 = (bf16[256,512]{1,0:T(8,128)(2,1)S(1)}, bf16[256,512]{1,0:T(8,128)(2,1)S(1)}, u32[]{:S(2)}, u32[]{:S(2)}) collective-permute-start(bf16[256,512]{1,0:T(8,128)(2,1)S(1)} %broadcast_select_fusion.7.refs_5_), channel_id=1, source_target_pairs={{0,1},{1,0},{4,5},{5,4},{2,3},{3,2},{6,7},{7,6},{10,11},{11,10},{1... | collective-permute-start | bytes 786440 | tf_op jit(solution)/shard_map/ppermute | solution.py:472
  185.7 21.2 %copy-start.9 = (bf16[4,128,512]{2,1,0:T(8,128)(2,1)S(1)}, bf16[4,128,512]{2,1,0:T(8,128)(2,1)}, u32[]{:S(2)}) copy-start(bf16[4,128,512]{2,1,0:T(8,128)(2,1)} %copy-done.8) | copy-start | bytes 1572868
  185.7 21.2 %copy-start.15 = (bf16[128,128]{1,0:T(8,128)(2,1)S(1)}, bf16[128,128]{1,0:T(8,128)(2,1)}, u32[]{:S(2)}) copy-start(bf16[128,128]{1,0:T(8,128)(2,1)} %copy-done.14) | copy-start | bytes 98308
  185.7 21.2 %copy-start.16 = (s32[2]{0:T(128)S(1)}, s32[2]{0:T(128)}, u32[]{:S(2)}) copy-start(s32[2]{0:T(128)} %iota_xor_fusion.refs_0_) | copy-start | bytes 28
  (15 other events, 61.1 us)

commit v4 on v3

--- a/solution.py
+++ b/solution.py
@@ -220,7 +220,7 @@
             out_specs=pl.BlockSpec((ways * b, cols), lambda s, *pre: (s, 0)),
         ),
         out_shape=shape((source.shape[0] * b, cols), f32),
-        compiler_params=pltpu.CompilerParams(vmem_limit_bytes=32 << 20),
+        compiler_params=pltpu.CompilerParams(vmem_limit_bytes=60 << 20),
         name=name,
     )(source, kept, scale, *([front] * ways), mask, *[array for array, _, _ in adds])
 
@@ -366,7 +366,6 @@
         table_rows = table_hop(table_rows, at)
         head = table_hop(head, at - 1)
         rest = table_hop(rest, at - 2)
-        w_lead = lead_hop(w_lead, at - 2)
         table_rows, head, rest, w_lead = lax.optimization_barrier((table_rows, head, rest, w_lead))
     table = table_rows[0, :count].astype(jnp.int32)
 
@@ -393,13 +392,14 @@
     first = first + flip(first, "grp", CORE)
     head = table_hop(head, last)
     rest = table_hop(rest, last - 1)
-    head, rest, diagonal, first = lax.optimization_barrier((head, rest, diagonal, first))
+    w_lead = lead_hop(w_lead, 0)
+    head, rest, w_lead, diagonal, first = lax.optimization_barrier(
+        (head, rest, w_lead, diagonal, first)
+    )
     first = first + flip(first, "grp", CHIP)
-    far = [rows_at(n + i * ways, ways, [(diagonal, 0, i)], "far_sum") for i in range(2)]
-    head, far = lax.optimization_barrier((head, far))
-    far = [flip(part, "grp", CHIP) for part in far]
     rest = table_hop(rest, last)
-    w_lead = lead_hop(w_lead, last - 1)
+    for at in range(1, last):
+        w_lead = lead_hop(w_lead, at)
 
     work = [pltpu.VMEM((b, 2 * b), f32)]
     sq = shape((b, b), f32)
@@ -419,6 +419,17 @@
         name="leaf_two",
     )(head, front, front, mask)
 
+    p01, diagonal = lax.optimization_barrier((p01, diagonal))
+    far = [rows_at(n + i * ways, ways, [(diagonal, 0, i)], "far_sum") for i in range(2)]
+    far = [flip(part, "grp", CHIP) for part in far]
+
+    def across(value):
+        far_value = flip(value, "grp", CHIP)
+        both = jnp.concatenate([value, far_value], axis=0)
+        return jnp.concatenate([both, flip(both, "grp", CORE)], axis=0)
+
+    d01 = across(p01)
+    rest, d01 = lax.optimization_barrier((rest, d01))
     w_lead = lead_hop(w_lead, last)
     w_lead = w_lead[0] if leads == 1 else jnp.concatenate(w_lead, axis=1)
     lead_rows = (PL * b + LOG_ROWS) * pr // cols
@@ -439,56 +450,57 @@
             found = found | (zone == (g ^ h))
         return found
 
-    def to_rows(value, staged):
-        have, held, ready = [0], value, None
-        order = list(reversed(bits(groups)))
-        for at, bit in enumerate(order):
-            if at == len(order) - 1:
-                ready = (list(have), held)
-            pairs = []
-            for gi in range(groups):
-                for h in have:
-                    for j in range(spread):
-                        src = (gi ^ h) * spread + j
-                        dst = (gi ^ h ^ bit) * spread + j
-                        pairs.append((gi * members + src, gi * members + dst))
-            got = lax.ppermute(held, ("grp", "mem"), pairs)
-            new = [h ^ bit for h in have]
-            held = jnp.where(among(new), got, held)
-            have = have + new
+    def zone_hop(state):
+        have, held, _ = state
+        bit = groups // 2 // len(have)
+        pairs = []
+        for gi in range(groups):
+            for h in have:
+                for j in range(spread):
+                    src = (gi ^ h) * spread + j
+                    dst = (gi ^ h ^ bit) * spread + j
+                    pairs.append((gi * members + src, gi * members + dst))
+        got = lax.ppermute(held, ("grp", "mem"), pairs)
+        new = [h ^ bit for h in have]
+        return have + new, jnp.where(among(new), got, held), (new, got)
+
+    def inner_hop(stage, i):
+        offsets, value = stage
+        pairs = []
+        for gi in range(groups):
+            for h in offsets:
+                for j in range(spread):
+                    at = gi * members + (gi ^ h) * spread
+                    pairs.append((at + j, at + (j ^ i)))
+        return lax.ppermute(value, ("grp", "mem"), pairs)
+
+    def inner_hops(state, early=None):
+        have, held, last_stage = state
         slots = [held]
-        stages = [(have, held)]
-        if staged:
-            stages = [ready, (new, got)]
         for i in range(1, spread):
-            part = None
-            for offsets, sent_part in stages:
-                pairs = []
-                for gi in range(groups):
-                    for h in offsets:
-                        for j in range(spread):
-                            at = gi * members + (gi ^ h) * spread
-                            pairs.append((at + j, at + (j ^ i)))
-                got = lax.ppermute(sent_part, ("grp", "mem"), pairs)
-                part = got if part is None else jnp.where(among(offsets), got, part)
-            slots.append(part)
+            if early is None:
+                slots.append(inner_hop((have, held), i))
+            else:
+                got = inner_hop(last_stage, i)
+                slots.append(jnp.where(among(last_stage[0]), got, early[i - 1]))
         return slots
 
-    def across(value):
-        far_value = flip(value, "grp", CHIP)
-        both = jnp.concatenate([value, far_value], axis=0)
-        return jnp.concatenate([both, flip(both, "grp", CORE)], axis=0)
+    def early_hops(state):
+        return [inner_hop((state[0], state[1]), i) for i in range(1, spread)]
 
     corner = [first[:, :lead_cols]] * leads
     for at in range(last + 1):
         corner = lead_hop(corner, at)
     corner = corner[0] if leads == 1 else jnp.concatenate(corner, axis=1)
-    d01 = across(p01)
-    r01 = to_rows(d01, True)
+    s01 = zone_hop(([0], d01, None))
+    pack, far[0] = lax.optimization_barrier((pack, far[0]))
     pack = across(pack)
-    pack, far[0] = lax.optimization_barrier((pack, far[0]))
+    pack, held = lax.optimization_barrier((pack, s01[1]))
+    s01 = (s01[0], held, None)
+    early01 = early_hops(s01)
+    s01 = zone_hop(s01)
     d2 = pack.reshape(groups, b + lead_rows, cols)[:, :b].reshape(groups * b, cols)
-    r2 = to_rows(d2, True)
+    s2 = zone_hop(([0], d2, None))
     leaves = jnp.stack([g, g ^ CHIP, g ^ CORE, g ^ (CORE | CHIP)])
     q, rinv0, rinv1, rx, logs_out = pl.pallas_call(
         root_step,
@@ -498,7 +510,13 @@
         compiler_params=pltpu.CompilerParams(vmem_limit_bytes=32 << 20),
         name="root_step",
     )(leaves, corner, first, d01, pack)
-    rq = to_rows(q, False)
+    q, far[1], held = lax.optimization_barrier((q, far[1], s2[1]))
+    s2 = (s2[0], held, None)
+    rq = inner_hops(zone_hop(zone_hop(([0], q, None))))
+    early2 = early_hops(s2)
+    s2 = zone_hop(s2)
+    r01 = inner_hops(s01, early01)
+    r2 = inner_hops(s2, early2)
 
     base = rows_at(
         3 * n, n, [(root_front, 0, 0), (near, 0, 0), (far[0], 0, 0), (far[1], 1, 0)], "base_rows"

time: 221 us -> 231 us (1.045)
  local copies, waits for them, and re-layouts: 23.3 us -> 8.9 us
  Pallas kernels: 49.6 us -> 61.3 us
  waiting for transfers between devices: 68.9 us -> 78.5 us
  starting transfers between devices: 54 us -> 59.5 us
    ppermute x19, waiting for transfers between devices: 27.6 us -> 50.1 us  [flip(): return lax.ppermute(value, axis, [(i, i ^ bit) for i in range(size)])]
    unnamed x56 -> x30, local copies, waits for them, and re-layouts: 18.5 us -> 3.62 us
    pallas_call x6, Pallas kernels: 12.3 us -> 21.6 us  [take_rows(): pl.pallas_call(body, grid_spec=pltpu.PrefetchScalarGridSpec(num_scalar_pr...]
    ppermute x11, waiting for transfers between devices: 36.8 us -> 28.3 us  [the longest x5 21.5 us: inner_hop(): return lax.ppermute(value, ('grp', 'mem'), pairs)]
    ppermute x19, starting transfers between devices: 16.9 us -> 23.1 us  [flip(): return lax.ppermute(value, axis, [(i, i ^ bit) for i in range(size)])]
    ppermute x6, waiting for transfers between devices: 4.52 us -> 0.02 us  [lead_hop(): got = lax.ppermute(held, 'mem', pairs)]
    add x9, other arithmetic: 4.05 us -> 6.58 us  [table_hop(): return value + flip(value, 'mem', hops[at])]
    select_n x8, other arithmetic: 6.36 us -> 3.86 us  [the longest x6 3.69 us: zone_hop(): return (have + new, jnp.where(among(new), got, held), (new, got))]
  transfers between devices with their start and end apart: 36 -> 36, of which waited for: 15 -> 14; matrix products, arithmetic and copies ran while one was open for 11% -> 10% of each run, Pallas kernels for 20% -> 19%
where the time goes in v4:
time: 231 us; the launch traced here: 230 us
  waiting for transfers between devices  78.5 us (34%)
  Pallas kernels  61.3 us (27%)
  starting transfers between devices  59.5 us (26%)
  other arithmetic  20.6 us (9%)
  local copies, waits for them, and re-layouts  8.9 us (4%)
    ppermute x19, waiting for transfers between devices, flip(): return lax.ppermute(value, axis, [(i, i ^ bit) for i in range(size)])  50.1 us
    ppermute x19, starting transfers between devices, flip(): return lax.ppermute(value, axis, [(i, i ^ bit) for i in range(size)])  23.1 us
    pallas_call x6, Pallas kernels, take_rows(): pl.pallas_call(body, grid_spec=pltpu.PrefetchScalarGridSpec(num_scalar_pr...  21.6 us
    ppermute x5, waiting for transfers between devices, inner_hop(): return lax.ppermute(value, ('grp', 'mem'), pairs)  21.5 us
    ppermute x6, starting transfers between devices, lead_hop(): got = lax.ppermute(held, 'mem', pairs)  21.2 us
    pallas_call x1, Pallas kernels, local(): pl.pallas_call(leaf_two, grid=(1,), in_specs=[vmem, w_spec(0), w_spec(1),...  10.1 us
    pallas_call x1, Pallas kernels, local(): pl.pallas_call(root_step, in_specs=[smem] + [vmem] * 4, out_shape=(shape(...  9.75 us
    ppermute x5, starting transfers between devices, inner_hop(): return lax.ppermute(value, ('grp', 'mem'), pairs)  7.97 us
  transfers between devices with their start and end apart: 36, of which 14 were waited for; matrix products, arithmetic and copies ran while one was open for 10% of the time, Pallas kernels for 19%

profile of v4, /device:TPU:1, one launch (start us, length us, event | category | flops | bytes accessed | tf_op | source)
XLA Modules:
  0.0 229.7 jit_solution(13945740424785755452)
XLA Ops:
  0.6 2.1 pick_pivots.1
  2.7 2.1 collective-permute-start
  6.7 1.5 collective-permute-start.1
  8.2 1.3 collective-permute-done.1
  11.4 1.4 collective-permute-start.4
  13.3 2.3 %collective-permute-start.3 = (f32[8,128]{1,0:T(8,128)S(1)}, f32[8,128]{1,0:T(8,128)S(1)}, u32[]{:S(2)}, u32[]{:S(2)}) collective-permute-start(f32[8,128]{1,0:T(8,128)S(1)} %add.161), channel_id=1, source_target_pairs={{0,4},{1,5},{2,6},{3,7},{4,0},{5,1},{6,2},{7,3},{8,12},{9,13},{10,... | collective-permute-start | bytes 12296 | tf_op jit(solution)/shard_map/ppermute | solution.py:43
  20.9 3.4 %far_rows.1 = f32[1024,512]{1,0:T(8,128)} custom-call(s32[8]{0:T(128)} %get-tuple-element.93.refs_0_, s32[8]{0:T(128)} %get-tuple-element.90.refs_1_, s32[1]{0:T(128)} %constant.83.clone.1.refs_2_, f32[4096,512]{1,0:T(8,128)} %bitcast.30, f32[4096,512]{1,0:T(8,128)} %bitcast.31, f32[4096,512]{1,0:T(8,128)} %bitcast.32, f32[4096,512]{1,0:T(8,128)} %bitcast.33, ...), custom_call_target="tpu_custom_call" | custom-call | tf_op jit(solution)/shard_map/far_rows/pallas_call | solution.py:214
  24.3 3.3 %collective-permute-start.10 = (f32[1024,512]{1,0:T(8,128)}, f32[1024,512]{1,0:T(8,128)S(1)}, u32[]{:S(2)}, u32[]{:S(2)}) collective-permute-start(f32[1024,512]{1,0:T(8,128)} %far_rows.1), channel_id=1, source_target_pairs={{0,8},{8,0},{16,24},{24,16},{1,9},{9,1},{17,25},{25,17},{2,10},{10... | collective-permute-start | bytes 6291464 | tf_op jit(solution)/shard_map/ppermute | solution.py:43
  27.6 5.0 %collective-permute-start.9 = (f32[384,256]{1,0:T(8,128)S(1)}, f32[384,256]{1,0:T(8,128)}, u32[]{:S(2)}, u32[]{:S(2)}) collective-permute-start(f32[384,256]{1,0:T(8,128)S(1)} %copy-done.13), channel_id=1, source_target_pairs={{0,4},{8,12},{16,20},{24,28}} | collective-permute-start | bytes 1179656 | tf_op jit(solution)/shard_map/ppermute | solution.py:340
  33.7 2.8 %first_rows.1 = f32[256,512]{1,0:T(8,128)} custom-call(s32[2]{0:T(128)} %slice.55.refs_0_, s32[2]{0:T(128)} %slice.56.refs_1_, s32[1]{0:T(128)} %bitcast.10.refs_2_, f32[4096,512]{1,0:T(8,128)} %bitcast.34, f32[4096,512]{1,0:T(8,128)} %bitcast.35, f32[8,512]{1,0:T(8,128)} %get-tuple-element.52.refs_7_.refs_5_.mask_ref, f32[1024,512]{1,0:T(8,128)} %refs_8_.1), custom_call_target="tpu_custom_call" | custom-call | tf_op jit(solution)/shard_map/first_rows/pallas_call | solution.py:214
  36.7 8.3 %collective-permute-done.7 = f32[384,128]{1,0:T(8,128)} collective-permute-done((f32[384,128]{1,0:T(8,128)S(1)}, f32[384,128]{1,0:T(8,128)}, u32[]{:S(2)}, u32[]{:S(2)}) %collective-permute-start.7) | collective-permute-done | bytes 196640 | tf_op jit(solution)/shard_map/ppermute | solution.py:43
  45.0 1.6 add.168.head_ref
  46.7 2.1 collective-permute-done.8
  48.8 1.6 add.169
  52.6 10.1 %leaf_two.1 = (bf16[256,512]{1,0:T(8,128)(2,1)}, f32[128,128]{1,0:T(8,128)}, f32[128,128]{1,0:T(8,128)}, bf16[128,128]{1,0:T(8,128)(2,1)}, f32[8,128]{1,0:T(8,128)}) custom-call(f32[384,128]{1,0:T(8,128)} %add.168.head_ref, f32[4096,512]{1,0:T(8,128)} %bitcast.36, f32[4096,512]{1,0:T(8,128)} %bitcast.37, f32[8,512]{1,0:T(8,128)} %get-tuple-element.52.refs_7_.refs_5_.mask_ref), custom_call_target="tpu_custom_call" | custom-call | tf_op jit(solution)/shard_map/leaf_two/pallas_call | solution.py:412
  63.9 5.0 %collective-permute-start.15 = (f32[384,256]{1,0:T(8,128)S(1)}, f32[384,256]{1,0:T(8,128)S(1)}, u32[]{:S(2)}, u32[]{:S(2)}) collective-permute-start(f32[384,256]{1,0:T(8,128)S(1)} %broadcast_select_fusion.10), channel_id=1, source_target_pairs={{0,2},{4,6},{8,10},{12,14},{16,18},{20,22},{24,26},{28,30}} | collective-permute-start | bytes 1179656 | tf_op jit(solution)/shard_map/ppermute | solution.py:340
  70.2 3.5 %far_sum.2 = f32[512,512]{1,0:T(8,128)} custom-call(s32[4]{0:T(128)} %get-tuple-element.89.refs_0_, s32[4]{0:T(128)} %get-tuple-element.87.refs_1_, s32[1]{0:T(128)} %constant.83.clone.1.refs_2_, f32[4096,512]{1,0:T(8,128)} %bitcast.41, f32[4096,512]{1,0:T(8,128)} %bitcast.39, f32[4096,512]{1,0:T(8,128)} %bitcast.40, f32[4096,512]{1,0:T(8,128)} %bitcast.38, ...), custom_call_target="tpu_custom_call" | custom-call | tf_op jit(solution)/shard_map/far_sum/pallas_call | solution.py:214
  76.0 1.6 collective-permute-start.14
  77.6 2.1 collective-permute-start.16
  79.7 3.2 %collective-permute-start.12 = (f32[384,128]{1,0:T(8,128)S(1)}, f32[384,128]{1,0:T(8,128)S(1)}, u32[]{:S(2)}, u32[]{:S(2)}) collective-permute-start(f32[384,128]{1,0:T(8,128)S(1)} %copy-done.12), channel_id=1, source_target_pairs={{0,4},{1,5},{2,6},{3,7},{4,0},{5,1},{6,2},{7,3},{8,12},{9,13},{10,... | collective-permute-start | bytes 589832 | tf_op jit(solution)/shard_map/ppermute | solution.py:43
  82.9 8.9 %collective-permute-done.12 = f32[384,128]{1,0:T(8,128)S(1)} collective-permute-done((f32[384,128]{1,0:T(8,128)S(1)}, f32[384,128]{1,0:T(8,128)S(1)}, u32[]{:S(2)}, u32[]{:S(2)}) %collective-permute-start.12) | collective-permute-done | bytes 196640 | tf_op jit(solution)/shard_map/ppermute | solution.py:43
  92.5 16.2 %collective-permute-done.18 = f32[256,512]{1,0:T(8,128)S(1)} collective-permute-done((f32[256,512]{1,0:T(8,128)S(1)}, f32[256,512]{1,0:T(8,128)S(1)}, u32[]{:S(2)}, u32[]{:S(2)}) %collective-permute-start.18) | collective-permute-done | bytes 524320 | tf_op jit(solution)/shard_map/ppermute | solution.py:43
  108.8 5.8 %collective-permute-start.19 = (f32[256,256]{1,0:T(8,128)S(1)}, f32[256,256]{1,0:T(8,128)}, u32[]{:S(2)}, u32[]{:S(2)}) collective-permute-start(f32[256,256]{1,0:T(8,128)S(1)} %slice.66), channel_id=1, source_target_pairs={{0,4},{8,12},{16,20},{24,28}} | collective-permute-start | bytes 786440 | tf_op jit(solution)/shard_map/ppermute | solution.py:340
  117.5 7.6 %leaf_last.1 = bf16[336,512]{1,0:T(8,128)(2,1)} custom-call(f32[384,128]{1,0:T(8,128)} %add.172.rest_ref, f32[4096,512]{1,0:T(8,128)} %bitcast.42, f32[384,256]{1,0:T(8,128)} %broadcast_select_fusion.9.w_lead_ref, f32[8,128]{1,0:T(8,128)} %copy-done.14, f32[8,512]{1,0:T(8,128)} %get-tuple-element.52.refs_7_.refs_5_.mask_ref, ...), custom_call_target="tpu_custom_call" | custom-call | tf_op jit(solution)/shard_map/leaf_last/pallas_call | solution.py:436
  125.4 1.4 collective-permute-start.20
  126.8 5.2 %collective-permute-done.22 = bf16[336,512]{1,0:T(8,128)(2,1)S(1)} collective-permute-done((bf16[336,512]{1,0:T(8,128)(2,1)}, bf16[336,512]{1,0:T(8,128)(2,1)S(1)}, u32[]{:S(2)}, u32[]{:S(2)}) %collective-permute-start.22) | collective-permute-done | bytes 344096 | tf_op jit(solution)/shard_map/ppermute | solution.py:43
  132.8 1.9 pad_maximum_fusion.2
  134.7 3.8 %collective-permute-start.23 = (bf16[672,512]{1,0:T(8,128)(2,1)}, bf16[672,512]{1,0:T(8,128)(2,1)}, u32[]{:S(2)}, u32[]{:S(2)}) collective-permute-start(bf16[672,512]{1,0:T(8,128)(2,1)} %pad_maximum_fusion.2), channel_id=1, source_target_pairs={{0,8},{8,0},{16,24},{24,16},{1,9},{9,1},{17,25},{25,17},{2,10},{10... | collective-permute-start | bytes 2064392 | tf_op jit(solution)/shard_map/ppermute | solution.py:43
  138.5 3.3 %near_rows.1 = f32[1024,512]{1,0:T(8,128)} custom-call(s32[8]{0:T(128)} %get-tuple-element.94.refs_0_, s32[8]{0:T(128)} %get-tuple-element.91.refs_1_, s32[1]{0:T(128)} %constant.83.clone.1.refs_2_, f32[4096,512]{1,0:T(8,128)} %bitcast.43, f32[4096,512]{1,0:T(8,128)} %bitcast.44, f32[4096,512]{1,0:T(8,128)} %bitcast.45, f32[4096,512]{1,0:T(8,128)} %bitcast.46, ...), custom_call_target="tpu_custom_call" | custom-call | tf_op jit(solution)/shard_map/near_rows/pallas_call | solution.py:214
  141.8 3.4 %far_sum.3 = f32[512,512]{1,0:T(8,128)} custom-call(s32[4]{0:T(128)} %get-tuple-element.88.refs_0_, s32[4]{0:T(128)} %get-tuple-element.86.refs_1_, s32[1]{0:T(128)} %constant.83.clone.1.refs_2_, f32[4096,512]{1,0:T(8,128)} %bitcast.47, f32[4096,512]{1,0:T(8,128)} %bitcast.48, f32[4096,512]{1,0:T(8,128)} %bitcast.49, f32[4096,512]{1,0:T(8,128)} %bitcast.50, ...), custom_call_target="tpu_custom_call" | custom-call | tf_op jit(solution)/shard_map/far_sum/pallas_call | solution.py:214
  146.2 2.0 collective-permute-start.21
  150.5 1.5 collective-permute-start.26
  152.1 1.5 collective-permute-start.27
  154.7 9.7 %root_step.1 = (bf16[256,512]{1,0:T(8,128)(2,1)}, f32[128,128]{1,0:T(8,128)S(1)}, f32[128,128]{1,0:T(8,128)S(1)}, bf16[128,128]{1,0:T(8,128)(2,1)S(1)}, f32[8,128]{1,0:T(8,128)S(1)}) custom-call(s32[4]{0:T(128)S(1)} %pad_add_fusion.1.leaf_ref, f32[256,256]{1,0:T(8,128)S(1)} %broadcast_select_fusion.13.corner_ref, f32[256,512]{1,0:T(8,128)S(1)} %add.174.first_ref, ...), custom_call_target="tpu_custom_call" | custom-call | tf_op jit(solution)/shard_map/root_step/pallas_call | solution.py:505
  165.7 4.0 %collective-permute-done.25.refs_11_ = f32[512,512]{1,0:T(8,128)} collective-permute-done((f32[512,512]{1,0:T(8,128)}, f32[512,512]{1,0:T(8,128)}, u32[]{:S(2)}, u32[]{:S(2)}) %collective-permute-start.25) | collective-permute-done | bytes 1048608 | tf_op jit(solution)/shard_map/ppermute | solution.py:43
  169.7 1.3 collective-permute-start.30
  171.8 1.7 collective-permute-start.29
  174.6 5.4 %base_rows.1.refs_1_ = f32[1024,512]{1,0:T(8,128)} custom-call(s32[8]{0:T(128)} %get-tuple-element.95.refs_0_, s32[8]{0:T(128)} %get-tuple-element.92.refs_1_, s32[1]{0:T(128)} %constant.83.clone.1.refs_2_, f32[4096,512]{1,0:T(8,128)} %bitcast.51, f32[4096,512]{1,0:T(8,128)} %bitcast.52, f32[4096,512]{1,0:T(8,128)} %bitcast.53, f32[4096,512]{1,0:T(8,128)} %bitcast.54, ...), custom_call_target="tpu_custom_call" | custom-call | tf_op jit(solution)/shard_map/base_rows/pallas_call | solution.py:214
  181.1 1.3 collective-permute-start.34
  182.4 1.9 collective-permute-start.31
  184.3 3.6 %collective-permute-start.28 = (bf16[1024,512]{1,0:T(8,128)(2,1)}, bf16[1024,512]{1,0:T(8,128)(2,1)S(1)}, u32[]{:S(2)}, u32[]{:S(2)}) collective-permute-start(bf16[1024,512]{1,0:T(8,128)(2,1)} %collective-permute-done.27), channel_id=1, source_target_pairs={{2,3},{3,2},{6,7},{7,6},{8,9},{9,8},{12,13},{13,12},{22,23},{23,22... | collective-permute-start | bytes 3145736 | tf_op jit(solution)/shard_map/ppermute | solution.py:475
  188.0 6.8 %collective-permute-done.34 = bf16[256,512]{1,0:T(8,128)(2,1)S(1)} collective-permute-done((bf16[256,512]{1,0:T(8,128)(2,1)S(1)}, bf16[256,512]{1,0:T(8,128)(2,1)S(1)}, u32[]{:S(2)}, u32[]{:S(2)}) %collective-permute-start.34) | collective-permute-done | bytes 262176 | tf_op jit(solution)/shard_map/ppermute | solution.py:463
  194.9 1.3 broadcast_select_fusion.1.refs_4_
  196.3 2.1 collective-permute-done.31
  198.5 19.4 %collective-permute-done.28 = bf16[1024,512]{1,0:T(8,128)(2,1)S(1)} collective-permute-done((bf16[1024,512]{1,0:T(8,128)(2,1)}, bf16[1024,512]{1,0:T(8,128)(2,1)S(1)}, u32[]{:S(2)}, u32[]{:S(2)}) %collective-permute-start.28) | collective-permute-done | bytes 1048608 | tf_op jit(solution)/shard_map/ppermute | solution.py:475
  218.0 7.0 %update.1 = (f32[1024,512]{1,0:T(8,128)}, f32[1024,256]{1,0:T(8,128)S(1)}) custom-call(s32[2]{0:T(128)S(1)} %iota_xor_fusion.refs_0_, f32[1024,512]{1,0:T(8,128)} %base_rows.1.refs_1_, bf16[1024,512]{1,0:T(8,128)(2,1)S(1)} %pad_maximum_fusion.1.d01_ref.refs_2_, bf16[512,512]{1,0:T(8,128)(2,1)S(1)} %bitcast.28, ...), custom_call_target="tpu_custom_call" | custom-call | tf_op jit(solution)/shard_map/update/pallas_call | solution.py:533
  225.0 1.6 copy-done
  226.6 3.2 %finish.1 = f32[1024,512]{1,0:T(8,128)} custom-call(s32[2]{0:T(128)S(1)} %iota_xor_fusion.refs_0_, s32[3]{0:T(128)S(1)} %pad_add_fusion.refs_1_, f32[1024,512]{1,0:T(8,128)S(1)} %copy-done, f32[1024,256]{1,0:T(8,128)S(1)} %get-tuple-element.81.refs_3_, bf16[256,512]{1,0:T(8,128)(2,1)} %get-tuple-element.82.refs_4_, ...), custom_call_target="tpu_custom_call" | custom-call | tf_op jit(solution)/shard_map/finish/pallas_call | solution.py:558
  (121 shorter events, 31.9 us)
Async XLA Ops:
  2.7 3.3 %collective-permute-start = (f32[8,128]{1,0:T(8,128)}, f32[8,128]{1,0:T(8,128)S(1)}, u32[]{:S(2)}, u32[]{:S(2)}) collective-permute-start(f32[8,128]{1,0:T(8,128)} %get-tuple-element.43), channel_id=1, source_target_pairs={{0,1},{1,0},{2,3},{3,2},{4,5},{5,4},{6,7},{7,6},{8,9},{9,8},{10,11... | collective-permute-start | bytes 12296 | tf_op jit(solution)/shard_map/ppermute | solution.py:43
  4.8 5.7 %collective-permute-start.2 = (f32[384,128]{1,0:T(8,128)}, f32[384,128]{1,0:T(8,128)S(1)}, u32[]{:S(2)}, u32[]{:S(2)}) collective-permute-start(f32[384,128]{1,0:T(8,128)} %get-tuple-element.44), channel_id=1, source_target_pairs={{0,1},{1,0},{2,3},{3,2},{4,5},{5,4},{6,7},{7,6},{8,9},{9,8},{10,11... | collective-permute-start | bytes 589832 | tf_op jit(solution)/shard_map/ppermute | solution.py:43
  6.7 2.8 %collective-permute-start.1 = (f32[8,128]{1,0:T(8,128)S(1)}, f32[8,128]{1,0:T(8,128)S(1)}, u32[]{:S(2)}, u32[]{:S(2)}) collective-permute-start(f32[8,128]{1,0:T(8,128)S(1)} %add.160), channel_id=1, source_target_pairs={{0,2},{1,3},{2,0},{3,1},{4,6},{5,7},{6,4},{7,5},{8,10},{9,11},{10,... | collective-permute-start | bytes 12296 | tf_op jit(solution)/shard_map/ppermute | solution.py:43
  11.4 5.3 %collective-permute-start.4 = (f32[384,128]{1,0:T(8,128)S(1)}, f32[384,128]{1,0:T(8,128)S(1)}, u32[]{:S(2)}, u32[]{:S(2)}) collective-permute-start(f32[384,128]{1,0:T(8,128)S(1)} %add.162), channel_id=1, source_target_pairs={{0,2},{1,3},{2,0},{3,1},{4,6},{5,7},{6,4},{7,5},{8,10},{9,11},{10,... | collective-permute-start | bytes 589832 | tf_op jit(solution)/shard_map/ppermute | solution.py:43
  12.8 5.0 %collective-permute-start.5 = (f32[384,128]{1,0:T(8,128)}, f32[384,128]{1,0:T(8,128)S(1)}, u32[]{:S(2)}, u32[]{:S(2)}) collective-permute-start(f32[384,128]{1,0:T(8,128)} %get-tuple-element.49), channel_id=1, source_target_pairs={{0,1},{1,0},{2,3},{3,2},{4,5},{5,4},{6,7},{7,6},{8,9},{9,8},{10,11... | collective-permute-start | bytes 589832 | tf_op jit(solution)/shard_map/ppermute | solution.py:43
  13.3 3.5 %collective-permute-start.3 = (f32[8,128]{1,0:T(8,128)S(1)}, f32[8,128]{1,0:T(8,128)S(1)}, u32[]{:S(2)}, u32[]{:S(2)}) collective-permute-start(f32[8,128]{1,0:T(8,128)S(1)} %add.161), channel_id=1, source_target_pairs={{0,4},{1,5},{2,6},{3,7},{4,0},{5,1},{6,2},{7,3},{8,12},{9,13},{10,... | collective-permute-start | bytes 12296 | tf_op jit(solution)/shard_map/ppermute | solution.py:43
  16.7 7.6 %copy-start.14 = (f32[8,128]{1,0:T(8,128)}, f32[8,128]{1,0:T(8,128)S(1)}, u32[]{:S(2)}) copy-start(f32[8,128]{1,0:T(8,128)S(1)} %add.163.table_ref) | copy-start | bytes 12292
  20.9 6.7 %copy-start.13 = (f32[384,256]{1,0:T(8,128)S(1)}, f32[384,256]{1,0:T(8,128)}, u32[]{:S(2)}) copy-start(f32[384,256]{1,0:T(8,128)} %get-tuple-element.55) | copy-start | bytes 1179652
  24.3 28.3 %collective-permute-start.10 = (f32[1024,512]{1,0:T(8,128)}, f32[1024,512]{1,0:T(8,128)S(1)}, u32[]{:S(2)}, u32[]{:S(2)}) collective-permute-start(f32[1024,512]{1,0:T(8,128)} %far_rows.1), channel_id=1, source_target_pairs={{0,8},{8,0},{16,24},{24,16},{1,9},{9,1},{17,25},{25,17},{2,10},{10... | collective-permute-start | bytes 6291464 | tf_op jit(solution)/shard_map/ppermute | solution.py:43
  27.6 22.8 %collective-permute-start.9 = (f32[384,256]{1,0:T(8,128)S(1)}, f32[384,256]{1,0:T(8,128)}, u32[]{:S(2)}, u32[]{:S(2)}) collective-permute-start(f32[384,256]{1,0:T(8,128)S(1)} %copy-done.13), channel_id=1, source_target_pairs={{0,4},{8,12},{16,20},{24,28}} | collective-permute-start | bytes 1179656 | tf_op jit(solution)/shard_map/ppermute | solution.py:340
  36.4 15.0 %copy-start.9 = (f32[256,512]{1,0:T(8,128)S(1)}, f32[256,512]{1,0:T(8,128)}, u32[]{:S(2)}) copy-start(f32[256,512]{1,0:T(8,128)} %first_rows.1) | copy-start | bytes 1572868
  36.4 15.0 %collective-permute-start.11 = (f32[256,512]{1,0:T(8,128)}, f32[256,512]{1,0:T(8,128)}, u32[]{:S(2)}, u32[]{:S(2)}) collective-permute-start(f32[256,512]{1,0:T(8,128)} %first_rows.1), channel_id=1, source_target_pairs={{0,8},{8,0},{16,24},{24,16},{1,9},{9,1},{17,25},{25,17},{2,10},{10... | collective-permute-start | bytes 1572872 | tf_op jit(solution)/shard_map/ppermute | solution.py:43
  36.7 8.3 %collective-permute-start.7 = (f32[384,128]{1,0:T(8,128)S(1)}, f32[384,128]{1,0:T(8,128)}, u32[]{:S(2)}, u32[]{:S(2)}) collective-permute-start(f32[384,128]{1,0:T(8,128)S(1)} %add.164), channel_id=1, source_target_pairs={{0,4},{1,5},{2,6},{3,7},{4,0},{5,1},{6,2},{7,3},{8,12},{9,13},{10,... | collective-permute-start | bytes 589832 | tf_op jit(solution)/shard_map/ppermute | solution.py:43
  36.7 12.0 %collective-permute-start.8 = (f32[384,128]{1,0:T(8,128)S(1)}, f32[384,128]{1,0:T(8,128)}, u32[]{:S(2)}, u32[]{:S(2)}) collective-permute-start(f32[384,128]{1,0:T(8,128)S(1)} %add.165), channel_id=1, source_target_pairs={{0,2},{1,3},{2,0},{3,1},{4,6},{5,7},{6,4},{7,5},{8,10},{9,11},{10,... | collective-permute-start | bytes 589832 | tf_op jit(solution)/shard_map/ppermute | solution.py:43
  52.6 10.1 %copy-start.5 = (f32[1024,512]{1,0:T(8,128)}, f32[1024,512]{1,0:T(8,128)S(1)}, u32[]{:S(2)}) copy-start(f32[1024,512]{1,0:T(8,128)S(1)} %collective-permute-done.10.refs_8_) | copy-start | bytes 6291460
  62.7 12.5 %collective-permute-start.13 = (bf16[256,512]{1,0:T(8,128)(2,1)}, bf16[256,512]{1,0:T(8,128)(2,1)S(1)}, u32[]{:S(2)}, u32[]{:S(2)}) collective-permute-start(bf16[256,512]{1,0:T(8,128)(2,1)} %get-tuple-element.60.p_ref), channel_id=1, source_target_pairs={{0,16},{8,24},{16,0},{24,8},{1,17},{9,25},{17,1},{25,9},{2,18},{10... | collective-permute-start | bytes 786440 | tf_op jit(solution)/shard_map/ppermute | solution.py:43
  63.9 13.7 %collective-permute-start.15 = (f32[384,256]{1,0:T(8,128)S(1)}, f32[384,256]{1,0:T(8,128)S(1)}, u32[]{:S(2)}, u32[]{:S(2)}) collective-permute-start(f32[384,256]{1,0:T(8,128)S(1)} %broadcast_select_fusion.10), channel_id=1, source_target_pairs={{0,2},{4,6},{8,10},{12,14},{16,18},{20,22},{24,26},{28,30}} | collective-permute-start | bytes 1179656 | tf_op jit(solution)/shard_map/ppermute | solution.py:340
  70.2 4.9 %copy-start.8 = (bf16[256,512]{1,0:T(8,128)(2,1)S(1)}, bf16[256,512]{1,0:T(8,128)(2,1)}, u32[]{:S(2)}) copy-start(bf16[256,512]{1,0:T(8,128)(2,1)} %get-tuple-element.60.p_ref) | copy-start | bytes 786436
  73.7 6.0 %copy-start.12 = (f32[384,128]{1,0:T(8,128)S(1)}, f32[384,128]{1,0:T(8,128)}, u32[]{:S(2)}) copy-start(f32[384,128]{1,0:T(8,128)} %add.169) | copy-start | bytes 589828
  73.7 51.5 %collective-permute-start.17 = (f32[512,512]{1,0:T(8,128)}, f32[512,512]{1,0:T(8,128)}, u32[]{:S(2)}, u32[]{:S(2)}) collective-permute-start(f32[512,512]{1,0:T(8,128)} %far_sum.2), channel_id=1, source_target_pairs={{0,16},{8,24},{16,0},{24,8},{1,17},{9,25},{17,1},{25,9},{2,18},{10... | collective-permute-start | bytes 3145736 | tf_op jit(solution)/shard_map/ppermute | solution.py:43
  73.9 34.8 %collective-permute-start.18 = (f32[256,512]{1,0:T(8,128)S(1)}, f32[256,512]{1,0:T(8,128)S(1)}, u32[]{:S(2)}, u32[]{:S(2)}) collective-permute-start(f32[256,512]{1,0:T(8,128)S(1)} %add.171), channel_id=1, source_target_pairs={{0,16},{8,24},{16,0},{24,8},{1,17},{9,25},{17,1},{25,9},{2,18},{10... | collective-permute-start | bytes 1572872 | tf_op jit(solution)/shard_map/ppermute | solution.py:43
  76.0 38.7 %collective-permute-start.14 = (bf16[512,512]{1,0:T(8,128)(2,1)}, bf16[512,512]{1,0:T(8,128)(2,1)}, u32[]{:S(2)}, u32[]{:S(2)}) collective-permute-start(bf16[512,512]{1,0:T(8,128)(2,1)} %pad_maximum_fusion.3), channel_id=1, source_target_pairs={{0,8},{8,0},{16,24},{24,16},{1,9},{9,1},{17,25},{25,17},{2,10},{10... | collective-permute-start | bytes 1572872 | tf_op jit(solution)/shard_map/ppermute | solution.py:43
  77.6 39.1 %collective-permute-start.16 = (f32[384,256]{1,0:T(8,128)S(1)}, f32[384,256]{1,0:T(8,128)}, u32[]{:S(2)}, u32[]{:S(2)}) collective-permute-start(f32[384,256]{1,0:T(8,128)S(1)} %broadcast_select_fusion.8), channel_id=1, source_target_pairs={{0,1},{2,3},{4,5},{6,7},{8,9},{10,11},{12,13},{14,15},{16,17},{18,... | collective-permute-start | bytes 1179656 | tf_op jit(solution)/shard_map/ppermute | solution.py:340
  79.7 12.1 %collective-permute-start.12 = (f32[384,128]{1,0:T(8,128)S(1)}, f32[384,128]{1,0:T(8,128)S(1)}, u32[]{:S(2)}, u32[]{:S(2)}) collective-permute-start(f32[384,128]{1,0:T(8,128)S(1)} %copy-done.12), channel_id=1, source_target_pairs={{0,4},{1,5},{2,6},{3,7},{4,0},{5,1},{6,2},{7,3},{8,12},{9,13},{10,... | collective-permute-start | bytes 589832 | tf_op jit(solution)/shard_map/ppermute | solution.py:43
  108.8 16.6 %collective-permute-start.19 = (f32[256,256]{1,0:T(8,128)S(1)}, f32[256,256]{1,0:T(8,128)}, u32[]{:S(2)}, u32[]{:S(2)}) collective-permute-start(f32[256,256]{1,0:T(8,128)S(1)} %slice.66), channel_id=1, source_target_pairs={{0,4},{8,12},{16,20},{24,28}} | collective-permute-start | bytes 786440 | tf_op jit(solution)/shard_map/ppermute | solution.py:340
  115.8 32.4 %collective-permute-start.24 = (bf16[1024,512]{1,0:T(8,128)(2,1)S(1)}, bf16[1024,512]{1,0:T(8,128)(2,1)S(1)}, u32[]{:S(2)}, u32[]{:S(2)}) collective-permute-start(bf16[1024,512]{1,0:T(8,128)(2,1)S(1)} %pad_maximum_fusion.1.d01_ref.refs_2_), channel_id=1, source_target_pairs={{0,4},{1,5},{10,14},{11,15},{20,16},{21,17},{30,26},{31,27}} | collective-permute-start | bytes 3145736 | tf_op jit(solution)/shard_map/ppermute | solution.py:463
  125.1 6.9 %collective-permute-start.22 = (bf16[336,512]{1,0:T(8,128)(2,1)}, bf16[336,512]{1,0:T(8,128)(2,1)S(1)}, u32[]{:S(2)}, u32[]{:S(2)}) collective-permute-start(bf16[336,512]{1,0:T(8,128)(2,1)} %leaf_last.1), channel_id=1, source_target_pairs={{0,16},{8,24},{16,0},{24,8},{1,17},{9,25},{17,1},{25,9},{2,18},{10... | collective-permute-start | bytes 1032200 | tf_op jit(solution)/shard_map/ppermute | solution.py:43
  125.4 20.0 %collective-permute-start.20 = (f32[256,256]{1,0:T(8,128)S(1)}, f32[256,256]{1,0:T(8,128)S(1)}, u32[]{:S(2)}, u32[]{:S(2)}) collective-permute-start(f32[256,256]{1,0:T(8,128)S(1)} %broadcast_select_fusion.11), channel_id=1, source_target_pairs={{0,2},{4,6},{8,10},{12,14},{16,18},{20,22},{24,26},{28,30}} | collective-permute-start | bytes 786440 | tf_op jit(solution)/shard_map/ppermute | solution.py:340
  134.7 14.6 %collective-permute-start.23 = (bf16[672,512]{1,0:T(8,128)(2,1)}, bf16[672,512]{1,0:T(8,128)(2,1)}, u32[]{:S(2)}, u32[]{:S(2)}) collective-permute-start(bf16[672,512]{1,0:T(8,128)(2,1)} %pad_maximum_fusion.2), channel_id=1, source_target_pairs={{0,8},{8,0},{16,24},{24,16},{1,9},{9,1},{17,25},{25,17},{2,10},{10... | collective-permute-start | bytes 2064392 | tf_op jit(solution)/shard_map/ppermute | solution.py:43
  141.8 32.1 %collective-permute-start.6 = (f32[1024,512]{1,0:T(8,128)}, f32[1024,512]{1,0:T(8,128)}, u32[]{:S(2)}, u32[]{:S(2)}) collective-permute-start(f32[1024,512]{1,0:T(8,128)} %near_rows.1), channel_id=1, source_target_pairs={{0,8},{8,0},{16,24},{24,16},{1,9},{9,1},{17,25},{25,17},{2,10},{10... | collective-permute-start | bytes 6291464 | tf_op jit(solution)/shard_map/ppermute | solution.py:43
  145.2 4.1 %copy-start.7 = (bf16[336,512]{1,0:T(8,128)(2,1)S(1)}, bf16[336,512]{1,0:T(8,128)(2,1)}, u32[]{:S(2)}) copy-start(bf16[336,512]{1,0:T(8,128)(2,1)} %leaf_last.1) | copy-start | bytes 1032196
  145.2 4.1 %copy-start.11 = (bf16[336,512]{1,0:T(8,128)(2,1)S(1)}, bf16[336,512]{1,0:T(8,128)(2,1)}, u32[]{:S(2)}) copy-start(bf16[336,512]{1,0:T(8,128)(2,1)} %copy-done.10) | copy-start | bytes 1032196
  145.2 24.5 %collective-permute-start.25 = (f32[512,512]{1,0:T(8,128)}, f32[512,512]{1,0:T(8,128)}, u32[]{:S(2)}, u32[]{:S(2)}) collective-permute-start(f32[512,512]{1,0:T(8,128)} %far_sum.3), channel_id=1, source_target_pairs={{0,16},{8,24},{16,0},{24,8},{1,17},{9,25},{17,1},{25,9},{2,18},{10... | collective-permute-start | bytes 3145736 | tf_op jit(solution)/shard_map/ppermute | solution.py:43
  146.2 7.5 %collective-permute-start.21 = (f32[256,256]{1,0:T(8,128)}, f32[256,256]{1,0:T(8,128)}, u32[]{:S(2)}, u32[]{:S(2)}) collective-permute-start(f32[256,256]{1,0:T(8,128)} %broadcast_select_fusion.12), channel_id=1, source_target_pairs={{0,1},{2,3},{4,5},{6,7},{8,9},{10,11},{12,13},{14,15},{16,17},{18,... | collective-permute-start | bytes 786440 | tf_op jit(solution)/shard_map/ppermute | solution.py:340
  150.5 15.1 %collective-permute-start.26 = (bf16[512,512]{1,0:T(8,128)(2,1)S(1)}, bf16[512,512]{1,0:T(8,128)(2,1)}, u32[]{:S(2)}, u32[]{:S(2)}) collective-permute-start(bf16[512,512]{1,0:T(8,128)(2,1)S(1)} %bitcast.27), channel_id=1, source_target_pairs={{0,4},{1,5},{10,14},{11,15},{20,16},{21,17},{30,26},{31,27}} | collective-permute-start | bytes 1572872 | tf_op jit(solution)/shard_map/ppermute | solution.py:463
  152.1 32.2 %collective-permute-start.27 = (bf16[1024,512]{1,0:T(8,128)(2,1)}, bf16[1024,512]{1,0:T(8,128)(2,1)}, u32[]{:S(2)}, u32[]{:S(2)}) collective-permute-start(bf16[1024,512]{1,0:T(8,128)(2,1)} %broadcast_select_fusion.2), channel_id=1, source_target_pairs={{0,2},{1,3},{4,6},{5,7},{10,8},{11,9},{14,12},{15,13},{20,22},{21,... | collective-permute-start | bytes 3145736 | tf_op jit(solution)/shard_map/ppermute | solution.py:463
  169.7 12.7 %collective-permute-start.30 = (bf16[512,512]{1,0:T(8,128)(2,1)S(1)}, bf16[512,512]{1,0:T(8,128)(2,1)S(1)}, u32[]{:S(2)}, u32[]{:S(2)}) collective-permute-start(bf16[512,512]{1,0:T(8,128)(2,1)S(1)} %broadcast_select_fusion.5), channel_id=1, source_target_pairs={{0,2},{1,3},{4,6},{5,7},{10,8},{11,9},{14,12},{15,13},{20,22},{21,... | collective-permute-start | bytes 1572872 | tf_op jit(solution)/shard_map/ppermute | solution.py:463
  171.0 9.0 %collective-permute-start.33 = (bf16[256,512]{1,0:T(8,128)(2,1)}, bf16[256,512]{1,0:T(8,128)(2,1)S(1)}, u32[]{:S(2)}, u32[]{:S(2)}) collective-permute-start(bf16[256,512]{1,0:T(8,128)(2,1)} %get-tuple-element.82.refs_4_), channel_id=1, source_target_pairs={{0,4},{1,5},{10,14},{11,15},{20,16},{21,17},{30,26},{31,27}} | collective-permute-start | bytes 786440 | tf_op jit(solution)/shard_map/ppermute | solution.py:463
  171.8 26.7 %collective-permute-start.29 = (bf16[1024,512]{1,0:T(8,128)(2,1)}, bf16[1024,512]{1,0:T(8,128)(2,1)}, u32[]{:S(2)}, u32[]{:S(2)}) collective-permute-start(bf16[1024,512]{1,0:T(8,128)(2,1)} %broadcast_select_fusion.2), channel_id=1, source_target_pairs={{0,1},{1,0},{4,5},{5,4},{10,11},{11,10},{14,15},{15,14},{20,21},{2... | collective-permute-start | bytes 3145736 | tf_op jit(solution)/shard_map/ppermute | solution.py:475
  173.9 22.4 %collective-permute-start.32 = (bf16[512,512]{1,0:T(8,128)(2,1)S(1)}, bf16[512,512]{1,0:T(8,128)(2,1)S(1)}, u32[]{:S(2)}, u32[]{:S(2)}) collective-permute-start(bf16[512,512]{1,0:T(8,128)(2,1)S(1)} %broadcast_select_fusion.5), channel_id=1, source_target_pairs={{0,1},{1,0},{4,5},{5,4},{10,11},{11,10},{14,15},{15,14},{20,21},{2... | collective-permute-start | bytes 1572872 | tf_op jit(solution)/shard_map/ppermute | solution.py:475
  180.0 14.9 %copy-start.6 = (bf16[1024,512]{1,0:T(8,128)(2,1)S(1)}, bf16[1024,512]{1,0:T(8,128)(2,1)}, u32[]{:S(2)}) copy-start(bf16[1024,512]{1,0:T(8,128)(2,1)} %broadcast_select_fusion.2) | copy-start | bytes 3145732
  181.1 13.7 %collective-permute-start.34 = (bf16[256,512]{1,0:T(8,128)(2,1)S(1)}, bf16[256,512]{1,0:T(8,128)(2,1)S(1)}, u32[]{:S(2)}, u32[]{:S(2)}) collective-permute-start(bf16[256,512]{1,0:T(8,128)(2,1)S(1)} %broadcast_select_fusion.6), channel_id=1, source_target_pairs={{0,2},{1,3},{4,6},{5,7},{10,8},{11,9},{14,12},{15,13},{20,22},{21,... | collective-permute-start | bytes 786440 | tf_op jit(solution)/shard_map/ppermute | solution.py:463
  182.4 16.0 %collective-permute-start.31 = (bf16[512,512]{1,0:T(8,128)(2,1)S(1)}, bf16[512,512]{1,0:T(8,128)(2,1)S(1)}, u32[]{:S(2)}, u32[]{:S(2)}) collective-permute-start(bf16[512,512]{1,0:T(8,128)(2,1)S(1)} %collective-permute-done.30), channel_id=1, source_target_pairs={{2,3},{3,2},{6,7},{7,6},{8,9},{9,8},{12,13},{13,12},{22,23},{23,22... | collective-permute-start | bytes 1572872 | tf_op jit(solution)/shard_map/ppermute | solution.py:475
  184.3 33.5 %collective-permute-start.28 = (bf16[1024,512]{1,0:T(8,128)(2,1)}, bf16[1024,512]{1,0:T(8,128)(2,1)S(1)}, u32[]{:S(2)}, u32[]{:S(2)}) collective-permute-start(bf16[1024,512]{1,0:T(8,128)(2,1)} %collective-permute-done.27), channel_id=1, source_target_pairs={{2,3},{3,2},{6,7},{7,6},{8,9},{9,8},{12,13},{13,12},{22,23},{23,22... | collective-permute-start | bytes 3145736 | tf_op jit(solution)/shard_map/ppermute | solution.py:475
  194.9 30.1 %collective-permute-start.35 = (bf16[256,512]{1,0:T(8,128)(2,1)S(1)}, bf16[256,512]{1,0:T(8,128)(2,1)S(1)}, u32[]{:S(2)}, u32[]{:S(2)}) collective-permute-start(bf16[256,512]{1,0:T(8,128)(2,1)S(1)} %broadcast_select_fusion.7.refs_5_), channel_id=1, source_target_pairs={{0,1},{1,0},{4,5},{5,4},{2,3},{3,2},{6,7},{7,6},{10,11},{11,10},{1... | collective-permute-start | bytes 786440 | tf_op jit(solution)/shard_map/ppermute | solution.py:475
  196.3 21.7 %copy-start.2 = (f32[128,128]{1,0:T(8,128)S(1)}, f32[128,128]{1,0:T(8,128)}, u32[]{:S(2)}) copy-start(f32[128,128]{1,0:T(8,128)} %copy-done.1) | copy-start | bytes 196612
  196.3 21.7 %copy-start.4 = (bf16[128,128]{1,0:T(8,128)(2,1)S(1)}, bf16[128,128]{1,0:T(8,128)(2,1)}, u32[]{:S(2)}) copy-start(bf16[128,128]{1,0:T(8,128)(2,1)} %copy-done.3) | copy-start | bytes 98308
  225.0 1.6 copy-start
  (3 other events, 2.0 us)

commit v5 on v4

--- a/solution.py
+++ b/solution.py
@@ -359,14 +359,11 @@
     def table_hop(value, at):
         return value + flip(value, "mem", hops[at])
 
-    table_rows = table_hop(table_hop(table_rows, 0), 1)
+    tie = lax.optimization_barrier
+    for at in range(last + 1):
+        table_rows = table_hop(table_rows, at)
     head = table_hop(head, 0)
-    table_rows, head, w_lead, rest = lax.optimization_barrier((table_rows, head, w_lead, rest))
-    for at in range(2, last + 1):
-        table_rows = table_hop(table_rows, at)
-        head = table_hop(head, at - 1)
-        rest = table_hop(rest, at - 2)
-        table_rows, head, rest, w_lead = lax.optimization_barrier((table_rows, head, rest, w_lead))
+    table_rows, head, rest, w_lead = tie((table_rows, head, rest, w_lead))
     table = table_rows[0, :count].astype(jnp.int32)
 
     starts = [g ^ (CORE | CHIP), g ^ CHIP, g ^ CORE, g]
@@ -385,17 +382,22 @@
             adds, name,
         )
 
-    diagonal = flip(rows_at(0, n, [], "far_rows"), "grp", CORE)
+    diagonal = rows_at(0, n, [], "far_rows")
     first = rows_at(
         4 * n, PR, [(root_front, 0, 0)], "first_rows", (g == 0).astype(jnp.int32).reshape(1), PR
     )
+    for at in range(1, last):
+        head = table_hop(head, at)
+        rest = table_hop(rest, at - 1)
+    head, rest, diagonal, first, w_lead = tie((head, rest, diagonal, first, w_lead))
+    near = rows_at(2 * n, n, [], "near_rows")
+    diagonal = flip(diagonal, "grp", CORE)
     first = first + flip(first, "grp", CORE)
     head = table_hop(head, last)
     rest = table_hop(rest, last - 1)
     w_lead = lead_hop(w_lead, 0)
-    head, rest, w_lead, diagonal, first = lax.optimization_barrier(
-        (head, rest, w_lead, diagonal, first)
-    )
+    head, rest, w_lead, diagonal, first, near = tie((head, rest, w_lead, diagonal, first, near))
+    near = flip(near, "grp", CORE)
     first = first + flip(first, "grp", CHIP)
     rest = table_hop(rest, last)
     for at in range(1, last):
@@ -419,9 +421,7 @@
         name="leaf_two",
     )(head, front, front, mask)
 
-    p01, diagonal = lax.optimization_barrier((p01, diagonal))
-    far = [rows_at(n + i * ways, ways, [(diagonal, 0, i)], "far_sum") for i in range(2)]
-    far = [flip(part, "grp", CHIP) for part in far]
+    p01, rest, w_lead, first = tie((p01, rest, w_lead, first))
 
     def across(value):
         far_value = flip(value, "grp", CHIP)
@@ -429,7 +429,8 @@
         return jnp.concatenate([both, flip(both, "grp", CORE)], axis=0)
 
     d01 = across(p01)
-    rest, d01 = lax.optimization_barrier((rest, d01))
+    rest, d01 = tie((rest, d01))
+    corner = lead_hop([first[:, :lead_cols]] * leads, 0)
     w_lead = lead_hop(w_lead, last)
     w_lead = w_lead[0] if leads == 1 else jnp.concatenate(w_lead, axis=1)
     lead_rows = (PL * b + LOG_ROWS) * pr // cols
@@ -442,7 +443,6 @@
         scratch_shapes=[pltpu.VMEM((b, b), f32)] + work,
         name="leaf_last",
     )(rest, front, w_lead, table_rows, mask, p01, inv0, inv1, x01, log01)
-    near = flip(rows_at(2 * n, n, [], "near_rows"), "grp", CORE)
 
     def among(offsets):
         found = jnp.zeros((), jnp.bool_)
@@ -488,15 +488,18 @@
     def early_hops(state):
         return [inner_hop((state[0], state[1]), i) for i in range(1, spread)]
 
-    corner = [first[:, :lead_cols]] * leads
-    for at in range(last + 1):
+    s01 = zone_hop(([0], d01, None))
+    pack_far = flip(pack, "grp", CHIP)
+    pack, pack_far, diagonal, *corner = tie((pack, pack_far, diagonal, *corner))
+    far_in = [rows_at(n + i * ways, ways, [(diagonal, 0, i)], "far_sum") for i in range(2)]
+    for at in range(1, last + 1):
         corner = lead_hop(corner, at)
     corner = corner[0] if leads == 1 else jnp.concatenate(corner, axis=1)
-    s01 = zone_hop(([0], d01, None))
-    pack, far[0] = lax.optimization_barrier((pack, far[0]))
-    pack = across(pack)
-    pack, held = lax.optimization_barrier((pack, s01[1]))
+    pack = jnp.concatenate([pack, pack_far], axis=0)
+    pack = jnp.concatenate([pack, flip(pack, "grp", CORE)], axis=0)
+    pack, held, *far_in = tie((pack, s01[1], *far_in))
     s01 = (s01[0], held, None)
+    far = [flip(part, "grp", CHIP) for part in far_in]
     early01 = early_hops(s01)
     s01 = zone_hop(s01)
     d2 = pack.reshape(groups, b + lead_rows, cols)[:, :b].reshape(groups * b, cols)
@@ -510,7 +513,7 @@
         compiler_params=pltpu.CompilerParams(vmem_limit_bytes=32 << 20),
         name="root_step",
     )(leaves, corner, first, d01, pack)
-    q, far[1], held = lax.optimization_barrier((q, far[1], s2[1]))
+    q, held, far[0], *early01 = tie((q, s2[1], far[0], *early01))
     s2 = (s2[0], held, None)
     rq = inner_hops(zone_hop(zone_hop(([0], q, None))))
     early2 = early_hops(s2)

time: 231 us -> 211 us (0.913)
  the two profiles are of different devices: /device:TPU:1 before, /device:TPU:28 now
where the time goes in v5:
time: 211 us; the launch traced here: 210 us
  waiting for transfers between devices  86.7 us (41%)
  Pallas kernels  59.1 us (28%)
  starting transfers between devices  35.1 us (17%)
  other arithmetic  19 us (9%)
  local copies, waits for them, and re-layouts  8.58 us (4%)
    ppermute x19, waiting for transfers between devices, flip(): return lax.ppermute(value, axis, [(i, i ^ bit) for i in range(size)])  55.4 us
    ppermute x6, waiting for transfers between devices, lead_hop(): got = lax.ppermute(held, 'mem', pairs)  22 us
    pallas_call x6, Pallas kernels, take_rows(): pl.pallas_call(body, grid_spec=pltpu.PrefetchScalarGridSpec(num_scalar_pr...  21.8 us
    ppermute x19, starting transfers between devices, flip(): return lax.ppermute(value, axis, [(i, i ^ bit) for i in range(size)])  12.6 us
    pallas_call x1, Pallas kernels, local(): pl.pallas_call(leaf_two, grid=(1,), in_specs=[vmem, w_spec(0), w_spec(1),...  9.41 us
    pallas_call x1, Pallas kernels, local(): pl.pallas_call(root_step, in_specs=[smem] + [vmem] * 4, out_shape=(shape(...  8.95 us
    ppermute x6, starting transfers between devices, lead_hop(): got = lax.ppermute(held, 'mem', pairs)  8.2 us
    ppermute x6, starting transfers between devices, zone_hop(): got = lax.ppermute(held, ('grp', 'mem'), pairs)  7.98 us
  transfers between devices with their start and end apart: 36, of which 13 were waited for; matrix products, arithmetic and copies ran while one was open for 10% of the time, Pallas kernels for 26%

profile of v5, /device:TPU:28, one launch (start us, length us, event | category | flops | bytes accessed | tf_op | source)
XLA Modules:
  0.0 209.7 jit_solution(16275386187841211417)
XLA Ops:
  0.6 2.1 %pick_pivots.1 = (f32[8,128]{1,0:T(8,128)}, f32[384,128]{1,0:T(8,128)}, f32[384,128]{1,0:T(8,128)}, f32[8,512]{1,0:T(8,128)}, f32[384,256]{1,0:T(8,128)}) custom-call(s32[4]{0:T(128)} %bitcast.55, s32[1]{0:T(128)} %bitcast.2.at_ref, f32[4096,512]{1,0:T(8,128)} %bitcast.29), custom_call_target="tpu_custom_call" | custom-call | tf_op jit(solution)/shard_map/pick_pivots/pallas_call | solution.py:344
  3.2 1.5 collective-permute-start.3
  4.9 1.7 collective-permute-done
  7.7 3.2 %collective-permute-done.1 = f32[8,128]{1,0:T(8,128)S(1)} collective-permute-done((f32[8,128]{1,0:T(8,128)S(1)}, f32[8,128]{1,0:T(8,128)S(1)}, u32[]{:S(2)}, u32[]{:S(2)}) %collective-permute-start.1) | collective-permute-done | bytes 4128 | tf_op jit(solution)/shard_map/ppermute | solution.py:43
  11.3 4.1 %collective-permute-done.2 = f32[8,128]{1,0:T(8,128)S(1)} collective-permute-done((f32[8,128]{1,0:T(8,128)S(1)}, f32[8,128]{1,0:T(8,128)S(1)}, u32[]{:S(2)}, u32[]{:S(2)}) %collective-permute-start.2) | collective-permute-done | bytes 4128 | tf_op jit(solution)/shard_map/ppermute | solution.py:43
  20.6 3.4 %far_rows.1 = f32[1024,512]{1,0:T(8,128)} custom-call(s32[8]{0:T(128)} %get-tuple-element.112.refs_0_, s32[8]{0:T(128)} %get-tuple-element.109.refs_1_, s32[1]{0:T(128)} %constant.83.clone.1.refs_2_, f32[4096,512]{1,0:T(8,128)} %bitcast.30, f32[4096,512]{1,0:T(8,128)} %bitcast.31, f32[4096,512]{1,0:T(8,128)} %bitcast.32, f32[4096,512]{1,0:T(8,128)} %bitcast.33, ...), custom_call_target="tpu_custom_call" | custom-call | tf_op jit(solution)/shard_map/far_rows/pallas_call | solution.py:214
  23.9 2.9 %first_rows.1 = f32[256,512]{1,0:T(8,128)} custom-call(s32[2]{0:T(128)} %slice.53.refs_0_, s32[2]{0:T(128)} %slice.54.refs_1_, s32[1]{0:T(128)} %bitcast.10.refs_2_, f32[4096,512]{1,0:T(8,128)} %bitcast.34, f32[4096,512]{1,0:T(8,128)} %bitcast.35, f32[8,512]{1,0:T(8,128)} %get-tuple-element.57.refs_7_.refs_5_.mask_ref, f32[1024,512]{1,0:T(8,128)} %refs_8_.1), custom_call_target="tpu_custom_call" | custom-call | tf_op jit(solution)/shard_map/first_rows/pallas_call | solution.py:214
  27.0 1.4 collective-permute-start.8
  28.9 1.9 collective-permute-start.7
  30.8 3.3 %near_rows.1 = f32[1024,512]{1,0:T(8,128)} custom-call(s32[8]{0:T(128)} %get-tuple-element.111.refs_0_, s32[8]{0:T(128)} %get-tuple-element.108.refs_1_, s32[1]{0:T(128)} %constant.83.clone.1.refs_2_, f32[4096,512]{1,0:T(8,128)} %bitcast.36, f32[4096,512]{1,0:T(8,128)} %bitcast.37, f32[4096,512]{1,0:T(8,128)} %bitcast.38, f32[4096,512]{1,0:T(8,128)} %bitcast.39, ...), custom_call_target="tpu_custom_call" | custom-call | tf_op jit(solution)/shard_map/near_rows/pallas_call | solution.py:214
  34.1 6.8 %collective-permute-done.6 = f32[384,128]{1,0:T(8,128)S(1)} collective-permute-done((f32[384,128]{1,0:T(8,128)S(1)}, f32[384,128]{1,0:T(8,128)S(1)}, u32[]{:S(2)}, u32[]{:S(2)}) %collective-permute-start.6) | collective-permute-done | bytes 196640 | tf_op jit(solution)/shard_map/ppermute | solution.py:43
  42.9 1.5 collective-permute-start.13
  44.3 1.4 collective-permute-start.14
  46.7 9.4 %leaf_two.1 = (bf16[256,512]{1,0:T(8,128)(2,1)}, f32[128,128]{1,0:T(8,128)}, f32[128,128]{1,0:T(8,128)}, bf16[128,128]{1,0:T(8,128)(2,1)}, f32[8,128]{1,0:T(8,128)}) custom-call(f32[384,128]{1,0:T(8,128)} %add.168.head_ref, f32[4096,512]{1,0:T(8,128)} %bitcast.41, f32[4096,512]{1,0:T(8,128)} %bitcast.40, f32[8,512]{1,0:T(8,128)} %get-tuple-element.57.refs_7_.refs_5_.mask_ref), custom_call_target="tpu_custom_call" | custom-call | tf_op jit(solution)/shard_map/leaf_two/pallas_call | solution.py:414
  56.1 1.6 add.173.rest_ref
  60.1 1.3 collective-permute-start.17
  61.4 5.9 %collective-permute-done.15 = bf16[256,512]{1,0:T(8,128)(2,1)S(1)} collective-permute-done((bf16[256,512]{1,0:T(8,128)(2,1)S(1)}, bf16[256,512]{1,0:T(8,128)(2,1)S(1)}, u32[]{:S(2)}, u32[]{:S(2)}) %collective-permute-start.15) | collective-permute-done | bytes 262176 | tf_op jit(solution)/shard_map/ppermute | solution.py:43
  67.4 1.4 collective-permute-start.19
  68.8 13.6 %collective-permute-done.17 = f32[384,256]{1,0:T(8,128)S(1)} collective-permute-done((f32[384,256]{1,0:T(8,128)S(1)}, f32[384,256]{1,0:T(8,128)S(1)}, u32[]{:S(2)}, u32[]{:S(2)}) %collective-permute-start.17) | collective-permute-done | bytes 393248 | tf_op jit(solution)/shard_map/ppermute | solution.py:340
  83.3 7.6 %leaf_last.1 = bf16[336,512]{1,0:T(8,128)(2,1)} custom-call(f32[384,128]{1,0:T(8,128)} %add.173.rest_ref, f32[4096,512]{1,0:T(8,128)} %bitcast.42, f32[384,256]{1,0:T(8,128)} %broadcast_select_fusion.8.w_lead_ref, f32[8,128]{1,0:T(8,128)} %copy-done.16, f32[8,512]{1,0:T(8,128)} %get-tuple-element.57.refs_7_.refs_5_.mask_ref, ...), custom_call_target="tpu_custom_call" | custom-call | tf_op jit(solution)/shard_map/leaf_last/pallas_call | solution.py:437
  92.0 1.6 collective-permute-start.23
  93.6 5.8 %collective-permute-done.18 = bf16[336,512]{1,0:T(8,128)(2,1)S(1)} collective-permute-done((bf16[336,512]{1,0:T(8,128)(2,1)}, bf16[336,512]{1,0:T(8,128)(2,1)S(1)}, u32[]{:S(2)}, u32[]{:S(2)}) %collective-permute-start.18) | collective-permute-done | bytes 344096 | tf_op jit(solution)/shard_map/ppermute | solution.py:43
  103.0 1.3 collective-permute-start.20
  104.3 3.3 %far_sum.2 = f32[512,512]{1,0:T(8,128)} custom-call(s32[4]{0:T(128)} %get-tuple-element.107.refs_0_, s32[4]{0:T(128)} %get-tuple-element.105.refs_1_, s32[1]{0:T(128)} %constant.83.clone.1.refs_2_, f32[4096,512]{1,0:T(8,128)} %bitcast.43, f32[4096,512]{1,0:T(8,128)} %bitcast.44, f32[4096,512]{1,0:T(8,128)} %bitcast.45, f32[4096,512]{1,0:T(8,128)} %bitcast.46, ...), custom_call_target="tpu_custom_call" | custom-call | tf_op jit(solution)/shard_map/far_sum/pallas_call | solution.py:214
  107.7 3.5 %far_sum.3 = f32[512,512]{1,0:T(8,128)} custom-call(s32[4]{0:T(128)} %get-tuple-element.106.refs_0_, s32[4]{0:T(128)} %get-tuple-element.104.refs_1_, s32[1]{0:T(128)} %constant.83.clone.1.refs_2_, f32[4096,512]{1,0:T(8,128)} %bitcast.47, f32[4096,512]{1,0:T(8,128)} %bitcast.48, f32[4096,512]{1,0:T(8,128)} %bitcast.49, f32[4096,512]{1,0:T(8,128)} %bitcast.50, ...), custom_call_target="tpu_custom_call" | custom-call | tf_op jit(solution)/shard_map/far_sum/pallas_call | solution.py:214
  111.2 1.2 pad_maximum_fusion.pack_ref
  113.5 1.4 collective-permute-start.24
  114.9 1.7 broadcast_select_fusion.12
  116.6 1.3 collective-permute-start.21
  118.7 1.5 collective-permute-start.28
  120.2 8.4 %collective-permute-done.21 = f32[256,256]{1,0:T(8,128)} collective-permute-done((f32[256,256]{1,0:T(8,128)}, f32[256,256]{1,0:T(8,128)}, u32[]{:S(2)}, u32[]{:S(2)}) %collective-permute-start.21) | collective-permute-done | bytes 262176 | tf_op jit(solution)/shard_map/ppermute | solution.py:340
  128.6 2.0 collective-permute-start.27
  131.8 9.0 %root_step.1 = (bf16[256,512]{1,0:T(8,128)(2,1)S(1)}, f32[128,128]{1,0:T(8,128)S(1)}, f32[128,128]{1,0:T(8,128)S(1)}, bf16[128,128]{1,0:T(8,128)(2,1)S(1)}, f32[8,128]{1,0:T(8,128)S(1)}) custom-call(s32[4]{0:T(128)S(1)} %pad_add_fusion.1.leaf_ref, f32[256,256]{1,0:T(8,128)S(1)} %broadcast_select_fusion.13.corner_ref, f32[256,512]{1,0:T(8,128)S(1)} %add.174.first_ref, ...), custom_call_target="tpu_custom_call" | custom-call | tf_op jit(solution)/shard_map/root_step/pallas_call | solution.py:508
  142.2 10.8 %collective-permute-done.25.refs_10_ = f32[512,512]{1,0:T(8,128)S(1)} collective-permute-done((f32[512,512]{1,0:T(8,128)}, f32[512,512]{1,0:T(8,128)S(1)}, u32[]{:S(2)}, u32[]{:S(2)}) %collective-permute-start.25) | collective-permute-done | bytes 1048608 | tf_op jit(solution)/shard_map/ppermute | solution.py:43
  152.9 1.3 collective-permute-start.30
  154.2 1.5 collective-permute-start.32
  156.4 1.9 collective-permute-start.29
  158.4 17.1 %collective-permute-done.27.refs_11_ = f32[512,512]{1,0:T(8,128)S(1)} collective-permute-done((f32[512,512]{1,0:T(8,128)}, f32[512,512]{1,0:T(8,128)S(1)}, u32[]{:S(2)}, u32[]{:S(2)}) %collective-permute-start.27) | collective-permute-done | bytes 1048608 | tf_op jit(solution)/shard_map/ppermute | solution.py:43
  176.4 5.5 %base_rows.1.refs_1_ = f32[1024,512]{1,0:T(8,128)} custom-call(s32[8]{0:T(128)} %get-tuple-element.113.refs_0_, s32[8]{0:T(128)} %get-tuple-element.110.refs_1_, s32[1]{0:T(128)} %constant.83.clone.1.refs_2_, f32[4096,512]{1,0:T(8,128)} %bitcast.51, f32[4096,512]{1,0:T(8,128)} %bitcast.52, f32[4096,512]{1,0:T(8,128)} %bitcast.53, f32[4096,512]{1,0:T(8,128)} %bitcast.54, ...), custom_call_target="tpu_custom_call" | custom-call | tf_op jit(solution)/shard_map/base_rows/pallas_call | solution.py:214
  181.9 1.3 broadcast_select_fusion.1.refs_4_
  183.3 1.4 collective-permute-start.34
  184.8 2.2 %collective-permute-start.31 = (bf16[512,512]{1,0:T(8,128)(2,1)}, bf16[512,512]{1,0:T(8,128)(2,1)S(1)}, u32[]{:S(2)}, u32[]{:S(2)}) collective-permute-start(bf16[512,512]{1,0:T(8,128)(2,1)} %collective-permute-done.30), channel_id=1, source_target_pairs={{2,3},{3,2},{6,7},{7,6},{8,9},{9,8},{12,13},{13,12},{22,23},{23,22... | collective-permute-start | bytes 1572872 | tf_op jit(solution)/shard_map/ppermute | solution.py:475
  188.1 3.7 %collective-permute-done.34 = bf16[256,512]{1,0:T(8,128)(2,1)S(1)} collective-permute-done((bf16[256,512]{1,0:T(8,128)(2,1)S(1)}, bf16[256,512]{1,0:T(8,128)(2,1)S(1)}, u32[]{:S(2)}, u32[]{:S(2)}) %collective-permute-start.34) | collective-permute-done | bytes 262176 | tf_op jit(solution)/shard_map/ppermute | solution.py:463
  191.8 1.3 broadcast_select_fusion.refs_5_
  193.2 5.6 %collective-permute-done.31 = bf16[512,512]{1,0:T(8,128)(2,1)S(1)} collective-permute-done((bf16[512,512]{1,0:T(8,128)(2,1)}, bf16[512,512]{1,0:T(8,128)(2,1)S(1)}, u32[]{:S(2)}, u32[]{:S(2)}) %collective-permute-start.31) | collective-permute-done | bytes 524320 | tf_op jit(solution)/shard_map/ppermute | solution.py:475
  198.9 7.0 %update.1 = (f32[1024,512]{1,0:T(8,128)}, f32[1024,256]{1,0:T(8,128)S(1)}) custom-call(s32[2]{0:T(128)S(1)} %iota_xor_fusion.refs_0_, f32[1024,512]{1,0:T(8,128)} %base_rows.1.refs_1_, bf16[1024,512]{1,0:T(8,128)(2,1)S(1)} %pad_maximum_fusion.1.d01_ref.refs_2_, bf16[512,512]{1,0:T(8,128)(2,1)S(1)} %bitcast.28, ...), custom_call_target="tpu_custom_call" | custom-call | tf_op jit(solution)/shard_map/update/pallas_call | solution.py:536
  205.9 1.6 copy-done
  207.5 2.2 %finish.1 = f32[1024,512]{1,0:T(8,128)} custom-call(s32[2]{0:T(128)S(1)} %iota_xor_fusion.refs_0_, s32[3]{0:T(128)S(1)} %pad_add_fusion.refs_1_, f32[1024,512]{1,0:T(8,128)S(1)} %copy-done, f32[1024,256]{1,0:T(8,128)S(1)} %get-tuple-element.99.refs_3_, bf16[256,512]{1,0:T(8,128)(2,1)S(1)} %get-tuple-element.100.refs_4_, ...), custom_call_target="tpu_custom_call" | custom-call | tf_op jit(solution)/shard_map/finish/pallas_call | solution.py:561
  (125 shorter events, 26.1 us)
Async XLA Ops:
  2.7 3.8 %collective-permute-start = (f32[8,128]{1,0:T(8,128)}, f32[8,128]{1,0:T(8,128)S(1)}, u32[]{:S(2)}, u32[]{:S(2)}) collective-permute-start(f32[8,128]{1,0:T(8,128)} %get-tuple-element.52), channel_id=1, source_target_pairs={{0,1},{1,0},{2,3},{3,2},{4,5},{5,4},{6,7},{7,6},{8,9},{9,8},{10,11... | collective-permute-start | bytes 12296 | tf_op jit(solution)/shard_map/ppermute | solution.py:43
  3.2 12.1 %collective-permute-start.3 = (f32[384,128]{1,0:T(8,128)}, f32[384,128]{1,0:T(8,128)S(1)}, u32[]{:S(2)}, u32[]{:S(2)}) collective-permute-start(f32[384,128]{1,0:T(8,128)} %get-tuple-element.53), channel_id=1, source_target_pairs={{0,1},{1,0},{2,3},{3,2},{4,5},{5,4},{6,7},{7,6},{8,9},{9,8},{10,11... | collective-permute-start | bytes 589832 | tf_op jit(solution)/shard_map/ppermute | solution.py:43
  7.3 3.6 %collective-permute-start.1 = (f32[8,128]{1,0:T(8,128)S(1)}, f32[8,128]{1,0:T(8,128)S(1)}, u32[]{:S(2)}, u32[]{:S(2)}) collective-permute-start(f32[8,128]{1,0:T(8,128)S(1)} %add.160), channel_id=1, source_target_pairs={{0,2},{1,3},{2,0},{3,1},{4,6},{5,7},{6,4},{7,5},{8,10},{9,11},{10,... | collective-permute-start | bytes 12296 | tf_op jit(solution)/shard_map/ppermute | solution.py:43
  10.9 4.5 %collective-permute-start.2 = (f32[8,128]{1,0:T(8,128)S(1)}, f32[8,128]{1,0:T(8,128)S(1)}, u32[]{:S(2)}, u32[]{:S(2)}) collective-permute-start(f32[8,128]{1,0:T(8,128)S(1)} %add.161), channel_id=1, source_target_pairs={{0,4},{1,5},{2,6},{3,7},{4,0},{5,1},{6,2},{7,3},{8,12},{9,13},{10,... | collective-permute-start | bytes 12296 | tf_op jit(solution)/shard_map/ppermute | solution.py:43
  15.4 8.6 %copy-start.16 = (f32[8,128]{1,0:T(8,128)}, f32[8,128]{1,0:T(8,128)S(1)}, u32[]{:S(2)}) copy-start(f32[8,128]{1,0:T(8,128)S(1)} %add.162.table_ref) | copy-start | bytes 12292
  18.4 8.4 %collective-permute-start.4 = (f32[384,128]{1,0:T(8,128)S(1)}, f32[384,128]{1,0:T(8,128)S(1)}, u32[]{:S(2)}, u32[]{:S(2)}) collective-permute-start(f32[384,128]{1,0:T(8,128)S(1)} %add.163), channel_id=1, source_target_pairs={{0,2},{1,3},{2,0},{3,1},{4,6},{5,7},{6,4},{7,5},{8,10},{9,11},{10,... | collective-permute-start | bytes 589832 | tf_op jit(solution)/shard_map/ppermute | solution.py:43
  18.9 8.0 %collective-permute-start.5 = (f32[384,128]{1,0:T(8,128)}, f32[384,128]{1,0:T(8,128)S(1)}, u32[]{:S(2)}, u32[]{:S(2)}) collective-permute-start(f32[384,128]{1,0:T(8,128)} %get-tuple-element.59), channel_id=1, source_target_pairs={{0,1},{1,0},{2,3},{3,2},{4,5},{5,4},{6,7},{7,6},{8,9},{9,8},{10,11... | collective-permute-start | bytes 589832 | tf_op jit(solution)/shard_map/ppermute | solution.py:43
  23.9 3.1 %copy-start.14 = (f32[384,256]{1,0:T(8,128)S(1)}, f32[384,256]{1,0:T(8,128)}, u32[]{:S(2)}) copy-start(f32[384,256]{1,0:T(8,128)} %get-tuple-element.63) | copy-start | bytes 1179652
  26.9 15.9 %collective-permute-start.9 = (f32[1024,512]{1,0:T(8,128)}, f32[1024,512]{1,0:T(8,128)S(1)}, u32[]{:S(2)}, u32[]{:S(2)}) collective-permute-start(f32[1024,512]{1,0:T(8,128)} %far_rows.1), channel_id=1, source_target_pairs={{0,8},{8,0},{16,24},{24,16},{1,9},{9,1},{17,25},{25,17},{2,10},{10... | collective-permute-start | bytes 6291464 | tf_op jit(solution)/shard_map/ppermute | solution.py:43
  27.0 14.6 %collective-permute-start.8 = (f32[384,256]{1,0:T(8,128)S(1)}, f32[384,256]{1,0:T(8,128)}, u32[]{:S(2)}, u32[]{:S(2)}) collective-permute-start(f32[384,256]{1,0:T(8,128)S(1)} %copy-done.14), channel_id=1, source_target_pairs={{0,4},{8,12},{16,20},{24,28}} | collective-permute-start | bytes 1179656 | tf_op jit(solution)/shard_map/ppermute | solution.py:340
  28.4 13.3 %collective-permute-start.10 = (f32[256,512]{1,0:T(8,128)}, f32[256,512]{1,0:T(8,128)}, u32[]{:S(2)}, u32[]{:S(2)}) collective-permute-start(f32[256,512]{1,0:T(8,128)} %first_rows.1), channel_id=1, source_target_pairs={{0,8},{8,0},{16,24},{24,16},{1,9},{9,1},{17,25},{25,17},{2,10},{10... | collective-permute-start | bytes 1572872 | tf_op jit(solution)/shard_map/ppermute | solution.py:43
  28.9 12.0 %collective-permute-start.6 = (f32[384,128]{1,0:T(8,128)S(1)}, f32[384,128]{1,0:T(8,128)S(1)}, u32[]{:S(2)}, u32[]{:S(2)}) collective-permute-start(f32[384,128]{1,0:T(8,128)S(1)} %add.166), channel_id=1, source_target_pairs={{0,4},{1,5},{2,6},{3,7},{4,0},{5,1},{6,2},{7,3},{8,12},{9,13},{10,... | collective-permute-start | bytes 589832 | tf_op jit(solution)/shard_map/ppermute | solution.py:43
  28.9 12.7 %collective-permute-start.7 = (f32[384,128]{1,0:T(8,128)S(1)}, f32[384,128]{1,0:T(8,128)S(1)}, u32[]{:S(2)}, u32[]{:S(2)}) collective-permute-start(f32[384,128]{1,0:T(8,128)S(1)} %add.167), channel_id=1, source_target_pairs={{0,2},{1,3},{2,0},{3,1},{4,6},{5,7},{6,4},{7,5},{8,10},{9,11},{10,... | collective-permute-start | bytes 589832 | tf_op jit(solution)/shard_map/ppermute | solution.py:43
  34.1 7.6 %copy-start.7 = (f32[256,512]{1,0:T(8,128)S(1)}, f32[256,512]{1,0:T(8,128)}, u32[]{:S(2)}) copy-start(f32[256,512]{1,0:T(8,128)} %first_rows.1) | copy-start | bytes 1572868
  42.8 13.2 %copy-start.3 = (f32[1024,512]{1,0:T(8,128)}, f32[1024,512]{1,0:T(8,128)S(1)}, u32[]{:S(2)}) copy-start(f32[1024,512]{1,0:T(8,128)S(1)} %collective-permute-done.9.refs_8_) | copy-start | bytes 6291460
  42.9 14.9 %collective-permute-start.13 = (f32[384,256]{1,0:T(8,128)S(1)}, f32[384,256]{1,0:T(8,128)}, u32[]{:S(2)}, u32[]{:S(2)}) collective-permute-start(f32[384,256]{1,0:T(8,128)S(1)} %broadcast_select_fusion.10), channel_id=1, source_target_pairs={{0,2},{4,6},{8,10},{12,14},{16,18},{20,22},{24,26},{28,30}} | collective-permute-start | bytes 1179656 | tf_op jit(solution)/shard_map/ppermute | solution.py:340
  44.3 13.5 %collective-permute-start.14 = (f32[256,512]{1,0:T(8,128)S(1)}, f32[256,512]{1,0:T(8,128)}, u32[]{:S(2)}, u32[]{:S(2)}) collective-permute-start(f32[256,512]{1,0:T(8,128)S(1)} %add.171), channel_id=1, source_target_pairs={{0,16},{8,24},{16,0},{24,8},{1,17},{9,25},{17,1},{25,9},{2,18},{10... | collective-permute-start | bytes 1572872 | tf_op jit(solution)/shard_map/ppermute | solution.py:43
  45.8 10.4 %collective-permute-start.12 = (f32[384,128]{1,0:T(8,128)S(1)}, f32[384,128]{1,0:T(8,128)}, u32[]{:S(2)}, u32[]{:S(2)}) collective-permute-start(f32[384,128]{1,0:T(8,128)S(1)} %add.169), channel_id=1, source_target_pairs={{0,4},{1,5},{2,6},{3,7},{4,0},{5,1},{6,2},{7,3},{8,12},{9,13},{10,... | collective-permute-start | bytes 589832 | tf_op jit(solution)/shard_map/ppermute | solution.py:43
  59.0 8.3 %collective-permute-start.15 = (bf16[256,512]{1,0:T(8,128)(2,1)S(1)}, bf16[256,512]{1,0:T(8,128)(2,1)S(1)}, u32[]{:S(2)}, u32[]{:S(2)}) collective-permute-start(bf16[256,512]{1,0:T(8,128)(2,1)S(1)} %copy-done.6), channel_id=1, source_target_pairs={{0,16},{8,24},{16,0},{24,8},{1,17},{9,25},{17,1},{25,9},{2,18},{10... | collective-permute-start | bytes 786440 | tf_op jit(solution)/shard_map/ppermute | solution.py:43
  60.1 22.3 %collective-permute-start.17 = (f32[384,256]{1,0:T(8,128)S(1)}, f32[384,256]{1,0:T(8,128)S(1)}, u32[]{:S(2)}, u32[]{:S(2)}) collective-permute-start(f32[384,256]{1,0:T(8,128)S(1)} %broadcast_select_fusion.9), channel_id=1, source_target_pairs={{0,1},{2,3},{4,5},{6,7},{8,9},{10,11},{12,13},{14,15},{16,17},{18,... | collective-permute-start | bytes 1179656 | tf_op jit(solution)/shard_map/ppermute | solution.py:340
  67.3 15.9 %collective-permute-start.16 = (bf16[512,512]{1,0:T(8,128)(2,1)S(1)}, bf16[512,512]{1,0:T(8,128)(2,1)S(1)}, u32[]{:S(2)}, u32[]{:S(2)}) collective-permute-start(bf16[512,512]{1,0:T(8,128)(2,1)S(1)} %pad_maximum_fusion.3), channel_id=1, source_target_pairs={{0,8},{8,0},{16,24},{24,16},{1,9},{9,1},{17,25},{25,17},{2,10},{10... | collective-permute-start | bytes 1572872 | tf_op jit(solution)/shard_map/ppermute | solution.py:43
  67.4 23.8 %collective-permute-start.19 = (f32[256,256]{1,0:T(8,128)S(1)}, f32[256,256]{1,0:T(8,128)}, u32[]{:S(2)}, u32[]{:S(2)}) collective-permute-start(f32[256,256]{1,0:T(8,128)S(1)} %slice.57), channel_id=1, source_target_pairs={{0,4},{8,12},{16,20},{24,28}} | collective-permute-start | bytes 786440 | tf_op jit(solution)/shard_map/ppermute | solution.py:340
  90.9 8.5 %collective-permute-start.18 = (bf16[336,512]{1,0:T(8,128)(2,1)}, bf16[336,512]{1,0:T(8,128)(2,1)S(1)}, u32[]{:S(2)}, u32[]{:S(2)}) collective-permute-start(bf16[336,512]{1,0:T(8,128)(2,1)} %leaf_last.1), channel_id=1, source_target_pairs={{0,16},{8,24},{16,0},{24,8},{1,17},{9,25},{17,1},{25,9},{2,18},{10... | collective-permute-start | bytes 1032200 | tf_op jit(solution)/shard_map/ppermute | solution.py:43
  92.0 20.4 %collective-permute-start.23 = (bf16[1024,512]{1,0:T(8,128)(2,1)S(1)}, bf16[1024,512]{1,0:T(8,128)(2,1)}, u32[]{:S(2)}, u32[]{:S(2)}) collective-permute-start(bf16[1024,512]{1,0:T(8,128)(2,1)S(1)} %pad_maximum_fusion.1.d01_ref.refs_2_), channel_id=1, source_target_pairs={{0,4},{1,5},{10,14},{11,15},{20,16},{21,17},{30,26},{31,27}} | collective-permute-start | bytes 3145736 | tf_op jit(solution)/shard_map/ppermute | solution.py:463
  101.2 10.0 %collective-permute-start.22 = (bf16[672,512]{1,0:T(8,128)(2,1)S(1)}, bf16[672,512]{1,0:T(8,128)(2,1)}, u32[]{:S(2)}, u32[]{:S(2)}) collective-permute-start(bf16[672,512]{1,0:T(8,128)(2,1)S(1)} %pad_maximum_fusion.2), channel_id=1, source_target_pairs={{0,8},{8,0},{16,24},{24,16},{1,9},{9,1},{17,25},{25,17},{2,10},{10... | collective-permute-start | bytes 2064392 | tf_op jit(solution)/shard_map/ppermute | solution.py:43
  102.5 53.3 %collective-permute-start.11 = (f32[1024,512]{1,0:T(8,128)}, f32[1024,512]{1,0:T(8,128)}, u32[]{:S(2)}, u32[]{:S(2)}) collective-permute-start(f32[1024,512]{1,0:T(8,128)} %near_rows.1), channel_id=1, source_target_pairs={{0,8},{8,0},{16,24},{24,16},{1,9},{9,1},{17,25},{25,17},{2,10},{10... | collective-permute-start | bytes 6291464 | tf_op jit(solution)/shard_map/ppermute | solution.py:43
  103.0 12.0 %collective-permute-start.20 = (f32[256,256]{1,0:T(8,128)}, f32[256,256]{1,0:T(8,128)}, u32[]{:S(2)}, u32[]{:S(2)}) collective-permute-start(f32[256,256]{1,0:T(8,128)} %broadcast_select_fusion.11), channel_id=1, source_target_pairs={{0,2},{4,6},{8,10},{12,14},{16,18},{20,22},{24,26},{28,30}} | collective-permute-start | bytes 786440 | tf_op jit(solution)/shard_map/ppermute | solution.py:340
  107.6 3.5 %copy-start.5 = (bf16[336,512]{1,0:T(8,128)(2,1)S(1)}, bf16[336,512]{1,0:T(8,128)(2,1)}, u32[]{:S(2)}) copy-start(bf16[336,512]{1,0:T(8,128)(2,1)} %leaf_last.1) | copy-start | bytes 1032196
  107.6 3.5 %copy-start.9 = (bf16[336,512]{1,0:T(8,128)(2,1)S(1)}, bf16[336,512]{1,0:T(8,128)(2,1)}, u32[]{:S(2)}) copy-start(bf16[336,512]{1,0:T(8,128)(2,1)} %copy-done.8) | copy-start | bytes 1032196
  113.5 15.1 %collective-permute-start.24 = (bf16[512,512]{1,0:T(8,128)(2,1)S(1)}, bf16[512,512]{1,0:T(8,128)(2,1)}, u32[]{:S(2)}, u32[]{:S(2)}) collective-permute-start(bf16[512,512]{1,0:T(8,128)(2,1)S(1)} %bitcast.27), channel_id=1, source_target_pairs={{0,4},{1,5},{10,14},{11,15},{20,16},{21,17},{30,26},{31,27}} | collective-permute-start | bytes 1572872 | tf_op jit(solution)/shard_map/ppermute | solution.py:463
  116.6 12.0 %collective-permute-start.21 = (f32[256,256]{1,0:T(8,128)}, f32[256,256]{1,0:T(8,128)}, u32[]{:S(2)}, u32[]{:S(2)}) collective-permute-start(f32[256,256]{1,0:T(8,128)} %broadcast_select_fusion.12), channel_id=1, source_target_pairs={{0,1},{2,3},{4,5},{6,7},{8,9},{10,11},{12,13},{14,15},{16,17},{18,... | collective-permute-start | bytes 786440 | tf_op jit(solution)/shard_map/ppermute | solution.py:340
  117.9 35.0 %collective-permute-start.26 = (bf16[1024,512]{1,0:T(8,128)(2,1)}, bf16[1024,512]{1,0:T(8,128)(2,1)S(1)}, u32[]{:S(2)}, u32[]{:S(2)}) collective-permute-start(bf16[1024,512]{1,0:T(8,128)(2,1)} %broadcast_select_fusion.2), channel_id=1, source_target_pairs={{0,1},{1,0},{4,5},{5,4},{10,11},{11,10},{14,15},{15,14},{20,21},{2... | collective-permute-start | bytes 3145736 | tf_op jit(solution)/shard_map/ppermute | solution.py:475
  118.7 37.7 %collective-permute-start.28 = (bf16[1024,512]{1,0:T(8,128)(2,1)}, bf16[1024,512]{1,0:T(8,128)(2,1)}, u32[]{:S(2)}, u32[]{:S(2)}) collective-permute-start(bf16[1024,512]{1,0:T(8,128)(2,1)} %broadcast_select_fusion.2), channel_id=1, source_target_pairs={{0,2},{1,3},{4,6},{5,7},{10,8},{11,9},{14,12},{15,13},{20,22},{21,... | collective-permute-start | bytes 3145736 | tf_op jit(solution)/shard_map/ppermute | solution.py:463
  128.6 24.4 %collective-permute-start.25 = (f32[512,512]{1,0:T(8,128)}, f32[512,512]{1,0:T(8,128)S(1)}, u32[]{:S(2)}, u32[]{:S(2)}) collective-permute-start(f32[512,512]{1,0:T(8,128)} %far_sum.2), channel_id=1, source_target_pairs={{0,16},{8,24},{16,0},{24,8},{1,17},{9,25},{17,1},{25,9},{2,18},{10... | collective-permute-start | bytes 3145736 | tf_op jit(solution)/shard_map/ppermute | solution.py:43
  128.6 46.8 %collective-permute-start.27 = (f32[512,512]{1,0:T(8,128)}, f32[512,512]{1,0:T(8,128)S(1)}, u32[]{:S(2)}, u32[]{:S(2)}) collective-permute-start(f32[512,512]{1,0:T(8,128)} %far_sum.3), channel_id=1, source_target_pairs={{0,16},{8,24},{16,0},{24,8},{1,17},{9,25},{17,1},{25,9},{2,18},{10... | collective-permute-start | bytes 3145736 | tf_op jit(solution)/shard_map/ppermute | solution.py:43
  140.7 15.0 %copy-start.1 = (f32[128,128]{1,0:T(8,128)}, f32[128,128]{1,0:T(8,128)S(1)}, u32[]{:S(2)}) copy-start(f32[128,128]{1,0:T(8,128)S(1)} %get-tuple-element.96.refs_9_) | copy-start | bytes 196612
  152.9 22.5 %copy-start.10 = (f32[512,512]{1,0:T(8,128)}, f32[512,512]{1,0:T(8,128)S(1)}, u32[]{:S(2)}) copy-start(f32[512,512]{1,0:T(8,128)S(1)} %collective-permute-done.25.refs_10_) | copy-start | bytes 3145732
  152.9 22.5 %copy-start.12 = (bf16[1024,512]{1,0:T(8,128)(2,1)}, bf16[1024,512]{1,0:T(8,128)(2,1)S(1)}, u32[]{:S(2)}) copy-start(bf16[1024,512]{1,0:T(8,128)(2,1)S(1)} %collective-permute-done.26) | copy-start | bytes 3145732
  152.9 31.8 %collective-permute-start.30 = (bf16[512,512]{1,0:T(8,128)(2,1)}, bf16[512,512]{1,0:T(8,128)(2,1)}, u32[]{:S(2)}, u32[]{:S(2)}) collective-permute-start(bf16[512,512]{1,0:T(8,128)(2,1)} %broadcast_select_fusion.5), channel_id=1, source_target_pairs={{0,2},{1,3},{4,6},{5,7},{10,8},{11,9},{14,12},{15,13},{20,22},{21,... | collective-permute-start | bytes 1572872 | tf_op jit(solution)/shard_map/ppermute | solution.py:463
  154.2 39.0 %collective-permute-start.32 = (bf16[512,512]{1,0:T(8,128)(2,1)}, bf16[512,512]{1,0:T(8,128)(2,1)}, u32[]{:S(2)}, u32[]{:S(2)}) collective-permute-start(bf16[512,512]{1,0:T(8,128)(2,1)} %broadcast_select_fusion.5), channel_id=1, source_target_pairs={{0,1},{1,0},{4,5},{5,4},{10,11},{11,10},{14,15},{15,14},{20,21},{2... | collective-permute-start | bytes 1572872 | tf_op jit(solution)/shard_map/ppermute | solution.py:475
  155.7 27.5 %collective-permute-start.33 = (bf16[256,512]{1,0:T(8,128)(2,1)S(1)}, bf16[256,512]{1,0:T(8,128)(2,1)S(1)}, u32[]{:S(2)}, u32[]{:S(2)}) collective-permute-start(bf16[256,512]{1,0:T(8,128)(2,1)S(1)} %get-tuple-element.100.refs_4_), channel_id=1, source_target_pairs={{0,4},{1,5},{10,14},{11,15},{20,16},{21,17},{30,26},{31,27}} | collective-permute-start | bytes 786440 | tf_op jit(solution)/shard_map/ppermute | solution.py:463
  156.4 35.4 %collective-permute-start.29 = (bf16[1024,512]{1,0:T(8,128)(2,1)}, bf16[1024,512]{1,0:T(8,128)(2,1)}, u32[]{:S(2)}, u32[]{:S(2)}) collective-permute-start(bf16[1024,512]{1,0:T(8,128)(2,1)} %collective-permute-done.28), channel_id=1, source_target_pairs={{2,3},{3,2},{6,7},{7,6},{8,9},{9,8},{12,13},{13,12},{22,23},{23,22... | collective-permute-start | bytes 3145736 | tf_op jit(solution)/shard_map/ppermute | solution.py:475
  176.4 5.5 %copy-start.4 = (bf16[1024,512]{1,0:T(8,128)(2,1)S(1)}, bf16[1024,512]{1,0:T(8,128)(2,1)}, u32[]{:S(2)}) copy-start(bf16[1024,512]{1,0:T(8,128)(2,1)} %broadcast_select_fusion.2) | copy-start | bytes 3145732
  183.2 8.6 %copy-start.13 = (bf16[1024,512]{1,0:T(8,128)(2,1)S(1)}, bf16[1024,512]{1,0:T(8,128)(2,1)}, u32[]{:S(2)}) copy-start(bf16[1024,512]{1,0:T(8,128)(2,1)} %copy-done.12) | copy-start | bytes 3145732
  183.3 8.4 %collective-permute-start.34 = (bf16[256,512]{1,0:T(8,128)(2,1)S(1)}, bf16[256,512]{1,0:T(8,128)(2,1)S(1)}, u32[]{:S(2)}, u32[]{:S(2)}) collective-permute-start(bf16[256,512]{1,0:T(8,128)(2,1)S(1)} %broadcast_select_fusion.6), channel_id=1, source_target_pairs={{0,2},{1,3},{4,6},{5,7},{10,8},{11,9},{14,12},{15,13},{20,22},{21,... | collective-permute-start | bytes 786440 | tf_op jit(solution)/shard_map/ppermute | solution.py:463
  184.8 14.1 %collective-permute-start.31 = (bf16[512,512]{1,0:T(8,128)(2,1)}, bf16[512,512]{1,0:T(8,128)(2,1)S(1)}, u32[]{:S(2)}, u32[]{:S(2)}) collective-permute-start(bf16[512,512]{1,0:T(8,128)(2,1)} %collective-permute-done.30), channel_id=1, source_target_pairs={{2,3},{3,2},{6,7},{7,6},{8,9},{9,8},{12,13},{13,12},{22,23},{23,22... | collective-permute-start | bytes 1572872 | tf_op jit(solution)/shard_map/ppermute | solution.py:475
  191.7 7.2 %copy-start.2 = (f32[128,128]{1,0:T(8,128)S(1)}, f32[128,128]{1,0:T(8,128)}, u32[]{:S(2)}) copy-start(f32[128,128]{1,0:T(8,128)} %copy-done.1) | copy-start | bytes 196612
  191.7 14.1 %collective-permute-start.35 = (bf16[256,512]{1,0:T(8,128)(2,1)S(1)}, bf16[256,512]{1,0:T(8,128)(2,1)S(1)}, u32[]{:S(2)}, u32[]{:S(2)}) collective-permute-start(bf16[256,512]{1,0:T(8,128)(2,1)S(1)} %broadcast_select_fusion.7.refs_5_), channel_id=1, source_target_pairs={{0,1},{1,0},{4,5},{5,4},{2,3},{3,2},{6,7},{7,6},{10,11},{11,10},{1... | collective-permute-start | bytes 786440 | tf_op jit(solution)/shard_map/ppermute | solution.py:475
  (5 other events, 9.2 us)

commit v6 on v5

--- a/solution.py
+++ b/solution.py
@@ -331,14 +331,18 @@
     smem = pl.BlockSpec(memory_space=pltpu.SMEM)
     vmem = pl.BlockSpec(memory_space=pltpu.VMEM)
 
+    hops = bits(members)
+    last = len(hops) - 1
+    lead_order = [hops[-1], hops[0]] + hops[-2:0:-1]
+
     def lead_hop(value, at):
-        bit = bits(members)[-1 - at]
+        bit, used = lead_order[at], sum(lead_order[:at])
         parts = []
         for root in range(leads):
             held = value[root]
-            pairs = [(root ^ i, root ^ i ^ bit) for i in range(0, members, 2 * bit)]
-            got = lax.ppermute(held, "mem", pairs)
-            parts.append(jnp.where((m ^ root) % (2 * bit) == bit, got, held))
+            sources = [root ^ i for i in range(members) if i & ~used == 0]
+            got = lax.ppermute(held, "mem", [(src, src ^ bit) for src in sources])
+            parts.append(jnp.where((m ^ root) & ~used == bit, got, held))
         return parts
 
     table_rows, head, rest, mask, w_lead = pl.pallas_call(
@@ -352,8 +356,6 @@
         ),
         name="pick_pivots",
     )(owner, (m * per).reshape(1), front)
-    hops = bits(members)
-    last = len(hops) - 1
     w_lead = [w_lead] * leads
 
     def table_hop(value, at):
@@ -363,6 +365,7 @@
     for at in range(last + 1):
         table_rows = table_hop(table_rows, at)
     head = table_hop(head, 0)
+    w_lead = lead_hop(w_lead, 0)
     table_rows, head, rest, w_lead = tie((table_rows, head, rest, w_lead))
     table = table_rows[0, :count].astype(jnp.int32)
 
@@ -391,16 +394,16 @@
         rest = table_hop(rest, at - 1)
     head, rest, diagonal, first, w_lead = tie((head, rest, diagonal, first, w_lead))
     near = rows_at(2 * n, n, [], "near_rows")
-    diagonal = flip(diagonal, "grp", CORE)
     first = first + flip(first, "grp", CORE)
     head = table_hop(head, last)
     rest = table_hop(rest, last - 1)
-    w_lead = lead_hop(w_lead, 0)
+    w_lead = lead_hop(w_lead, 1)
     head, rest, w_lead, diagonal, first, near = tie((head, rest, w_lead, diagonal, first, near))
     near = flip(near, "grp", CORE)
+    diagonal = flip(diagonal, "grp", CORE)
     first = first + flip(first, "grp", CHIP)
     rest = table_hop(rest, last)
-    for at in range(1, last):
+    for at in range(2, last + 1):
         w_lead = lead_hop(w_lead, at)
 
     work = [pltpu.VMEM((b, 2 * b), f32)]
@@ -429,9 +432,9 @@
         return jnp.concatenate([both, flip(both, "grp", CORE)], axis=0)
 
     d01 = across(p01)
-    rest, d01 = tie((rest, d01))
     corner = lead_hop([first[:, :lead_cols]] * leads, 0)
-    w_lead = lead_hop(w_lead, last)
+    rest, d01, corner = tie((rest, d01, corner))
+    corner = lead_hop(corner, 1)
     w_lead = w_lead[0] if leads == 1 else jnp.concatenate(w_lead, axis=1)
     lead_rows = (PL * b + LOG_ROWS) * pr // cols
     pack = pl.pallas_call(
@@ -490,16 +493,16 @@
 
     s01 = zone_hop(([0], d01, None))
     pack_far = flip(pack, "grp", CHIP)
-    pack, pack_far, diagonal, *corner = tie((pack, pack_far, diagonal, *corner))
-    far_in = [rows_at(n + i * ways, ways, [(diagonal, 0, i)], "far_sum") for i in range(2)]
-    for at in range(1, last + 1):
+    pack, pack_far, diagonal, corner = tie((pack, pack_far, diagonal, corner))
+    far_in = rows_at(n, ways, [(diagonal, 0, 0)], "far_sum")
+    for at in range(2, last + 1):
         corner = lead_hop(corner, at)
-    corner = corner[0] if leads == 1 else jnp.concatenate(corner, axis=1)
     pack = jnp.concatenate([pack, pack_far], axis=0)
     pack = jnp.concatenate([pack, flip(pack, "grp", CORE)], axis=0)
-    pack, held, *far_in = tie((pack, s01[1], *far_in))
+    pack, held, far_in, corner = tie((pack, s01[1], far_in, corner))
+    corner = corner[0] if leads == 1 else jnp.concatenate(corner, axis=1)
     s01 = (s01[0], held, None)
-    far = [flip(part, "grp", CHIP) for part in far_in]
+    far = [flip(far_in, "grp", CHIP)]
     early01 = early_hops(s01)
     s01 = zone_hop(s01)
     d2 = pack.reshape(groups, b + lead_rows, cols)[:, :b].reshape(groups * b, cols)
@@ -513,9 +516,16 @@
         compiler_params=pltpu.CompilerParams(vmem_limit_bytes=32 << 20),
         name="root_step",
     )(leaves, corner, first, d01, pack)
-    q, held, far[0], *early01 = tie((q, s2[1], far[0], *early01))
+    q, diagonal = tie((q, diagonal))
+    sq_hop = zone_hop(([0], q, None))
+    far_in = rows_at(n + ways, ways, [(diagonal, 0, 1)], "far_sum")
+    far.append(flip(far_in, "grp", CHIP))
+    q_held, held, far[0], s01_held, s01_got, *early01 = tie(
+        (sq_hop[1], s2[1], far[0], s01[1], s01[2][1], *early01)
+    )
+    s01 = (s01[0], s01_held, (s01[2][0], s01_got))
     s2 = (s2[0], held, None)
-    rq = inner_hops(zone_hop(zone_hop(([0], q, None))))
+    rq = inner_hops(zone_hop((sq_hop[0], q_held, None)))
     early2 = early_hops(s2)
     s2 = zone_hop(s2)
     r01 = inner_hops(s01, early01)

time: 211 us -> 210 us (level)
  the two profiles are of different devices: /device:TPU:28 before, /device:TPU:10 now
where the time goes in v6:
time: 210 us; the launch traced here: 209 us
  waiting for transfers between devices  83.3 us (40%)
  Pallas kernels  58.7 us (28%)
  starting transfers between devices  43.4 us (21%)
  other arithmetic  15.6 us (7%)
  local copies, waits for them, and re-layouts  6.82 us (3%)
    ppermute x19, waiting for transfers between devices, flip(): return lax.ppermute(value, axis, [(i, i ^ bit) for i in range(size)])  53.6 us
    ppermute x19, starting transfers between devices, flip(): return lax.ppermute(value, axis, [(i, i ^ bit) for i in range(size)])  22.7 us
    pallas_call x6, Pallas kernels, take_rows(): pl.pallas_call(body, grid_spec=pltpu.PrefetchScalarGridSpec(num_scalar_pr...  21.4 us
    ppermute x6, waiting for transfers between devices, zone_hop(): got = lax.ppermute(held, ('grp', 'mem'), pairs)  14.7 us
    ppermute x6, waiting for transfers between devices, lead_hop(): got = lax.ppermute(held, 'mem', [(src, src ^ bit) for src in sources])  12.1 us
    pallas_call x1, Pallas kernels, local(): pl.pallas_call(leaf_two, grid=(1,), in_specs=[vmem, w_spec(0), w_spec(1),...  9.42 us
    ppermute x5, starting transfers between devices, inner_hop(): return lax.ppermute(value, ('grp', 'mem'), pairs)  9.25 us
    pallas_call x1, Pallas kernels, local(): pl.pallas_call(root_step, in_specs=[smem] + [vmem] * 4, out_shape=(shape(...  8.95 us
  transfers between devices with their start and end apart: 36, of which 13 were waited for; matrix products, arithmetic and copies ran while one was open for 8% of the time, Pallas kernels for 26%

profile of v6, /device:TPU:10, one launch (start us, length us, event | category | flops | bytes accessed | tf_op | source)
XLA Modules:
  0.0 208.9 jit_solution(751592227554869599)
XLA Ops:
  0.6 2.1 %pick_pivots.1 = (f32[8,128]{1,0:T(8,128)}, f32[384,128]{1,0:T(8,128)}, f32[384,128]{1,0:T(8,128)}, f32[8,512]{1,0:T(8,128)}, f32[384,256]{1,0:T(8,128)}) custom-call(s32[4]{0:T(128)} %bitcast.55, s32[1]{0:T(128)} %bitcast.2.at_ref, f32[4096,512]{1,0:T(8,128)} %bitcast.29), custom_call_target="tpu_custom_call" | custom-call | tf_op jit(solution)/shard_map/pick_pivots/pallas_call | solution.py:348
  2.7 1.5 collective-permute-start
  7.3 3.3 %collective-permute-start.1 = (f32[8,128]{1,0:T(8,128)S(1)}, f32[8,128]{1,0:T(8,128)S(1)}, u32[]{:S(2)}, u32[]{:S(2)}) collective-permute-start(f32[8,128]{1,0:T(8,128)S(1)} %add.150), channel_id=1, source_target_pairs={{0,2},{1,3},{2,0},{3,1},{4,6},{5,7},{6,4},{7,5},{8,10},{9,11},{10,... | collective-permute-start | bytes 12296 | tf_op jit(solution)/shard_map/ppermute | solution.py:43
  10.6 7.7 %collective-permute-done.1 = f32[8,128]{1,0:T(8,128)S(1)} collective-permute-done((f32[8,128]{1,0:T(8,128)S(1)}, f32[8,128]{1,0:T(8,128)S(1)}, u32[]{:S(2)}, u32[]{:S(2)}) %collective-permute-start.1) | collective-permute-done | bytes 4128 | tf_op jit(solution)/shard_map/ppermute | solution.py:43
  18.4 4.4 %collective-permute-done.2 = f32[8,128]{1,0:T(8,128)S(1)} collective-permute-done((f32[8,128]{1,0:T(8,128)S(1)}, f32[8,128]{1,0:T(8,128)S(1)}, u32[]{:S(2)}, u32[]{:S(2)}) %collective-permute-start.2) | collective-permute-done | bytes 4128 | tf_op jit(solution)/shard_map/ppermute | solution.py:43
  22.8 0.9 add.153
  23.8 1.1 broadcast_select_fusion.10
  28.0 3.3 %far_rows.1 = f32[1024,512]{1,0:T(8,128)} custom-call(s32[8]{0:T(128)} %get-tuple-element.122.refs_0_, s32[8]{0:T(128)} %get-tuple-element.119.refs_1_, s32[1]{0:T(128)} %constant.63.clone.1.refs_2_, f32[4096,512]{1,0:T(8,128)} %bitcast.30, f32[4096,512]{1,0:T(8,128)} %bitcast.31, f32[4096,512]{1,0:T(8,128)} %bitcast.32, f32[4096,512]{1,0:T(8,128)} %bitcast.33, ...), custom_call_target="tpu_custom_call" | custom-call | tf_op jit(solution)/shard_map/far_rows/pallas_call | solution.py:214
  31.4 2.7 %first_rows.1 = f32[256,512]{1,0:T(8,128)} custom-call(s32[2]{0:T(128)} %slice.53.refs_0_, s32[2]{0:T(128)} %slice.54.refs_1_, s32[1]{0:T(128)} %bitcast.10.refs_2_, f32[4096,512]{1,0:T(8,128)} %bitcast.34, f32[4096,512]{1,0:T(8,128)} %bitcast.35, f32[8,512]{1,0:T(8,128)} %get-tuple-element.62.refs_7_.refs_5_.mask_ref, f32[1024,512]{1,0:T(8,128)} %refs_8_.1), custom_call_target="tpu_custom_call" | custom-call | tf_op jit(solution)/shard_map/first_rows/pallas_call | solution.py:214
  35.0 5.4 %collective-permute-start.8 = (f32[384,128]{1,0:T(8,128)S(1)}, f32[384,128]{1,0:T(8,128)S(1)}, u32[]{:S(2)}, u32[]{:S(2)}) collective-permute-start(f32[384,128]{1,0:T(8,128)S(1)} %add.157), channel_id=1, source_target_pairs={{0,2},{1,3},{2,0},{3,1},{4,6},{5,7},{6,4},{7,5},{8,10},{9,11},{10,... | collective-permute-start | bytes 589832 | tf_op jit(solution)/shard_map/ppermute | solution.py:43
  40.4 3.3 %near_rows.1 = f32[1024,512]{1,0:T(8,128)} custom-call(s32[8]{0:T(128)} %get-tuple-element.121.refs_0_, s32[8]{0:T(128)} %get-tuple-element.118.refs_1_, s32[1]{0:T(128)} %constant.63.clone.1.refs_2_, f32[4096,512]{1,0:T(8,128)} %bitcast.36, f32[4096,512]{1,0:T(8,128)} %bitcast.37, f32[4096,512]{1,0:T(8,128)} %bitcast.38, f32[4096,512]{1,0:T(8,128)} %bitcast.39, ...), custom_call_target="tpu_custom_call" | custom-call | tf_op jit(solution)/shard_map/near_rows/pallas_call | solution.py:214
  44.4 5.6 %collective-permute-done.8 = f32[384,128]{1,0:T(8,128)S(1)} collective-permute-done((f32[384,128]{1,0:T(8,128)S(1)}, f32[384,128]{1,0:T(8,128)S(1)}, u32[]{:S(2)}, u32[]{:S(2)}) %collective-permute-start.8) | collective-permute-done | bytes 196640 | tf_op jit(solution)/shard_map/ppermute | solution.py:43
  50.2 1.3 collective-permute-start.13
  52.2 9.4 %leaf_two.1 = (bf16[256,512]{1,0:T(8,128)(2,1)}, f32[128,128]{1,0:T(8,128)}, f32[128,128]{1,0:T(8,128)}, bf16[128,128]{1,0:T(8,128)(2,1)}, f32[8,128]{1,0:T(8,128)}) custom-call(f32[384,128]{1,0:T(8,128)} %add.158.head_ref, f32[4096,512]{1,0:T(8,128)} %bitcast.41, f32[4096,512]{1,0:T(8,128)} %bitcast.40, f32[8,512]{1,0:T(8,128)} %get-tuple-element.62.refs_7_.refs_5_.mask_ref), custom_call_target="tpu_custom_call" | custom-call | tf_op jit(solution)/shard_map/leaf_two/pallas_call | solution.py:417
  62.4 1.8 collective-permute-done.13
  64.9 1.0 collective-permute-done.14
  66.6 7.3 %collective-permute-done.15 = bf16[256,512]{1,0:T(8,128)(2,1)S(1)} collective-permute-done((bf16[256,512]{1,0:T(8,128)(2,1)S(1)}, bf16[256,512]{1,0:T(8,128)(2,1)S(1)}, u32[]{:S(2)}, u32[]{:S(2)}) %collective-permute-start.15) | collective-permute-done | bytes 262176 | tf_op jit(solution)/shard_map/ppermute | solution.py:43
  74.9 1.1 collective-permute-done.16
  76.9 7.6 %leaf_last.1 = bf16[336,512]{1,0:T(8,128)(2,1)} custom-call(f32[384,128]{1,0:T(8,128)} %add.161.rest_ref, f32[4096,512]{1,0:T(8,128)} %bitcast.42, f32[384,256]{1,0:T(8,128)} %broadcast_select_fusion.8.w_lead_ref, f32[8,128]{1,0:T(8,128)} %copy-done.5, f32[8,512]{1,0:T(8,128)} %get-tuple-element.62.refs_7_.refs_5_.mask_ref, ...), custom_call_target="tpu_custom_call" | custom-call | tf_op jit(solution)/shard_map/leaf_last/pallas_call | solution.py:440
  86.5 8.4 %collective-permute-done.18 = bf16[336,512]{1,0:T(8,128)(2,1)S(1)} collective-permute-done((bf16[336,512]{1,0:T(8,128)(2,1)}, bf16[336,512]{1,0:T(8,128)(2,1)S(1)}, u32[]{:S(2)}, u32[]{:S(2)}) %collective-permute-start.18) | collective-permute-done | bytes 344096 | tf_op jit(solution)/shard_map/ppermute | solution.py:43
  94.9 1.3 collective-permute-start.23
  96.2 1.9 pad_maximum_fusion.2
  99.2 3.4 %far_sum.2 = f32[512,512]{1,0:T(8,128)} custom-call(s32[4]{0:T(128)} %get-tuple-element.117.refs_0_, s32[4]{0:T(128)} %get-tuple-element.115.refs_1_, s32[1]{0:T(128)} %constant.63.clone.1.refs_2_, f32[4096,512]{1,0:T(8,128)} %bitcast.43, f32[4096,512]{1,0:T(8,128)} %bitcast.44, f32[4096,512]{1,0:T(8,128)} %bitcast.45, f32[4096,512]{1,0:T(8,128)} %bitcast.46, ...), custom_call_target="tpu_custom_call" | custom-call | tf_op jit(solution)/shard_map/far_sum/pallas_call | solution.py:214
  102.6 10.3 %collective-permute-done.23 = f32[256,256]{1,0:T(8,128)S(1)} collective-permute-done((f32[256,256]{1,0:T(8,128)S(1)}, f32[256,256]{1,0:T(8,128)S(1)}, u32[]{:S(2)}, u32[]{:S(2)}) %collective-permute-start.23) | collective-permute-done | bytes 262176 | tf_op jit(solution)/shard_map/ppermute | solution.py:344
  113.0 1.1 broadcast_select_fusion.2
  114.1 1.2 pad_maximum_fusion.pack_ref
  115.3 1.3 collective-permute-start.27
  116.7 8.9 %root_step.1 = (bf16[256,512]{1,0:T(8,128)(2,1)S(1)}, f32[128,128]{1,0:T(8,128)S(1)}, f32[128,128]{1,0:T(8,128)S(1)}, bf16[128,128]{1,0:T(8,128)(2,1)S(1)}, f32[8,128]{1,0:T(8,128)S(1)}) custom-call(s32[4]{0:T(128)S(1)} %pad_add_fusion.1.leaf_ref, f32[256,256]{1,0:T(8,128)S(1)} %broadcast_select_fusion.11.corner_ref, f32[256,512]{1,0:T(8,128)S(1)} %add.162.first_ref, ...), custom_call_target="tpu_custom_call" | custom-call | tf_op jit(solution)/shard_map/root_step/pallas_call | solution.py:511
  127.0 9.3 %collective-permute-start.26 = (f32[512,512]{1,0:T(8,128)}, f32[512,512]{1,0:T(8,128)}, u32[]{:S(2)}, u32[]{:S(2)}) collective-permute-start(f32[512,512]{1,0:T(8,128)} %far_sum.2), channel_id=1, source_target_pairs={{0,16},{8,24},{16,0},{24,8},{1,17},{9,25},{17,1},{25,9},{2,18},{10... | collective-permute-start | bytes 3145736 | tf_op jit(solution)/shard_map/ppermute | solution.py:43
  136.4 1.7 collective-permute-start.28
  138.0 3.3 %far_sum.3 = f32[512,512]{1,0:T(8,128)} custom-call(s32[4]{0:T(128)} %get-tuple-element.116.refs_0_, s32[4]{0:T(128)} %get-tuple-element.114.refs_1_, s32[1]{0:T(128)} %constant.63.clone.1.refs_2_, f32[4096,512]{1,0:T(8,128)} %bitcast.47, f32[4096,512]{1,0:T(8,128)} %bitcast.48, f32[4096,512]{1,0:T(8,128)} %bitcast.49, f32[4096,512]{1,0:T(8,128)} %bitcast.50, ...), custom_call_target="tpu_custom_call" | custom-call | tf_op jit(solution)/shard_map/far_sum/pallas_call | solution.py:214
  142.4 1.3 broadcast_select_fusion.1.refs_4_
  143.7 17.0 %collective-permute-done.26.refs_10_ = f32[512,512]{1,0:T(8,128)} collective-permute-done((f32[512,512]{1,0:T(8,128)}, f32[512,512]{1,0:T(8,128)}, u32[]{:S(2)}, u32[]{:S(2)}) %collective-permute-start.26) | collective-permute-done | bytes 1048608 | tf_op jit(solution)/shard_map/ppermute | solution.py:43
  160.7 1.3 collective-permute-start.31
  162.1 1.3 collective-permute-start.34
  163.4 1.9 collective-permute-start.30
  165.4 1.5 collective-permute-start.33
  166.8 14.7 %collective-permute-done.31 = bf16[512,512]{1,0:T(8,128)(2,1)} collective-permute-done((bf16[512,512]{1,0:T(8,128)(2,1)}, bf16[512,512]{1,0:T(8,128)(2,1)}, u32[]{:S(2)}, u32[]{:S(2)}) %collective-permute-start.31) | collective-permute-done | bytes 524320 | tf_op jit(solution)/shard_map/ppermute | solution.py:466
  181.5 2.4 %collective-permute-start.32 = (bf16[512,512]{1,0:T(8,128)(2,1)}, bf16[512,512]{1,0:T(8,128)(2,1)}, u32[]{:S(2)}, u32[]{:S(2)}) collective-permute-start(bf16[512,512]{1,0:T(8,128)(2,1)} %collective-permute-done.31), channel_id=1, source_target_pairs={{2,3},{3,2},{6,7},{7,6},{8,9},{9,8},{12,13},{13,12},{22,23},{23,22... | collective-permute-start | bytes 1572872 | tf_op jit(solution)/shard_map/ppermute | solution.py:478
  184.5 5.3 %base_rows.1.refs_1_ = f32[1024,512]{1,0:T(8,128)} custom-call(s32[8]{0:T(128)} %get-tuple-element.123.refs_0_, s32[8]{0:T(128)} %get-tuple-element.120.refs_1_, s32[1]{0:T(128)} %constant.63.clone.1.refs_2_, f32[4096,512]{1,0:T(8,128)} %bitcast.51, f32[4096,512]{1,0:T(8,128)} %bitcast.52, f32[4096,512]{1,0:T(8,128)} %bitcast.53, f32[4096,512]{1,0:T(8,128)} %bitcast.54, ...), custom_call_target="tpu_custom_call" | custom-call | tf_op jit(solution)/shard_map/base_rows/pallas_call | solution.py:214
  189.8 1.8 collective-permute-start.35
  191.6 1.1 broadcast_select_fusion.4.refs_6_
  192.8 3.0 %collective-permute-done.32 = bf16[512,512]{1,0:T(8,128)(2,1)} collective-permute-done((bf16[512,512]{1,0:T(8,128)(2,1)}, bf16[512,512]{1,0:T(8,128)(2,1)}, u32[]{:S(2)}, u32[]{:S(2)}) %collective-permute-start.32) | collective-permute-done | bytes 524320 | tf_op jit(solution)/shard_map/ppermute | solution.py:478
  195.7 1.1 broadcast_select_fusion.3.refs_7_
  196.8 1.3 broadcast_select_fusion.refs_5_
  198.2 7.0 %update.1 = (f32[1024,512]{1,0:T(8,128)}, f32[1024,256]{1,0:T(8,128)S(1)}) custom-call(s32[2]{0:T(128)S(1)} %iota_xor_fusion.refs_0_, f32[1024,512]{1,0:T(8,128)} %base_rows.1.refs_1_, bf16[1024,512]{1,0:T(8,128)(2,1)S(1)} %pad_maximum_fusion.1.d01_ref.refs_2_, bf16[512,512]{1,0:T(8,128)(2,1)S(1)} %bitcast.28, ...), custom_call_target="tpu_custom_call" | custom-call | tf_op jit(solution)/shard_map/update/pallas_call | solution.py:546
  205.1 1.6 copy-done
  206.7 2.2 %finish.1 = f32[1024,512]{1,0:T(8,128)} custom-call(s32[2]{0:T(128)S(1)} %iota_xor_fusion.refs_0_, s32[3]{0:T(128)S(1)} %pad_add_fusion.refs_1_, f32[1024,512]{1,0:T(8,128)S(1)} %copy-done, f32[1024,256]{1,0:T(8,128)S(1)} %get-tuple-element.109.refs_3_, bf16[256,512]{1,0:T(8,128)(2,1)S(1)} %get-tuple-element.96.refs_4_, ...), custom_call_target="tpu_custom_call" | custom-call | tf_op jit(solution)/shard_map/finish/pallas_call | solution.py:571
  (103 shorter events, 18.9 us)
Async XLA Ops:
  2.7 24.7 %copy-start.4 = (f32[384,128]{1,0:T(8,128)S(1)}, f32[384,128]{1,0:T(8,128)}, u32[]{:S(2)}) copy-start(f32[384,128]{1,0:T(8,128)} %get-tuple-element.64) | copy-start | bytes 589828
  2.7 3.8 %collective-permute-start = (f32[8,128]{1,0:T(8,128)}, f32[8,128]{1,0:T(8,128)S(1)}, u32[]{:S(2)}, u32[]{:S(2)}) collective-permute-start(f32[8,128]{1,0:T(8,128)} %get-tuple-element.57), channel_id=1, source_target_pairs={{0,1},{1,0},{2,3},{3,2},{4,5},{5,4},{6,7},{7,6},{8,9},{9,8},{10,11... | collective-permute-start | bytes 12296 | tf_op jit(solution)/shard_map/ppermute | solution.py:43
  4.3 18.6 %collective-permute-start.3 = (f32[384,128]{1,0:T(8,128)}, f32[384,128]{1,0:T(8,128)S(1)}, u32[]{:S(2)}, u32[]{:S(2)}) collective-permute-start(f32[384,128]{1,0:T(8,128)} %get-tuple-element.58), channel_id=1, source_target_pairs={{0,1},{1,0},{2,3},{3,2},{4,5},{5,4},{6,7},{7,6},{8,9},{9,8},{10,11... | collective-permute-start | bytes 589832 | tf_op jit(solution)/shard_map/ppermute | solution.py:43
  4.8 19.0 %collective-permute-start.4 = (f32[384,256]{1,0:T(8,128)}, f32[384,256]{1,0:T(8,128)S(1)}, u32[]{:S(2)}, u32[]{:S(2)}) collective-permute-start(f32[384,256]{1,0:T(8,128)} %get-tuple-element.60), channel_id=1, source_target_pairs={{0,4},{8,12},{16,20},{24,28}} | collective-permute-start | bytes 1179656 | tf_op jit(solution)/shard_map/ppermute | solution.py:344
  7.3 11.1 %collective-permute-start.1 = (f32[8,128]{1,0:T(8,128)S(1)}, f32[8,128]{1,0:T(8,128)S(1)}, u32[]{:S(2)}, u32[]{:S(2)}) collective-permute-start(f32[8,128]{1,0:T(8,128)S(1)} %add.150), channel_id=1, source_target_pairs={{0,2},{1,3},{2,0},{3,1},{4,6},{5,7},{6,4},{7,5},{8,10},{9,11},{10,... | collective-permute-start | bytes 12296 | tf_op jit(solution)/shard_map/ppermute | solution.py:43
  18.3 4.5 %collective-permute-start.2 = (f32[8,128]{1,0:T(8,128)S(1)}, f32[8,128]{1,0:T(8,128)S(1)}, u32[]{:S(2)}, u32[]{:S(2)}) collective-permute-start(f32[8,128]{1,0:T(8,128)S(1)} %add.151), channel_id=1, source_target_pairs={{0,4},{1,5},{2,6},{3,7},{4,0},{5,1},{6,2},{7,3},{8,12},{9,13},{10,... | collective-permute-start | bytes 12296 | tf_op jit(solution)/shard_map/ppermute | solution.py:43
  22.8 8.6 %copy-start.5 = (f32[8,128]{1,0:T(8,128)}, f32[8,128]{1,0:T(8,128)S(1)}, u32[]{:S(2)}) copy-start(f32[8,128]{1,0:T(8,128)S(1)} %add.152.table_ref) | copy-start | bytes 12292
  27.4 6.7 %collective-permute-start.5 = (f32[384,128]{1,0:T(8,128)S(1)}, f32[384,128]{1,0:T(8,128)S(1)}, u32[]{:S(2)}, u32[]{:S(2)}) collective-permute-start(f32[384,128]{1,0:T(8,128)S(1)} %add.153), channel_id=1, source_target_pairs={{0,2},{1,3},{2,0},{3,1},{4,6},{5,7},{6,4},{7,5},{8,10},{9,11},{10,... | collective-permute-start | bytes 589832 | tf_op jit(solution)/shard_map/ppermute | solution.py:43
  27.4 6.7 %collective-permute-start.6 = (f32[384,128]{1,0:T(8,128)S(1)}, f32[384,128]{1,0:T(8,128)S(1)}, u32[]{:S(2)}, u32[]{:S(2)}) collective-permute-start(f32[384,128]{1,0:T(8,128)S(1)} %copy-done.4), channel_id=1, source_target_pairs={{0,1},{1,0},{2,3},{3,2},{4,5},{5,4},{6,7},{7,6},{8,9},{9,8},{10,11... | collective-permute-start | bytes 589832 | tf_op jit(solution)/shard_map/ppermute | solution.py:43
  34.2 15.9 %collective-permute-start.9 = (f32[384,256]{1,0:T(8,128)S(1)}, f32[384,256]{1,0:T(8,128)S(1)}, u32[]{:S(2)}, u32[]{:S(2)}) collective-permute-start(f32[384,256]{1,0:T(8,128)S(1)} %broadcast_select_fusion.10), channel_id=1, source_target_pairs={{0,1},{4,5},{8,9},{12,13},{16,17},{20,21},{24,25},{28,29}} | collective-permute-start | bytes 1179656 | tf_op jit(solution)/shard_map/ppermute | solution.py:344
  34.9 15.2 %collective-permute-start.10 = (f32[256,512]{1,0:T(8,128)}, f32[256,512]{1,0:T(8,128)S(1)}, u32[]{:S(2)}, u32[]{:S(2)}) collective-permute-start(f32[256,512]{1,0:T(8,128)} %first_rows.1), channel_id=1, source_target_pairs={{0,8},{8,0},{16,24},{24,16},{1,9},{9,1},{17,25},{25,17},{2,10},{10... | collective-permute-start | bytes 1572872 | tf_op jit(solution)/shard_map/ppermute | solution.py:43
  35.0 8.7 %collective-permute-start.7 = (f32[384,128]{1,0:T(8,128)S(1)}, f32[384,128]{1,0:T(8,128)S(1)}, u32[]{:S(2)}, u32[]{:S(2)}) collective-permute-start(f32[384,128]{1,0:T(8,128)S(1)} %add.156), channel_id=1, source_target_pairs={{0,4},{1,5},{2,6},{3,7},{4,0},{5,1},{6,2},{7,3},{8,12},{9,13},{10,... | collective-permute-start | bytes 589832 | tf_op jit(solution)/shard_map/ppermute | solution.py:43
  35.0 15.0 %collective-permute-start.8 = (f32[384,128]{1,0:T(8,128)S(1)}, f32[384,128]{1,0:T(8,128)S(1)}, u32[]{:S(2)}, u32[]{:S(2)}) collective-permute-start(f32[384,128]{1,0:T(8,128)S(1)} %add.157), channel_id=1, source_target_pairs={{0,2},{1,3},{2,0},{3,1},{4,6},{5,7},{6,4},{7,5},{8,10},{9,11},{10,... | collective-permute-start | bytes 589832 | tf_op jit(solution)/shard_map/ppermute | solution.py:43
  43.7 6.4 %copy-start.3 = (f32[256,512]{1,0:T(8,128)S(1)}, f32[256,512]{1,0:T(8,128)}, u32[]{:S(2)}) copy-start(f32[256,512]{1,0:T(8,128)} %first_rows.1) | copy-start | bytes 1572868
  50.2 13.9 %collective-permute-start.13 = (f32[384,256]{1,0:T(8,128)S(1)}, f32[384,256]{1,0:T(8,128)S(1)}, u32[]{:S(2)}, u32[]{:S(2)}) collective-permute-start(f32[384,256]{1,0:T(8,128)S(1)} %broadcast_select_fusion.9), channel_id=1, source_target_pairs={{0,2},{1,3},{4,6},{5,7},{8,10},{9,11},{12,14},{13,15},{16,18},{17,... | collective-permute-start | bytes 1179656 | tf_op jit(solution)/shard_map/ppermute | solution.py:344
  51.5 43.3 %collective-permute-start.19 = (f32[1024,512]{1,0:T(8,128)}, f32[1024,512]{1,0:T(8,128)}, u32[]{:S(2)}, u32[]{:S(2)}) collective-permute-start(f32[1024,512]{1,0:T(8,128)} %far_rows.1), channel_id=1, source_target_pairs={{0,8},{8,0},{16,24},{24,16},{1,9},{9,1},{17,25},{25,17},{2,10},{10... | collective-permute-start | bytes 6291464 | tf_op jit(solution)/shard_map/ppermute | solution.py:43
  51.6 14.3 %collective-permute-start.14 = (f32[256,512]{1,0:T(8,128)S(1)}, f32[256,512]{1,0:T(8,128)S(1)}, u32[]{:S(2)}, u32[]{:S(2)}) collective-permute-start(f32[256,512]{1,0:T(8,128)S(1)} %add.160), channel_id=1, source_target_pairs={{0,16},{8,24},{16,0},{24,8},{1,17},{9,25},{17,1},{25,9},{2,18},{10... | collective-permute-start | bytes 1572872 | tf_op jit(solution)/shard_map/ppermute | solution.py:43
  52.2 9.4 %collective-permute-start.12 = (f32[384,128]{1,0:T(8,128)S(1)}, f32[384,128]{1,0:T(8,128)S(1)}, u32[]{:S(2)}, u32[]{:S(2)}) collective-permute-start(f32[384,128]{1,0:T(8,128)S(1)} %add.159), channel_id=1, source_target_pairs={{0,4},{1,5},{2,6},{3,7},{4,0},{5,1},{6,2},{7,3},{8,12},{9,13},{10,... | collective-permute-start | bytes 589832 | tf_op jit(solution)/shard_map/ppermute | solution.py:43
  61.6 4.4 %copy-start.2 = (bf16[256,512]{1,0:T(8,128)(2,1)S(1)}, bf16[256,512]{1,0:T(8,128)(2,1)}, u32[]{:S(2)}) copy-start(bf16[256,512]{1,0:T(8,128)(2,1)} %get-tuple-element.78.p_ref) | copy-start | bytes 786436
  66.0 7.9 %collective-permute-start.15 = (bf16[256,512]{1,0:T(8,128)(2,1)S(1)}, bf16[256,512]{1,0:T(8,128)(2,1)S(1)}, u32[]{:S(2)}, u32[]{:S(2)}) collective-permute-start(bf16[256,512]{1,0:T(8,128)(2,1)S(1)} %copy-done.2), channel_id=1, source_target_pairs={{0,16},{8,24},{16,0},{24,8},{1,17},{9,25},{17,1},{25,9},{2,18},{10... | collective-permute-start | bytes 786440 | tf_op jit(solution)/shard_map/ppermute | solution.py:43
  74.0 2.0 collective-permute-start.16
  74.1 0.7 collective-permute-start.17
  76.1 10.4 %collective-permute-start.20 = (f32[256,256]{1,0:T(8,128)S(1)}, f32[256,256]{1,0:T(8,128)S(1)}, u32[]{:S(2)}, u32[]{:S(2)}) collective-permute-start(f32[256,256]{1,0:T(8,128)S(1)} %broadcast_select_fusion.13), channel_id=1, source_target_pairs={{0,1},{4,5},{8,9},{12,13},{16,17},{20,21},{24,25},{28,29}} | collective-permute-start | bytes 786440 | tf_op jit(solution)/shard_map/ppermute | solution.py:344
  84.5 10.3 %collective-permute-start.18 = (bf16[336,512]{1,0:T(8,128)(2,1)}, bf16[336,512]{1,0:T(8,128)(2,1)S(1)}, u32[]{:S(2)}, u32[]{:S(2)}) collective-permute-start(bf16[336,512]{1,0:T(8,128)(2,1)} %leaf_last.1), channel_id=1, source_target_pairs={{0,16},{8,24},{16,0},{24,8},{1,17},{9,25},{17,1},{25,9},{2,18},{10... | collective-permute-start | bytes 1032200 | tf_op jit(solution)/shard_map/ppermute | solution.py:43
  85.1 27.9 %collective-permute-start.22 = (bf16[1024,512]{1,0:T(8,128)(2,1)S(1)}, bf16[1024,512]{1,0:T(8,128)(2,1)S(1)}, u32[]{:S(2)}, u32[]{:S(2)}) collective-permute-start(bf16[1024,512]{1,0:T(8,128)(2,1)S(1)} %pad_maximum_fusion.1.d01_ref.refs_2_), channel_id=1, source_target_pairs={{0,4},{1,5},{10,14},{11,15},{20,16},{21,17},{30,26},{31,27}} | collective-permute-start | bytes 3145736 | tf_op jit(solution)/shard_map/ppermute | solution.py:466
  94.9 18.1 %collective-permute-start.23 = (f32[256,256]{1,0:T(8,128)S(1)}, f32[256,256]{1,0:T(8,128)S(1)}, u32[]{:S(2)}, u32[]{:S(2)}) collective-permute-start(f32[256,256]{1,0:T(8,128)S(1)} %broadcast_select_fusion.12), channel_id=1, source_target_pairs={{0,2},{1,3},{4,6},{5,7},{8,10},{9,11},{12,14},{13,15},{16,18},{17,... | collective-permute-start | bytes 786440 | tf_op jit(solution)/shard_map/ppermute | solution.py:344
  98.0 16.0 %collective-permute-start.21 = (bf16[672,512]{1,0:T(8,128)(2,1)}, bf16[672,512]{1,0:T(8,128)(2,1)}, u32[]{:S(2)}, u32[]{:S(2)}) collective-permute-start(bf16[672,512]{1,0:T(8,128)(2,1)} %pad_maximum_fusion.2), channel_id=1, source_target_pairs={{0,8},{8,0},{16,24},{24,16},{1,9},{9,1},{17,25},{25,17},{2,10},{10... | collective-permute-start | bytes 2064392 | tf_op jit(solution)/shard_map/ppermute | solution.py:43
  98.7 66.7 %collective-permute-start.11 = (f32[1024,512]{1,0:T(8,128)}, f32[1024,512]{1,0:T(8,128)}, u32[]{:S(2)}, u32[]{:S(2)}) collective-permute-start(f32[1024,512]{1,0:T(8,128)} %near_rows.1), channel_id=1, source_target_pairs={{0,8},{8,0},{16,24},{24,16},{1,9},{9,1},{17,25},{25,17},{2,10},{10... | collective-permute-start | bytes 6291464 | tf_op jit(solution)/shard_map/ppermute | solution.py:43
  102.6 11.5 %copy-start.1 = (bf16[336,512]{1,0:T(8,128)(2,1)S(1)}, bf16[336,512]{1,0:T(8,128)(2,1)}, u32[]{:S(2)}) copy-start(bf16[336,512]{1,0:T(8,128)(2,1)} %leaf_last.1) | copy-start | bytes 1032196
  115.3 27.1 %collective-permute-start.27 = (bf16[1024,512]{1,0:T(8,128)(2,1)}, bf16[1024,512]{1,0:T(8,128)(2,1)}, u32[]{:S(2)}, u32[]{:S(2)}) collective-permute-start(bf16[1024,512]{1,0:T(8,128)(2,1)} %broadcast_select_fusion.2), channel_id=1, source_target_pairs={{0,2},{1,3},{4,6},{5,7},{10,8},{11,9},{14,12},{15,13},{20,22},{21,... | collective-permute-start | bytes 3145736 | tf_op jit(solution)/shard_map/ppermute | solution.py:466
  125.6 10.7 %collective-permute-start.24 = (bf16[256,512]{1,0:T(8,128)(2,1)S(1)}, bf16[256,512]{1,0:T(8,128)(2,1)S(1)}, u32[]{:S(2)}, u32[]{:S(2)}) collective-permute-start(bf16[256,512]{1,0:T(8,128)(2,1)S(1)} %get-tuple-element.96.refs_4_), channel_id=1, source_target_pairs={{0,4},{1,5},{10,14},{11,15},{20,16},{21,17},{30,26},{31,27}} | collective-permute-start | bytes 786440 | tf_op jit(solution)/shard_map/ppermute | solution.py:466
  126.3 15.0 %collective-permute-start.25 = (bf16[512,512]{1,0:T(8,128)(2,1)S(1)}, bf16[512,512]{1,0:T(8,128)(2,1)S(1)}, u32[]{:S(2)}, u32[]{:S(2)}) collective-permute-start(bf16[512,512]{1,0:T(8,128)(2,1)S(1)} %bitcast.27), channel_id=1, source_target_pairs={{0,4},{1,5},{10,14},{11,15},{20,16},{21,17},{30,26},{31,27}} | collective-permute-start | bytes 1572872 | tf_op jit(solution)/shard_map/ppermute | solution.py:466
  127.0 33.7 %collective-permute-start.26 = (f32[512,512]{1,0:T(8,128)}, f32[512,512]{1,0:T(8,128)}, u32[]{:S(2)}, u32[]{:S(2)}) collective-permute-start(f32[512,512]{1,0:T(8,128)} %far_sum.2), channel_id=1, source_target_pairs={{0,16},{8,24},{16,0},{24,8},{1,17},{9,25},{17,1},{25,9},{2,18},{10... | collective-permute-start | bytes 3145736 | tf_op jit(solution)/shard_map/ppermute | solution.py:43
  136.4 24.4 %collective-permute-start.28 = (bf16[1024,512]{1,0:T(8,128)(2,1)}, bf16[1024,512]{1,0:T(8,128)(2,1)}, u32[]{:S(2)}, u32[]{:S(2)}) collective-permute-start(bf16[1024,512]{1,0:T(8,128)(2,1)} %broadcast_select_fusion.2), channel_id=1, source_target_pairs={{0,1},{1,0},{4,5},{5,4},{10,11},{11,10},{14,15},{15,14},{20,21},{2... | collective-permute-start | bytes 3145736 | tf_op jit(solution)/shard_map/ppermute | solution.py:478
  141.4 43.1 %collective-permute-start.29 = (f32[512,512]{1,0:T(8,128)}, f32[512,512]{1,0:T(8,128)}, u32[]{:S(2)}, u32[]{:S(2)}) collective-permute-start(f32[512,512]{1,0:T(8,128)} %far_sum.3), channel_id=1, source_target_pairs={{0,16},{8,24},{16,0},{24,8},{1,17},{9,25},{17,1},{25,9},{2,18},{10... | collective-permute-start | bytes 3145736 | tf_op jit(solution)/shard_map/ppermute | solution.py:43
  160.7 20.8 %collective-permute-start.31 = (bf16[512,512]{1,0:T(8,128)(2,1)}, bf16[512,512]{1,0:T(8,128)(2,1)}, u32[]{:S(2)}, u32[]{:S(2)}) collective-permute-start(bf16[512,512]{1,0:T(8,128)(2,1)} %broadcast_select_fusion.5), channel_id=1, source_target_pairs={{0,2},{1,3},{4,6},{5,7},{10,8},{11,9},{14,12},{15,13},{20,22},{21,... | collective-permute-start | bytes 1572872 | tf_op jit(solution)/shard_map/ppermute | solution.py:466
  162.1 27.7 %collective-permute-start.34 = (bf16[256,512]{1,0:T(8,128)(2,1)S(1)}, bf16[256,512]{1,0:T(8,128)(2,1)S(1)}, u32[]{:S(2)}, u32[]{:S(2)}) collective-permute-start(bf16[256,512]{1,0:T(8,128)(2,1)S(1)} %broadcast_select_fusion.7), channel_id=1, source_target_pairs={{0,2},{1,3},{4,6},{5,7},{10,8},{11,9},{14,12},{15,13},{20,22},{21,... | collective-permute-start | bytes 786440 | tf_op jit(solution)/shard_map/ppermute | solution.py:466
  163.4 33.4 %collective-permute-start.30 = (bf16[1024,512]{1,0:T(8,128)(2,1)}, bf16[1024,512]{1,0:T(8,128)(2,1)}, u32[]{:S(2)}, u32[]{:S(2)}) collective-permute-start(bf16[1024,512]{1,0:T(8,128)(2,1)} %collective-permute-done.27), channel_id=1, source_target_pairs={{2,3},{3,2},{6,7},{7,6},{8,9},{9,8},{12,13},{13,12},{22,23},{23,22... | collective-permute-start | bytes 3145736 | tf_op jit(solution)/shard_map/ppermute | solution.py:478
  165.4 27.4 %collective-permute-start.33 = (bf16[512,512]{1,0:T(8,128)(2,1)}, bf16[512,512]{1,0:T(8,128)(2,1)}, u32[]{:S(2)}, u32[]{:S(2)}) collective-permute-start(bf16[512,512]{1,0:T(8,128)(2,1)} %broadcast_select_fusion.5), channel_id=1, source_target_pairs={{0,1},{1,0},{4,5},{5,4},{10,11},{11,10},{14,15},{15,14},{20,21},{2... | collective-permute-start | bytes 1572872 | tf_op jit(solution)/shard_map/ppermute | solution.py:478
  181.5 14.2 %collective-permute-start.32 = (bf16[512,512]{1,0:T(8,128)(2,1)}, bf16[512,512]{1,0:T(8,128)(2,1)}, u32[]{:S(2)}, u32[]{:S(2)}) collective-permute-start(bf16[512,512]{1,0:T(8,128)(2,1)} %collective-permute-done.31), channel_id=1, source_target_pairs={{2,3},{3,2},{6,7},{7,6},{8,9},{9,8},{12,13},{13,12},{22,23},{23,22... | collective-permute-start | bytes 1572872 | tf_op jit(solution)/shard_map/ppermute | solution.py:478
  189.8 15.3 %collective-permute-start.35 = (bf16[256,512]{1,0:T(8,128)(2,1)S(1)}, bf16[256,512]{1,0:T(8,128)(2,1)S(1)}, u32[]{:S(2)}, u32[]{:S(2)}) collective-permute-start(bf16[256,512]{1,0:T(8,128)(2,1)S(1)} %broadcast_select_fusion.6.refs_5_), channel_id=1, source_target_pairs={{0,1},{1,0},{4,5},{5,4},{2,3},{3,2},{6,7},{7,6},{10,11},{11,10},{1... | collective-permute-start | bytes 786440 | tf_op jit(solution)/shard_map/ppermute | solution.py:478
  205.1 1.6 copy-start

commit v7 on v6

--- a/solution.py
+++ b/solution.py
@@ -266,41 +266,39 @@
 
 
 def update_kernel(slots, *refs):
-    place_ref, base_ref, d01_ref, d2_ref = refs[:4]
-    r01, r2 = refs[4 : 4 + slots], refs[4 + slots : 4 + 2 * slots]
-    inv0_ref, inv1_ref, x_ref, out_ref, panel_ref = refs[4 + 2 * slots :]
-    b = inv0_ref.shape[0]
-    cols = out_ref.shape[1]
+    place_ref, base_ref, d01_ref = refs[:3]
+    r01, out_ref = refs[3 : 3 + slots], refs[3 + slots]
 
     def at_slot(i):
-        total = base_ref[...] - tdot(r01[i][...], d01_ref[...]) - tdot(r2[i][...], d2_ref[...])
-        out_ref[...] = total
-        if cols >= PR * b:
-            q0 = mm_t(total[:, :b], inv0_ref[...])
-            inside = jnp.dot(q0.astype(bf16), x_ref[...], preferred_element_type=f32)
-            panel_ref[:, :b] = q0
-            panel_ref[:, b:] = mm_t(total[:, b : PR * b] - inside, inv1_ref[...])
-        else:
-            panel_ref[...] = jnp.zeros_like(panel_ref)
+        out_ref[...] = base_ref[...] - tdot(r01[i][...], d01_ref[...])
 
     for i in range(slots):
         pl.when(pl.program_id(0) == i)(lambda i=i: at_slot(i))
 
 
-def finish_kernel(slots, *refs):
-    place_ref, info_ref, part_ref, panel_ref, q_ref = refs[:5]
-    rq, out_ref = refs[5 : 5 + slots], refs[5 + slots]
+def finish_kernel(slots, whole_panel, *refs):
+    place_ref, info_ref, part_ref = refs[:3]
+    d2_ref, q_ref, inv0_ref, inv1_ref, x_ref, panel_ref = refs[3:9]
+    r2, rq = refs[9 : 9 + slots], refs[9 + slots : 9 + 2 * slots]
+    out_ref = refs[9 + 2 * slots]
     rows, cols = out_ref.shape
     wide = q_ref.shape[0]
     b = wide // PR
 
     def at_slot(i):
+        total = part_ref[...] - tdot(r2[i][...], d2_ref[...])
         row = info_ref[i] + lax.broadcasted_iota(jnp.int32, (rows, cols), 0)
-        total = part_ref[...] - tdot(rq[i][...], q_ref[...])
+        width = min(wide, cols)
+        if whole_panel:
+            q0 = mm_t(total[:, :b], inv0_ref[...])
+            x_part = jnp.dot(q0.astype(bf16), x_ref[...], preferred_element_type=f32)
+            q1 = mm_t(total[:, b:wide] - x_part, inv1_ref[...])
+            panel = jnp.concatenate([q0, q1], axis=1)
+        else:
+            panel = panel_ref[pl.ds(pl.multiple_of(i * rows, rows), rows), :]
+        total = total - tdot(rq[i][...], q_ref[...])
         total = jnp.where(row >= wide, total, 0.0)
-        width = min(wide, cols)
         col = info_ref[slots] + lax.broadcasted_iota(jnp.int32, (rows, width), 1)
-        panel = panel_ref[...]
         panel = jnp.where((row[:, :width] >= b) | (col < b), panel, 0.0)
         out_ref[:, :width] = jnp.where(col < wide, panel, total[:, :width])
         if width < cols:
@@ -424,7 +422,8 @@
         name="leaf_two",
     )(head, front, front, mask)
 
-    p01, rest, w_lead, first = tie((p01, rest, w_lead, first))
+    p01, rest, w_lead, first, diagonal = tie((p01, rest, w_lead, first, diagonal))
+    far_near = flip(rows_at(n, ways, [(diagonal, 0, 0)], "far_sum"), "grp", CHIP)
 
     def across(value):
         far_value = flip(value, "grp", CHIP)
@@ -493,8 +492,10 @@
 
     s01 = zone_hop(([0], d01, None))
     pack_far = flip(pack, "grp", CHIP)
-    pack, pack_far, diagonal, corner = tie((pack, pack_far, diagonal, corner))
-    far_in = rows_at(n, ways, [(diagonal, 0, 0)], "far_sum")
+    pack, pack_far, diagonal, corner, far_near = tie(
+        (pack, pack_far, diagonal, corner, far_near)
+    )
+    far_in = rows_at(n + ways, ways, [(diagonal, 0, 1)], "far_sum")
     for at in range(2, last + 1):
         corner = lead_hop(corner, at)
     pack = jnp.concatenate([pack, pack_far], axis=0)
@@ -502,7 +503,7 @@
     pack, held, far_in, corner = tie((pack, s01[1], far_in, corner))
     corner = corner[0] if leads == 1 else jnp.concatenate(corner, axis=1)
     s01 = (s01[0], held, None)
-    far = [flip(far_in, "grp", CHIP)]
+    far_last = flip(far_in, "grp", CHIP)
     early01 = early_hops(s01)
     s01 = zone_hop(s01)
     d2 = pack.reshape(groups, b + lead_rows, cols)[:, :b].reshape(groups * b, cols)
@@ -516,24 +517,20 @@
         compiler_params=pltpu.CompilerParams(vmem_limit_bytes=32 << 20),
         name="root_step",
     )(leaves, corner, first, d01, pack)
-    q, diagonal = tie((q, diagonal))
     sq_hop = zone_hop(([0], q, None))
-    far_in = rows_at(n + ways, ways, [(diagonal, 0, 1)], "far_sum")
-    far.append(flip(far_in, "grp", CHIP))
-    q_held, held, far[0], s01_held, s01_got, *early01 = tie(
-        (sq_hop[1], s2[1], far[0], s01[1], s01[2][1], *early01)
-    )
+    q_held, held, s01_held, s01_got = tie((sq_hop[1], s2[1], s01[1], s01[2][1]))
     s01 = (s01[0], s01_held, (s01[2][0], s01_got))
     s2 = (s2[0], held, None)
-    rq = inner_hops(zone_hop((sq_hop[0], q_held, None)))
+    sq_hop = zone_hop((sq_hop[0], q_held, None))
     early2 = early_hops(s2)
     s2 = zone_hop(s2)
+    q_held, far_last, *early01 = tie((sq_hop[1], far_last, *early01))
+    rq = inner_hops((sq_hop[0], q_held, None))
     r01 = inner_hops(s01, early01)
     r2 = inner_hops(s2, early2)
 
-    base = rows_at(
-        3 * n, n, [(root_front, 0, 0), (near, 0, 0), (far[0], 0, 0), (far[1], 1, 0)], "base_rows"
-    )
+    adds = [(root_front, 0, 0), (near, 0, 0), (far_near, 0, 0), (far_last, 1, 0)]
+    base = rows_at(3 * n, n, adds, "base_rows")
     slot_of = inner ^ jnp.arange(spread, dtype=jnp.int32)
 
     def update_body(*refs):
@@ -542,49 +539,44 @@
     def whole_spec(array):
         return pl.BlockSpec(array.shape, lambda s, *pre: (0, 0))
 
-    fixed = [d01, d2] + r01 + r2 + [rinv0, rinv1, rx]
-    part, panel = pl.pallas_call(
+    part = pl.pallas_call(
         update_body,
         grid_spec=pltpu.PrefetchScalarGridSpec(
             num_scalar_prefetch=1,
             grid=(spread,),
             in_specs=[pl.BlockSpec((cols, cols), lambda s, place: (place[s], 0))]
-            + [whole_spec(array) for array in fixed],
-            out_specs=[
-                pl.BlockSpec((cols, cols), lambda s, place: (s, 0)),
-                pl.BlockSpec((cols, lead_cols if leads > 1 else pr), lambda s, place: (s, 0)),
-            ],
+            + [whole_spec(array) for array in [d01] + r01],
+            out_specs=pl.BlockSpec((cols, cols), lambda s, place: (s, 0)),
         ),
-        out_shape=(shape((quarter, cols), f32), shape((quarter, lead_cols), f32)),
-        compiler_params=pltpu.CompilerParams(vmem_limit_bytes=48 << 20),
+        out_shape=shape((quarter, cols), f32),
+        compiler_params=pltpu.CompilerParams(vmem_limit_bytes=40 << 20),
         name="update",
-    )(slot_of, base, *fixed)
+    )(slot_of, base, d01, *r01)
     if leads > 1:
         first_col = jnp.minimum(m, leads - 1) * lead_cols
         panel = jnp.concatenate([rows.astype(f32).T for rows in rq], axis=0)
         panel = lax.dynamic_slice_in_dim(panel, first_col, lead_cols, 1)
+    else:
+        panel = jnp.zeros((8, lead_cols), f32)
     info = jnp.concatenate([g * quarter + slot_of * cols, (m * cols).reshape(1)])
 
     def finish_body(*refs):
-        finish_kernel(spread, *refs)
-
+        finish_kernel(spread, leads == 1, *refs)
+
+    fixed = [d2, q, rinv0, rinv1, rx, panel] + r2 + rq
     root_factor = pl.pallas_call(
         finish_body,
         grid_spec=pltpu.PrefetchScalarGridSpec(
             num_scalar_prefetch=2,
             grid=(spread,),
-            in_specs=[
-                pl.BlockSpec((cols, cols), lambda s, place, info: (s, 0)),
-                pl.BlockSpec((cols, lead_cols), lambda s, place, info: (s, 0)),
-                whole_spec(q),
-            ]
-            + [whole_spec(rows) for rows in rq],
+            in_specs=[pl.BlockSpec((cols, cols), lambda s, place, info: (s, 0))]
+            + [whole_spec(array) for array in fixed],
             out_specs=pl.BlockSpec((cols, cols), lambda s, place, info: (place[s], 0)),
         ),
         out_shape=shape((quarter, cols), f32),
-        compiler_params=pltpu.CompilerParams(vmem_limit_bytes=32 << 20),
+        compiler_params=pltpu.CompilerParams(vmem_limit_bytes=40 << 20),
         name="finish",
-    )(slot_of, info, part, panel, q, *rq)
+    )(slot_of, info, part, *fixed)
     return root_factor, logs_out[0, : groups + 1]
 
 

time: 210 us -> 202 us (0.962)
  the two profiles are of different devices: /device:TPU:10 before, /device:TPU:1 now
where the time goes in v7:
time: 202 us; the launch traced here: 200 us
  waiting for transfers between devices  62 us (31%)
  starting transfers between devices  57.4 us (28%)
  Pallas kernels  56.6 us (28%)
  other arithmetic  16.6 us (8%)
  local copies, waits for them, and re-layouts  5.95 us (3%)
    ppermute x19, waiting for transfers between devices, flip(): return lax.ppermute(value, axis, [(i, i ^ bit) for i in range(size)])  37 us
    ppermute x19, starting transfers between devices, flip(): return lax.ppermute(value, axis, [(i, i ^ bit) for i in range(size)])  23.1 us
    pallas_call x6, Pallas kernels, take_rows(): pl.pallas_call(body, grid_spec=pltpu.PrefetchScalarGridSpec(num_scalar_pr...  21.5 us
    ppermute x6, starting transfers between devices, lead_hop(): got = lax.ppermute(held, 'mem', [(src, src ^ bit) for src in sources])  18.7 us
    ppermute x6, waiting for transfers between devices, zone_hop(): got = lax.ppermute(held, ('grp', 'mem'), pairs)  11.9 us
    ppermute x5, waiting for transfers between devices, inner_hop(): return lax.ppermute(value, ('grp', 'mem'), pairs)  11.4 us
    pallas_call x1, Pallas kernels, local(): pl.pallas_call(leaf_two, grid=(1,), in_specs=[vmem, w_spec(0), w_spec(1),...  9.43 us
    pallas_call x1, Pallas kernels, local(): pl.pallas_call(root_step, in_specs=[smem] + [vmem] * 4, out_shape=(shape(...  8.95 us
  transfers between devices with their start and end apart: 36, of which 12 were waited for; matrix products, arithmetic and copies ran while one was open for 9% of the time, Pallas kernels for 25%

profile of v7, /device:TPU:1, one launch (start us, length us, event | category | flops | bytes accessed | tf_op | source)
XLA Modules:
  0.0 199.7 jit_solution(3817139470077063479)
XLA Ops:
  0.6 2.1 %pick_pivots.1 = (f32[8,128]{1,0:T(8,128)}, f32[384,128]{1,0:T(8,128)}, f32[384,128]{1,0:T(8,128)}, f32[8,512]{1,0:T(8,128)}, f32[384,256]{1,0:T(8,128)}) custom-call(s32[4]{0:T(128)} %bitcast.55, s32[1]{0:T(128)} %bitcast.2.at_ref, f32[4096,512]{1,0:T(8,128)} %bitcast.29), custom_call_target="tpu_custom_call" | custom-call | tf_op jit(solution)/shard_map/pick_pivots/pallas_call | solution.py:346
  2.7 2.1 %collective-permute-start = (f32[8,128]{1,0:T(8,128)}, f32[8,128]{1,0:T(8,128)S(1)}, u32[]{:S(2)}, u32[]{:S(2)}) collective-permute-start(f32[8,128]{1,0:T(8,128)} %get-tuple-element.56), channel_id=1, source_target_pairs={{0,1},{1,0},{2,3},{3,2},{4,5},{5,4},{6,7},{7,6},{8,9},{9,8},{10,11... | collective-permute-start | bytes 12296 | tf_op jit(solution)/shard_map/ppermute | solution.py:43
  4.9 4.4 %collective-permute-start.4 = (f32[384,256]{1,0:T(8,128)}, f32[384,256]{1,0:T(8,128)S(1)}, u32[]{:S(2)}, u32[]{:S(2)}) collective-permute-start(f32[384,256]{1,0:T(8,128)} %get-tuple-element.59), channel_id=1, source_target_pairs={{0,4},{8,12},{16,20},{24,28}} | collective-permute-start | bytes 1179656 | tf_op jit(solution)/shard_map/ppermute | solution.py:342
  10.1 6.6 %collective-permute-done.1 = f32[8,128]{1,0:T(8,128)S(1)} collective-permute-done((f32[8,128]{1,0:T(8,128)S(1)}, f32[8,128]{1,0:T(8,128)S(1)}, u32[]{:S(2)}, u32[]{:S(2)}) %collective-permute-start.1) | collective-permute-done | bytes 4128 | tf_op jit(solution)/shard_map/ppermute | solution.py:43
  16.8 3.2 %collective-permute-done.2 = f32[8,128]{1,0:T(8,128)S(1)} collective-permute-done((f32[8,128]{1,0:T(8,128)S(1)}, f32[8,128]{1,0:T(8,128)S(1)}, u32[]{:S(2)}, u32[]{:S(2)}) %collective-permute-start.2) | collective-permute-done | bytes 4128 | tf_op jit(solution)/shard_map/ppermute | solution.py:43
  24.2 1.9 collective-permute-start.5
  27.4 3.3 %far_rows.1 = f32[1024,512]{1,0:T(8,128)} custom-call(s32[8]{0:T(128)} %get-tuple-element.120.refs_0_, s32[8]{0:T(128)} %get-tuple-element.117.refs_1_, s32[1]{0:T(128)} %constant.64.clone.1.refs_2_, f32[4096,512]{1,0:T(8,128)} %bitcast.30, f32[4096,512]{1,0:T(8,128)} %bitcast.31, f32[4096,512]{1,0:T(8,128)} %bitcast.32, f32[4096,512]{1,0:T(8,128)} %bitcast.33, ...), custom_call_target="tpu_custom_call" | custom-call | tf_op jit(solution)/shard_map/far_rows/pallas_call | solution.py:214
  30.7 2.8 %first_rows.1 = f32[256,512]{1,0:T(8,128)} custom-call(s32[2]{0:T(128)} %slice.53.refs_0_, s32[2]{0:T(128)} %slice.54.refs_1_, s32[1]{0:T(128)} %bitcast.10.refs_2_, f32[4096,512]{1,0:T(8,128)} %bitcast.34, f32[4096,512]{1,0:T(8,128)} %bitcast.35, f32[8,512]{1,0:T(8,128)} %get-tuple-element.61.refs_7_.refs_5_.mask_ref, f32[1024,512]{1,0:T(8,128)} %refs_8_.1), custom_call_target="tpu_custom_call" | custom-call | tf_op jit(solution)/shard_map/first_rows/pallas_call | solution.py:214
  33.5 3.4 %collective-permute-start.9 = (f32[384,256]{1,0:T(8,128)S(1)}, f32[384,256]{1,0:T(8,128)S(1)}, u32[]{:S(2)}, u32[]{:S(2)}) collective-permute-start(f32[384,256]{1,0:T(8,128)S(1)} %broadcast_select_fusion.10), channel_id=1, source_target_pairs={{0,1},{4,5},{8,9},{12,13},{16,17},{20,21},{24,25},{28,29}} | collective-permute-start | bytes 1179656 | tf_op jit(solution)/shard_map/ppermute | solution.py:342
  36.9 4.6 %collective-permute-start.10 = (f32[256,512]{1,0:T(8,128)}, f32[256,512]{1,0:T(8,128)S(1)}, u32[]{:S(2)}, u32[]{:S(2)}) collective-permute-start(f32[256,512]{1,0:T(8,128)} %first_rows.1), channel_id=1, source_target_pairs={{0,8},{8,0},{16,24},{24,16},{1,9},{9,1},{17,25},{25,17},{2,10},{10... | collective-permute-start | bytes 1572872 | tf_op jit(solution)/shard_map/ppermute | solution.py:43
  41.5 3.3 %near_rows.1 = f32[1024,512]{1,0:T(8,128)} custom-call(s32[8]{0:T(128)} %get-tuple-element.119.refs_0_, s32[8]{0:T(128)} %get-tuple-element.116.refs_1_, s32[1]{0:T(128)} %constant.64.clone.1.refs_2_, f32[4096,512]{1,0:T(8,128)} %bitcast.36, f32[4096,512]{1,0:T(8,128)} %bitcast.37, f32[4096,512]{1,0:T(8,128)} %bitcast.38, f32[4096,512]{1,0:T(8,128)} %bitcast.39, ...), custom_call_target="tpu_custom_call" | custom-call | tf_op jit(solution)/shard_map/near_rows/pallas_call | solution.py:214
  44.8 4.8 %collective-permute-done.7 = f32[384,128]{1,0:T(8,128)S(1)} collective-permute-done((f32[384,128]{1,0:T(8,128)S(1)}, f32[384,128]{1,0:T(8,128)S(1)}, u32[]{:S(2)}, u32[]{:S(2)}) %collective-permute-start.7) | collective-permute-done | bytes 196640 | tf_op jit(solution)/shard_map/ppermute | solution.py:43
  50.3 1.7 collective-permute-done.8
  53.3 1.9 collective-permute-start.13
  55.2 1.3 collective-permute-start.14
  56.5 9.4 %leaf_two.1 = (bf16[256,512]{1,0:T(8,128)(2,1)}, f32[128,128]{1,0:T(8,128)}, f32[128,128]{1,0:T(8,128)}, bf16[128,128]{1,0:T(8,128)(2,1)}, f32[8,128]{1,0:T(8,128)}) custom-call(f32[384,128]{1,0:T(8,128)} %add.158.head_ref, f32[4096,512]{1,0:T(8,128)} %bitcast.41, f32[4096,512]{1,0:T(8,128)} %bitcast.40, f32[8,512]{1,0:T(8,128)} %get-tuple-element.61.refs_7_.refs_5_.mask_ref), custom_call_target="tpu_custom_call" | custom-call | tf_op jit(solution)/shard_map/leaf_two/pallas_call | solution.py:415
  65.9 2.0 collective-permute-done.12
  69.5 1.3 collective-permute-start.16
  71.4 5.0 %collective-permute-start.18 = (f32[256,256]{1,0:T(8,128)S(1)}, f32[256,256]{1,0:T(8,128)S(1)}, u32[]{:S(2)}, u32[]{:S(2)}) collective-permute-start(f32[256,256]{1,0:T(8,128)S(1)} %slice.57), channel_id=1, source_target_pairs={{0,4},{8,12},{16,20},{24,28}} | collective-permute-start | bytes 786440 | tf_op jit(solution)/shard_map/ppermute | solution.py:342
  76.7 1.8 collective-permute-start.17
  79.1 3.3 %far_sum.2 = f32[512,512]{1,0:T(8,128)} custom-call(s32[4]{0:T(128)} %get-tuple-element.115.refs_0_, s32[4]{0:T(128)} %get-tuple-element.113.refs_1_, s32[1]{0:T(128)} %constant.64.clone.1.refs_2_, f32[4096,512]{1,0:T(8,128)} %bitcast.42, f32[4096,512]{1,0:T(8,128)} %bitcast.43, f32[4096,512]{1,0:T(8,128)} %bitcast.44, f32[4096,512]{1,0:T(8,128)} %bitcast.45, ...), custom_call_target="tpu_custom_call" | custom-call | tf_op jit(solution)/shard_map/far_sum/pallas_call | solution.py:214
  82.4 1.2 collective-permute-start.21
  84.8 2.0 collective-permute-start.20
  86.8 7.6 %leaf_last.1 = bf16[336,512]{1,0:T(8,128)(2,1)} custom-call(f32[384,128]{1,0:T(8,128)} %add.161.rest_ref, f32[4096,512]{1,0:T(8,128)} %bitcast.46, f32[384,256]{1,0:T(8,128)} %broadcast_select_fusion.8.w_lead_ref, f32[8,128]{1,0:T(8,128)} %copy-done.9, f32[8,512]{1,0:T(8,128)} %get-tuple-element.61.refs_7_.refs_5_.mask_ref, ...), custom_call_target="tpu_custom_call" | custom-call | tf_op jit(solution)/shard_map/leaf_last/pallas_call | solution.py:439
  94.6 1.6 collective-permute-start.23
  96.3 11.1 %collective-permute-done.21.refs_10_ = f32[512,512]{1,0:T(8,128)S(1)} collective-permute-done((f32[512,512]{1,0:T(8,128)}, f32[512,512]{1,0:T(8,128)S(1)}, u32[]{:S(2)}, u32[]{:S(2)}) %collective-permute-start.21) | collective-permute-done | bytes 1048608 | tf_op jit(solution)/shard_map/ppermute | solution.py:43
  107.4 7.4 %collective-permute-done.19 = bf16[336,512]{1,0:T(8,128)(2,1)S(1)} collective-permute-done((bf16[336,512]{1,0:T(8,128)(2,1)}, bf16[336,512]{1,0:T(8,128)(2,1)S(1)}, u32[]{:S(2)}, u32[]{:S(2)}) %collective-permute-start.19) | collective-permute-done | bytes 344096 | tf_op jit(solution)/shard_map/ppermute | solution.py:43
  114.8 1.9 pad_maximum_fusion.2
  117.4 2.0 collective-permute-start.24
  119.4 3.4 %far_sum.3 = f32[512,512]{1,0:T(8,128)} custom-call(s32[4]{0:T(128)} %get-tuple-element.114.refs_0_, s32[4]{0:T(128)} %get-tuple-element.112.refs_1_, s32[1]{0:T(128)} %constant.64.clone.1.refs_2_, f32[4096,512]{1,0:T(8,128)} %bitcast.47, f32[4096,512]{1,0:T(8,128)} %bitcast.48, f32[4096,512]{1,0:T(8,128)} %bitcast.49, f32[4096,512]{1,0:T(8,128)} %bitcast.50, ...), custom_call_target="tpu_custom_call" | custom-call | tf_op jit(solution)/shard_map/far_sum/pallas_call | solution.py:214
  122.9 1.8 collective-permute-done.24
  127.0 1.3 collective-permute-start.27
  128.3 5.7 %collective-permute-start.11 = (f32[1024,512]{1,0:T(8,128)}, f32[1024,512]{1,0:T(8,128)}, u32[]{:S(2)}, u32[]{:S(2)}) collective-permute-start(f32[1024,512]{1,0:T(8,128)} %near_rows.1), channel_id=1, source_target_pairs={{0,8},{8,0},{16,24},{24,16},{1,9},{9,1},{17,25},{25,17},{2,10},{10... | collective-permute-start | bytes 6291464 | tf_op jit(solution)/shard_map/ppermute | solution.py:43
  134.1 1.5 collective-permute-start.26
  135.6 9.0 %root_step.1 = (bf16[256,512]{1,0:T(8,128)(2,1)S(1)}, f32[128,128]{1,0:T(8,128)S(1)}, f32[128,128]{1,0:T(8,128)S(1)}, bf16[128,128]{1,0:T(8,128)(2,1)S(1)}, f32[8,128]{1,0:T(8,128)S(1)}) custom-call(s32[4]{0:T(128)S(1)} %pad_add_fusion.1.leaf_ref, f32[256,256]{1,0:T(8,128)S(1)} %broadcast_select_fusion.11.corner_ref, f32[256,512]{1,0:T(8,128)S(1)} %add.162.first_ref, ...), custom_call_target="tpu_custom_call" | custom-call | tf_op jit(solution)/shard_map/root_step/pallas_call | solution.py:512
  145.9 1.6 collective-permute-start.30
  149.7 1.3 broadcast_select_fusion.1.refs_3_
  151.1 1.3 collective-permute-start.28
  152.4 1.9 collective-permute-start.31
  154.3 11.0 %collective-permute-done.28 = bf16[256,512]{1,0:T(8,128)(2,1)} collective-permute-done((bf16[256,512]{1,0:T(8,128)(2,1)S(1)}, bf16[256,512]{1,0:T(8,128)(2,1)}, u32[]{:S(2)}, u32[]{:S(2)}) %collective-permute-start.28) | collective-permute-done | bytes 262176 | tf_op jit(solution)/shard_map/ppermute | solution.py:465
  165.3 1.3 collective-permute-start.32
  168.2 1.5 collective-permute-start.34
  169.7 5.4 %base_rows.1.refs_1_ = f32[1024,512]{1,0:T(8,128)} custom-call(s32[8]{0:T(128)} %get-tuple-element.121.refs_0_, s32[8]{0:T(128)} %get-tuple-element.118.refs_1_, s32[1]{0:T(128)} %constant.64.clone.1.refs_2_, f32[4096,512]{1,0:T(8,128)} %bitcast.51, f32[4096,512]{1,0:T(8,128)} %bitcast.52, f32[4096,512]{1,0:T(8,128)} %bitcast.53, f32[4096,512]{1,0:T(8,128)} %bitcast.54, ...), custom_call_target="tpu_custom_call" | custom-call | tf_op jit(solution)/shard_map/base_rows/pallas_call | solution.py:214
  175.9 2.9 %collective-permute-start.33 = (bf16[512,512]{1,0:T(8,128)(2,1)}, bf16[512,512]{1,0:T(8,128)(2,1)S(1)}, u32[]{:S(2)}, u32[]{:S(2)}) collective-permute-start(bf16[512,512]{1,0:T(8,128)(2,1)} %collective-permute-done.32), channel_id=1, source_target_pairs={{2,3},{3,2},{6,7},{7,6},{8,9},{9,8},{12,13},{13,12},{22,23},{23,22... | collective-permute-start | bytes 1572872 | tf_op jit(solution)/shard_map/ppermute | solution.py:477
  179.9 1.3 broadcast_select_fusion.refs_4_
  181.3 2.1 %update.1.refs_2_ = f32[1024,512]{1,0:T(8,128)S(1)} custom-call(s32[2]{0:T(128)S(1)} %iota_xor_fusion.refs_0_, f32[1024,512]{1,0:T(8,128)S(1)} %copy-done, bf16[1024,512]{1,0:T(8,128)(2,1)S(1)} %pad_maximum_fusion.1.d01_ref.refs_2_, bf16[1024,512]{1,0:T(8,128)(2,1)S(1)} %broadcast_select_fusion.1.refs_3_, bf16[1024,512]{1,0:T(8,128)(2,1)S(1)} %broadcast_select_fusion.refs_4_), custom_call_target="tpu_custom_call" | custom-call | tf_op jit(solution)/shard_map/update/pallas_call | solution.py:542
  183.3 11.3 %collective-permute-done.33 = bf16[512,512]{1,0:T(8,128)(2,1)S(1)} collective-permute-done((bf16[512,512]{1,0:T(8,128)(2,1)}, bf16[512,512]{1,0:T(8,128)(2,1)S(1)}, u32[]{:S(2)}, u32[]{:S(2)}) %collective-permute-start.33) | collective-permute-done | bytes 524320 | tf_op jit(solution)/shard_map/ppermute | solution.py:477
  194.8 4.9 %finish.1 = f32[1024,512]{1,0:T(8,128)} custom-call(s32[2]{0:T(128)S(1)} %iota_xor_fusion.refs_0_, s32[3]{0:T(128)S(1)} %pad_add_fusion.refs_1_, f32[1024,512]{1,0:T(8,128)S(1)} %update.1.refs_2_, bf16[512,512]{1,0:T(8,128)(2,1)S(1)} %bitcast.28, bf16[256,512]{1,0:T(8,128)(2,1)S(1)} %get-tuple-element.96.refs_4_, f32[128,128]{1,0:T(8,128)S(1)} %get-tuple-element.104.refs_5_, ...), custom_call_target="tpu_custom_call" | custom-call | tf_op jit(solution)/shard_map/finish/pallas_call | solution.py:567
  (112 shorter events, 23.1 us)
Async XLA Ops:
  2.7 23.3 %copy-start.8 = (f32[384,128]{1,0:T(8,128)S(1)}, f32[384,128]{1,0:T(8,128)}, u32[]{:S(2)}) copy-start(f32[384,128]{1,0:T(8,128)} %get-tuple-element.63) | copy-start | bytes 589828
  2.7 6.7 %collective-permute-start = (f32[8,128]{1,0:T(8,128)}, f32[8,128]{1,0:T(8,128)S(1)}, u32[]{:S(2)}, u32[]{:S(2)}) collective-permute-start(f32[8,128]{1,0:T(8,128)} %get-tuple-element.56), channel_id=1, source_target_pairs={{0,1},{1,0},{2,3},{3,2},{4,5},{5,4},{6,7},{7,6},{8,9},{9,8},{10,11... | collective-permute-start | bytes 12296 | tf_op jit(solution)/shard_map/ppermute | solution.py:43
  4.8 15.3 %collective-permute-start.3 = (f32[384,128]{1,0:T(8,128)}, f32[384,128]{1,0:T(8,128)S(1)}, u32[]{:S(2)}, u32[]{:S(2)}) collective-permute-start(f32[384,128]{1,0:T(8,128)} %get-tuple-element.57), channel_id=1, source_target_pairs={{0,1},{1,0},{2,3},{3,2},{4,5},{5,4},{6,7},{7,6},{8,9},{9,8},{10,11... | collective-permute-start | bytes 589832 | tf_op jit(solution)/shard_map/ppermute | solution.py:43
  4.9 16.2 %collective-permute-start.4 = (f32[384,256]{1,0:T(8,128)}, f32[384,256]{1,0:T(8,128)S(1)}, u32[]{:S(2)}, u32[]{:S(2)}) collective-permute-start(f32[384,256]{1,0:T(8,128)} %get-tuple-element.59), channel_id=1, source_target_pairs={{0,4},{8,12},{16,20},{24,28}} | collective-permute-start | bytes 1179656 | tf_op jit(solution)/shard_map/ppermute | solution.py:342
  10.1 6.6 %collective-permute-start.1 = (f32[8,128]{1,0:T(8,128)S(1)}, f32[8,128]{1,0:T(8,128)S(1)}, u32[]{:S(2)}, u32[]{:S(2)}) collective-permute-start(f32[8,128]{1,0:T(8,128)S(1)} %add.150), channel_id=1, source_target_pairs={{0,2},{1,3},{2,0},{3,1},{4,6},{5,7},{6,4},{7,5},{8,10},{9,11},{10,... | collective-permute-start | bytes 12296 | tf_op jit(solution)/shard_map/ppermute | solution.py:43
  16.7 3.4 %collective-permute-start.2 = (f32[8,128]{1,0:T(8,128)S(1)}, f32[8,128]{1,0:T(8,128)S(1)}, u32[]{:S(2)}, u32[]{:S(2)}) collective-permute-start(f32[8,128]{1,0:T(8,128)S(1)} %add.151), channel_id=1, source_target_pairs={{0,4},{1,5},{2,6},{3,7},{4,0},{5,1},{6,2},{7,3},{8,12},{9,13},{10,... | collective-permute-start | bytes 12296 | tf_op jit(solution)/shard_map/ppermute | solution.py:43
  20.1 10.6 %copy-start.9 = (f32[8,128]{1,0:T(8,128)}, f32[8,128]{1,0:T(8,128)S(1)}, u32[]{:S(2)}) copy-start(f32[8,128]{1,0:T(8,128)S(1)} %add.152.table_ref) | copy-start | bytes 12292
  24.2 9.3 %collective-permute-start.5 = (f32[384,128]{1,0:T(8,128)S(1)}, f32[384,128]{1,0:T(8,128)S(1)}, u32[]{:S(2)}, u32[]{:S(2)}) collective-permute-start(f32[384,128]{1,0:T(8,128)S(1)} %add.153), channel_id=1, source_target_pairs={{0,2},{1,3},{2,0},{3,1},{4,6},{5,7},{6,4},{7,5},{8,10},{9,11},{10,... | collective-permute-start | bytes 589832 | tf_op jit(solution)/shard_map/ppermute | solution.py:43
  26.1 7.4 %collective-permute-start.6 = (f32[384,128]{1,0:T(8,128)S(1)}, f32[384,128]{1,0:T(8,128)S(1)}, u32[]{:S(2)}, u32[]{:S(2)}) collective-permute-start(f32[384,128]{1,0:T(8,128)S(1)} %copy-done.8), channel_id=1, source_target_pairs={{0,1},{1,0},{2,3},{3,2},{4,5},{5,4},{6,7},{7,6},{8,9},{9,8},{10,11... | collective-permute-start | bytes 589832 | tf_op jit(solution)/shard_map/ppermute | solution.py:43
  33.5 18.5 %collective-permute-start.9 = (f32[384,256]{1,0:T(8,128)S(1)}, f32[384,256]{1,0:T(8,128)S(1)}, u32[]{:S(2)}, u32[]{:S(2)}) collective-permute-start(f32[384,256]{1,0:T(8,128)S(1)} %broadcast_select_fusion.10), channel_id=1, source_target_pairs={{0,1},{4,5},{8,9},{12,13},{16,17},{20,21},{24,25},{28,29}} | collective-permute-start | bytes 1179656 | tf_op jit(solution)/shard_map/ppermute | solution.py:342
  36.9 15.2 %collective-permute-start.10 = (f32[256,512]{1,0:T(8,128)}, f32[256,512]{1,0:T(8,128)S(1)}, u32[]{:S(2)}, u32[]{:S(2)}) collective-permute-start(f32[256,512]{1,0:T(8,128)} %first_rows.1), channel_id=1, source_target_pairs={{0,8},{8,0},{16,24},{24,16},{1,9},{9,1},{17,25},{25,17},{2,10},{10... | collective-permute-start | bytes 1572872 | tf_op jit(solution)/shard_map/ppermute | solution.py:43
  41.5 8.1 %collective-permute-start.7 = (f32[384,128]{1,0:T(8,128)S(1)}, f32[384,128]{1,0:T(8,128)S(1)}, u32[]{:S(2)}, u32[]{:S(2)}) collective-permute-start(f32[384,128]{1,0:T(8,128)S(1)} %add.156), channel_id=1, source_target_pairs={{0,4},{1,5},{2,6},{3,7},{4,0},{5,1},{6,2},{7,3},{8,12},{9,13},{10,... | collective-permute-start | bytes 589832 | tf_op jit(solution)/shard_map/ppermute | solution.py:43
  41.5 10.6 %collective-permute-start.8 = (f32[384,128]{1,0:T(8,128)S(1)}, f32[384,128]{1,0:T(8,128)S(1)}, u32[]{:S(2)}, u32[]{:S(2)}) collective-permute-start(f32[384,128]{1,0:T(8,128)S(1)} %add.157), channel_id=1, source_target_pairs={{0,2},{1,3},{2,0},{3,1},{4,6},{5,7},{6,4},{7,5},{8,10},{9,11},{10,... | collective-permute-start | bytes 589832 | tf_op jit(solution)/shard_map/ppermute | solution.py:43
  44.8 7.4 %copy-start.5 = (f32[256,512]{1,0:T(8,128)S(1)}, f32[256,512]{1,0:T(8,128)}, u32[]{:S(2)}) copy-start(f32[256,512]{1,0:T(8,128)} %first_rows.1) | copy-start | bytes 1572868
  52.3 17.3 %collective-permute-start.15 = (f32[1024,512]{1,0:T(8,128)}, f32[1024,512]{1,0:T(8,128)}, u32[]{:S(2)}, u32[]{:S(2)}) collective-permute-start(f32[1024,512]{1,0:T(8,128)} %far_rows.1), channel_id=1, source_target_pairs={{0,8},{8,0},{16,24},{24,16},{1,9},{9,1},{17,25},{25,17},{2,10},{10... | collective-permute-start | bytes 6291464 | tf_op jit(solution)/shard_map/ppermute | solution.py:43
  53.3 15.3 %collective-permute-start.13 = (f32[384,256]{1,0:T(8,128)S(1)}, f32[384,256]{1,0:T(8,128)S(1)}, u32[]{:S(2)}, u32[]{:S(2)}) collective-permute-start(f32[384,256]{1,0:T(8,128)S(1)} %broadcast_select_fusion.9), channel_id=1, source_target_pairs={{0,2},{1,3},{4,6},{5,7},{8,10},{9,11},{12,14},{13,15},{16,18},{17,... | collective-permute-start | bytes 1179656 | tf_op jit(solution)/shard_map/ppermute | solution.py:342
  55.2 14.2 %collective-permute-start.14 = (f32[256,512]{1,0:T(8,128)S(1)}, f32[256,512]{1,0:T(8,128)S(1)}, u32[]{:S(2)}, u32[]{:S(2)}) collective-permute-start(f32[256,512]{1,0:T(8,128)S(1)} %add.160), channel_id=1, source_target_pairs={{0,16},{8,24},{16,0},{24,8},{1,17},{9,25},{17,1},{25,9},{2,18},{10... | collective-permute-start | bytes 1572872 | tf_op jit(solution)/shard_map/ppermute | solution.py:43
  56.5 11.4 %collective-permute-start.12 = (f32[384,128]{1,0:T(8,128)S(1)}, f32[384,128]{1,0:T(8,128)S(1)}, u32[]{:S(2)}, u32[]{:S(2)}) collective-permute-start(f32[384,128]{1,0:T(8,128)S(1)} %add.159), channel_id=1, source_target_pairs={{0,4},{1,5},{2,6},{3,7},{4,0},{5,1},{6,2},{7,3},{8,12},{9,13},{10,... | collective-permute-start | bytes 589832 | tf_op jit(solution)/shard_map/ppermute | solution.py:43
  65.9 3.6 %copy-start.4 = (bf16[256,512]{1,0:T(8,128)(2,1)S(1)}, bf16[256,512]{1,0:T(8,128)(2,1)}, u32[]{:S(2)}) copy-start(bf16[256,512]{1,0:T(8,128)(2,1)} %get-tuple-element.78.p_ref) | copy-start | bytes 786436
  69.5 7.1 %collective-permute-start.16 = (bf16[256,512]{1,0:T(8,128)(2,1)S(1)}, bf16[256,512]{1,0:T(8,128)(2,1)S(1)}, u32[]{:S(2)}, u32[]{:S(2)}) collective-permute-start(bf16[256,512]{1,0:T(8,128)(2,1)S(1)} %copy-done.4), channel_id=1, source_target_pairs={{0,16},{8,24},{16,0},{24,8},{1,17},{9,25},{17,1},{25,9},{2,18},{10... | collective-permute-start | bytes 786440 | tf_op jit(solution)/shard_map/ppermute | solution.py:43
  71.4 12.2 %collective-permute-start.18 = (f32[256,256]{1,0:T(8,128)S(1)}, f32[256,256]{1,0:T(8,128)S(1)}, u32[]{:S(2)}, u32[]{:S(2)}) collective-permute-start(f32[256,256]{1,0:T(8,128)S(1)} %slice.57), channel_id=1, source_target_pairs={{0,4},{8,12},{16,20},{24,28}} | collective-permute-start | bytes 786440 | tf_op jit(solution)/shard_map/ppermute | solution.py:342
  76.7 7.0 %collective-permute-start.17 = (bf16[512,512]{1,0:T(8,128)(2,1)S(1)}, bf16[512,512]{1,0:T(8,128)(2,1)}, u32[]{:S(2)}, u32[]{:S(2)}) collective-permute-start(bf16[512,512]{1,0:T(8,128)(2,1)S(1)} %pad_maximum_fusion.3), channel_id=1, source_target_pairs={{0,8},{8,0},{16,24},{24,16},{1,9},{9,1},{17,25},{25,17},{2,10},{10... | collective-permute-start | bytes 1572872 | tf_op jit(solution)/shard_map/ppermute | solution.py:43
  82.4 25.0 %collective-permute-start.21 = (f32[512,512]{1,0:T(8,128)}, f32[512,512]{1,0:T(8,128)S(1)}, u32[]{:S(2)}, u32[]{:S(2)}) collective-permute-start(f32[512,512]{1,0:T(8,128)} %far_sum.2), channel_id=1, source_target_pairs={{0,16},{8,24},{16,0},{24,8},{1,17},{9,25},{17,1},{25,9},{2,18},{10... | collective-permute-start | bytes 3145736 | tf_op jit(solution)/shard_map/ppermute | solution.py:43
  84.8 11.5 %collective-permute-start.20 = (f32[256,256]{1,0:T(8,128)S(1)}, f32[256,256]{1,0:T(8,128)}, u32[]{:S(2)}, u32[]{:S(2)}) collective-permute-start(f32[256,256]{1,0:T(8,128)S(1)} %broadcast_select_fusion.13), channel_id=1, source_target_pairs={{0,1},{4,5},{8,9},{12,13},{16,17},{20,21},{24,25},{28,29}} | collective-permute-start | bytes 786440 | tf_op jit(solution)/shard_map/ppermute | solution.py:342
  94.4 20.4 %collective-permute-start.19 = (bf16[336,512]{1,0:T(8,128)(2,1)}, bf16[336,512]{1,0:T(8,128)(2,1)S(1)}, u32[]{:S(2)}, u32[]{:S(2)}) collective-permute-start(bf16[336,512]{1,0:T(8,128)(2,1)} %leaf_last.1), channel_id=1, source_target_pairs={{0,16},{8,24},{16,0},{24,8},{1,17},{9,25},{17,1},{25,9},{2,18},{10... | collective-permute-start | bytes 1032200 | tf_op jit(solution)/shard_map/ppermute | solution.py:43
  94.6 31.3 %collective-permute-start.23 = (bf16[1024,512]{1,0:T(8,128)(2,1)S(1)}, bf16[1024,512]{1,0:T(8,128)(2,1)}, u32[]{:S(2)}, u32[]{:S(2)}) collective-permute-start(bf16[1024,512]{1,0:T(8,128)(2,1)S(1)} %pad_maximum_fusion.1.d01_ref.refs_2_), channel_id=1, source_target_pairs={{0,4},{1,5},{10,14},{11,15},{20,16},{21,17},{30,26},{31,27}} | collective-permute-start | bytes 3145736 | tf_op jit(solution)/shard_map/ppermute | solution.py:465
  107.4 15.5 %copy-start.6 = (f32[512,512]{1,0:T(8,128)}, f32[512,512]{1,0:T(8,128)S(1)}, u32[]{:S(2)}) copy-start(f32[512,512]{1,0:T(8,128)S(1)} %collective-permute-done.21.refs_10_) | copy-start | bytes 3145732
  116.6 8.0 %collective-permute-start.22 = (bf16[672,512]{1,0:T(8,128)(2,1)}, bf16[672,512]{1,0:T(8,128)(2,1)}, u32[]{:S(2)}, u32[]{:S(2)}) collective-permute-start(bf16[672,512]{1,0:T(8,128)(2,1)} %pad_maximum_fusion.2), channel_id=1, source_target_pairs={{0,8},{8,0},{16,24},{24,16},{1,9},{9,1},{17,25},{25,17},{2,10},{10... | collective-permute-start | bytes 2064392 | tf_op jit(solution)/shard_map/ppermute | solution.py:43
  117.4 7.2 %collective-permute-start.24 = (f32[256,256]{1,0:T(8,128)S(1)}, f32[256,256]{1,0:T(8,128)}, u32[]{:S(2)}, u32[]{:S(2)}) collective-permute-start(f32[256,256]{1,0:T(8,128)S(1)} %broadcast_select_fusion.12), channel_id=1, source_target_pairs={{0,2},{1,3},{4,6},{5,7},{8,10},{9,11},{12,14},{13,15},{16,18},{17,... | collective-permute-start | bytes 786440 | tf_op jit(solution)/shard_map/ppermute | solution.py:342
  119.4 5.3 %copy-start.3 = (bf16[336,512]{1,0:T(8,128)(2,1)S(1)}, bf16[336,512]{1,0:T(8,128)(2,1)}, u32[]{:S(2)}) copy-start(bf16[336,512]{1,0:T(8,128)(2,1)} %leaf_last.1) | copy-start | bytes 1032196
  127.0 22.7 %collective-permute-start.27 = (bf16[1024,512]{1,0:T(8,128)(2,1)}, bf16[1024,512]{1,0:T(8,128)(2,1)}, u32[]{:S(2)}, u32[]{:S(2)}) collective-permute-start(bf16[1024,512]{1,0:T(8,128)(2,1)} %broadcast_select_fusion.2), channel_id=1, source_target_pairs={{0,2},{1,3},{4,6},{5,7},{10,8},{11,9},{14,12},{15,13},{20,22},{21,... | collective-permute-start | bytes 3145736 | tf_op jit(solution)/shard_map/ppermute | solution.py:465
  128.3 41.4 %collective-permute-start.11 = (f32[1024,512]{1,0:T(8,128)}, f32[1024,512]{1,0:T(8,128)}, u32[]{:S(2)}, u32[]{:S(2)}) collective-permute-start(f32[1024,512]{1,0:T(8,128)} %near_rows.1), channel_id=1, source_target_pairs={{0,8},{8,0},{16,24},{24,16},{1,9},{9,1},{17,25},{25,17},{2,10},{10... | collective-permute-start | bytes 6291464 | tf_op jit(solution)/shard_map/ppermute | solution.py:43
  134.1 14.7 %collective-permute-start.26 = (bf16[512,512]{1,0:T(8,128)(2,1)S(1)}, bf16[512,512]{1,0:T(8,128)(2,1)}, u32[]{:S(2)}, u32[]{:S(2)}) collective-permute-start(bf16[512,512]{1,0:T(8,128)(2,1)S(1)} %bitcast.27), channel_id=1, source_target_pairs={{0,4},{1,5},{10,14},{11,15},{20,16},{21,17},{30,26},{31,27}} | collective-permute-start | bytes 1572872 | tf_op jit(solution)/shard_map/ppermute | solution.py:465
  144.6 0.6 copy-start.1
  145.2 2.3 %collective-permute-start.25 = (bf16[256,512]{1,0:T(8,128)(2,1)S(1)}, bf16[256,512]{1,0:T(8,128)(2,1)S(1)}, u32[]{:S(2)}, u32[]{:S(2)}) collective-permute-start(bf16[256,512]{1,0:T(8,128)(2,1)S(1)} %get-tuple-element.96.refs_4_), channel_id=1, source_target_pairs={{0,4},{1,5},{10,14},{11,15},{20,16},{21,17},{30,26},{31,27}} | collective-permute-start | bytes 786440 | tf_op jit(solution)/shard_map/ppermute | solution.py:465
  145.9 23.8 %collective-permute-start.30 = (bf16[1024,512]{1,0:T(8,128)(2,1)}, bf16[1024,512]{1,0:T(8,128)(2,1)}, u32[]{:S(2)}, u32[]{:S(2)}) collective-permute-start(bf16[1024,512]{1,0:T(8,128)(2,1)} %broadcast_select_fusion.2), channel_id=1, source_target_pairs={{0,1},{1,0},{4,5},{5,4},{10,11},{11,10},{14,15},{15,14},{20,21},{2... | collective-permute-start | bytes 3145736 | tf_op jit(solution)/shard_map/ppermute | solution.py:477
  147.5 20.7 %collective-permute-start.29 = (f32[512,512]{1,0:T(8,128)}, f32[512,512]{1,0:T(8,128)}, u32[]{:S(2)}, u32[]{:S(2)}) collective-permute-start(f32[512,512]{1,0:T(8,128)} %far_sum.3), channel_id=1, source_target_pairs={{0,16},{8,24},{16,0},{24,8},{1,17},{9,25},{17,1},{25,9},{2,18},{10... | collective-permute-start | bytes 3145736 | tf_op jit(solution)/shard_map/ppermute | solution.py:43
  148.8 2.3 %copy-start.7 = (bf16[256,512]{1,0:T(8,128)(2,1)}, bf16[256,512]{1,0:T(8,128)(2,1)S(1)}, u32[]{:S(2)}) copy-start(bf16[256,512]{1,0:T(8,128)(2,1)S(1)} %broadcast_select_fusion.6) | copy-start | bytes 786436
  151.1 14.3 %collective-permute-start.28 = (bf16[256,512]{1,0:T(8,128)(2,1)S(1)}, bf16[256,512]{1,0:T(8,128)(2,1)}, u32[]{:S(2)}, u32[]{:S(2)}) collective-permute-start(bf16[256,512]{1,0:T(8,128)(2,1)S(1)} %broadcast_select_fusion.6), channel_id=1, source_target_pairs={{0,2},{1,3},{4,6},{5,7},{10,8},{11,9},{14,12},{15,13},{20,22},{21,... | collective-permute-start | bytes 786440 | tf_op jit(solution)/shard_map/ppermute | solution.py:465
  152.4 27.5 %collective-permute-start.31 = (bf16[1024,512]{1,0:T(8,128)(2,1)}, bf16[1024,512]{1,0:T(8,128)(2,1)}, u32[]{:S(2)}, u32[]{:S(2)}) collective-permute-start(bf16[1024,512]{1,0:T(8,128)(2,1)} %collective-permute-done.27), channel_id=1, source_target_pairs={{2,3},{3,2},{6,7},{7,6},{8,9},{9,8},{12,13},{13,12},{22,23},{23,22... | collective-permute-start | bytes 3145736 | tf_op jit(solution)/shard_map/ppermute | solution.py:477
  165.3 10.5 %collective-permute-start.32 = (bf16[512,512]{1,0:T(8,128)(2,1)}, bf16[512,512]{1,0:T(8,128)(2,1)}, u32[]{:S(2)}, u32[]{:S(2)}) collective-permute-start(bf16[512,512]{1,0:T(8,128)(2,1)} %broadcast_select_fusion.5), channel_id=1, source_target_pairs={{0,2},{1,3},{4,6},{5,7},{10,8},{11,9},{14,12},{15,13},{20,22},{21,... | collective-permute-start | bytes 1572872 | tf_op jit(solution)/shard_map/ppermute | solution.py:465
  168.2 15.1 %collective-permute-start.34 = (bf16[512,512]{1,0:T(8,128)(2,1)}, bf16[512,512]{1,0:T(8,128)(2,1)}, u32[]{:S(2)}, u32[]{:S(2)}) collective-permute-start(bf16[512,512]{1,0:T(8,128)(2,1)} %broadcast_select_fusion.5), channel_id=1, source_target_pairs={{0,1},{1,0},{4,5},{5,4},{10,11},{11,10},{14,15},{15,14},{20,21},{2... | collective-permute-start | bytes 1572872 | tf_op jit(solution)/shard_map/ppermute | solution.py:477
  169.7 25.1 %collective-permute-start.35 = (bf16[256,512]{1,0:T(8,128)(2,1)S(1)}, bf16[256,512]{1,0:T(8,128)(2,1)S(1)}, u32[]{:S(2)}, u32[]{:S(2)}) collective-permute-start(bf16[256,512]{1,0:T(8,128)(2,1)S(1)} %broadcast_select_fusion.7.refs_11_), channel_id=1, source_target_pairs={{0,1},{1,0},{4,5},{5,4},{2,3},{3,2},{6,7},{7,6},{10,11},{11,10},{1... | collective-permute-start | bytes 786440 | tf_op jit(solution)/shard_map/ppermute | solution.py:477
  175.0 6.2 %copy-start = (f32[1024,512]{1,0:T(8,128)S(1)}, f32[1024,512]{1,0:T(8,128)}, u32[]{:S(2)}) copy-start(f32[1024,512]{1,0:T(8,128)} %base_rows.1.refs_1_) | copy-start | bytes 6291460
  175.9 18.8 %collective-permute-start.33 = (bf16[512,512]{1,0:T(8,128)(2,1)}, bf16[512,512]{1,0:T(8,128)(2,1)S(1)}, u32[]{:S(2)}, u32[]{:S(2)}) collective-permute-start(bf16[512,512]{1,0:T(8,128)(2,1)} %collective-permute-done.32), channel_id=1, source_target_pairs={{2,3},{3,2},{6,7},{7,6},{8,9},{9,8},{12,13},{13,12},{22,23},{23,22... | collective-permute-start | bytes 1572872 | tf_op jit(solution)/shard_map/ppermute | solution.py:477
  181.3 13.5 %copy-start.2 = (bf16[128,128]{1,0:T(8,128)(2,1)S(1)}, bf16[128,128]{1,0:T(8,128)(2,1)}, u32[]{:S(2)}) copy-start(bf16[128,128]{1,0:T(8,128)(2,1)} %copy-done.1) | copy-start | bytes 98308

commit v8 on v7

--- a/solution.py
+++ b/solution.py
@@ -422,8 +422,7 @@
         name="leaf_two",
     )(head, front, front, mask)
 
-    p01, rest, w_lead, first, diagonal = tie((p01, rest, w_lead, first, diagonal))
-    far_near = flip(rows_at(n, ways, [(diagonal, 0, 0)], "far_sum"), "grp", CHIP)
+    p01, rest, w_lead, first = tie((p01, rest, w_lead, first))
 
     def across(value):
         far_value = flip(value, "grp", CHIP)
@@ -492,10 +491,12 @@
 
     s01 = zone_hop(([0], d01, None))
     pack_far = flip(pack, "grp", CHIP)
-    pack, pack_far, diagonal, corner, far_near = tie(
-        (pack, pack_far, diagonal, corner, far_near)
-    )
-    far_in = rows_at(n + ways, ways, [(diagonal, 0, 1)], "far_sum")
+    pack, pack_far, diagonal, corner = tie((pack, pack_far, diagonal, corner))
+    part = n // 4
+    far_in = [
+        rows_at(n, part, [(diagonal, 0, 0)], "far_sum", ways=part),
+        rows_at(n + part, n - part, [(diagonal, 0, 1)], "far_sum", ways=part),
+    ]
     for at in range(2, last + 1):
         corner = lead_hop(corner, at)
     pack = jnp.concatenate([pack, pack_far], axis=0)
@@ -503,7 +504,7 @@
     pack, held, far_in, corner = tie((pack, s01[1], far_in, corner))
     corner = corner[0] if leads == 1 else jnp.concatenate(corner, axis=1)
     s01 = (s01[0], held, None)
-    far_last = flip(far_in, "grp", CHIP)
+    far = [flip(value, "grp", CHIP) for value in far_in]
     early01 = early_hops(s01)
     s01 = zone_hop(s01)
     d2 = pack.reshape(groups, b + lead_rows, cols)[:, :b].reshape(groups * b, cols)
@@ -517,6 +518,7 @@
         compiler_params=pltpu.CompilerParams(vmem_limit_bytes=32 << 20),
         name="root_step",
     )(leaves, corner, first, d01, pack)
+    q, far[0] = tie((q, far[0]))
     sq_hop = zone_hop(([0], q, None))
     q_held, held, s01_held, s01_got = tie((sq_hop[1], s2[1], s01[1], s01[2][1]))
     s01 = (s01[0], s01_held, (s01[2][0], s01_got))
@@ -524,13 +526,14 @@
     sq_hop = zone_hop((sq_hop[0], q_held, None))
     early2 = early_hops(s2)
     s2 = zone_hop(s2)
-    q_held, far_last, *early01 = tie((sq_hop[1], far_last, *early01))
+    q_held, s2_held, s2_got, *early01 = tie((sq_hop[1], s2[1], s2[2][1], *early01))
+    s2 = (s2[0], s2_held, (s2[2][0], s2_got))
     rq = inner_hops((sq_hop[0], q_held, None))
     r01 = inner_hops(s01, early01)
     r2 = inner_hops(s2, early2)
 
-    adds = [(root_front, 0, 0), (near, 0, 0), (far_near, 0, 0), (far_last, 1, 0)]
-    base = rows_at(3 * n, n, adds, "base_rows")
+    adds = [(root_front, 0, 0), (near, 0, 0), (far[0], 0, 0), (far[1], 1, 0)]
+    base = rows_at(3 * n, n, adds, "base_rows", ways=part)
     slot_of = inner ^ jnp.arange(spread, dtype=jnp.int32)
 
     def update_body(*refs):

time: 202 us -> 210 us (1.040)
  waiting for transfers between devices: 62 us -> 65.9 us
    ppermute x6, waiting for transfers between devices: 11.9 us -> 18.7 us  [zone_hop(): got = lax.ppermute(held, ('grp', 'mem'), pairs)]
    ppermute x19, waiting for transfers between devices: 37 us -> 31.6 us  [flip(): return lax.ppermute(value, axis, [(i, i ^ bit) for i in range(size)])]
    ppermute x6, waiting for transfers between devices: 1.77 us -> 5.75 us  [lead_hop(): got = lax.ppermute(held, 'mem', [(src, src ^ bit) for src in sources])]
    ppermute x19, starting transfers between devices: 23.1 us -> 25.4 us  [flip(): return lax.ppermute(value, axis, [(i, i ^ bit) for i in range(size)])]
    ppermute x5, starting transfers between devices: 7.92 us -> 10.1 us  [inner_hop(): return lax.ppermute(value, ('grp', 'mem'), pairs)]
  transfers between devices with their start and end apart: 36 -> 36, of which waited for: 12 -> 11; matrix products, arithmetic and copies ran while one was open for 9% -> 8% of each run, Pallas kernels for 25% -> 25%
where the time goes in v8:
time: 210 us; the launch traced here: 207 us
  waiting for transfers between devices  65.9 us (31%)
  starting transfers between devices  59.2 us (28%)
  Pallas kernels  57.9 us (28%)
  other arithmetic  16.5 us (8%)
  local copies, waits for them, and re-layouts  6.34 us (3%)
    ppermute x19, waiting for transfers between devices, flip(): return lax.ppermute(value, axis, [(i, i ^ bit) for i in range(size)])  31.6 us
    ppermute x19, starting transfers between devices, flip(): return lax.ppermute(value, axis, [(i, i ^ bit) for i in range(size)])  25.4 us
    pallas_call x6, Pallas kernels, take_rows(): pl.pallas_call(body, grid_spec=pltpu.PrefetchScalarGridSpec(num_scalar_pr...  22.8 us
    ppermute x6, waiting for transfers between devices, zone_hop(): got = lax.ppermute(held, ('grp', 'mem'), pairs)  18.7 us
    ppermute x6, starting transfers between devices, lead_hop(): got = lax.ppermute(held, 'mem', [(src, src ^ bit) for src in sources])  17 us
    ppermute x5, starting transfers between devices, inner_hop(): return lax.ppermute(value, ('grp', 'mem'), pairs)  10.1 us
    ppermute x5, waiting for transfers between devices, inner_hop(): return lax.ppermute(value, ('grp', 'mem'), pairs)  9.93 us
    pallas_call x1, Pallas kernels, local(): pl.pallas_call(leaf_two, grid=(1,), in_specs=[vmem, w_spec(0), w_spec(1),...  9.4 us
  transfers between devices with their start and end apart: 36, of which 11 were waited for; matrix products, arithmetic and copies ran while one was open for 8% of the time, Pallas kernels for 25%

profile of v8, /device:TPU:1, one launch (start us, length us, event | category | flops | bytes accessed | tf_op | source)
XLA Modules:
  0.0 207.2 jit_solution(3700414552186103533)
XLA Ops:
  0.6 2.1 %pick_pivots.1 = (f32[8,128]{1,0:T(8,128)}, f32[384,128]{1,0:T(8,128)}, f32[384,128]{1,0:T(8,128)}, f32[8,512]{1,0:T(8,128)}, f32[384,256]{1,0:T(8,128)}) custom-call(s32[4]{0:T(128)} %bitcast.49, s32[1]{0:T(128)} %bitcast.2.at_ref, f32[4096,512]{1,0:T(8,128)} %bitcast.29), custom_call_target="tpu_custom_call" | custom-call | tf_op jit(solution)/shard_map/pick_pivots/pallas_call | solution.py:346
  2.8 2.1 collective-permute-start
  4.9 4.4 %collective-permute-start.4 = (f32[384,256]{1,0:T(8,128)}, f32[384,256]{1,0:T(8,128)S(1)}, u32[]{:S(2)}, u32[]{:S(2)}) collective-permute-start(f32[384,256]{1,0:T(8,128)} %get-tuple-element.61), channel_id=1, source_target_pairs={{0,4},{8,12},{16,20},{24,28}} | collective-permute-start | bytes 1179656 | tf_op jit(solution)/shard_map/ppermute | solution.py:342
  10.1 6.6 %collective-permute-done.1 = f32[8,128]{1,0:T(8,128)S(1)} collective-permute-done((f32[8,128]{1,0:T(8,128)S(1)}, f32[8,128]{1,0:T(8,128)S(1)}, u32[]{:S(2)}, u32[]{:S(2)}) %collective-permute-start.1) | collective-permute-done | bytes 4128 | tf_op jit(solution)/shard_map/ppermute | solution.py:43
  16.8 3.2 %collective-permute-done.2 = f32[8,128]{1,0:T(8,128)S(1)} collective-permute-done((f32[8,128]{1,0:T(8,128)S(1)}, f32[8,128]{1,0:T(8,128)S(1)}, u32[]{:S(2)}, u32[]{:S(2)}) %collective-permute-start.2) | collective-permute-done | bytes 4128 | tf_op jit(solution)/shard_map/ppermute | solution.py:43
  24.9 1.9 collective-permute-start.5
  26.8 3.3 %far_rows.1 = f32[1024,512]{1,0:T(8,128)} custom-call(s32[8]{0:T(128)} %get-tuple-element.124.refs_0_, s32[8]{0:T(128)} %get-tuple-element.121.refs_1_, s32[1]{0:T(128)} %constant.64.clone.1.refs_2_, f32[4096,512]{1,0:T(8,128)} %bitcast.30, f32[4096,512]{1,0:T(8,128)} %bitcast.31, f32[4096,512]{1,0:T(8,128)} %bitcast.32, f32[4096,512]{1,0:T(8,128)} %bitcast.33, ...), custom_call_target="tpu_custom_call" | custom-call | tf_op jit(solution)/shard_map/far_rows/pallas_call | solution.py:214
  30.7 2.8 %first_rows.1 = f32[256,512]{1,0:T(8,128)} custom-call(s32[2]{0:T(128)} %get-tuple-element.119.refs_0_, s32[2]{0:T(128)} %get-tuple-element.117.refs_1_, s32[1]{0:T(128)} %bitcast.10.refs_2_, f32[4096,512]{1,0:T(8,128)} %bitcast.34, f32[4096,512]{1,0:T(8,128)} %bitcast.35, f32[8,512]{1,0:T(8,128)} %get-tuple-element.63.refs_7_.refs_5_.mask_ref, ...), custom_call_target="tpu_custom_call" | custom-call | tf_op jit(solution)/shard_map/first_rows/pallas_call | solution.py:214
  33.6 3.4 %collective-permute-start.9 = (f32[384,256]{1,0:T(8,128)S(1)}, f32[384,256]{1,0:T(8,128)S(1)}, u32[]{:S(2)}, u32[]{:S(2)}) collective-permute-start(f32[384,256]{1,0:T(8,128)S(1)} %broadcast_select_fusion.10), channel_id=1, source_target_pairs={{0,1},{4,5},{8,9},{12,13},{16,17},{20,21},{24,25},{28,29}} | collective-permute-start | bytes 1179656 | tf_op jit(solution)/shard_map/ppermute | solution.py:342
  37.0 4.6 %collective-permute-start.10 = (f32[256,512]{1,0:T(8,128)}, f32[256,512]{1,0:T(8,128)S(1)}, u32[]{:S(2)}, u32[]{:S(2)}) collective-permute-start(f32[256,512]{1,0:T(8,128)} %first_rows.1), channel_id=1, source_target_pairs={{0,8},{8,0},{16,24},{24,16},{1,9},{9,1},{17,25},{25,17},{2,10},{10... | collective-permute-start | bytes 1572872 | tf_op jit(solution)/shard_map/ppermute | solution.py:43
  41.5 3.3 %near_rows.1 = f32[1024,512]{1,0:T(8,128)} custom-call(s32[8]{0:T(128)} %get-tuple-element.123.refs_0_, s32[8]{0:T(128)} %get-tuple-element.120.refs_1_, s32[1]{0:T(128)} %constant.64.clone.1.refs_2_, f32[4096,512]{1,0:T(8,128)} %bitcast.36, f32[4096,512]{1,0:T(8,128)} %bitcast.37, f32[4096,512]{1,0:T(8,128)} %bitcast.38, f32[4096,512]{1,0:T(8,128)} %bitcast.39, ...), custom_call_target="tpu_custom_call" | custom-call | tf_op jit(solution)/shard_map/near_rows/pallas_call | solution.py:214
  44.8 4.9 %collective-permute-done.7 = f32[384,128]{1,0:T(8,128)S(1)} collective-permute-done((f32[384,128]{1,0:T(8,128)S(1)}, f32[384,128]{1,0:T(8,128)S(1)}, u32[]{:S(2)}, u32[]{:S(2)}) %collective-permute-start.7) | collective-permute-done | bytes 196640 | tf_op jit(solution)/shard_map/ppermute | solution.py:43
  50.4 1.7 collective-permute-done.8
  52.3 2.2 %collective-permute-start.13 = (f32[384,256]{1,0:T(8,128)S(1)}, f32[384,256]{1,0:T(8,128)S(1)}, u32[]{:S(2)}, u32[]{:S(2)}) collective-permute-start(f32[384,256]{1,0:T(8,128)S(1)} %broadcast_select_fusion.9), channel_id=1, source_target_pairs={{0,2},{1,3},{4,6},{5,7},{8,10},{9,11},{12,14},{13,15},{16,18},{17,... | collective-permute-start | bytes 1179656 | tf_op jit(solution)/shard_map/ppermute | solution.py:342
  54.5 1.3 collective-permute-start.14
  57.0 9.4 %leaf_two.1 = (bf16[256,512]{1,0:T(8,128)(2,1)}, f32[128,128]{1,0:T(8,128)}, f32[128,128]{1,0:T(8,128)}, bf16[128,128]{1,0:T(8,128)(2,1)}, f32[8,128]{1,0:T(8,128)}) custom-call(f32[384,128]{1,0:T(8,128)} %add.158.head_ref, f32[4096,512]{1,0:T(8,128)} %bitcast.40, f32[4096,512]{1,0:T(8,128)} %bitcast.41, f32[8,512]{1,0:T(8,128)} %get-tuple-element.63.refs_7_.refs_5_.mask_ref), custom_call_target="tpu_custom_call" | custom-call | tf_op jit(solution)/shard_map/leaf_two/pallas_call | solution.py:415
  66.4 1.4 collective-permute-done.12
  69.8 7.2 %collective-permute-done.15 = bf16[256,512]{1,0:T(8,128)(2,1)S(1)} collective-permute-done((bf16[256,512]{1,0:T(8,128)(2,1)S(1)}, bf16[256,512]{1,0:T(8,128)(2,1)S(1)}, u32[]{:S(2)}, u32[]{:S(2)}) %collective-permute-start.15) | collective-permute-done | bytes 262176 | tf_op jit(solution)/shard_map/ppermute | solution.py:43
  77.0 1.3 collective-permute-start.16
  78.4 3.7 %collective-permute-start.17 = (f32[256,256]{1,0:T(8,128)S(1)}, f32[256,256]{1,0:T(8,128)S(1)}, u32[]{:S(2)}, u32[]{:S(2)}) collective-permute-start(f32[256,256]{1,0:T(8,128)S(1)} %slice.57), channel_id=1, source_target_pairs={{0,4},{8,12},{16,20},{24,28}} | collective-permute-start | bytes 786440 | tf_op jit(solution)/shard_map/ppermute | solution.py:342
  82.1 5.7 %collective-permute-done.17 = f32[256,256]{1,0:T(8,128)S(1)} collective-permute-done((f32[256,256]{1,0:T(8,128)S(1)}, f32[256,256]{1,0:T(8,128)S(1)}, u32[]{:S(2)}, u32[]{:S(2)}) %collective-permute-start.17) | collective-permute-done | bytes 262176 | tf_op jit(solution)/shard_map/ppermute | solution.py:342
  88.7 2.0 collective-permute-start.20
  90.7 7.6 %leaf_last.1 = bf16[336,512]{1,0:T(8,128)(2,1)} custom-call(f32[384,128]{1,0:T(8,128)} %add.161.rest_ref, f32[4096,512]{1,0:T(8,128)} %bitcast.42, f32[384,256]{1,0:T(8,128)} %broadcast_select_fusion.8.w_lead_ref, f32[8,128]{1,0:T(8,128)} %copy-done.16, f32[8,512]{1,0:T(8,128)} %get-tuple-element.63.refs_7_.refs_5_.mask_ref, ...), custom_call_target="tpu_custom_call" | custom-call | tf_op jit(solution)/shard_map/leaf_last/pallas_call | solution.py:438
  99.5 5.1 %collective-permute-done.18 = bf16[336,512]{1,0:T(8,128)(2,1)S(1)} collective-permute-done((bf16[336,512]{1,0:T(8,128)(2,1)}, bf16[336,512]{1,0:T(8,128)(2,1)S(1)}, u32[]{:S(2)}, u32[]{:S(2)}) %collective-permute-start.18) | collective-permute-done | bytes 344096 | tf_op jit(solution)/shard_map/ppermute | solution.py:43
  104.6 1.3 collective-permute-start.23
  105.9 1.9 pad_maximum_fusion.2
  107.8 6.6 %collective-permute-start.21 = (bf16[672,512]{1,0:T(8,128)(2,1)}, bf16[672,512]{1,0:T(8,128)(2,1)}, u32[]{:S(2)}, u32[]{:S(2)}) collective-permute-start(bf16[672,512]{1,0:T(8,128)(2,1)} %pad_maximum_fusion.2), channel_id=1, source_target_pairs={{0,8},{8,0},{16,24},{24,16},{1,9},{9,1},{17,25},{25,17},{2,10},{10... | collective-permute-start | bytes 2064392 | tf_op jit(solution)/shard_map/ppermute | solution.py:43
  115.7 2.8 %far_sum.2 = f32[256,512]{1,0:T(8,128)} custom-call(s32[2]{0:T(128)} %get-tuple-element.118.refs_0_, s32[2]{0:T(128)} %get-tuple-element.116.refs_1_, s32[1]{0:T(128)} %constant.64.clone.1.refs_2_, f32[4096,512]{1,0:T(8,128)} %bitcast.43, f32[4096,512]{1,0:T(8,128)} %bitcast.44, f32[8,512]{1,0:T(8,128)} %get-tuple-element.63.refs_7_.refs_5_.mask_ref, ...), custom_call_target="tpu_custom_call" | custom-call | tf_op jit(solution)/shard_map/far_sum/pallas_call | solution.py:214
  118.4 4.5 %far_sum.3 = f32[768,512]{1,0:T(8,128)} custom-call(s32[6]{0:T(128)} %slice.60.refs_0_, s32[6]{0:T(128)} %slice.61.refs_1_, s32[1]{0:T(128)} %constant.64.clone.1.refs_2_, f32[4096,512]{1,0:T(8,128)} %bitcast.45, f32[4096,512]{1,0:T(8,128)} %bitcast.46, f32[8,512]{1,0:T(8,128)} %get-tuple-element.63.refs_7_.refs_5_.mask_ref, ...), custom_call_target="tpu_custom_call" | custom-call | tf_op jit(solution)/shard_map/far_sum/pallas_call | solution.py:214
  126.1 1.3 collective-permute-start.28
  127.5 1.5 collective-permute-start.27
  129.0 4.7 %collective-permute-start.11 = (f32[1024,512]{1,0:T(8,128)}, f32[1024,512]{1,0:T(8,128)}, u32[]{:S(2)}, u32[]{:S(2)}) collective-permute-start(f32[1024,512]{1,0:T(8,128)} %near_rows.1), channel_id=1, source_target_pairs={{0,8},{8,0},{16,24},{24,16},{1,9},{9,1},{17,25},{25,17},{2,10},{10... | collective-permute-start | bytes 6291464 | tf_op jit(solution)/shard_map/ppermute | solution.py:43
  133.8 1.6 collective-permute-start.32
  136.4 9.0 %root_step.1 = (bf16[256,512]{1,0:T(8,128)(2,1)S(1)}, f32[128,128]{1,0:T(8,128)S(1)}, f32[128,128]{1,0:T(8,128)S(1)}, bf16[128,128]{1,0:T(8,128)(2,1)S(1)}, f32[8,128]{1,0:T(8,128)S(1)}) custom-call(s32[4]{0:T(128)S(1)} %pad_add_fusion.1.leaf_ref, f32[256,256]{1,0:T(8,128)S(1)} %copy-done.3, f32[256,512]{1,0:T(8,128)S(1)} %add.162.first_ref, ...), custom_call_target="tpu_custom_call" | custom-call | tf_op jit(solution)/shard_map/root_step/pallas_call | solution.py:513
  147.1 1.3 broadcast_select_fusion.1.refs_3_
  148.5 1.3 collective-permute-start.31
  149.8 1.3 collective-permute-start.30
  151.1 18.7 %collective-permute-done.30 = bf16[256,512]{1,0:T(8,128)(2,1)S(1)} collective-permute-done((bf16[256,512]{1,0:T(8,128)(2,1)S(1)}, bf16[256,512]{1,0:T(8,128)(2,1)S(1)}, u32[]{:S(2)}, u32[]{:S(2)}) %collective-permute-start.30) | collective-permute-done | bytes 262176 | tf_op jit(solution)/shard_map/ppermute | solution.py:464
  169.8 1.5 collective-permute-start.34
  171.3 3.4 %collective-permute-start.29 = (bf16[1024,512]{1,0:T(8,128)(2,1)}, bf16[1024,512]{1,0:T(8,128)(2,1)}, u32[]{:S(2)}, u32[]{:S(2)}) collective-permute-start(bf16[1024,512]{1,0:T(8,128)(2,1)} %collective-permute-done.28), channel_id=1, source_target_pairs={{2,3},{3,2},{6,7},{7,6},{8,9},{9,8},{12,13},{13,12},{22,23},{23,22... | collective-permute-start | bytes 3145736 | tf_op jit(solution)/shard_map/ppermute | solution.py:476
  175.8 2.2 %collective-permute-start.33 = (bf16[512,512]{1,0:T(8,128)(2,1)}, bf16[512,512]{1,0:T(8,128)(2,1)}, u32[]{:S(2)}, u32[]{:S(2)}) collective-permute-start(bf16[512,512]{1,0:T(8,128)(2,1)} %collective-permute-done.31), channel_id=1, source_target_pairs={{2,3},{3,2},{6,7},{7,6},{8,9},{9,8},{12,13},{13,12},{22,23},{23,22... | collective-permute-start | bytes 1572872 | tf_op jit(solution)/shard_map/ppermute | solution.py:476
  178.5 1.4 collective-permute-start.35
  180.0 1.5 collective-permute-done.25.refs_9_
  181.4 6.2 %base_rows.1.refs_1_ = f32[1024,512]{1,0:T(8,128)} custom-call(s32[8]{0:T(128)} %get-tuple-element.125.refs_0_, s32[8]{0:T(128)} %get-tuple-element.122.refs_1_, s32[1]{0:T(128)} %constant.64.clone.1.refs_2_, f32[4096,512]{1,0:T(8,128)} %bitcast.47, f32[4096,512]{1,0:T(8,128)} %bitcast.48, f32[8,512]{1,0:T(8,128)} %get-tuple-element.63.refs_7_.refs_5_.mask_ref, ...), custom_call_target="tpu_custom_call" | custom-call | tf_op jit(solution)/shard_map/base_rows/pallas_call | solution.py:214
  187.6 9.9 %collective-permute-done.33 = bf16[512,512]{1,0:T(8,128)(2,1)} collective-permute-done((bf16[512,512]{1,0:T(8,128)(2,1)}, bf16[512,512]{1,0:T(8,128)(2,1)}, u32[]{:S(2)}, u32[]{:S(2)}) %collective-permute-start.33) | collective-permute-done | bytes 524320 | tf_op jit(solution)/shard_map/ppermute | solution.py:476
  198.7 1.3 broadcast_select_fusion.refs_4_
  200.1 2.1 update.1.refs_2_
  202.2 5.0 %finish.1 = f32[1024,512]{1,0:T(8,128)} custom-call(s32[2]{0:T(128)S(1)} %iota_xor_fusion.refs_0_, s32[3]{0:T(128)S(1)} %pad_add_fusion.refs_1_, f32[1024,512]{1,0:T(8,128)S(1)} %update.1.refs_2_, bf16[512,512]{1,0:T(8,128)(2,1)S(1)} %bitcast.28, bf16[256,512]{1,0:T(8,128)(2,1)S(1)} %copy-done.2, f32[128,128]{1,0:T(8,128)S(1)} %get-tuple-element.107.refs_5_, ...), custom_call_target="tpu_custom_call" | custom-call | tf_op jit(solution)/shard_map/finish/pallas_call | solution.py:570
  (126 shorter events, 22.6 us)
Async XLA Ops:
  2.8 24.0 %copy-start.11 = (f32[384,128]{1,0:T(8,128)S(1)}, f32[384,128]{1,0:T(8,128)}, u32[]{:S(2)}) copy-start(f32[384,128]{1,0:T(8,128)} %get-tuple-element.65) | copy-start | bytes 589828
  2.8 6.7 %collective-permute-start = (f32[8,128]{1,0:T(8,128)}, f32[8,128]{1,0:T(8,128)S(1)}, u32[]{:S(2)}, u32[]{:S(2)}) collective-permute-start(f32[8,128]{1,0:T(8,128)} %get-tuple-element.58), channel_id=1, source_target_pairs={{0,1},{1,0},{2,3},{3,2},{4,5},{5,4},{6,7},{7,6},{8,9},{9,8},{10,11... | collective-permute-start | bytes 12296 | tf_op jit(solution)/shard_map/ppermute | solution.py:43
  4.8 15.3 %collective-permute-start.3 = (f32[384,128]{1,0:T(8,128)}, f32[384,128]{1,0:T(8,128)S(1)}, u32[]{:S(2)}, u32[]{:S(2)}) collective-permute-start(f32[384,128]{1,0:T(8,128)} %get-tuple-element.59), channel_id=1, source_target_pairs={{0,1},{1,0},{2,3},{3,2},{4,5},{5,4},{6,7},{7,6},{8,9},{9,8},{10,11... | collective-permute-start | bytes 589832 | tf_op jit(solution)/shard_map/ppermute | solution.py:43
  4.9 16.2 %collective-permute-start.4 = (f32[384,256]{1,0:T(8,128)}, f32[384,256]{1,0:T(8,128)S(1)}, u32[]{:S(2)}, u32[]{:S(2)}) collective-permute-start(f32[384,256]{1,0:T(8,128)} %get-tuple-element.61), channel_id=1, source_target_pairs={{0,4},{8,12},{16,20},{24,28}} | collective-permute-start | bytes 1179656 | tf_op jit(solution)/shard_map/ppermute | solution.py:342
  10.1 6.6 %collective-permute-start.1 = (f32[8,128]{1,0:T(8,128)S(1)}, f32[8,128]{1,0:T(8,128)S(1)}, u32[]{:S(2)}, u32[]{:S(2)}) collective-permute-start(f32[8,128]{1,0:T(8,128)S(1)} %add.150), channel_id=1, source_target_pairs={{0,2},{1,3},{2,0},{3,1},{4,6},{5,7},{6,4},{7,5},{8,10},{9,11},{10,... | collective-permute-start | bytes 12296 | tf_op jit(solution)/shard_map/ppermute | solution.py:43
  16.7 3.4 %collective-permute-start.2 = (f32[8,128]{1,0:T(8,128)S(1)}, f32[8,128]{1,0:T(8,128)S(1)}, u32[]{:S(2)}, u32[]{:S(2)}) collective-permute-start(f32[8,128]{1,0:T(8,128)S(1)} %add.151), channel_id=1, source_target_pairs={{0,4},{1,5},{2,6},{3,7},{4,0},{5,1},{6,2},{7,3},{8,12},{9,13},{10,... | collective-permute-start | bytes 12296 | tf_op jit(solution)/shard_map/ppermute | solution.py:43
  20.1 10.0 %copy-start.16 = (f32[8,128]{1,0:T(8,128)}, f32[8,128]{1,0:T(8,128)S(1)}, u32[]{:S(2)}) copy-start(f32[8,128]{1,0:T(8,128)S(1)} %add.152.table_ref) | copy-start | bytes 12292
  22.9 7.2 %copy-start.12 = (s32[34]{0:T(128)}, s32[34]{0:T(128)S(1)}, u32[]{:S(2)}) copy-start(s32[34]{0:T(128)S(1)} %get-tuple-element.114) | copy-start | bytes 412
  22.9 7.2 %copy-start.14 = (s32[34]{0:T(128)}, s32[34]{0:T(128)S(1)}, u32[]{:S(2)}) copy-start(s32[34]{0:T(128)S(1)} %get-tuple-element.115) | copy-start | bytes 412
  24.9 8.6 %collective-permute-start.5 = (f32[384,128]{1,0:T(8,128)S(1)}, f32[384,128]{1,0:T(8,128)S(1)}, u32[]{:S(2)}, u32[]{:S(2)}) collective-permute-start(f32[384,128]{1,0:T(8,128)S(1)} %add.153), channel_id=1, source_target_pairs={{0,2},{1,3},{2,0},{3,1},{4,6},{5,7},{6,4},{7,5},{8,10},{9,11},{10,... | collective-permute-start | bytes 589832 | tf_op jit(solution)/shard_map/ppermute | solution.py:43
  26.8 6.8 %collective-permute-start.6 = (f32[384,128]{1,0:T(8,128)S(1)}, f32[384,128]{1,0:T(8,128)S(1)}, u32[]{:S(2)}, u32[]{:S(2)}) collective-permute-start(f32[384,128]{1,0:T(8,128)S(1)} %copy-done.11), channel_id=1, source_target_pairs={{0,1},{1,0},{2,3},{3,2},{4,5},{5,4},{6,7},{7,6},{8,9},{9,8},{10,11... | collective-permute-start | bytes 589832 | tf_op jit(solution)/shard_map/ppermute | solution.py:43
  33.6 18.5 %collective-permute-start.9 = (f32[384,256]{1,0:T(8,128)S(1)}, f32[384,256]{1,0:T(8,128)S(1)}, u32[]{:S(2)}, u32[]{:S(2)}) collective-permute-start(f32[384,256]{1,0:T(8,128)S(1)} %broadcast_select_fusion.10), channel_id=1, source_target_pairs={{0,1},{4,5},{8,9},{12,13},{16,17},{20,21},{24,25},{28,29}} | collective-permute-start | bytes 1179656 | tf_op jit(solution)/shard_map/ppermute | solution.py:342
  37.0 15.2 %collective-permute-start.10 = (f32[256,512]{1,0:T(8,128)}, f32[256,512]{1,0:T(8,128)S(1)}, u32[]{:S(2)}, u32[]{:S(2)}) collective-permute-start(f32[256,512]{1,0:T(8,128)} %first_rows.1), channel_id=1, source_target_pairs={{0,8},{8,0},{16,24},{24,16},{1,9},{9,1},{17,25},{25,17},{2,10},{10... | collective-permute-start | bytes 1572872 | tf_op jit(solution)/shard_map/ppermute | solution.py:43
  41.5 8.2 %collective-permute-start.7 = (f32[384,128]{1,0:T(8,128)S(1)}, f32[384,128]{1,0:T(8,128)S(1)}, u32[]{:S(2)}, u32[]{:S(2)}) collective-permute-start(f32[384,128]{1,0:T(8,128)S(1)} %add.156), channel_id=1, source_target_pairs={{0,4},{1,5},{2,6},{3,7},{4,0},{5,1},{6,2},{7,3},{8,12},{9,13},{10,... | collective-permute-start | bytes 589832 | tf_op jit(solution)/shard_map/ppermute | solution.py:43
  41.5 10.6 %collective-permute-start.8 = (f32[384,128]{1,0:T(8,128)S(1)}, f32[384,128]{1,0:T(8,128)S(1)}, u32[]{:S(2)}, u32[]{:S(2)}) collective-permute-start(f32[384,128]{1,0:T(8,128)S(1)} %add.157), channel_id=1, source_target_pairs={{0,2},{1,3},{2,0},{3,1},{4,6},{5,7},{6,4},{7,5},{8,10},{9,11},{10,... | collective-permute-start | bytes 589832 | tf_op jit(solution)/shard_map/ppermute | solution.py:43
  44.8 7.4 %copy-start.10 = (f32[256,512]{1,0:T(8,128)S(1)}, f32[256,512]{1,0:T(8,128)}, u32[]{:S(2)}) copy-start(f32[256,512]{1,0:T(8,128)} %first_rows.1) | copy-start | bytes 1572868
  52.3 16.2 %collective-permute-start.13 = (f32[384,256]{1,0:T(8,128)S(1)}, f32[384,256]{1,0:T(8,128)S(1)}, u32[]{:S(2)}, u32[]{:S(2)}) collective-permute-start(f32[384,256]{1,0:T(8,128)S(1)} %broadcast_select_fusion.9), channel_id=1, source_target_pairs={{0,2},{1,3},{4,6},{5,7},{8,10},{9,11},{12,14},{13,15},{16,18},{17,... | collective-permute-start | bytes 1179656 | tf_op jit(solution)/shard_map/ppermute | solution.py:342
  54.5 14.8 %collective-permute-start.14 = (f32[256,512]{1,0:T(8,128)S(1)}, f32[256,512]{1,0:T(8,128)S(1)}, u32[]{:S(2)}, u32[]{:S(2)}) collective-permute-start(f32[256,512]{1,0:T(8,128)S(1)} %add.160), channel_id=1, source_target_pairs={{0,16},{8,24},{16,0},{24,8},{1,17},{9,25},{17,1},{25,9},{2,18},{10... | collective-permute-start | bytes 1572872 | tf_op jit(solution)/shard_map/ppermute | solution.py:43
  55.8 48.8 %collective-permute-start.19 = (f32[1024,512]{1,0:T(8,128)}, f32[1024,512]{1,0:T(8,128)}, u32[]{:S(2)}, u32[]{:S(2)}) collective-permute-start(f32[1024,512]{1,0:T(8,128)} %far_rows.1), channel_id=1, source_target_pairs={{0,8},{8,0},{16,24},{24,16},{1,9},{9,1},{17,25},{25,17},{2,10},{10... | collective-permute-start | bytes 6291464 | tf_op jit(solution)/shard_map/ppermute | solution.py:43
  57.0 10.8 %collective-permute-start.12 = (f32[384,128]{1,0:T(8,128)S(1)}, f32[384,128]{1,0:T(8,128)S(1)}, u32[]{:S(2)}, u32[]{:S(2)}) collective-permute-start(f32[384,128]{1,0:T(8,128)S(1)} %add.159), channel_id=1, source_target_pairs={{0,4},{1,5},{2,6},{3,7},{4,0},{5,1},{6,2},{7,3},{8,12},{9,13},{10,... | collective-permute-start | bytes 589832 | tf_op jit(solution)/shard_map/ppermute | solution.py:43
  66.4 3.0 %copy-start.9 = (bf16[256,512]{1,0:T(8,128)(2,1)S(1)}, bf16[256,512]{1,0:T(8,128)(2,1)}, u32[]{:S(2)}) copy-start(bf16[256,512]{1,0:T(8,128)(2,1)} %get-tuple-element.79.p_ref) | copy-start | bytes 786436
  69.5 7.5 %collective-permute-start.15 = (bf16[256,512]{1,0:T(8,128)(2,1)S(1)}, bf16[256,512]{1,0:T(8,128)(2,1)S(1)}, u32[]{:S(2)}, u32[]{:S(2)}) collective-permute-start(bf16[256,512]{1,0:T(8,128)(2,1)S(1)} %copy-done.9), channel_id=1, source_target_pairs={{0,16},{8,24},{16,0},{24,8},{1,17},{9,25},{17,1},{25,9},{2,18},{10... | collective-permute-start | bytes 786440 | tf_op jit(solution)/shard_map/ppermute | solution.py:43
  77.0 10.9 %collective-permute-start.16 = (bf16[512,512]{1,0:T(8,128)(2,1)S(1)}, bf16[512,512]{1,0:T(8,128)(2,1)S(1)}, u32[]{:S(2)}, u32[]{:S(2)}) collective-permute-start(bf16[512,512]{1,0:T(8,128)(2,1)S(1)} %pad_maximum_fusion.3), channel_id=1, source_target_pairs={{0,8},{8,0},{16,24},{24,16},{1,9},{9,1},{17,25},{25,17},{2,10},{10... | collective-permute-start | bytes 1572872 | tf_op jit(solution)/shard_map/ppermute | solution.py:43
  78.4 9.4 %collective-permute-start.17 = (f32[256,256]{1,0:T(8,128)S(1)}, f32[256,256]{1,0:T(8,128)S(1)}, u32[]{:S(2)}, u32[]{:S(2)}) collective-permute-start(f32[256,256]{1,0:T(8,128)S(1)} %slice.57), channel_id=1, source_target_pairs={{0,4},{8,12},{16,20},{24,28}} | collective-permute-start | bytes 786440 | tf_op jit(solution)/shard_map/ppermute | solution.py:342
  87.9 35.7 %collective-permute-start.22 = (bf16[1024,512]{1,0:T(8,128)(2,1)S(1)}, bf16[1024,512]{1,0:T(8,128)(2,1)S(1)}, u32[]{:S(2)}, u32[]{:S(2)}) collective-permute-start(bf16[1024,512]{1,0:T(8,128)(2,1)S(1)} %pad_maximum_fusion.1.d01_ref.refs_2_), channel_id=1, source_target_pairs={{0,4},{1,5},{10,14},{11,15},{20,16},{21,17},{30,26},{31,27}} | collective-permute-start | bytes 3145736 | tf_op jit(solution)/shard_map/ppermute | solution.py:464
  88.7 10.8 %collective-permute-start.20 = (f32[256,256]{1,0:T(8,128)S(1)}, f32[256,256]{1,0:T(8,128)}, u32[]{:S(2)}, u32[]{:S(2)}) collective-permute-start(f32[256,256]{1,0:T(8,128)S(1)} %broadcast_select_fusion.13), channel_id=1, source_target_pairs={{0,1},{4,5},{8,9},{12,13},{16,17},{20,21},{24,25},{28,29}} | collective-permute-start | bytes 786440 | tf_op jit(solution)/shard_map/ppermute | solution.py:342
  98.3 16.2 %copy-start.15 = (s32[34]{0:T(128)S(1)}, s32[34]{0:T(128)}, u32[]{:S(2)}) copy-start(s32[34]{0:T(128)} %copy-done.14) | copy-start | bytes 412
  98.3 16.8 %copy-start.13 = (s32[34]{0:T(128)S(1)}, s32[34]{0:T(128)}, u32[]{:S(2)}) copy-start(s32[34]{0:T(128)} %copy-done.12) | copy-start | bytes 412
  98.3 6.3 %collective-permute-start.18 = (bf16[336,512]{1,0:T(8,128)(2,1)}, bf16[336,512]{1,0:T(8,128)(2,1)S(1)}, u32[]{:S(2)}, u32[]{:S(2)}) collective-permute-start(bf16[336,512]{1,0:T(8,128)(2,1)} %leaf_last.1), channel_id=1, source_target_pairs={{0,16},{8,24},{16,0},{24,8},{1,17},{9,25},{17,1},{25,9},{2,18},{10... | collective-permute-start | bytes 1032200 | tf_op jit(solution)/shard_map/ppermute | solution.py:43
  104.6 18.3 %collective-permute-start.23 = (f32[256,256]{1,0:T(8,128)S(1)}, f32[256,256]{1,0:T(8,128)S(1)}, u32[]{:S(2)}, u32[]{:S(2)}) collective-permute-start(f32[256,256]{1,0:T(8,128)S(1)} %broadcast_select_fusion.12), channel_id=1, source_target_pairs={{0,2},{1,3},{4,6},{5,7},{8,10},{9,11},{12,14},{13,15},{16,18},{17,... | collective-permute-start | bytes 786440 | tf_op jit(solution)/shard_map/ppermute | solution.py:342
  107.8 17.0 %collective-permute-start.21 = (bf16[672,512]{1,0:T(8,128)(2,1)}, bf16[672,512]{1,0:T(8,128)(2,1)}, u32[]{:S(2)}, u32[]{:S(2)}) collective-permute-start(bf16[672,512]{1,0:T(8,128)(2,1)} %pad_maximum_fusion.2), channel_id=1, source_target_pairs={{0,8},{8,0},{16,24},{24,16},{1,9},{9,1},{17,25},{25,17},{2,10},{10... | collective-permute-start | bytes 2064392 | tf_op jit(solution)/shard_map/ppermute | solution.py:43
  126.1 21.0 %collective-permute-start.28 = (bf16[1024,512]{1,0:T(8,128)(2,1)}, bf16[1024,512]{1,0:T(8,128)(2,1)}, u32[]{:S(2)}, u32[]{:S(2)}) collective-permute-start(bf16[1024,512]{1,0:T(8,128)(2,1)} %broadcast_select_fusion.2), channel_id=1, source_target_pairs={{0,2},{1,3},{4,6},{5,7},{10,8},{11,9},{14,12},{15,13},{20,22},{21,... | collective-permute-start | bytes 3145736 | tf_op jit(solution)/shard_map/ppermute | solution.py:464
  127.4 18.0 %collective-permute-start.24 = (f32[256,512]{1,0:T(8,128)}, f32[256,512]{1,0:T(8,128)}, u32[]{:S(2)}, u32[]{:S(2)}) collective-permute-start(f32[256,512]{1,0:T(8,128)} %far_sum.2), channel_id=1, source_target_pairs={{0,16},{8,24},{16,0},{24,8},{1,17},{9,25},{17,1},{25,9},{2,18},{10... | collective-permute-start | bytes 1572872 | tf_op jit(solution)/shard_map/ppermute | solution.py:43
  127.5 18.0 %collective-permute-start.27 = (bf16[512,512]{1,0:T(8,128)(2,1)S(1)}, bf16[512,512]{1,0:T(8,128)(2,1)}, u32[]{:S(2)}, u32[]{:S(2)}) collective-permute-start(bf16[512,512]{1,0:T(8,128)(2,1)S(1)} %bitcast.27), channel_id=1, source_target_pairs={{0,4},{1,5},{10,14},{11,15},{20,16},{21,17},{30,26},{31,27}} | collective-permute-start | bytes 1572872 | tf_op jit(solution)/shard_map/ppermute | solution.py:464
  129.0 49.5 %collective-permute-start.11 = (f32[1024,512]{1,0:T(8,128)}, f32[1024,512]{1,0:T(8,128)}, u32[]{:S(2)}, u32[]{:S(2)}) collective-permute-start(f32[1024,512]{1,0:T(8,128)} %near_rows.1), channel_id=1, source_target_pairs={{0,8},{8,0},{16,24},{24,16},{1,9},{9,1},{17,25},{25,17},{2,10},{10... | collective-permute-start | bytes 6291464 | tf_op jit(solution)/shard_map/ppermute | solution.py:43
  133.8 42.0 %collective-permute-start.32 = (bf16[1024,512]{1,0:T(8,128)(2,1)}, bf16[1024,512]{1,0:T(8,128)(2,1)}, u32[]{:S(2)}, u32[]{:S(2)}) collective-permute-start(bf16[1024,512]{1,0:T(8,128)(2,1)} %broadcast_select_fusion.2), channel_id=1, source_target_pairs={{0,1},{1,0},{4,5},{5,4},{10,11},{11,10},{14,15},{15,14},{20,21},{2... | collective-permute-start | bytes 3145736 | tf_op jit(solution)/shard_map/ppermute | solution.py:476
  145.3 3.1 %copy-start.1 = (bf16[256,512]{1,0:T(8,128)(2,1)}, bf16[256,512]{1,0:T(8,128)(2,1)S(1)}, u32[]{:S(2)}) copy-start(bf16[256,512]{1,0:T(8,128)(2,1)S(1)} %get-tuple-element.100.refs_4_) | copy-start | bytes 786436
  145.3 3.1 %copy-start.4 = (f32[128,128]{1,0:T(8,128)}, f32[128,128]{1,0:T(8,128)S(1)}, u32[]{:S(2)}) copy-start(f32[128,128]{1,0:T(8,128)S(1)} %get-tuple-element.108.refs_6_) | copy-start | bytes 196612
  145.3 3.1 %copy-start.6 = (bf16[128,128]{1,0:T(8,128)(2,1)}, bf16[128,128]{1,0:T(8,128)(2,1)S(1)}, u32[]{:S(2)}) copy-start(bf16[128,128]{1,0:T(8,128)(2,1)S(1)} %get-tuple-element.109.refs_7_) | copy-start | bytes 98308
  145.4 36.1 %collective-permute-start.25 = (f32[768,512]{1,0:T(8,128)}, f32[768,512]{1,0:T(8,128)}, u32[]{:S(2)}, u32[]{:S(2)}) collective-permute-start(f32[768,512]{1,0:T(8,128)} %far_sum.3), channel_id=1, source_target_pairs={{0,16},{8,24},{16,0},{24,8},{1,17},{9,25},{17,1},{25,9},{2,18},{10... | collective-permute-start | bytes 4718600 | tf_op jit(solution)/shard_map/ppermute | solution.py:43
  145.4 1.6 collective-permute-start.26
  148.5 22.8 %collective-permute-start.31 = (bf16[512,512]{1,0:T(8,128)(2,1)}, bf16[512,512]{1,0:T(8,128)(2,1)}, u32[]{:S(2)}, u32[]{:S(2)}) collective-permute-start(bf16[512,512]{1,0:T(8,128)(2,1)} %broadcast_select_fusion.5), channel_id=1, source_target_pairs={{0,2},{1,3},{4,6},{5,7},{10,8},{11,9},{14,12},{15,13},{20,22},{21,... | collective-permute-start | bytes 1572872 | tf_op jit(solution)/shard_map/ppermute | solution.py:464
  149.8 20.0 %collective-permute-start.30 = (bf16[256,512]{1,0:T(8,128)(2,1)S(1)}, bf16[256,512]{1,0:T(8,128)(2,1)S(1)}, u32[]{:S(2)}, u32[]{:S(2)}) collective-permute-start(bf16[256,512]{1,0:T(8,128)(2,1)S(1)} %broadcast_select_fusion.7), channel_id=1, source_target_pairs={{0,2},{1,3},{4,6},{5,7},{10,8},{11,9},{14,12},{15,13},{20,22},{21,... | collective-permute-start | bytes 786440 | tf_op jit(solution)/shard_map/ppermute | solution.py:464
  169.8 17.9 %collective-permute-start.34 = (bf16[512,512]{1,0:T(8,128)(2,1)}, bf16[512,512]{1,0:T(8,128)(2,1)}, u32[]{:S(2)}, u32[]{:S(2)}) collective-permute-start(bf16[512,512]{1,0:T(8,128)(2,1)} %broadcast_select_fusion.5), channel_id=1, source_target_pairs={{0,1},{1,0},{4,5},{5,4},{10,11},{11,10},{14,15},{15,14},{20,21},{2... | collective-permute-start | bytes 1572872 | tf_op jit(solution)/shard_map/ppermute | solution.py:476
  171.3 27.4 %collective-permute-start.29 = (bf16[1024,512]{1,0:T(8,128)(2,1)}, bf16[1024,512]{1,0:T(8,128)(2,1)}, u32[]{:S(2)}, u32[]{:S(2)}) collective-permute-start(bf16[1024,512]{1,0:T(8,128)(2,1)} %collective-permute-done.28), channel_id=1, source_target_pairs={{2,3},{3,2},{6,7},{7,6},{8,9},{9,8},{12,13},{13,12},{22,23},{23,22... | collective-permute-start | bytes 3145736 | tf_op jit(solution)/shard_map/ppermute | solution.py:476
  175.8 21.8 %collective-permute-start.33 = (bf16[512,512]{1,0:T(8,128)(2,1)}, bf16[512,512]{1,0:T(8,128)(2,1)}, u32[]{:S(2)}, u32[]{:S(2)}) collective-permute-start(bf16[512,512]{1,0:T(8,128)(2,1)} %collective-permute-done.31), channel_id=1, source_target_pairs={{2,3},{3,2},{6,7},{7,6},{8,9},{9,8},{12,13},{13,12},{22,23},{23,22... | collective-permute-start | bytes 1572872 | tf_op jit(solution)/shard_map/ppermute | solution.py:476
  178.5 23.6 %collective-permute-start.35 = (bf16[256,512]{1,0:T(8,128)(2,1)S(1)}, bf16[256,512]{1,0:T(8,128)(2,1)S(1)}, u32[]{:S(2)}, u32[]{:S(2)}) collective-permute-start(bf16[256,512]{1,0:T(8,128)(2,1)S(1)} %broadcast_select_fusion.6.refs_11_), channel_id=1, source_target_pairs={{0,1},{1,0},{4,5},{5,4},{2,3},{3,2},{6,7},{7,6},{10,11},{11,10},{1... | collective-permute-start | bytes 786440 | tf_op jit(solution)/shard_map/ppermute | solution.py:476
  187.6 12.4 %copy-start = (f32[1024,512]{1,0:T(8,128)S(1)}, f32[1024,512]{1,0:T(8,128)}, u32[]{:S(2)}) copy-start(f32[1024,512]{1,0:T(8,128)} %base_rows.1.refs_1_) | copy-start | bytes 6291460
  (5 other events, 9.3 us)

commit v9 on v7

--- a/solution.py
+++ b/solution.py
@@ -360,9 +360,14 @@
         return value + flip(value, "mem", hops[at])
 
     tie = lax.optimization_barrier
-    for at in range(last + 1):
+    for at in range(last):
         table_rows = table_hop(table_rows, at)
     head = table_hop(head, 0)
+    table_rows, head, rest, w_lead = tie((table_rows, head, rest, w_lead))
+    table_rows = table_hop(table_rows, last)
+    for at in range(1, last):
+        head = table_hop(head, at)
+        rest = table_hop(rest, at - 1)
     w_lead = lead_hop(w_lead, 0)
     table_rows, head, rest, w_lead = tie((table_rows, head, rest, w_lead))
     table = table_rows[0, :count].astype(jnp.int32)
@@ -383,22 +388,18 @@
             adds, name,
         )
 
-    diagonal = rows_at(0, n, [], "far_rows")
     first = rows_at(
         4 * n, PR, [(root_front, 0, 0)], "first_rows", (g == 0).astype(jnp.int32).reshape(1), PR
     )
-    for at in range(1, last):
-        head = table_hop(head, at)
-        rest = table_hop(rest, at - 1)
-    head, rest, diagonal, first, w_lead = tie((head, rest, diagonal, first, w_lead))
-    near = rows_at(2 * n, n, [], "near_rows")
     first = first + flip(first, "grp", CORE)
     head = table_hop(head, last)
     rest = table_hop(rest, last - 1)
     w_lead = lead_hop(w_lead, 1)
-    head, rest, w_lead, diagonal, first, near = tie((head, rest, w_lead, diagonal, first, near))
+    diagonal = rows_at(0, n, [], "far_rows")
+    near = rows_at(2 * n, n, [], "near_rows")
+    head, rest, w_lead, first, diagonal, near = tie((head, rest, w_lead, first, diagonal, near))
+    diagonal = flip(diagonal, "grp", CORE)
     near = flip(near, "grp", CORE)
-    diagonal = flip(diagonal, "grp", CORE)
     first = first + flip(first, "grp", CHIP)
     rest = table_hop(rest, last)
     for at in range(2, last + 1):
@@ -422,8 +423,7 @@
         name="leaf_two",
     )(head, front, front, mask)
 
-    p01, rest, w_lead, first, diagonal = tie((p01, rest, w_lead, first, diagonal))
-    far_near = flip(rows_at(n, ways, [(diagonal, 0, 0)], "far_sum"), "grp", CHIP)
+    p01, rest, w_lead, first = tie((p01, rest, w_lead, first))
 
     def across(value):
         far_value = flip(value, "grp", CHIP)
@@ -491,16 +491,16 @@
         return [inner_hop((state[0], state[1]), i) for i in range(1, spread)]
 
     s01 = zone_hop(([0], d01, None))
+    pack, diagonal = tie((pack, diagonal))
     pack_far = flip(pack, "grp", CHIP)
-    pack, pack_far, diagonal, corner, far_near = tie(
-        (pack, pack_far, diagonal, corner, far_near)
-    )
+    far_near = flip(rows_at(n, ways, [(diagonal, 0, 0)], "far_sum"), "grp", CHIP)
+    pack, pack_far, diagonal, corner = tie((pack, pack_far, diagonal, corner))
     far_in = rows_at(n + ways, ways, [(diagonal, 0, 1)], "far_sum")
     for at in range(2, last + 1):
         corner = lead_hop(corner, at)
     pack = jnp.concatenate([pack, pack_far], axis=0)
     pack = jnp.concatenate([pack, flip(pack, "grp", CORE)], axis=0)
-    pack, held, far_in, corner = tie((pack, s01[1], far_in, corner))
+    pack, held, far_in, far_near, corner = tie((pack, s01[1], far_in, far_near, corner))
     corner = corner[0] if leads == 1 else jnp.concatenate(corner, axis=1)
     s01 = (s01[0], held, None)
     far_last = flip(far_in, "grp", CHIP)
@@ -524,7 +524,7 @@
     sq_hop = zone_hop((sq_hop[0], q_held, None))
     early2 = early_hops(s2)
     s2 = zone_hop(s2)
-    q_held, far_last, *early01 = tie((sq_hop[1], far_last, *early01))
+    q_held, *early01 = tie((sq_hop[1], *early01))
     rq = inner_hops((sq_hop[0], q_held, None))
     r01 = inner_hops(s01, early01)
     r2 = inner_hops(s2, early2)

time: 202 us -> 202 us (level)
  the two profiles are of different devices: /device:TPU:1 before, /device:TPU:0 now
where the time goes in v9:
time: 202 us; the launch traced here: 201 us
  starting transfers between devices  63.3 us (31%)
  waiting for transfers between devices  58.1 us (29%)
  Pallas kernels  56.9 us (28%)
  other arithmetic  15.3 us (8%)
  local copies, waits for them, and re-layouts  5.98 us (3%)
    ppermute x19, waiting for transfers between devices, flip(): return lax.ppermute(value, axis, [(i, i ^ bit) for i in range(size)])  42.7 us
    pallas_call x6, Pallas kernels, take_rows(): pl.pallas_call(body, grid_spec=pltpu.PrefetchScalarGridSpec(num_scalar_pr...  21.8 us
    ppermute x19, starting transfers between devices, flip(): return lax.ppermute(value, axis, [(i, i ^ bit) for i in range(size)])  21.4 us
    ppermute x6, starting transfers between devices, lead_hop(): got = lax.ppermute(held, 'mem', [(src, src ^ bit) for src in sources])  17.3 us
    ppermute x6, starting transfers between devices, zone_hop(): got = lax.ppermute(held, ('grp', 'mem'), pairs)  15.5 us
    pallas_call x1, Pallas kernels, local(): pl.pallas_call(leaf_two, grid=(1,), in_specs=[vmem, w_spec(0), w_spec(1),...  9.42 us
    ppermute x5, starting transfers between devices, inner_hop(): return lax.ppermute(value, ('grp', 'mem'), pairs)  9.07 us
    pallas_call x1, Pallas kernels, local(): pl.pallas_call(root_step, in_specs=[smem] + [vmem] * 4, out_shape=(shape(...  8.96 us
  transfers between devices with their start and end apart: 36, of which 14 were waited for; matrix products, arithmetic and copies ran while one was open for 10% of the time, Pallas kernels for 25%

profile of v9, /device:TPU:0, one launch (start us, length us, event | category | flops | bytes accessed | tf_op | source)
XLA Modules:
  0.0 200.7 jit_solution(10444465032796276344)
XLA Ops:
  0.6 2.1 %pick_pivots.1 = (f32[8,128]{1,0:T(8,128)}, f32[384,128]{1,0:T(8,128)}, f32[384,128]{1,0:T(8,128)}, f32[8,512]{1,0:T(8,128)}, f32[384,256]{1,0:T(8,128)}) custom-call(s32[4]{0:T(128)} %bitcast.55, s32[1]{0:T(128)} %bitcast.2.at_ref, f32[4096,512]{1,0:T(8,128)} %bitcast.29), custom_call_target="tpu_custom_call" | custom-call | tf_op jit(solution)/shard_map/pick_pivots/pallas_call | solution.py:346
  2.7 3.0 %collective-permute-start = (f32[8,128]{1,0:T(8,128)}, f32[8,128]{1,0:T(8,128)S(1)}, u32[]{:S(2)}, u32[]{:S(2)}) collective-permute-start(f32[8,128]{1,0:T(8,128)} %get-tuple-element.55), channel_id=1, source_target_pairs={{0,1},{1,0},{2,3},{3,2},{4,5},{5,4},{6,7},{7,6},{8,9},{9,8},{10,11... | collective-permute-start | bytes 12296 | tf_op jit(solution)/shard_map/ppermute | solution.py:43
  5.8 1.7 collective-permute-done
  8.2 2.1 %collective-permute-start.1 = (f32[8,128]{1,0:T(8,128)S(1)}, f32[8,128]{1,0:T(8,128)S(1)}, u32[]{:S(2)}, u32[]{:S(2)}) collective-permute-start(f32[8,128]{1,0:T(8,128)S(1)} %add.150), channel_id=1, source_target_pairs={{0,2},{1,3},{2,0},{3,1},{4,6},{5,7},{6,4},{7,5},{8,10},{9,11},{10,... | collective-permute-start | bytes 12296 | tf_op jit(solution)/shard_map/ppermute | solution.py:43
  10.4 1.5 collective-permute-done.1
  13.2 4.5 %collective-permute-start.6 = (f32[384,256]{1,0:T(8,128)}, f32[384,256]{1,0:T(8,128)S(1)}, u32[]{:S(2)}, u32[]{:S(2)}) collective-permute-start(f32[384,256]{1,0:T(8,128)} %get-tuple-element.62), channel_id=1, source_target_pairs={{0,4},{8,12},{16,20},{24,28}} | collective-permute-start | bytes 1179656 | tf_op jit(solution)/shard_map/ppermute | solution.py:342
  18.0 1.8 collective-permute-start.3
  19.9 9.6 %collective-permute-done.3 = f32[8,128]{1,0:T(8,128)S(1)} collective-permute-done((f32[8,128]{1,0:T(8,128)S(1)}, f32[8,128]{1,0:T(8,128)S(1)}, u32[]{:S(2)}, u32[]{:S(2)}) %collective-permute-start.3) | collective-permute-done | bytes 4128 | tf_op jit(solution)/shard_map/ppermute | solution.py:43
  33.9 2.8 %first_rows.1 = f32[256,512]{1,0:T(8,128)} custom-call(s32[2]{0:T(128)} %slice.51.refs_0_, s32[2]{0:T(128)} %slice.52.refs_1_, s32[1]{0:T(128)} %bitcast.10.refs_2_, f32[4096,512]{1,0:T(8,128)} %bitcast.30, f32[4096,512]{1,0:T(8,128)} %bitcast.31, f32[8,512]{1,0:T(8,128)} %get-tuple-element.64.refs_5_.refs_7_.mask_ref, f32[1024,512]{1,0:T(8,128)} %refs_8_.1), custom_call_target="tpu_custom_call" | custom-call | tf_op jit(solution)/shard_map/first_rows/pallas_call | solution.py:214
  37.3 3.4 %collective-permute-start.7 = (f32[384,128]{1,0:T(8,128)S(1)}, f32[384,128]{1,0:T(8,128)S(1)}, u32[]{:S(2)}, u32[]{:S(2)}) collective-permute-start(f32[384,128]{1,0:T(8,128)S(1)} %add.154), channel_id=1, source_target_pairs={{0,4},{1,5},{2,6},{3,7},{4,0},{5,1},{6,2},{7,3},{8,12},{9,13},{10,... | collective-permute-start | bytes 589832 | tf_op jit(solution)/shard_map/ppermute | solution.py:43
  41.3 3.3 %far_rows.1 = f32[1024,512]{1,0:T(8,128)} custom-call(s32[8]{0:T(128)} %get-tuple-element.118.refs_0_, s32[8]{0:T(128)} %get-tuple-element.115.refs_1_, s32[1]{0:T(128)} %constant.64.clone.1.refs_2_, f32[4096,512]{1,0:T(8,128)} %bitcast.32, f32[4096,512]{1,0:T(8,128)} %bitcast.33, f32[4096,512]{1,0:T(8,128)} %bitcast.34, f32[4096,512]{1,0:T(8,128)} %bitcast.35, ...), custom_call_target="tpu_custom_call" | custom-call | tf_op jit(solution)/shard_map/far_rows/pallas_call | solution.py:214
  44.7 3.3 %near_rows.1 = f32[1024,512]{1,0:T(8,128)} custom-call(s32[8]{0:T(128)} %get-tuple-element.117.refs_0_, s32[8]{0:T(128)} %get-tuple-element.114.refs_1_, s32[1]{0:T(128)} %constant.64.clone.1.refs_2_, f32[4096,512]{1,0:T(8,128)} %bitcast.36, f32[4096,512]{1,0:T(8,128)} %bitcast.37, f32[4096,512]{1,0:T(8,128)} %bitcast.38, f32[4096,512]{1,0:T(8,128)} %bitcast.39, ...), custom_call_target="tpu_custom_call" | custom-call | tf_op jit(solution)/shard_map/near_rows/pallas_call | solution.py:214
  48.0 2.6 %collective-permute-done.7 = f32[384,128]{1,0:T(8,128)S(1)} collective-permute-done((f32[384,128]{1,0:T(8,128)S(1)}, f32[384,128]{1,0:T(8,128)S(1)}, u32[]{:S(2)}, u32[]{:S(2)}) %collective-permute-start.7) | collective-permute-done | bytes 196640 | tf_op jit(solution)/shard_map/ppermute | solution.py:43
  51.6 2.9 %collective-permute-start.13 = (f32[384,256]{1,0:T(8,128)S(1)}, f32[384,256]{1,0:T(8,128)S(1)}, u32[]{:S(2)}, u32[]{:S(2)}) collective-permute-start(f32[384,256]{1,0:T(8,128)S(1)} %broadcast_select_fusion.9), channel_id=1, source_target_pairs={{0,2},{1,3},{4,6},{5,7},{8,10},{9,11},{12,14},{13,15},{16,18},{17,... | collective-permute-start | bytes 1179656 | tf_op jit(solution)/shard_map/ppermute | solution.py:342
  54.5 1.6 collective-permute-start.14
  56.3 9.4 %leaf_two.1 = (bf16[256,512]{1,0:T(8,128)(2,1)}, f32[128,128]{1,0:T(8,128)}, f32[128,128]{1,0:T(8,128)}, bf16[128,128]{1,0:T(8,128)(2,1)}, f32[8,128]{1,0:T(8,128)}) custom-call(f32[384,128]{1,0:T(8,128)} %add.158.head_ref, f32[4096,512]{1,0:T(8,128)} %bitcast.41, f32[4096,512]{1,0:T(8,128)} %bitcast.40, f32[8,512]{1,0:T(8,128)} %get-tuple-element.64.refs_5_.refs_7_.mask_ref), custom_call_target="tpu_custom_call" | custom-call | tf_op jit(solution)/shard_map/leaf_two/pallas_call | solution.py:416
  65.7 2.0 collective-permute-done.12
  69.3 1.6 collective-permute-start.15
  70.8 6.4 %collective-permute-done.15 = bf16[256,512]{1,0:T(8,128)(2,1)S(1)} collective-permute-done((bf16[256,512]{1,0:T(8,128)(2,1)S(1)}, bf16[256,512]{1,0:T(8,128)(2,1)S(1)}, u32[]{:S(2)}, u32[]{:S(2)}) %collective-permute-start.15) | collective-permute-done | bytes 262176 | tf_op jit(solution)/shard_map/ppermute | solution.py:43
  77.4 5.3 %collective-permute-start.17 = (f32[256,256]{1,0:T(8,128)S(1)}, f32[256,256]{1,0:T(8,128)S(1)}, u32[]{:S(2)}, u32[]{:S(2)}) collective-permute-start(f32[256,256]{1,0:T(8,128)S(1)} %slice.57), channel_id=1, source_target_pairs={{0,4},{8,12},{16,20},{24,28}} | collective-permute-start | bytes 786440 | tf_op jit(solution)/shard_map/ppermute | solution.py:342
  82.7 6.2 %collective-permute-done.17 = f32[256,256]{1,0:T(8,128)S(1)} collective-permute-done((f32[256,256]{1,0:T(8,128)S(1)}, f32[256,256]{1,0:T(8,128)S(1)}, u32[]{:S(2)}, u32[]{:S(2)}) %collective-permute-start.17) | collective-permute-done | bytes 262176 | tf_op jit(solution)/shard_map/ppermute | solution.py:342
  89.1 5.4 %collective-permute-start.22 = (bf16[1024,512]{1,0:T(8,128)(2,1)S(1)}, bf16[1024,512]{1,0:T(8,128)(2,1)S(1)}, u32[]{:S(2)}, u32[]{:S(2)}) collective-permute-start(bf16[1024,512]{1,0:T(8,128)(2,1)S(1)} %pad_maximum_fusion.1.d01_ref.refs_2_), channel_id=1, source_target_pairs={{0,4},{1,5},{10,14},{11,15},{20,16},{21,17},{30,26},{31,27}} | collective-permute-start | bytes 3145736 | tf_op jit(solution)/shard_map/ppermute | solution.py:465
  94.5 2.0 %collective-permute-start.20 = (f32[256,256]{1,0:T(8,128)S(1)}, f32[256,256]{1,0:T(8,128)}, u32[]{:S(2)}, u32[]{:S(2)}) collective-permute-start(f32[256,256]{1,0:T(8,128)S(1)} %broadcast_select_fusion.13), channel_id=1, source_target_pairs={{0,1},{4,5},{8,9},{12,13},{16,17},{20,21},{24,25},{28,29}} | collective-permute-start | bytes 786440 | tf_op jit(solution)/shard_map/ppermute | solution.py:342
  97.2 7.6 %leaf_last.1 = bf16[336,512]{1,0:T(8,128)(2,1)} custom-call(f32[384,128]{1,0:T(8,128)} %add.161.rest_ref, f32[4096,512]{1,0:T(8,128)} %bitcast.42, f32[384,256]{1,0:T(8,128)} %broadcast_select_fusion.8.w_lead_ref, f32[8,128]{1,0:T(8,128)} %copy-done.10, f32[8,512]{1,0:T(8,128)} %get-tuple-element.64.refs_5_.refs_7_.mask_ref, ...), custom_call_target="tpu_custom_call" | custom-call | tf_op jit(solution)/shard_map/leaf_last/pallas_call | solution.py:439
  106.2 3.5 %far_sum.3 = f32[512,512]{1,0:T(8,128)} custom-call(s32[4]{0:T(128)} %get-tuple-element.112.refs_0_, s32[4]{0:T(128)} %get-tuple-element.110.refs_1_, s32[1]{0:T(128)} %constant.64.clone.1.refs_2_, f32[4096,512]{1,0:T(8,128)} %bitcast.43, f32[4096,512]{1,0:T(8,128)} %bitcast.44, f32[4096,512]{1,0:T(8,128)} %bitcast.45, f32[4096,512]{1,0:T(8,128)} %bitcast.46, ...), custom_call_target="tpu_custom_call" | custom-call | tf_op jit(solution)/shard_map/far_sum/pallas_call | solution.py:214
  109.7 2.0 %collective-permute-start.23 = (f32[512,512]{1,0:T(8,128)}, f32[512,512]{1,0:T(8,128)}, u32[]{:S(2)}, u32[]{:S(2)}) collective-permute-start(f32[512,512]{1,0:T(8,128)} %far_sum.3), channel_id=1, source_target_pairs={{0,16},{8,24},{16,0},{24,8},{1,17},{9,25},{17,1},{25,9},{2,18},{10... | collective-permute-start | bytes 3145736 | tf_op jit(solution)/shard_map/ppermute | solution.py:43
  111.7 4.1 %collective-permute-done.19 = bf16[336,512]{1,0:T(8,128)(2,1)S(1)} collective-permute-done((bf16[336,512]{1,0:T(8,128)(2,1)}, bf16[336,512]{1,0:T(8,128)(2,1)S(1)}, u32[]{:S(2)}, u32[]{:S(2)}) %collective-permute-start.19) | collective-permute-done | bytes 344096 | tf_op jit(solution)/shard_map/ppermute | solution.py:43
  119.6 3.5 %far_sum.2 = f32[512,512]{1,0:T(8,128)} custom-call(s32[4]{0:T(128)} %get-tuple-element.113.refs_0_, s32[4]{0:T(128)} %get-tuple-element.111.refs_1_, s32[1]{0:T(128)} %constant.64.clone.1.refs_2_, f32[4096,512]{1,0:T(8,128)} %bitcast.47, f32[4096,512]{1,0:T(8,128)} %bitcast.48, f32[4096,512]{1,0:T(8,128)} %bitcast.49, f32[4096,512]{1,0:T(8,128)} %bitcast.50, ...), custom_call_target="tpu_custom_call" | custom-call | tf_op jit(solution)/shard_map/far_sum/pallas_call | solution.py:214
  123.1 1.7 collective-permute-done.24
  126.0 8.8 %collective-permute-done.23.refs_10_ = f32[512,512]{1,0:T(8,128)} collective-permute-done((f32[512,512]{1,0:T(8,128)}, f32[512,512]{1,0:T(8,128)}, u32[]{:S(2)}, u32[]{:S(2)}) %collective-permute-start.23) | collective-permute-done | bytes 1048608 | tf_op jit(solution)/shard_map/ppermute | solution.py:43
  134.8 2.3 %collective-permute-start.28 = (bf16[1024,512]{1,0:T(8,128)(2,1)}, bf16[1024,512]{1,0:T(8,128)(2,1)}, u32[]{:S(2)}, u32[]{:S(2)}) collective-permute-start(bf16[1024,512]{1,0:T(8,128)(2,1)} %broadcast_select_fusion.2), channel_id=1, source_target_pairs={{0,2},{1,3},{4,6},{5,7},{10,8},{11,9},{14,12},{15,13},{20,22},{21,... | collective-permute-start | bytes 3145736 | tf_op jit(solution)/shard_map/ppermute | solution.py:465
  137.2 3.1 %collective-permute-start.27 = (bf16[512,512]{1,0:T(8,128)(2,1)S(1)}, bf16[512,512]{1,0:T(8,128)(2,1)S(1)}, u32[]{:S(2)}, u32[]{:S(2)}) collective-permute-start(bf16[512,512]{1,0:T(8,128)(2,1)S(1)} %bitcast.27), channel_id=1, source_target_pairs={{0,4},{1,5},{10,14},{11,15},{20,16},{21,17},{30,26},{31,27}} | collective-permute-start | bytes 1572872 | tf_op jit(solution)/shard_map/ppermute | solution.py:465
  140.3 9.0 %root_step.1 = (bf16[256,512]{1,0:T(8,128)(2,1)S(1)}, f32[128,128]{1,0:T(8,128)S(1)}, f32[128,128]{1,0:T(8,128)S(1)}, bf16[128,128]{1,0:T(8,128)(2,1)S(1)}, f32[8,128]{1,0:T(8,128)S(1)}) custom-call(s32[4]{0:T(128)S(1)} %pad_add_fusion.1.leaf_ref, f32[256,256]{1,0:T(8,128)S(1)} %broadcast_select_fusion.11.corner_ref, f32[256,512]{1,0:T(8,128)S(1)} %add.162.first_ref, ...), custom_call_target="tpu_custom_call" | custom-call | tf_op jit(solution)/shard_map/root_step/pallas_call | solution.py:512
  151.2 1.9 collective-permute-start.31
  153.1 3.9 %collective-permute-done.26 = bf16[256,512]{1,0:T(8,128)(2,1)S(1)} collective-permute-done((bf16[256,512]{1,0:T(8,128)(2,1)S(1)}, bf16[256,512]{1,0:T(8,128)(2,1)S(1)}, u32[]{:S(2)}, u32[]{:S(2)}) %collective-permute-start.26) | collective-permute-done | bytes 262176 | tf_op jit(solution)/shard_map/ppermute | solution.py:465
  157.1 4.9 %collective-permute-start.25 = (f32[512,512]{1,0:T(8,128)}, f32[512,512]{1,0:T(8,128)}, u32[]{:S(2)}, u32[]{:S(2)}) collective-permute-start(f32[512,512]{1,0:T(8,128)} %far_sum.2), channel_id=1, source_target_pairs={{0,16},{8,24},{16,0},{24,8},{1,17},{9,25},{17,1},{25,9},{2,18},{10... | collective-permute-start | bytes 3145736 | tf_op jit(solution)/shard_map/ppermute | solution.py:43
  163.0 1.3 broadcast_select_fusion.1.refs_3_
  164.3 2.1 %collective-permute-start.32 = (bf16[512,512]{1,0:T(8,128)(2,1)}, bf16[512,512]{1,0:T(8,128)(2,1)}, u32[]{:S(2)}, u32[]{:S(2)}) collective-permute-start(bf16[512,512]{1,0:T(8,128)(2,1)} %broadcast_select_fusion.5), channel_id=1, source_target_pairs={{0,2},{1,3},{4,6},{5,7},{10,8},{11,9},{14,12},{15,13},{20,22},{21,... | collective-permute-start | bytes 1572872 | tf_op jit(solution)/shard_map/ppermute | solution.py:465
  166.4 1.7 collective-permute-start.29
  169.5 5.5 %collective-permute-done.25.refs_11_ = f32[512,512]{1,0:T(8,128)} collective-permute-done((f32[512,512]{1,0:T(8,128)}, f32[512,512]{1,0:T(8,128)}, u32[]{:S(2)}, u32[]{:S(2)}) %collective-permute-start.25) | collective-permute-done | bytes 1048608 | tf_op jit(solution)/shard_map/ppermute | solution.py:43
  175.1 1.9 collective-permute-start.34
  177.0 1.5 collective-permute-start.33
  179.0 5.5 %base_rows.1.refs_1_ = f32[1024,512]{1,0:T(8,128)} custom-call(s32[8]{0:T(128)} %get-tuple-element.119.refs_0_, s32[8]{0:T(128)} %get-tuple-element.116.refs_1_, s32[1]{0:T(128)} %constant.64.clone.1.refs_2_, f32[4096,512]{1,0:T(8,128)} %bitcast.51, f32[4096,512]{1,0:T(8,128)} %bitcast.52, f32[4096,512]{1,0:T(8,128)} %bitcast.53, f32[4096,512]{1,0:T(8,128)} %bitcast.54, ...), custom_call_target="tpu_custom_call" | custom-call | tf_op jit(solution)/shard_map/base_rows/pallas_call | solution.py:214
  184.5 2.1 %collective-permute-start.35 = (bf16[256,512]{1,0:T(8,128)(2,1)S(1)}, bf16[256,512]{1,0:T(8,128)(2,1)S(1)}, u32[]{:S(2)}, u32[]{:S(2)}) collective-permute-start(bf16[256,512]{1,0:T(8,128)(2,1)S(1)} %broadcast_select_fusion.6.refs_11_), channel_id=1, source_target_pairs={{0,1},{1,0},{4,5},{5,4},{2,3},{3,2},{6,7},{7,6},{10,11},{11,10},{1... | collective-permute-start | bytes 786440 | tf_op jit(solution)/shard_map/ppermute | solution.py:477
  187.7 3.5 %collective-permute-done.34 = bf16[512,512]{1,0:T(8,128)(2,1)} collective-permute-done((bf16[512,512]{1,0:T(8,128)(2,1)}, bf16[512,512]{1,0:T(8,128)(2,1)}, u32[]{:S(2)}, u32[]{:S(2)}) %collective-permute-start.34) | collective-permute-done | bytes 524320 | tf_op jit(solution)/shard_map/ppermute | solution.py:477
  192.3 1.4 broadcast_select_fusion.refs_4_
  193.7 2.1 %update.1.refs_2_ = f32[1024,512]{1,0:T(8,128)S(1)} custom-call(s32[2]{0:T(128)S(1)} %iota_xor_fusion.refs_0_, f32[1024,512]{1,0:T(8,128)S(1)} %copy-done, bf16[1024,512]{1,0:T(8,128)(2,1)S(1)} %pad_maximum_fusion.1.d01_ref.refs_2_, bf16[1024,512]{1,0:T(8,128)(2,1)S(1)} %broadcast_select_fusion.1.refs_3_, bf16[1024,512]{1,0:T(8,128)(2,1)S(1)} %broadcast_select_fusion.refs_4_), custom_call_target="tpu_custom_call" | custom-call | tf_op jit(solution)/shard_map/update/pallas_call | solution.py:542
  195.8 4.9 %finish.1 = f32[1024,512]{1,0:T(8,128)} custom-call(s32[2]{0:T(128)S(1)} %iota_xor_fusion.refs_0_, s32[3]{0:T(128)S(1)} %pad_add_fusion.refs_1_, f32[1024,512]{1,0:T(8,128)S(1)} %update.1.refs_2_, bf16[512,512]{1,0:T(8,128)(2,1)S(1)} %bitcast.28, bf16[256,512]{1,0:T(8,128)(2,1)S(1)} %get-tuple-element.96.refs_4_, f32[128,128]{1,0:T(8,128)S(1)} %get-tuple-element.102.refs_5_, ...), custom_call_target="tpu_custom_call" | custom-call | tf_op jit(solution)/shard_map/finish/pallas_call | solution.py:567
  (114 shorter events, 25.5 us)
Async XLA Ops:
  2.7 27.7 %copy-start.9 = (f32[384,256]{1,0:T(8,128)S(1)}, f32[384,256]{1,0:T(8,128)}, u32[]{:S(2)}) copy-start(f32[384,256]{1,0:T(8,128)} %get-tuple-element.62) | copy-start | bytes 1179652
  2.7 4.8 %collective-permute-start = (f32[8,128]{1,0:T(8,128)}, f32[8,128]{1,0:T(8,128)S(1)}, u32[]{:S(2)}, u32[]{:S(2)}) collective-permute-start(f32[8,128]{1,0:T(8,128)} %get-tuple-element.55), channel_id=1, source_target_pairs={{0,1},{1,0},{2,3},{3,2},{4,5},{5,4},{6,7},{7,6},{8,9},{9,8},{10,11... | collective-permute-start | bytes 12296 | tf_op jit(solution)/shard_map/ppermute | solution.py:43
  5.7 6.6 %collective-permute-start.2 = (f32[384,128]{1,0:T(8,128)}, f32[384,128]{1,0:T(8,128)S(1)}, u32[]{:S(2)}, u32[]{:S(2)}) collective-permute-start(f32[384,128]{1,0:T(8,128)} %get-tuple-element.56), channel_id=1, source_target_pairs={{0,1},{1,0},{2,3},{3,2},{4,5},{5,4},{6,7},{7,6},{8,9},{9,8},{10,11... | collective-permute-start | bytes 589832 | tf_op jit(solution)/shard_map/ppermute | solution.py:43
  8.2 3.7 %collective-permute-start.1 = (f32[8,128]{1,0:T(8,128)S(1)}, f32[8,128]{1,0:T(8,128)S(1)}, u32[]{:S(2)}, u32[]{:S(2)}) collective-permute-start(f32[8,128]{1,0:T(8,128)S(1)} %add.150), channel_id=1, source_target_pairs={{0,2},{1,3},{2,0},{3,1},{4,6},{5,7},{6,4},{7,5},{8,10},{9,11},{10,... | collective-permute-start | bytes 12296 | tf_op jit(solution)/shard_map/ppermute | solution.py:43
  13.2 17.2 %collective-permute-start.6 = (f32[384,256]{1,0:T(8,128)}, f32[384,256]{1,0:T(8,128)S(1)}, u32[]{:S(2)}, u32[]{:S(2)}) collective-permute-start(f32[384,256]{1,0:T(8,128)} %get-tuple-element.62), channel_id=1, source_target_pairs={{0,4},{8,12},{16,20},{24,28}} | collective-permute-start | bytes 1179656 | tf_op jit(solution)/shard_map/ppermute | solution.py:342
  17.8 11.6 %collective-permute-start.4 = (f32[384,128]{1,0:T(8,128)S(1)}, f32[384,128]{1,0:T(8,128)S(1)}, u32[]{:S(2)}, u32[]{:S(2)}) collective-permute-start(f32[384,128]{1,0:T(8,128)S(1)} %add.152), channel_id=1, source_target_pairs={{0,2},{1,3},{2,0},{3,1},{4,6},{5,7},{6,4},{7,5},{8,10},{9,11},{10,... | collective-permute-start | bytes 589832 | tf_op jit(solution)/shard_map/ppermute | solution.py:43
  17.9 11.6 %collective-permute-start.5 = (f32[384,128]{1,0:T(8,128)}, f32[384,128]{1,0:T(8,128)S(1)}, u32[]{:S(2)}, u32[]{:S(2)}) collective-permute-start(f32[384,128]{1,0:T(8,128)} %get-tuple-element.61), channel_id=1, source_target_pairs={{0,1},{1,0},{2,3},{3,2},{4,5},{5,4},{6,7},{7,6},{8,9},{9,8},{10,11... | collective-permute-start | bytes 589832 | tf_op jit(solution)/shard_map/ppermute | solution.py:43
  18.0 11.5 %collective-permute-start.3 = (f32[8,128]{1,0:T(8,128)S(1)}, f32[8,128]{1,0:T(8,128)S(1)}, u32[]{:S(2)}, u32[]{:S(2)}) collective-permute-start(f32[8,128]{1,0:T(8,128)S(1)} %add.151), channel_id=1, source_target_pairs={{0,4},{1,5},{2,6},{3,7},{4,0},{5,1},{6,2},{7,3},{8,12},{9,13},{10,... | collective-permute-start | bytes 12296 | tf_op jit(solution)/shard_map/ppermute | solution.py:43
  29.5 7.2 %copy-start.10 = (f32[8,128]{1,0:T(8,128)}, f32[8,128]{1,0:T(8,128)S(1)}, u32[]{:S(2)}) copy-start(f32[8,128]{1,0:T(8,128)S(1)} %add.153.table_ref) | copy-start | bytes 12292
  30.5 20.8 %collective-permute-start.9 = (f32[384,256]{1,0:T(8,128)S(1)}, f32[384,256]{1,0:T(8,128)S(1)}, u32[]{:S(2)}, u32[]{:S(2)}) collective-permute-start(f32[384,256]{1,0:T(8,128)S(1)} %broadcast_select_fusion.10), channel_id=1, source_target_pairs={{0,1},{4,5},{8,9},{12,13},{16,17},{20,21},{24,25},{28,29}} | collective-permute-start | bytes 1179656 | tf_op jit(solution)/shard_map/ppermute | solution.py:342
  36.6 14.8 %collective-permute-start.10 = (f32[256,512]{1,0:T(8,128)}, f32[256,512]{1,0:T(8,128)S(1)}, u32[]{:S(2)}, u32[]{:S(2)}) collective-permute-start(f32[256,512]{1,0:T(8,128)} %first_rows.1), channel_id=1, source_target_pairs={{0,8},{8,0},{16,24},{24,16},{1,9},{9,1},{17,25},{25,17},{2,10},{10... | collective-permute-start | bytes 1572872 | tf_op jit(solution)/shard_map/ppermute | solution.py:43
  37.3 13.3 %collective-permute-start.7 = (f32[384,128]{1,0:T(8,128)S(1)}, f32[384,128]{1,0:T(8,128)S(1)}, u32[]{:S(2)}, u32[]{:S(2)}) collective-permute-start(f32[384,128]{1,0:T(8,128)S(1)} %add.154), channel_id=1, source_target_pairs={{0,4},{1,5},{2,6},{3,7},{4,0},{5,1},{6,2},{7,3},{8,12},{9,13},{10,... | collective-permute-start | bytes 589832 | tf_op jit(solution)/shard_map/ppermute | solution.py:43
  40.7 10.6 %collective-permute-start.8 = (f32[384,128]{1,0:T(8,128)S(1)}, f32[384,128]{1,0:T(8,128)S(1)}, u32[]{:S(2)}, u32[]{:S(2)}) collective-permute-start(f32[384,128]{1,0:T(8,128)S(1)} %add.155), channel_id=1, source_target_pairs={{0,2},{1,3},{2,0},{3,1},{4,6},{5,7},{6,4},{7,5},{8,10},{9,11},{10,... | collective-permute-start | bytes 589832 | tf_op jit(solution)/shard_map/ppermute | solution.py:43
  48.0 3.5 %copy-start.5 = (f32[256,512]{1,0:T(8,128)S(1)}, f32[256,512]{1,0:T(8,128)}, u32[]{:S(2)}) copy-start(f32[256,512]{1,0:T(8,128)} %first_rows.1) | copy-start | bytes 1572868
  51.5 53.2 %collective-permute-start.18 = (f32[1024,512]{1,0:T(8,128)}, f32[1024,512]{1,0:T(8,128)}, u32[]{:S(2)}, u32[]{:S(2)}) collective-permute-start(f32[1024,512]{1,0:T(8,128)} %far_rows.1), channel_id=1, source_target_pairs={{0,8},{8,0},{16,24},{24,16},{1,9},{9,1},{17,25},{25,17},{2,10},{10... | collective-permute-start | bytes 6291464 | tf_op jit(solution)/shard_map/ppermute | solution.py:43
  51.6 16.7 %collective-permute-start.13 = (f32[384,256]{1,0:T(8,128)S(1)}, f32[384,256]{1,0:T(8,128)S(1)}, u32[]{:S(2)}, u32[]{:S(2)}) collective-permute-start(f32[384,256]{1,0:T(8,128)S(1)} %broadcast_select_fusion.9), channel_id=1, source_target_pairs={{0,2},{1,3},{4,6},{5,7},{8,10},{9,11},{12,14},{13,15},{16,18},{17,... | collective-permute-start | bytes 1179656 | tf_op jit(solution)/shard_map/ppermute | solution.py:342
  54.5 14.7 %collective-permute-start.14 = (f32[256,512]{1,0:T(8,128)S(1)}, f32[256,512]{1,0:T(8,128)S(1)}, u32[]{:S(2)}, u32[]{:S(2)}) collective-permute-start(f32[256,512]{1,0:T(8,128)S(1)} %add.160), channel_id=1, source_target_pairs={{0,16},{8,24},{16,0},{24,8},{1,17},{9,25},{17,1},{25,9},{2,18},{10... | collective-permute-start | bytes 1572872 | tf_op jit(solution)/shard_map/ppermute | solution.py:43
  56.0 11.6 %collective-permute-start.12 = (f32[384,128]{1,0:T(8,128)S(1)}, f32[384,128]{1,0:T(8,128)S(1)}, u32[]{:S(2)}, u32[]{:S(2)}) collective-permute-start(f32[384,128]{1,0:T(8,128)S(1)} %add.159), channel_id=1, source_target_pairs={{0,4},{1,5},{2,6},{3,7},{4,0},{5,1},{6,2},{7,3},{8,12},{9,13},{10,... | collective-permute-start | bytes 589832 | tf_op jit(solution)/shard_map/ppermute | solution.py:43
  65.7 3.5 %copy-start.4 = (bf16[256,512]{1,0:T(8,128)(2,1)S(1)}, bf16[256,512]{1,0:T(8,128)(2,1)}, u32[]{:S(2)}) copy-start(bf16[256,512]{1,0:T(8,128)(2,1)} %get-tuple-element.75.p_ref) | copy-start | bytes 786436
  69.3 8.0 %collective-permute-start.15 = (bf16[256,512]{1,0:T(8,128)(2,1)S(1)}, bf16[256,512]{1,0:T(8,128)(2,1)S(1)}, u32[]{:S(2)}, u32[]{:S(2)}) collective-permute-start(bf16[256,512]{1,0:T(8,128)(2,1)S(1)} %copy-done.4), channel_id=1, source_target_pairs={{0,16},{8,24},{16,0},{24,8},{1,17},{9,25},{17,1},{25,9},{2,18},{10... | collective-permute-start | bytes 786440 | tf_op jit(solution)/shard_map/ppermute | solution.py:43
  77.3 11.7 %collective-permute-start.16 = (bf16[512,512]{1,0:T(8,128)(2,1)S(1)}, bf16[512,512]{1,0:T(8,128)(2,1)S(1)}, u32[]{:S(2)}, u32[]{:S(2)}) collective-permute-start(bf16[512,512]{1,0:T(8,128)(2,1)S(1)} %pad_maximum_fusion.3), channel_id=1, source_target_pairs={{0,8},{8,0},{16,24},{24,16},{1,9},{9,1},{17,25},{25,17},{2,10},{10... | collective-permute-start | bytes 1572872 | tf_op jit(solution)/shard_map/ppermute | solution.py:43
  77.4 11.5 %collective-permute-start.17 = (f32[256,256]{1,0:T(8,128)S(1)}, f32[256,256]{1,0:T(8,128)S(1)}, u32[]{:S(2)}, u32[]{:S(2)}) collective-permute-start(f32[256,256]{1,0:T(8,128)S(1)} %slice.57), channel_id=1, source_target_pairs={{0,4},{8,12},{16,20},{24,28}} | collective-permute-start | bytes 786440 | tf_op jit(solution)/shard_map/ppermute | solution.py:342
  89.1 29.4 %collective-permute-start.22 = (bf16[1024,512]{1,0:T(8,128)(2,1)S(1)}, bf16[1024,512]{1,0:T(8,128)(2,1)S(1)}, u32[]{:S(2)}, u32[]{:S(2)}) collective-permute-start(bf16[1024,512]{1,0:T(8,128)(2,1)S(1)} %pad_maximum_fusion.1.d01_ref.refs_2_), channel_id=1, source_target_pairs={{0,4},{1,5},{10,14},{11,15},{20,16},{21,17},{30,26},{31,27}} | collective-permute-start | bytes 3145736 | tf_op jit(solution)/shard_map/ppermute | solution.py:465
  94.5 10.9 %collective-permute-start.20 = (f32[256,256]{1,0:T(8,128)S(1)}, f32[256,256]{1,0:T(8,128)}, u32[]{:S(2)}, u32[]{:S(2)}) collective-permute-start(f32[256,256]{1,0:T(8,128)S(1)} %broadcast_select_fusion.13), channel_id=1, source_target_pairs={{0,1},{4,5},{8,9},{12,13},{16,17},{20,21},{24,25},{28,29}} | collective-permute-start | bytes 786440 | tf_op jit(solution)/shard_map/ppermute | solution.py:342
  104.8 11.0 %collective-permute-start.19 = (bf16[336,512]{1,0:T(8,128)(2,1)}, bf16[336,512]{1,0:T(8,128)(2,1)S(1)}, u32[]{:S(2)}, u32[]{:S(2)}) collective-permute-start(bf16[336,512]{1,0:T(8,128)(2,1)} %leaf_last.1), channel_id=1, source_target_pairs={{0,16},{8,24},{16,0},{24,8},{1,17},{9,25},{17,1},{25,9},{2,18},{10... | collective-permute-start | bytes 1032200 | tf_op jit(solution)/shard_map/ppermute | solution.py:43
  106.2 9.6 %copy-start.3 = (bf16[336,512]{1,0:T(8,128)(2,1)S(1)}, bf16[336,512]{1,0:T(8,128)(2,1)}, u32[]{:S(2)}) copy-start(bf16[336,512]{1,0:T(8,128)(2,1)} %leaf_last.1) | copy-start | bytes 1032196
  109.7 25.1 %collective-permute-start.23 = (f32[512,512]{1,0:T(8,128)}, f32[512,512]{1,0:T(8,128)}, u32[]{:S(2)}, u32[]{:S(2)}) collective-permute-start(f32[512,512]{1,0:T(8,128)} %far_sum.3), channel_id=1, source_target_pairs={{0,16},{8,24},{16,0},{24,8},{1,17},{9,25},{17,1},{25,9},{2,18},{10... | collective-permute-start | bytes 3145736 | tf_op jit(solution)/shard_map/ppermute | solution.py:43
  116.7 8.1 %collective-permute-start.21 = (bf16[672,512]{1,0:T(8,128)(2,1)}, bf16[672,512]{1,0:T(8,128)(2,1)}, u32[]{:S(2)}, u32[]{:S(2)}) collective-permute-start(bf16[672,512]{1,0:T(8,128)(2,1)} %pad_maximum_fusion.2), channel_id=1, source_target_pairs={{0,8},{8,0},{16,24},{24,16},{1,9},{9,1},{17,25},{25,17},{2,10},{10... | collective-permute-start | bytes 2064392 | tf_op jit(solution)/shard_map/ppermute | solution.py:43
  116.7 51.5 %collective-permute-start.11 = (f32[1024,512]{1,0:T(8,128)}, f32[1024,512]{1,0:T(8,128)}, u32[]{:S(2)}, u32[]{:S(2)}) collective-permute-start(f32[1024,512]{1,0:T(8,128)} %near_rows.1), channel_id=1, source_target_pairs={{0,8},{8,0},{16,24},{24,16},{1,9},{9,1},{17,25},{25,17},{2,10},{10... | collective-permute-start | bytes 6291464 | tf_op jit(solution)/shard_map/ppermute | solution.py:43
  117.2 7.6 %collective-permute-start.24 = (f32[256,256]{1,0:T(8,128)}, f32[256,256]{1,0:T(8,128)S(1)}, u32[]{:S(2)}, u32[]{:S(2)}) collective-permute-start(f32[256,256]{1,0:T(8,128)} %broadcast_select_fusion.12), channel_id=1, source_target_pairs={{0,2},{1,3},{4,6},{5,7},{8,10},{9,11},{12,14},{13,15},{16,18},{17,... | collective-permute-start | bytes 786440 | tf_op jit(solution)/shard_map/ppermute | solution.py:342
  119.6 5.2 %copy-start.8 = (f32[256,256]{1,0:T(8,128)S(1)}, f32[256,256]{1,0:T(8,128)}, u32[]{:S(2)}) copy-start(f32[256,256]{1,0:T(8,128)} %broadcast_select_fusion.12) | copy-start | bytes 786436
  134.8 28.2 %collective-permute-start.28 = (bf16[1024,512]{1,0:T(8,128)(2,1)}, bf16[1024,512]{1,0:T(8,128)(2,1)}, u32[]{:S(2)}, u32[]{:S(2)}) collective-permute-start(bf16[1024,512]{1,0:T(8,128)(2,1)} %broadcast_select_fusion.2), channel_id=1, source_target_pairs={{0,2},{1,3},{4,6},{5,7},{10,8},{11,9},{14,12},{15,13},{20,22},{21,... | collective-permute-start | bytes 3145736 | tf_op jit(solution)/shard_map/ppermute | solution.py:465
  137.2 24.9 %collective-permute-start.27 = (bf16[512,512]{1,0:T(8,128)(2,1)S(1)}, bf16[512,512]{1,0:T(8,128)(2,1)S(1)}, u32[]{:S(2)}, u32[]{:S(2)}) collective-permute-start(bf16[512,512]{1,0:T(8,128)(2,1)S(1)} %bitcast.27), channel_id=1, source_target_pairs={{0,4},{1,5},{10,14},{11,15},{20,16},{21,17},{30,26},{31,27}} | collective-permute-start | bytes 1572872 | tf_op jit(solution)/shard_map/ppermute | solution.py:465
  149.3 0.6 copy-start.1
  149.9 7.2 %collective-permute-start.26 = (bf16[256,512]{1,0:T(8,128)(2,1)S(1)}, bf16[256,512]{1,0:T(8,128)(2,1)S(1)}, u32[]{:S(2)}, u32[]{:S(2)}) collective-permute-start(bf16[256,512]{1,0:T(8,128)(2,1)S(1)} %get-tuple-element.96.refs_4_), channel_id=1, source_target_pairs={{0,4},{1,5},{10,14},{11,15},{20,16},{21,17},{30,26},{31,27}} | collective-permute-start | bytes 786440 | tf_op jit(solution)/shard_map/ppermute | solution.py:465
  151.2 33.3 %collective-permute-start.31 = (bf16[1024,512]{1,0:T(8,128)(2,1)}, bf16[1024,512]{1,0:T(8,128)(2,1)}, u32[]{:S(2)}, u32[]{:S(2)}) collective-permute-start(bf16[1024,512]{1,0:T(8,128)(2,1)} %broadcast_select_fusion.2), channel_id=1, source_target_pairs={{0,1},{1,0},{4,5},{5,4},{10,11},{11,10},{14,15},{15,14},{20,21},{2... | collective-permute-start | bytes 3145736 | tf_op jit(solution)/shard_map/ppermute | solution.py:477
  157.1 18.0 %collective-permute-start.25 = (f32[512,512]{1,0:T(8,128)}, f32[512,512]{1,0:T(8,128)}, u32[]{:S(2)}, u32[]{:S(2)}) collective-permute-start(f32[512,512]{1,0:T(8,128)} %far_sum.2), channel_id=1, source_target_pairs={{0,16},{8,24},{16,0},{24,8},{1,17},{9,25},{17,1},{25,9},{2,18},{10... | collective-permute-start | bytes 3145736 | tf_op jit(solution)/shard_map/ppermute | solution.py:43
  162.0 6.1 %copy-start.6 = (bf16[256,512]{1,0:T(8,128)(2,1)}, bf16[256,512]{1,0:T(8,128)(2,1)S(1)}, u32[]{:S(2)}) copy-start(bf16[256,512]{1,0:T(8,128)(2,1)S(1)} %broadcast_select_fusion.7) | copy-start | bytes 786436
  164.3 12.7 %collective-permute-start.32 = (bf16[512,512]{1,0:T(8,128)(2,1)}, bf16[512,512]{1,0:T(8,128)(2,1)}, u32[]{:S(2)}, u32[]{:S(2)}) collective-permute-start(bf16[512,512]{1,0:T(8,128)(2,1)} %broadcast_select_fusion.5), channel_id=1, source_target_pairs={{0,2},{1,3},{4,6},{5,7},{10,8},{11,9},{14,12},{15,13},{20,22},{21,... | collective-permute-start | bytes 1572872 | tf_op jit(solution)/shard_map/ppermute | solution.py:465
  166.4 25.9 %collective-permute-start.29 = (bf16[1024,512]{1,0:T(8,128)(2,1)}, bf16[1024,512]{1,0:T(8,128)(2,1)}, u32[]{:S(2)}, u32[]{:S(2)}) collective-permute-start(bf16[1024,512]{1,0:T(8,128)(2,1)} %collective-permute-done.28), channel_id=1, source_target_pairs={{2,3},{3,2},{6,7},{7,6},{8,9},{9,8},{12,13},{13,12},{22,23},{23,22... | collective-permute-start | bytes 3145736 | tf_op jit(solution)/shard_map/ppermute | solution.py:477
  168.2 16.3 %collective-permute-start.30 = (bf16[256,512]{1,0:T(8,128)(2,1)S(1)}, bf16[256,512]{1,0:T(8,128)(2,1)S(1)}, u32[]{:S(2)}, u32[]{:S(2)}) collective-permute-start(bf16[256,512]{1,0:T(8,128)(2,1)S(1)} %broadcast_select_fusion.7), channel_id=1, source_target_pairs={{0,2},{1,3},{4,6},{5,7},{10,8},{11,9},{14,12},{15,13},{20,22},{21,... | collective-permute-start | bytes 786440 | tf_op jit(solution)/shard_map/ppermute | solution.py:465
  175.1 16.1 %collective-permute-start.34 = (bf16[512,512]{1,0:T(8,128)(2,1)}, bf16[512,512]{1,0:T(8,128)(2,1)}, u32[]{:S(2)}, u32[]{:S(2)}) collective-permute-start(bf16[512,512]{1,0:T(8,128)(2,1)} %broadcast_select_fusion.5), channel_id=1, source_target_pairs={{0,1},{1,0},{4,5},{5,4},{10,11},{11,10},{14,15},{15,14},{20,21},{2... | collective-permute-start | bytes 1572872 | tf_op jit(solution)/shard_map/ppermute | solution.py:477
  177.0 14.2 %collective-permute-start.33 = (bf16[512,512]{1,0:T(8,128)(2,1)}, bf16[512,512]{1,0:T(8,128)(2,1)}, u32[]{:S(2)}, u32[]{:S(2)}) collective-permute-start(bf16[512,512]{1,0:T(8,128)(2,1)} %collective-permute-done.32), channel_id=1, source_target_pairs={{2,3},{3,2},{6,7},{7,6},{8,9},{9,8},{12,13},{13,12},{22,23},{23,22... | collective-permute-start | bytes 1572872 | tf_op jit(solution)/shard_map/ppermute | solution.py:477
  179.0 5.5 %copy-start.7 = (bf16[256,512]{1,0:T(8,128)(2,1)S(1)}, bf16[256,512]{1,0:T(8,128)(2,1)}, u32[]{:S(2)}) copy-start(bf16[256,512]{1,0:T(8,128)(2,1)} %copy-done.6) | copy-start | bytes 786436
  184.5 11.3 %collective-permute-start.35 = (bf16[256,512]{1,0:T(8,128)(2,1)S(1)}, bf16[256,512]{1,0:T(8,128)(2,1)S(1)}, u32[]{:S(2)}, u32[]{:S(2)}) collective-permute-start(bf16[256,512]{1,0:T(8,128)(2,1)S(1)} %broadcast_select_fusion.6.refs_11_), channel_id=1, source_target_pairs={{0,1},{1,0},{4,5},{5,4},{2,3},{3,2},{6,7},{7,6},{10,11},{11,10},{1... | collective-permute-start | bytes 786440 | tf_op jit(solution)/shard_map/ppermute | solution.py:477
  187.7 6.0 %copy-start = (f32[1024,512]{1,0:T(8,128)S(1)}, f32[1024,512]{1,0:T(8,128)}, u32[]{:S(2)}) copy-start(f32[1024,512]{1,0:T(8,128)} %base_rows.1.refs_1_) | copy-start | bytes 6291460
  193.7 2.1 %copy-start.2 = (bf16[128,128]{1,0:T(8,128)(2,1)S(1)}, bf16[128,128]{1,0:T(8,128)(2,1)}, u32[]{:S(2)}) copy-start(bf16[128,128]{1,0:T(8,128)(2,1)} %copy-done.1) | copy-start | bytes 98308

commit v10 on v9

--- a/solution.py
+++ b/solution.py
@@ -491,13 +491,15 @@
         return [inner_hop((state[0], state[1]), i) for i in range(1, spread)]
 
     s01 = zone_hop(([0], d01, None))
-    pack, diagonal = tie((pack, diagonal))
+    pack, diagonal, corner = tie((pack, diagonal, corner))
     pack_far = flip(pack, "grp", CHIP)
-    far_near = flip(rows_at(n, ways, [(diagonal, 0, 0)], "far_sum"), "grp", CHIP)
-    pack, pack_far, diagonal, corner = tie((pack, pack_far, diagonal, corner))
-    far_in = rows_at(n + ways, ways, [(diagonal, 0, 1)], "far_sum")
     for at in range(2, last + 1):
         corner = lead_hop(corner, at)
+    few = n // 4
+    far_near = rows_at(n, few, [(diagonal, 0, 0)], "far_sum", ways=few)
+    far_near = flip(far_near, "grp", CHIP)
+    pack, pack_far, diagonal, corner = tie((pack, pack_far, diagonal, corner))
+    far_in = rows_at(n + few, n - few, [(diagonal, 0, 1)], "far_sum", ways=few)
     pack = jnp.concatenate([pack, pack_far], axis=0)
     pack = jnp.concatenate([pack, flip(pack, "grp", CORE)], axis=0)
     pack, held, far_in, far_near, corner = tie((pack, s01[1], far_in, far_near, corner))
@@ -530,7 +532,7 @@
     r2 = inner_hops(s2, early2)
 
     adds = [(root_front, 0, 0), (near, 0, 0), (far_near, 0, 0), (far_last, 1, 0)]
-    base = rows_at(3 * n, n, adds, "base_rows")
+    base = rows_at(3 * n, n, adds, "base_rows", ways=few)
     slot_of = inner ^ jnp.arange(spread, dtype=jnp.int32)
 
     def update_body(*refs):

time: 202 us -> 205 us (1.015)
  the two profiles are of different devices: /device:TPU:0 before, /device:TPU:1 now
where the time goes in v10:
time: 205 us; the launch traced here: 202 us
  waiting for transfers between devices  62.9 us (31%)
  starting transfers between devices  58.7 us (29%)
  Pallas kernels  58 us (28%)
  other arithmetic  15.5 us (8%)
  local copies, waits for them, and re-layouts  5.4 us (3%)
    ppermute x19, waiting for transfers between devices, flip(): return lax.ppermute(value, axis, [(i, i ^ bit) for i in range(size)])  31.1 us
    ppermute x19, starting transfers between devices, flip(): return lax.ppermute(value, axis, [(i, i ^ bit) for i in range(size)])  28.8 us
    pallas_call x6, Pallas kernels, take_rows(): pl.pallas_call(body, grid_spec=pltpu.PrefetchScalarGridSpec(num_scalar_pr...  22.9 us
    ppermute x6, waiting for transfers between devices, zone_hop(): got = lax.ppermute(held, ('grp', 'mem'), pairs)  17.1 us
    ppermute x6, starting transfers between devices, lead_hop(): got = lax.ppermute(held, 'mem', [(src, src ^ bit) for src in sources])  14.4 us
    ppermute x6, waiting for transfers between devices, lead_hop(): got = lax.ppermute(held, 'mem', [(src, src ^ bit) for src in sources])  10.7 us
    pallas_call x1, Pallas kernels, local(): pl.pallas_call(leaf_two, grid=(1,), in_specs=[vmem, w_spec(0), w_spec(1),...  9.4 us
    pallas_call x1, Pallas kernels, local(): pl.pallas_call(root_step, in_specs=[smem] + [vmem] * 4, out_shape=(shape(...  8.96 us
  transfers between devices with their start and end apart: 36, of which 14 were waited for; matrix products, arithmetic and copies ran while one was open for 10% of the time, Pallas kernels for 25%

profile of v10, /device:TPU:1, one launch (start us, length us, event | category | flops | bytes accessed | tf_op | source)
XLA Modules:
  0.0 201.6 jit_solution(5450453440219638217)
XLA Ops:
  0.6 2.1 %pick_pivots.1 = (f32[8,128]{1,0:T(8,128)}, f32[384,128]{1,0:T(8,128)}, f32[384,128]{1,0:T(8,128)}, f32[8,512]{1,0:T(8,128)}, f32[384,256]{1,0:T(8,128)}) custom-call(s32[4]{0:T(128)} %bitcast.49, s32[1]{0:T(128)} %bitcast.2.at_ref, f32[4096,512]{1,0:T(8,128)} %bitcast.29), custom_call_target="tpu_custom_call" | custom-call | tf_op jit(solution)/shard_map/pick_pivots/pallas_call | solution.py:346
  2.7 2.1 %collective-permute-start = (f32[8,128]{1,0:T(8,128)}, f32[8,128]{1,0:T(8,128)S(1)}, u32[]{:S(2)}, u32[]{:S(2)}) collective-permute-start(f32[8,128]{1,0:T(8,128)} %get-tuple-element.56), channel_id=1, source_target_pairs={{0,1},{1,0},{2,3},{3,2},{4,5},{5,4},{6,7},{7,6},{8,9},{9,8},{10,11... | collective-permute-start | bytes 12296 | tf_op jit(solution)/shard_map/ppermute | solution.py:43
  6.7 1.5 collective-permute-start.1
  11.4 4.2 %collective-permute-start.6 = (f32[384,256]{1,0:T(8,128)}, f32[384,256]{1,0:T(8,128)S(1)}, u32[]{:S(2)}, u32[]{:S(2)}) collective-permute-start(f32[384,256]{1,0:T(8,128)} %get-tuple-element.63), channel_id=1, source_target_pairs={{0,4},{8,12},{16,20},{24,28}} | collective-permute-start | bytes 1179656 | tf_op jit(solution)/shard_map/ppermute | solution.py:342
  16.4 10.3 %collective-permute-done.3 = f32[8,128]{1,0:T(8,128)S(1)} collective-permute-done((f32[8,128]{1,0:T(8,128)S(1)}, f32[8,128]{1,0:T(8,128)S(1)}, u32[]{:S(2)}, u32[]{:S(2)}) %collective-permute-start.3) | collective-permute-done | bytes 4128 | tf_op jit(solution)/shard_map/ppermute | solution.py:43
  27.8 1.3 collective-permute-start.9
  31.1 2.8 %first_rows.1 = f32[256,512]{1,0:T(8,128)} custom-call(s32[2]{0:T(128)} %get-tuple-element.115.refs_0_, s32[2]{0:T(128)} %get-tuple-element.113.refs_1_, s32[1]{0:T(128)} %bitcast.10.refs_2_, f32[4096,512]{1,0:T(8,128)} %bitcast.30, f32[4096,512]{1,0:T(8,128)} %bitcast.31, f32[8,512]{1,0:T(8,128)} %get-tuple-element.65.refs_5_.refs_7_.mask_ref, ...), custom_call_target="tpu_custom_call" | custom-call | tf_op jit(solution)/shard_map/first_rows/pallas_call | solution.py:214
  33.9 2.8 %collective-permute-start.10 = (f32[256,512]{1,0:T(8,128)}, f32[256,512]{1,0:T(8,128)S(1)}, u32[]{:S(2)}, u32[]{:S(2)}) collective-permute-start(f32[256,512]{1,0:T(8,128)} %first_rows.1), channel_id=1, source_target_pairs={{0,8},{8,0},{16,24},{24,16},{1,9},{9,1},{17,25},{25,17},{2,10},{10... | collective-permute-start | bytes 1572872 | tf_op jit(solution)/shard_map/ppermute | solution.py:43
  37.4 3.1 %collective-permute-start.7 = (f32[384,128]{1,0:T(8,128)S(1)}, f32[384,128]{1,0:T(8,128)S(1)}, u32[]{:S(2)}, u32[]{:S(2)}) collective-permute-start(f32[384,128]{1,0:T(8,128)S(1)} %add.154), channel_id=1, source_target_pairs={{0,4},{1,5},{2,6},{3,7},{4,0},{5,1},{6,2},{7,3},{8,12},{9,13},{10,... | collective-permute-start | bytes 589832 | tf_op jit(solution)/shard_map/ppermute | solution.py:43
  41.2 3.3 %far_rows.1 = f32[1024,512]{1,0:T(8,128)} custom-call(s32[8]{0:T(128)} %get-tuple-element.120.refs_0_, s32[8]{0:T(128)} %get-tuple-element.117.refs_1_, s32[1]{0:T(128)} %constant.64.clone.1.refs_2_, f32[4096,512]{1,0:T(8,128)} %bitcast.32, f32[4096,512]{1,0:T(8,128)} %bitcast.33, f32[4096,512]{1,0:T(8,128)} %bitcast.34, f32[4096,512]{1,0:T(8,128)} %bitcast.35, ...), custom_call_target="tpu_custom_call" | custom-call | tf_op jit(solution)/shard_map/far_rows/pallas_call | solution.py:214
  44.5 3.3 %near_rows.1 = f32[1024,512]{1,0:T(8,128)} custom-call(s32[8]{0:T(128)} %get-tuple-element.119.refs_0_, s32[8]{0:T(128)} %get-tuple-element.116.refs_1_, s32[1]{0:T(128)} %constant.64.clone.1.refs_2_, f32[4096,512]{1,0:T(8,128)} %bitcast.36, f32[4096,512]{1,0:T(8,128)} %bitcast.37, f32[4096,512]{1,0:T(8,128)} %bitcast.38, f32[4096,512]{1,0:T(8,128)} %bitcast.39, ...), custom_call_target="tpu_custom_call" | custom-call | tf_op jit(solution)/shard_map/near_rows/pallas_call | solution.py:214
  47.8 2.2 %collective-permute-done.7 = f32[384,128]{1,0:T(8,128)S(1)} collective-permute-done((f32[384,128]{1,0:T(8,128)S(1)}, f32[384,128]{1,0:T(8,128)S(1)}, u32[]{:S(2)}, u32[]{:S(2)}) %collective-permute-start.7) | collective-permute-done | bytes 196640 | tf_op jit(solution)/shard_map/ppermute | solution.py:43
  50.9 2.5 %collective-permute-start.13 = (f32[384,256]{1,0:T(8,128)S(1)}, f32[384,256]{1,0:T(8,128)S(1)}, u32[]{:S(2)}, u32[]{:S(2)}) collective-permute-start(f32[384,256]{1,0:T(8,128)S(1)} %broadcast_select_fusion.9), channel_id=1, source_target_pairs={{0,2},{1,3},{4,6},{5,7},{8,10},{9,11},{12,14},{13,15},{16,18},{17,... | collective-permute-start | bytes 1179656 | tf_op jit(solution)/shard_map/ppermute | solution.py:342
  55.8 9.4 %leaf_two.1 = (bf16[256,512]{1,0:T(8,128)(2,1)}, f32[128,128]{1,0:T(8,128)}, f32[128,128]{1,0:T(8,128)}, bf16[128,128]{1,0:T(8,128)(2,1)}, f32[8,128]{1,0:T(8,128)}) custom-call(f32[384,128]{1,0:T(8,128)} %add.158.head_ref, f32[4096,512]{1,0:T(8,128)} %bitcast.40, f32[4096,512]{1,0:T(8,128)} %bitcast.41, f32[8,512]{1,0:T(8,128)} %get-tuple-element.65.refs_5_.refs_7_.mask_ref), custom_call_target="tpu_custom_call" | custom-call | tf_op jit(solution)/shard_map/leaf_two/pallas_call | solution.py:416
  65.2 1.4 collective-permute-done.12
  68.1 1.3 collective-permute-start.15
  69.4 5.8 %collective-permute-done.15 = bf16[256,512]{1,0:T(8,128)(2,1)S(1)} collective-permute-done((bf16[256,512]{1,0:T(8,128)(2,1)S(1)}, bf16[256,512]{1,0:T(8,128)(2,1)S(1)}, u32[]{:S(2)}, u32[]{:S(2)}) %collective-permute-start.15) | collective-permute-done | bytes 262176 | tf_op jit(solution)/shard_map/ppermute | solution.py:43
  75.2 1.8 collective-permute-start.16
  77.1 3.7 %collective-permute-start.17 = (f32[256,256]{1,0:T(8,128)S(1)}, f32[256,256]{1,0:T(8,128)S(1)}, u32[]{:S(2)}, u32[]{:S(2)}) collective-permute-start(f32[256,256]{1,0:T(8,128)S(1)} %slice.57), channel_id=1, source_target_pairs={{0,4},{8,12},{16,20},{24,28}} | collective-permute-start | bytes 786440 | tf_op jit(solution)/shard_map/ppermute | solution.py:342
  80.8 5.7 %collective-permute-done.17 = f32[256,256]{1,0:T(8,128)S(1)} collective-permute-done((f32[256,256]{1,0:T(8,128)S(1)}, f32[256,256]{1,0:T(8,128)S(1)}, u32[]{:S(2)}, u32[]{:S(2)}) %collective-permute-start.17) | collective-permute-done | bytes 262176 | tf_op jit(solution)/shard_map/ppermute | solution.py:342
  86.7 1.3 collective-permute-start.19
  88.0 1.7 collective-permute-start.23
  89.6 7.6 %leaf_last.1 = bf16[336,512]{1,0:T(8,128)(2,1)} custom-call(f32[384,128]{1,0:T(8,128)} %add.161.rest_ref, f32[4096,512]{1,0:T(8,128)} %bitcast.42, f32[384,256]{1,0:T(8,128)} %broadcast_select_fusion.8.w_lead_ref, f32[8,128]{1,0:T(8,128)} %copy-done.9, f32[8,512]{1,0:T(8,128)} %get-tuple-element.65.refs_5_.refs_7_.mask_ref, ...), custom_call_target="tpu_custom_call" | custom-call | tf_op jit(solution)/shard_map/leaf_last/pallas_call | solution.py:439
  97.3 1.3 collective-permute-start.21
  98.6 1.2 collective-permute-start.20
  99.8 4.9 %collective-permute-done.21 = f32[256,256]{1,0:T(8,128)S(1)} collective-permute-done((f32[256,256]{1,0:T(8,128)S(1)}, f32[256,256]{1,0:T(8,128)S(1)}, u32[]{:S(2)}, u32[]{:S(2)}) %collective-permute-start.21) | collective-permute-done | bytes 262176 | tf_op jit(solution)/shard_map/ppermute | solution.py:342
  105.0 1.9 pad_maximum_fusion.2
  106.8 7.2 %collective-permute-start.22 = (bf16[672,512]{1,0:T(8,128)(2,1)}, bf16[672,512]{1,0:T(8,128)(2,1)S(1)}, u32[]{:S(2)}, u32[]{:S(2)}) collective-permute-start(bf16[672,512]{1,0:T(8,128)(2,1)} %pad_maximum_fusion.2), channel_id=1, source_target_pairs={{0,8},{8,0},{16,24},{24,16},{1,9},{9,1},{17,25},{25,17},{2,10},{10... | collective-permute-start | bytes 2064392 | tf_op jit(solution)/shard_map/ppermute | solution.py:43
  115.3 2.8 %far_sum.3 = f32[256,512]{1,0:T(8,128)} custom-call(s32[2]{0:T(128)} %get-tuple-element.114.refs_0_, s32[2]{0:T(128)} %get-tuple-element.112.refs_1_, s32[1]{0:T(128)} %constant.64.clone.1.refs_2_, f32[4096,512]{1,0:T(8,128)} %bitcast.43, f32[4096,512]{1,0:T(8,128)} %bitcast.44, f32[8,512]{1,0:T(8,128)} %get-tuple-element.65.refs_5_.refs_7_.mask_ref, ...), custom_call_target="tpu_custom_call" | custom-call | tf_op jit(solution)/shard_map/far_sum/pallas_call | solution.py:214
  119.2 4.6 %far_sum.2 = f32[768,512]{1,0:T(8,128)} custom-call(s32[6]{0:T(128)} %slice.58.refs_0_, s32[6]{0:T(128)} %slice.59.refs_1_, s32[1]{0:T(128)} %constant.64.clone.1.refs_2_, f32[4096,512]{1,0:T(8,128)} %bitcast.45, f32[4096,512]{1,0:T(8,128)} %bitcast.46, f32[8,512]{1,0:T(8,128)} %get-tuple-element.65.refs_5_.refs_7_.mask_ref, ...), custom_call_target="tpu_custom_call" | custom-call | tf_op jit(solution)/shard_map/far_sum/pallas_call | solution.py:214
  123.9 7.9 %collective-permute-done.24.refs_8_ = f32[256,512]{1,0:T(8,128)S(1)} collective-permute-done((f32[256,512]{1,0:T(8,128)}, f32[256,512]{1,0:T(8,128)S(1)}, u32[]{:S(2)}, u32[]{:S(2)}) %collective-permute-start.24) | collective-permute-done | bytes 524320 | tf_op jit(solution)/shard_map/ppermute | solution.py:43
  131.8 1.3 collective-permute-start.28
  133.1 4.9 %collective-permute-start.11 = (f32[1024,512]{1,0:T(8,128)}, f32[1024,512]{1,0:T(8,128)}, u32[]{:S(2)}, u32[]{:S(2)}) collective-permute-start(f32[1024,512]{1,0:T(8,128)} %near_rows.1), channel_id=1, source_target_pairs={{0,8},{8,0},{16,24},{24,16},{1,9},{9,1},{17,25},{25,17},{2,10},{10... | collective-permute-start | bytes 6291464 | tf_op jit(solution)/shard_map/ppermute | solution.py:43
  138.8 9.0 %root_step.1 = (bf16[256,512]{1,0:T(8,128)(2,1)S(1)}, f32[128,128]{1,0:T(8,128)S(1)}, f32[128,128]{1,0:T(8,128)S(1)}, bf16[128,128]{1,0:T(8,128)(2,1)S(1)}, f32[8,128]{1,0:T(8,128)S(1)}) custom-call(s32[4]{0:T(128)S(1)} %pad_add_fusion.1.leaf_ref, f32[256,256]{1,0:T(8,128)S(1)} %broadcast_select_fusion.11.corner_ref, f32[256,512]{1,0:T(8,128)S(1)} %add.162.first_ref, ...), custom_call_target="tpu_custom_call" | custom-call | tf_op jit(solution)/shard_map/root_step/pallas_call | solution.py:514
  148.4 1.6 collective-permute-start.31
  151.1 1.3 broadcast_select_fusion.1.refs_3_
  152.4 1.3 collective-permute-start.32
  153.7 1.3 collective-permute-start.30
  155.1 1.9 collective-permute-start.29
  157.1 17.1 %collective-permute-done.30 = bf16[256,512]{1,0:T(8,128)(2,1)} collective-permute-done((bf16[256,512]{1,0:T(8,128)(2,1)S(1)}, bf16[256,512]{1,0:T(8,128)(2,1)}, u32[]{:S(2)}, u32[]{:S(2)}) %collective-permute-start.30) | collective-permute-done | bytes 262176 | tf_op jit(solution)/shard_map/ppermute | solution.py:465
  174.1 1.5 collective-permute-start.34
  175.6 2.1 %collective-permute-start.33 = (bf16[512,512]{1,0:T(8,128)(2,1)}, bf16[512,512]{1,0:T(8,128)(2,1)}, u32[]{:S(2)}, u32[]{:S(2)}) collective-permute-start(bf16[512,512]{1,0:T(8,128)(2,1)} %collective-permute-done.32), channel_id=1, source_target_pairs={{2,3},{3,2},{6,7},{7,6},{8,9},{9,8},{12,13},{13,12},{22,23},{23,22... | collective-permute-start | bytes 1572872 | tf_op jit(solution)/shard_map/ppermute | solution.py:477
  179.2 1.5 collective-permute-start.35
  180.7 6.2 %base_rows.1.refs_1_ = f32[1024,512]{1,0:T(8,128)} custom-call(s32[8]{0:T(128)} %get-tuple-element.121.refs_0_, s32[8]{0:T(128)} %get-tuple-element.118.refs_1_, s32[1]{0:T(128)} %constant.64.clone.1.refs_2_, f32[4096,512]{1,0:T(8,128)} %bitcast.47, f32[4096,512]{1,0:T(8,128)} %bitcast.48, f32[8,512]{1,0:T(8,128)} %get-tuple-element.65.refs_5_.refs_7_.mask_ref, ...), custom_call_target="tpu_custom_call" | custom-call | tf_op jit(solution)/shard_map/base_rows/pallas_call | solution.py:214
  188.1 3.5 %collective-permute-done.33 = bf16[512,512]{1,0:T(8,128)(2,1)} collective-permute-done((bf16[512,512]{1,0:T(8,128)(2,1)}, bf16[512,512]{1,0:T(8,128)(2,1)}, u32[]{:S(2)}, u32[]{:S(2)}) %collective-permute-start.33) | collective-permute-done | bytes 524320 | tf_op jit(solution)/shard_map/ppermute | solution.py:477
  192.7 1.3 broadcast_select_fusion.refs_4_
  194.1 2.1 %update.1.refs_2_ = f32[1024,512]{1,0:T(8,128)S(1)} custom-call(s32[2]{0:T(128)S(1)} %iota_xor_fusion.refs_0_, f32[1024,512]{1,0:T(8,128)S(1)} %copy-done, bf16[1024,512]{1,0:T(8,128)(2,1)S(1)} %pad_maximum_fusion.1.d01_ref.refs_2_, bf16[1024,512]{1,0:T(8,128)(2,1)S(1)} %broadcast_select_fusion.1.refs_3_, bf16[1024,512]{1,0:T(8,128)(2,1)S(1)} %broadcast_select_fusion.refs_4_), custom_call_target="tpu_custom_call" | custom-call | tf_op jit(solution)/shard_map/update/pallas_call | solution.py:544
  196.7 4.9 %finish.1 = f32[1024,512]{1,0:T(8,128)} custom-call(s32[2]{0:T(128)S(1)} %iota_xor_fusion.refs_0_, s32[3]{0:T(128)S(1)} %pad_add_fusion.refs_1_, f32[1024,512]{1,0:T(8,128)S(1)} %update.1.refs_2_, bf16[512,512]{1,0:T(8,128)(2,1)S(1)} %bitcast.28, bf16[256,512]{1,0:T(8,128)(2,1)S(1)} %get-tuple-element.98.refs_4_, f32[128,128]{1,0:T(8,128)S(1)} %get-tuple-element.104.refs_5_, ...), custom_call_target="tpu_custom_call" | custom-call | tf_op jit(solution)/shard_map/finish/pallas_call | solution.py:569
  (112 shorter events, 24.7 us)
Async XLA Ops:
  2.7 25.0 %copy-start.8 = (f32[384,256]{1,0:T(8,128)S(1)}, f32[384,256]{1,0:T(8,128)}, u32[]{:S(2)}) copy-start(f32[384,256]{1,0:T(8,128)} %get-tuple-element.63) | copy-start | bytes 1179652
  2.7 3.3 %collective-permute-start = (f32[8,128]{1,0:T(8,128)}, f32[8,128]{1,0:T(8,128)S(1)}, u32[]{:S(2)}, u32[]{:S(2)}) collective-permute-start(f32[8,128]{1,0:T(8,128)} %get-tuple-element.56), channel_id=1, source_target_pairs={{0,1},{1,0},{2,3},{3,2},{4,5},{5,4},{6,7},{7,6},{8,9},{9,8},{10,11... | collective-permute-start | bytes 12296 | tf_op jit(solution)/shard_map/ppermute | solution.py:43
  4.8 5.7 %collective-permute-start.2 = (f32[384,128]{1,0:T(8,128)}, f32[384,128]{1,0:T(8,128)S(1)}, u32[]{:S(2)}, u32[]{:S(2)}) collective-permute-start(f32[384,128]{1,0:T(8,128)} %get-tuple-element.57), channel_id=1, source_target_pairs={{0,1},{1,0},{2,3},{3,2},{4,5},{5,4},{6,7},{7,6},{8,9},{9,8},{10,11... | collective-permute-start | bytes 589832 | tf_op jit(solution)/shard_map/ppermute | solution.py:43
  6.7 2.8 %collective-permute-start.1 = (f32[8,128]{1,0:T(8,128)S(1)}, f32[8,128]{1,0:T(8,128)S(1)}, u32[]{:S(2)}, u32[]{:S(2)}) collective-permute-start(f32[8,128]{1,0:T(8,128)S(1)} %add.150), channel_id=1, source_target_pairs={{0,2},{1,3},{2,0},{3,1},{4,6},{5,7},{6,4},{7,5},{8,10},{9,11},{10,... | collective-permute-start | bytes 12296 | tf_op jit(solution)/shard_map/ppermute | solution.py:43
  11.4 16.3 %collective-permute-start.6 = (f32[384,256]{1,0:T(8,128)}, f32[384,256]{1,0:T(8,128)S(1)}, u32[]{:S(2)}, u32[]{:S(2)}) collective-permute-start(f32[384,256]{1,0:T(8,128)} %get-tuple-element.63), channel_id=1, source_target_pairs={{0,4},{8,12},{16,20},{24,28}} | collective-permute-start | bytes 1179656 | tf_op jit(solution)/shard_map/ppermute | solution.py:342
  15.7 11.0 %collective-permute-start.4 = (f32[384,128]{1,0:T(8,128)S(1)}, f32[384,128]{1,0:T(8,128)S(1)}, u32[]{:S(2)}, u32[]{:S(2)}) collective-permute-start(f32[384,128]{1,0:T(8,128)S(1)} %add.152), channel_id=1, source_target_pairs={{0,2},{1,3},{2,0},{3,1},{4,6},{5,7},{6,4},{7,5},{8,10},{9,11},{10,... | collective-permute-start | bytes 589832 | tf_op jit(solution)/shard_map/ppermute | solution.py:43
  15.8 11.0 %collective-permute-start.5 = (f32[384,128]{1,0:T(8,128)}, f32[384,128]{1,0:T(8,128)S(1)}, u32[]{:S(2)}, u32[]{:S(2)}) collective-permute-start(f32[384,128]{1,0:T(8,128)} %get-tuple-element.62), channel_id=1, source_target_pairs={{0,1},{1,0},{2,3},{3,2},{4,5},{5,4},{6,7},{7,6},{8,9},{9,8},{10,11... | collective-permute-start | bytes 589832 | tf_op jit(solution)/shard_map/ppermute | solution.py:43
  15.9 10.8 %collective-permute-start.3 = (f32[8,128]{1,0:T(8,128)S(1)}, f32[8,128]{1,0:T(8,128)S(1)}, u32[]{:S(2)}, u32[]{:S(2)}) collective-permute-start(f32[8,128]{1,0:T(8,128)S(1)} %add.151), channel_id=1, source_target_pairs={{0,4},{1,5},{2,6},{3,7},{4,0},{5,1},{6,2},{7,3},{8,12},{9,13},{10,... | collective-permute-start | bytes 12296 | tf_op jit(solution)/shard_map/ppermute | solution.py:43
  26.7 7.2 %copy-start.9 = (f32[8,128]{1,0:T(8,128)}, f32[8,128]{1,0:T(8,128)S(1)}, u32[]{:S(2)}) copy-start(f32[8,128]{1,0:T(8,128)S(1)} %add.153.table_ref) | copy-start | bytes 12292
  27.8 23.0 %collective-permute-start.9 = (f32[384,256]{1,0:T(8,128)S(1)}, f32[384,256]{1,0:T(8,128)S(1)}, u32[]{:S(2)}, u32[]{:S(2)}) collective-permute-start(f32[384,256]{1,0:T(8,128)S(1)} %broadcast_select_fusion.10), channel_id=1, source_target_pairs={{0,1},{4,5},{8,9},{12,13},{16,17},{20,21},{24,25},{28,29}} | collective-permute-start | bytes 1179656 | tf_op jit(solution)/shard_map/ppermute | solution.py:342
  33.9 16.9 %collective-permute-start.10 = (f32[256,512]{1,0:T(8,128)}, f32[256,512]{1,0:T(8,128)S(1)}, u32[]{:S(2)}, u32[]{:S(2)}) collective-permute-start(f32[256,512]{1,0:T(8,128)} %first_rows.1), channel_id=1, source_target_pairs={{0,8},{8,0},{16,24},{24,16},{1,9},{9,1},{17,25},{25,17},{2,10},{10... | collective-permute-start | bytes 1572872 | tf_op jit(solution)/shard_map/ppermute | solution.py:43
  37.4 12.6 %collective-permute-start.7 = (f32[384,128]{1,0:T(8,128)S(1)}, f32[384,128]{1,0:T(8,128)S(1)}, u32[]{:S(2)}, u32[]{:S(2)}) collective-permute-start(f32[384,128]{1,0:T(8,128)S(1)} %add.154), channel_id=1, source_target_pairs={{0,4},{1,5},{2,6},{3,7},{4,0},{5,1},{6,2},{7,3},{8,12},{9,13},{10,... | collective-permute-start | bytes 589832 | tf_op jit(solution)/shard_map/ppermute | solution.py:43
  40.5 10.2 %collective-permute-start.8 = (f32[384,128]{1,0:T(8,128)S(1)}, f32[384,128]{1,0:T(8,128)S(1)}, u32[]{:S(2)}, u32[]{:S(2)}) collective-permute-start(f32[384,128]{1,0:T(8,128)S(1)} %add.155), channel_id=1, source_target_pairs={{0,2},{1,3},{2,0},{3,1},{4,6},{5,7},{6,4},{7,5},{8,10},{9,11},{10,... | collective-permute-start | bytes 589832 | tf_op jit(solution)/shard_map/ppermute | solution.py:43
  47.8 3.1 %copy-start.5 = (f32[256,512]{1,0:T(8,128)S(1)}, f32[256,512]{1,0:T(8,128)}, u32[]{:S(2)}) copy-start(f32[256,512]{1,0:T(8,128)} %first_rows.1) | copy-start | bytes 1572868
  50.9 16.3 %collective-permute-start.13 = (f32[384,256]{1,0:T(8,128)S(1)}, f32[384,256]{1,0:T(8,128)S(1)}, u32[]{:S(2)}, u32[]{:S(2)}) collective-permute-start(f32[384,256]{1,0:T(8,128)S(1)} %broadcast_select_fusion.9), channel_id=1, source_target_pairs={{0,2},{1,3},{4,6},{5,7},{8,10},{9,11},{12,14},{13,15},{16,18},{17,... | collective-permute-start | bytes 1179656 | tf_op jit(solution)/shard_map/ppermute | solution.py:342
  53.4 43.9 %collective-permute-start.18 = (f32[1024,512]{1,0:T(8,128)}, f32[1024,512]{1,0:T(8,128)}, u32[]{:S(2)}, u32[]{:S(2)}) collective-permute-start(f32[1024,512]{1,0:T(8,128)} %far_rows.1), channel_id=1, source_target_pairs={{0,8},{8,0},{16,24},{24,16},{1,9},{9,1},{17,25},{25,17},{2,10},{10... | collective-permute-start | bytes 6291464 | tf_op jit(solution)/shard_map/ppermute | solution.py:43
  54.5 13.5 %collective-permute-start.14 = (f32[256,512]{1,0:T(8,128)S(1)}, f32[256,512]{1,0:T(8,128)S(1)}, u32[]{:S(2)}, u32[]{:S(2)}) collective-permute-start(f32[256,512]{1,0:T(8,128)S(1)} %add.160), channel_id=1, source_target_pairs={{0,16},{8,24},{16,0},{24,8},{1,17},{9,25},{17,1},{25,9},{2,18},{10... | collective-permute-start | bytes 1572872 | tf_op jit(solution)/shard_map/ppermute | solution.py:43
  55.8 10.8 %collective-permute-start.12 = (f32[384,128]{1,0:T(8,128)S(1)}, f32[384,128]{1,0:T(8,128)S(1)}, u32[]{:S(2)}, u32[]{:S(2)}) collective-permute-start(f32[384,128]{1,0:T(8,128)S(1)} %add.159), channel_id=1, source_target_pairs={{0,4},{1,5},{2,6},{3,7},{4,0},{5,1},{6,2},{7,3},{8,12},{9,13},{10,... | collective-permute-start | bytes 589832 | tf_op jit(solution)/shard_map/ppermute | solution.py:43
  65.2 3.0 %copy-start.4 = (bf16[256,512]{1,0:T(8,128)(2,1)S(1)}, bf16[256,512]{1,0:T(8,128)(2,1)}, u32[]{:S(2)}) copy-start(bf16[256,512]{1,0:T(8,128)(2,1)} %get-tuple-element.76.p_ref) | copy-start | bytes 786436
  68.1 7.0 %collective-permute-start.15 = (bf16[256,512]{1,0:T(8,128)(2,1)S(1)}, bf16[256,512]{1,0:T(8,128)(2,1)S(1)}, u32[]{:S(2)}, u32[]{:S(2)}) collective-permute-start(bf16[256,512]{1,0:T(8,128)(2,1)S(1)} %copy-done.4), channel_id=1, source_target_pairs={{0,16},{8,24},{16,0},{24,8},{1,17},{9,25},{17,1},{25,9},{2,18},{10... | collective-permute-start | bytes 786440 | tf_op jit(solution)/shard_map/ppermute | solution.py:43
  75.2 11.3 %collective-permute-start.16 = (bf16[512,512]{1,0:T(8,128)(2,1)S(1)}, bf16[512,512]{1,0:T(8,128)(2,1)S(1)}, u32[]{:S(2)}, u32[]{:S(2)}) collective-permute-start(bf16[512,512]{1,0:T(8,128)(2,1)S(1)} %pad_maximum_fusion.3), channel_id=1, source_target_pairs={{0,8},{8,0},{16,24},{24,16},{1,9},{9,1},{17,25},{25,17},{2,10},{10... | collective-permute-start | bytes 1572872 | tf_op jit(solution)/shard_map/ppermute | solution.py:43
  77.1 9.5 %collective-permute-start.17 = (f32[256,256]{1,0:T(8,128)S(1)}, f32[256,256]{1,0:T(8,128)S(1)}, u32[]{:S(2)}, u32[]{:S(2)}) collective-permute-start(f32[256,256]{1,0:T(8,128)S(1)} %slice.57), channel_id=1, source_target_pairs={{0,4},{8,12},{16,20},{24,28}} | collective-permute-start | bytes 786440 | tf_op jit(solution)/shard_map/ppermute | solution.py:342
  86.7 10.6 %collective-permute-start.19 = (f32[256,256]{1,0:T(8,128)S(1)}, f32[256,256]{1,0:T(8,128)S(1)}, u32[]{:S(2)}, u32[]{:S(2)}) collective-permute-start(f32[256,256]{1,0:T(8,128)S(1)} %broadcast_select_fusion.13), channel_id=1, source_target_pairs={{0,1},{4,5},{8,9},{12,13},{16,17},{20,21},{24,25},{28,29}} | collective-permute-start | bytes 786440 | tf_op jit(solution)/shard_map/ppermute | solution.py:342
  88.0 30.0 %collective-permute-start.23 = (bf16[1024,512]{1,0:T(8,128)(2,1)S(1)}, bf16[1024,512]{1,0:T(8,128)(2,1)}, u32[]{:S(2)}, u32[]{:S(2)}) collective-permute-start(bf16[1024,512]{1,0:T(8,128)(2,1)S(1)} %pad_maximum_fusion.1.d01_ref.refs_2_), channel_id=1, source_target_pairs={{0,4},{1,5},{10,14},{11,15},{20,16},{21,17},{30,26},{31,27}} | collective-permute-start | bytes 3145736 | tf_op jit(solution)/shard_map/ppermute | solution.py:465
  97.3 7.5 %collective-permute-start.21 = (f32[256,256]{1,0:T(8,128)S(1)}, f32[256,256]{1,0:T(8,128)S(1)}, u32[]{:S(2)}, u32[]{:S(2)}) collective-permute-start(f32[256,256]{1,0:T(8,128)S(1)} %broadcast_select_fusion.12), channel_id=1, source_target_pairs={{0,2},{1,3},{4,6},{5,7},{8,10},{9,11},{12,14},{13,15},{16,18},{17,... | collective-permute-start | bytes 786440 | tf_op jit(solution)/shard_map/ppermute | solution.py:342
  98.6 6.4 %collective-permute-start.20 = (bf16[336,512]{1,0:T(8,128)(2,1)}, bf16[336,512]{1,0:T(8,128)(2,1)S(1)}, u32[]{:S(2)}, u32[]{:S(2)}) collective-permute-start(bf16[336,512]{1,0:T(8,128)(2,1)} %leaf_last.1), channel_id=1, source_target_pairs={{0,16},{8,24},{16,0},{24,8},{1,17},{9,25},{17,1},{25,9},{2,18},{10... | collective-permute-start | bytes 1032200 | tf_op jit(solution)/shard_map/ppermute | solution.py:43
  106.8 16.9 %collective-permute-start.22 = (bf16[672,512]{1,0:T(8,128)(2,1)}, bf16[672,512]{1,0:T(8,128)(2,1)S(1)}, u32[]{:S(2)}, u32[]{:S(2)}) collective-permute-start(bf16[672,512]{1,0:T(8,128)(2,1)} %pad_maximum_fusion.2), channel_id=1, source_target_pairs={{0,8},{8,0},{16,24},{24,16},{1,9},{9,1},{17,25},{25,17},{2,10},{10... | collective-permute-start | bytes 2064392 | tf_op jit(solution)/shard_map/ppermute | solution.py:43
  118.0 13.8 %collective-permute-start.24 = (f32[256,512]{1,0:T(8,128)}, f32[256,512]{1,0:T(8,128)S(1)}, u32[]{:S(2)}, u32[]{:S(2)}) collective-permute-start(f32[256,512]{1,0:T(8,128)} %far_sum.3), channel_id=1, source_target_pairs={{0,16},{8,24},{16,0},{24,8},{1,17},{9,25},{17,1},{25,9},{2,18},{10... | collective-permute-start | bytes 1572872 | tf_op jit(solution)/shard_map/ppermute | solution.py:43
  119.2 4.6 %copy-start.3 = (bf16[336,512]{1,0:T(8,128)(2,1)S(1)}, bf16[336,512]{1,0:T(8,128)(2,1)}, u32[]{:S(2)}) copy-start(bf16[336,512]{1,0:T(8,128)(2,1)} %leaf_last.1) | copy-start | bytes 1032196
  131.8 6.2 %copy-start.7 = (f32[256,512]{1,0:T(8,128)}, f32[256,512]{1,0:T(8,128)S(1)}, u32[]{:S(2)}) copy-start(f32[256,512]{1,0:T(8,128)S(1)} %collective-permute-done.24.refs_8_) | copy-start | bytes 1572868
  131.8 19.3 %collective-permute-start.28 = (bf16[1024,512]{1,0:T(8,128)(2,1)}, bf16[1024,512]{1,0:T(8,128)(2,1)}, u32[]{:S(2)}, u32[]{:S(2)}) collective-permute-start(bf16[1024,512]{1,0:T(8,128)(2,1)} %broadcast_select_fusion.2), channel_id=1, source_target_pairs={{0,2},{1,3},{4,6},{5,7},{10,8},{11,9},{14,12},{15,13},{20,22},{21,... | collective-permute-start | bytes 3145736 | tf_op jit(solution)/shard_map/ppermute | solution.py:465
  133.1 46.1 %collective-permute-start.11 = (f32[1024,512]{1,0:T(8,128)}, f32[1024,512]{1,0:T(8,128)}, u32[]{:S(2)}, u32[]{:S(2)}) collective-permute-start(f32[1024,512]{1,0:T(8,128)} %near_rows.1), channel_id=1, source_target_pairs={{0,8},{8,0},{16,24},{24,16},{1,9},{9,1},{17,25},{25,17},{2,10},{10... | collective-permute-start | bytes 6291464 | tf_op jit(solution)/shard_map/ppermute | solution.py:43
  138.0 12.2 %collective-permute-start.27 = (bf16[512,512]{1,0:T(8,128)(2,1)S(1)}, bf16[512,512]{1,0:T(8,128)(2,1)S(1)}, u32[]{:S(2)}, u32[]{:S(2)}) collective-permute-start(bf16[512,512]{1,0:T(8,128)(2,1)S(1)} %bitcast.27), channel_id=1, source_target_pairs={{0,4},{1,5},{10,14},{11,15},{20,16},{21,17},{30,26},{31,27}} | collective-permute-start | bytes 1572872 | tf_op jit(solution)/shard_map/ppermute | solution.py:465
  147.7 3.3 %copy-start.1 = (bf16[128,128]{1,0:T(8,128)(2,1)}, bf16[128,128]{1,0:T(8,128)(2,1)S(1)}, u32[]{:S(2)}) copy-start(bf16[128,128]{1,0:T(8,128)(2,1)S(1)} %get-tuple-element.106.refs_7_) | copy-start | bytes 98308
  147.7 2.3 %collective-permute-start.26 = (bf16[256,512]{1,0:T(8,128)(2,1)S(1)}, bf16[256,512]{1,0:T(8,128)(2,1)S(1)}, u32[]{:S(2)}, u32[]{:S(2)}) collective-permute-start(bf16[256,512]{1,0:T(8,128)(2,1)S(1)} %get-tuple-element.98.refs_4_), channel_id=1, source_target_pairs={{0,4},{1,5},{10,14},{11,15},{20,16},{21,17},{30,26},{31,27}} | collective-permute-start | bytes 786440 | tf_op jit(solution)/shard_map/ppermute | solution.py:465
  148.4 6.6 %collective-permute-start.31 = (bf16[1024,512]{1,0:T(8,128)(2,1)}, bf16[1024,512]{1,0:T(8,128)(2,1)}, u32[]{:S(2)}, u32[]{:S(2)}) collective-permute-start(bf16[1024,512]{1,0:T(8,128)(2,1)} %broadcast_select_fusion.2), channel_id=1, source_target_pairs={{0,1},{1,0},{4,5},{5,4},{10,11},{11,10},{14,15},{15,14},{20,21},{2... | collective-permute-start | bytes 3145736 | tf_op jit(solution)/shard_map/ppermute | solution.py:477
  150.1 30.6 %collective-permute-start.25 = (f32[768,512]{1,0:T(8,128)}, f32[768,512]{1,0:T(8,128)}, u32[]{:S(2)}, u32[]{:S(2)}) collective-permute-start(f32[768,512]{1,0:T(8,128)} %far_sum.2), channel_id=1, source_target_pairs={{0,16},{8,24},{16,0},{24,8},{1,17},{9,25},{17,1},{25,9},{2,18},{10... | collective-permute-start | bytes 4718600 | tf_op jit(solution)/shard_map/ppermute | solution.py:43
  150.1 3.6 %copy-start.6 = (bf16[256,512]{1,0:T(8,128)(2,1)}, bf16[256,512]{1,0:T(8,128)(2,1)S(1)}, u32[]{:S(2)}) copy-start(bf16[256,512]{1,0:T(8,128)(2,1)S(1)} %broadcast_select_fusion.7) | copy-start | bytes 786436
  152.4 23.2 %collective-permute-start.32 = (bf16[512,512]{1,0:T(8,128)(2,1)}, bf16[512,512]{1,0:T(8,128)(2,1)}, u32[]{:S(2)}, u32[]{:S(2)}) collective-permute-start(bf16[512,512]{1,0:T(8,128)(2,1)} %broadcast_select_fusion.5), channel_id=1, source_target_pairs={{0,2},{1,3},{4,6},{5,7},{10,8},{11,9},{14,12},{15,13},{20,22},{21,... | collective-permute-start | bytes 1572872 | tf_op jit(solution)/shard_map/ppermute | solution.py:465
  153.7 20.4 %collective-permute-start.30 = (bf16[256,512]{1,0:T(8,128)(2,1)S(1)}, bf16[256,512]{1,0:T(8,128)(2,1)}, u32[]{:S(2)}, u32[]{:S(2)}) collective-permute-start(bf16[256,512]{1,0:T(8,128)(2,1)S(1)} %broadcast_select_fusion.7), channel_id=1, source_target_pairs={{0,2},{1,3},{4,6},{5,7},{10,8},{11,9},{14,12},{15,13},{20,22},{21,... | collective-permute-start | bytes 786440 | tf_op jit(solution)/shard_map/ppermute | solution.py:465
  155.1 37.7 %collective-permute-start.29 = (bf16[1024,512]{1,0:T(8,128)(2,1)}, bf16[1024,512]{1,0:T(8,128)(2,1)}, u32[]{:S(2)}, u32[]{:S(2)}) collective-permute-start(bf16[1024,512]{1,0:T(8,128)(2,1)} %collective-permute-done.28), channel_id=1, source_target_pairs={{2,3},{3,2},{6,7},{7,6},{8,9},{9,8},{12,13},{13,12},{22,23},{23,22... | collective-permute-start | bytes 3145736 | tf_op jit(solution)/shard_map/ppermute | solution.py:477
  174.1 14.0 %collective-permute-start.34 = (bf16[512,512]{1,0:T(8,128)(2,1)}, bf16[512,512]{1,0:T(8,128)(2,1)}, u32[]{:S(2)}, u32[]{:S(2)}) collective-permute-start(bf16[512,512]{1,0:T(8,128)(2,1)} %broadcast_select_fusion.5), channel_id=1, source_target_pairs={{0,1},{1,0},{4,5},{5,4},{10,11},{11,10},{14,15},{15,14},{20,21},{2... | collective-permute-start | bytes 1572872 | tf_op jit(solution)/shard_map/ppermute | solution.py:477
  175.6 16.0 %collective-permute-start.33 = (bf16[512,512]{1,0:T(8,128)(2,1)}, bf16[512,512]{1,0:T(8,128)(2,1)}, u32[]{:S(2)}, u32[]{:S(2)}) collective-permute-start(bf16[512,512]{1,0:T(8,128)(2,1)} %collective-permute-done.32), channel_id=1, source_target_pairs={{2,3},{3,2},{6,7},{7,6},{8,9},{9,8},{12,13},{13,12},{22,23},{23,22... | collective-permute-start | bytes 1572872 | tf_op jit(solution)/shard_map/ppermute | solution.py:477
  179.2 17.4 %collective-permute-start.35 = (bf16[256,512]{1,0:T(8,128)(2,1)S(1)}, bf16[256,512]{1,0:T(8,128)(2,1)S(1)}, u32[]{:S(2)}, u32[]{:S(2)}) collective-permute-start(bf16[256,512]{1,0:T(8,128)(2,1)S(1)} %broadcast_select_fusion.6.refs_11_), channel_id=1, source_target_pairs={{0,1},{1,0},{4,5},{5,4},{2,3},{3,2},{6,7},{7,6},{10,11},{11,10},{1... | collective-permute-start | bytes 786440 | tf_op jit(solution)/shard_map/ppermute | solution.py:477
  188.1 6.0 %copy-start = (f32[1024,512]{1,0:T(8,128)S(1)}, f32[1024,512]{1,0:T(8,128)}, u32[]{:S(2)}) copy-start(f32[1024,512]{1,0:T(8,128)} %base_rows.1.refs_1_) | copy-start | bytes 6291460
  194.1 2.6 %copy-start.2 = (bf16[128,128]{1,0:T(8,128)(2,1)S(1)}, bf16[128,128]{1,0:T(8,128)(2,1)}, u32[]{:S(2)}) copy-start(bf16[128,128]{1,0:T(8,128)(2,1)} %copy-done.1) | copy-start | bytes 98308

commit v11 on v10

--- a/solution.py
+++ b/solution.py
@@ -333,7 +333,7 @@
     last = len(hops) - 1
     lead_order = [hops[-1], hops[0]] + hops[-2:0:-1]
 
-    def lead_hop(value, at):
+    def lead_hop(value, at, lead_order=lead_order):
         bit, used = lead_order[at], sum(lead_order[:at])
         parts = []
         for root in range(leads):
@@ -431,9 +431,10 @@
         return jnp.concatenate([both, flip(both, "grp", CORE)], axis=0)
 
     d01 = across(p01)
-    corner = lead_hop([first[:, :lead_cols]] * leads, 0)
+    outward = hops[::-1]
+    corner = lead_hop([first[:, :lead_cols]] * leads, 0, outward)
     rest, d01, corner = tie((rest, d01, corner))
-    corner = lead_hop(corner, 1)
+    corner = lead_hop(corner, 1, outward)
     w_lead = w_lead[0] if leads == 1 else jnp.concatenate(w_lead, axis=1)
     lead_rows = (PL * b + LOG_ROWS) * pr // cols
     pack = pl.pallas_call(
@@ -491,15 +492,15 @@
         return [inner_hop((state[0], state[1]), i) for i in range(1, spread)]
 
     s01 = zone_hop(([0], d01, None))
-    pack, diagonal, corner = tie((pack, diagonal, corner))
+    pack, diagonal = tie((pack, diagonal))
     pack_far = flip(pack, "grp", CHIP)
-    for at in range(2, last + 1):
-        corner = lead_hop(corner, at)
     few = n // 4
     far_near = rows_at(n, few, [(diagonal, 0, 0)], "far_sum", ways=few)
     far_near = flip(far_near, "grp", CHIP)
     pack, pack_far, diagonal, corner = tie((pack, pack_far, diagonal, corner))
     far_in = rows_at(n + few, n - few, [(diagonal, 0, 1)], "far_sum", ways=few)
+    for at in range(2, last + 1):
+        corner = lead_hop(corner, at, outward)
     pack = jnp.concatenate([pack, pack_far], axis=0)
     pack = jnp.concatenate([pack, flip(pack, "grp", CORE)], axis=0)
     pack, held, far_in, far_near, corner = tie((pack, s01[1], far_in, far_near, corner))

time: 205 us -> 203 us (level)
  waiting for transfers between devices: 62.9 us -> 60.1 us
    ppermute x6, waiting for transfers between devices: 10.7 us -> 5.74 us  [lead_hop(): got = lax.ppermute(held, 'mem', [(src, src ^ bit) for src in sources])]
  transfers between devices with their start and end apart: 36 -> 36, of which waited for: 14 -> 13; matrix products, arithmetic and copies ran while one was open for 10% -> 10% of each run, Pallas kernels for 25% -> 26%
where the time goes in v11:
time: 203 us; the launch traced here: 199 us
  waiting for transfers between devices  60.1 us (30%)
  Pallas kernels  58 us (29%)
  starting transfers between devices  57.7 us (28%)
  other arithmetic  16.6 us (8%)
  local copies, waits for them, and re-layouts  5.84 us (3%)
    ppermute x19, waiting for transfers between devices, flip(): return lax.ppermute(value, axis, [(i, i ^ bit) for i in range(size)])  33 us
    ppermute x19, starting transfers between devices, flip(): return lax.ppermute(value, axis, [(i, i ^ bit) for i in range(size)])  27.3 us
    pallas_call x6, Pallas kernels, take_rows(): pl.pallas_call(body, grid_spec=pltpu.PrefetchScalarGridSpec(num_scalar_pr...  22.9 us
    ppermute x6, waiting for transfers between devices, zone_hop(): got = lax.ppermute(held, ('grp', 'mem'), pairs)  17.4 us
    ppermute x6, starting transfers between devices, lead_hop(): got = lax.ppermute(held, 'mem', [(src, src ^ bit) for src in sources])  15.8 us
    pallas_call x1, Pallas kernels, local(): pl.pallas_call(leaf_two, grid=(1,), in_specs=[vmem, w_spec(0), w_spec(1),...  9.42 us
    pallas_call x1, Pallas kernels, local(): pl.pallas_call(root_step, in_specs=[smem] + [vmem] * 4, out_shape=(shape(...  8.95 us
    ppermute x5, starting transfers between devices, inner_hop(): return lax.ppermute(value, ('grp', 'mem'), pairs)  8.66 us
  transfers between devices with their start and end apart: 36, of which 13 were waited for; matrix products, arithmetic and copies ran while one was open for 10% of the time, Pallas kernels for 26%

profile of v11, /device:TPU:1, one launch (start us, length us, event | category | flops | bytes accessed | tf_op | source)
XLA Modules:
  0.0 199.4 jit_solution(8680659922823058164)
XLA Ops:
  0.6 2.1 %pick_pivots.1 = (f32[8,128]{1,0:T(8,128)}, f32[384,128]{1,0:T(8,128)}, f32[384,128]{1,0:T(8,128)}, f32[8,512]{1,0:T(8,128)}, f32[384,256]{1,0:T(8,128)}) custom-call(s32[4]{0:T(128)} %bitcast.49, s32[1]{0:T(128)} %bitcast.2.at_ref, f32[4096,512]{1,0:T(8,128)} %bitcast.29), custom_call_target="tpu_custom_call" | custom-call | tf_op jit(solution)/shard_map/pick_pivots/pallas_call | solution.py:346
  2.8 2.1 %collective-permute-start = (f32[8,128]{1,0:T(8,128)}, f32[8,128]{1,0:T(8,128)S(1)}, u32[]{:S(2)}, u32[]{:S(2)}) collective-permute-start(f32[8,128]{1,0:T(8,128)} %get-tuple-element.55), channel_id=1, source_target_pairs={{0,1},{1,0},{2,3},{3,2},{4,5},{5,4},{6,7},{7,6},{8,9},{9,8},{10,11... | collective-permute-start | bytes 12296 | tf_op jit(solution)/shard_map/ppermute | solution.py:43
  6.7 1.5 collective-permute-start.1
  11.4 4.2 %collective-permute-start.6 = (f32[384,256]{1,0:T(8,128)}, f32[384,256]{1,0:T(8,128)S(1)}, u32[]{:S(2)}, u32[]{:S(2)}) collective-permute-start(f32[384,256]{1,0:T(8,128)} %get-tuple-element.62), channel_id=1, source_target_pairs={{0,4},{8,12},{16,20},{24,28}} | collective-permute-start | bytes 1179656 | tf_op jit(solution)/shard_map/ppermute | solution.py:342
  16.4 10.3 %collective-permute-done.3 = f32[8,128]{1,0:T(8,128)S(1)} collective-permute-done((f32[8,128]{1,0:T(8,128)S(1)}, f32[8,128]{1,0:T(8,128)S(1)}, u32[]{:S(2)}, u32[]{:S(2)}) %collective-permute-start.3) | collective-permute-done | bytes 4128 | tf_op jit(solution)/shard_map/ppermute | solution.py:43
  27.8 1.3 collective-permute-start.9
  31.1 2.8 %first_rows.1 = f32[256,512]{1,0:T(8,128)} custom-call(s32[2]{0:T(128)} %get-tuple-element.113.refs_0_, s32[2]{0:T(128)} %get-tuple-element.111.refs_1_, s32[1]{0:T(128)} %bitcast.10.refs_2_, f32[4096,512]{1,0:T(8,128)} %bitcast.30, f32[4096,512]{1,0:T(8,128)} %bitcast.31, f32[8,512]{1,0:T(8,128)} %get-tuple-element.64.refs_5_.refs_7_.mask_ref, ...), custom_call_target="tpu_custom_call" | custom-call | tf_op jit(solution)/shard_map/first_rows/pallas_call | solution.py:214
  33.9 2.8 %collective-permute-start.10 = (f32[256,512]{1,0:T(8,128)}, f32[256,512]{1,0:T(8,128)S(1)}, u32[]{:S(2)}, u32[]{:S(2)}) collective-permute-start(f32[256,512]{1,0:T(8,128)} %first_rows.1), channel_id=1, source_target_pairs={{0,8},{8,0},{16,24},{24,16},{1,9},{9,1},{17,25},{25,17},{2,10},{10... | collective-permute-start | bytes 1572872 | tf_op jit(solution)/shard_map/ppermute | solution.py:43
  37.3 3.1 %collective-permute-start.7 = (f32[384,128]{1,0:T(8,128)S(1)}, f32[384,128]{1,0:T(8,128)S(1)}, u32[]{:S(2)}, u32[]{:S(2)}) collective-permute-start(f32[384,128]{1,0:T(8,128)S(1)} %add.154), channel_id=1, source_target_pairs={{0,4},{1,5},{2,6},{3,7},{4,0},{5,1},{6,2},{7,3},{8,12},{9,13},{10,... | collective-permute-start | bytes 589832 | tf_op jit(solution)/shard_map/ppermute | solution.py:43
  41.0 3.3 %far_rows.1 = f32[1024,512]{1,0:T(8,128)} custom-call(s32[8]{0:T(128)} %get-tuple-element.118.refs_0_, s32[8]{0:T(128)} %get-tuple-element.115.refs_1_, s32[1]{0:T(128)} %constant.65.clone.1.refs_2_, f32[4096,512]{1,0:T(8,128)} %bitcast.32, f32[4096,512]{1,0:T(8,128)} %bitcast.33, f32[4096,512]{1,0:T(8,128)} %bitcast.34, f32[4096,512]{1,0:T(8,128)} %bitcast.35, ...), custom_call_target="tpu_custom_call" | custom-call | tf_op jit(solution)/shard_map/far_rows/pallas_call | solution.py:214
  44.3 3.3 %near_rows.1 = f32[1024,512]{1,0:T(8,128)} custom-call(s32[8]{0:T(128)} %get-tuple-element.117.refs_0_, s32[8]{0:T(128)} %get-tuple-element.114.refs_1_, s32[1]{0:T(128)} %constant.65.clone.1.refs_2_, f32[4096,512]{1,0:T(8,128)} %bitcast.36, f32[4096,512]{1,0:T(8,128)} %bitcast.37, f32[4096,512]{1,0:T(8,128)} %bitcast.38, f32[4096,512]{1,0:T(8,128)} %bitcast.39, ...), custom_call_target="tpu_custom_call" | custom-call | tf_op jit(solution)/shard_map/near_rows/pallas_call | solution.py:214
  47.6 2.3 %collective-permute-done.7 = f32[384,128]{1,0:T(8,128)S(1)} collective-permute-done((f32[384,128]{1,0:T(8,128)S(1)}, f32[384,128]{1,0:T(8,128)S(1)}, u32[]{:S(2)}, u32[]{:S(2)}) %collective-permute-start.7) | collective-permute-done | bytes 196640 | tf_op jit(solution)/shard_map/ppermute | solution.py:43
  50.9 2.5 %collective-permute-start.13 = (f32[384,256]{1,0:T(8,128)S(1)}, f32[384,256]{1,0:T(8,128)S(1)}, u32[]{:S(2)}, u32[]{:S(2)}) collective-permute-start(f32[384,256]{1,0:T(8,128)S(1)} %broadcast_select_fusion.9), channel_id=1, source_target_pairs={{0,2},{1,3},{4,6},{5,7},{8,10},{9,11},{12,14},{13,15},{16,18},{17,... | collective-permute-start | bytes 1179656 | tf_op jit(solution)/shard_map/ppermute | solution.py:342
  54.5 1.2 collective-permute-start.14
  55.7 9.4 %leaf_two.1 = (bf16[256,512]{1,0:T(8,128)(2,1)}, f32[128,128]{1,0:T(8,128)}, f32[128,128]{1,0:T(8,128)}, bf16[128,128]{1,0:T(8,128)(2,1)}, f32[8,128]{1,0:T(8,128)}) custom-call(f32[384,128]{1,0:T(8,128)} %add.158.head_ref, f32[4096,512]{1,0:T(8,128)} %bitcast.40, f32[4096,512]{1,0:T(8,128)} %bitcast.41, f32[8,512]{1,0:T(8,128)} %get-tuple-element.64.refs_5_.refs_7_.mask_ref), custom_call_target="tpu_custom_call" | custom-call | tf_op jit(solution)/shard_map/leaf_two/pallas_call | solution.py:416
  65.1 1.3 collective-permute-done.12
  68.1 1.3 collective-permute-start.15
  69.4 5.8 %collective-permute-done.15 = bf16[256,512]{1,0:T(8,128)(2,1)S(1)} collective-permute-done((bf16[256,512]{1,0:T(8,128)(2,1)S(1)}, bf16[256,512]{1,0:T(8,128)(2,1)S(1)}, u32[]{:S(2)}, u32[]{:S(2)}) %collective-permute-start.15) | collective-permute-done | bytes 262176 | tf_op jit(solution)/shard_map/ppermute | solution.py:43
  75.2 1.8 collective-permute-start.16
  77.0 3.7 %collective-permute-start.17 = (f32[256,256]{1,0:T(8,128)S(1)}, f32[256,256]{1,0:T(8,128)S(1)}, u32[]{:S(2)}, u32[]{:S(2)}) collective-permute-start(f32[256,256]{1,0:T(8,128)S(1)} %slice.57), channel_id=1, source_target_pairs={{0,4},{8,12},{16,20},{24,28}} | collective-permute-start | bytes 786440 | tf_op jit(solution)/shard_map/ppermute | solution.py:342
  80.7 5.7 %collective-permute-done.17 = f32[256,256]{1,0:T(8,128)S(1)} collective-permute-done((f32[256,256]{1,0:T(8,128)S(1)}, f32[256,256]{1,0:T(8,128)S(1)}, u32[]{:S(2)}, u32[]{:S(2)}) %collective-permute-start.17) | collective-permute-done | bytes 262176 | tf_op jit(solution)/shard_map/ppermute | solution.py:342
  87.3 2.0 %collective-permute-start.20 = (f32[256,256]{1,0:T(8,128)S(1)}, f32[256,256]{1,0:T(8,128)}, u32[]{:S(2)}, u32[]{:S(2)}) collective-permute-start(f32[256,256]{1,0:T(8,128)S(1)} %broadcast_select_fusion.13), channel_id=1, source_target_pairs={{0,2},{4,6},{8,10},{12,14},{16,18},{20,22},{24,26},{28,30}} | collective-permute-start | bytes 786440 | tf_op jit(solution)/shard_map/ppermute | solution.py:342
  89.4 7.6 %leaf_last.1 = bf16[336,512]{1,0:T(8,128)(2,1)} custom-call(f32[384,128]{1,0:T(8,128)} %add.161.rest_ref, f32[4096,512]{1,0:T(8,128)} %bitcast.42, f32[384,256]{1,0:T(8,128)} %broadcast_select_fusion.8.w_lead_ref, f32[8,128]{1,0:T(8,128)} %copy-done.8, f32[8,512]{1,0:T(8,128)} %get-tuple-element.64.refs_5_.refs_7_.mask_ref, ...), custom_call_target="tpu_custom_call" | custom-call | tf_op jit(solution)/shard_map/leaf_last/pallas_call | solution.py:440
  98.2 5.1 %collective-permute-done.19 = bf16[336,512]{1,0:T(8,128)(2,1)S(1)} collective-permute-done((bf16[336,512]{1,0:T(8,128)(2,1)}, bf16[336,512]{1,0:T(8,128)(2,1)S(1)}, u32[]{:S(2)}, u32[]{:S(2)}) %collective-permute-start.19) | collective-permute-done | bytes 344096 | tf_op jit(solution)/shard_map/ppermute | solution.py:43
  103.3 1.9 pad_maximum_fusion.2
  105.2 6.6 %collective-permute-start.21 = (bf16[672,512]{1,0:T(8,128)(2,1)}, bf16[672,512]{1,0:T(8,128)(2,1)}, u32[]{:S(2)}, u32[]{:S(2)}) collective-permute-start(bf16[672,512]{1,0:T(8,128)(2,1)} %pad_maximum_fusion.2), channel_id=1, source_target_pairs={{0,8},{8,0},{16,24},{24,16},{1,9},{9,1},{17,25},{25,17},{2,10},{10... | collective-permute-start | bytes 2064392 | tf_op jit(solution)/shard_map/ppermute | solution.py:43
  113.1 2.7 %far_sum.3 = f32[256,512]{1,0:T(8,128)} custom-call(s32[2]{0:T(128)} %get-tuple-element.112.refs_0_, s32[2]{0:T(128)} %get-tuple-element.110.refs_1_, s32[1]{0:T(128)} %constant.65.clone.1.refs_2_, f32[4096,512]{1,0:T(8,128)} %bitcast.43, f32[4096,512]{1,0:T(8,128)} %bitcast.44, f32[8,512]{1,0:T(8,128)} %get-tuple-element.64.refs_5_.refs_7_.mask_ref, ...), custom_call_target="tpu_custom_call" | custom-call | tf_op jit(solution)/shard_map/far_sum/pallas_call | solution.py:214
  115.8 2.0 %collective-permute-start.24 = (f32[256,256]{1,0:T(8,128)S(1)}, f32[256,256]{1,0:T(8,128)}, u32[]{:S(2)}, u32[]{:S(2)}) collective-permute-start(f32[256,256]{1,0:T(8,128)S(1)} %broadcast_select_fusion.12), channel_id=1, source_target_pairs={{0,1},{2,3},{4,5},{6,7},{8,9},{10,11},{12,13},{14,15},{16,17},{18,... | collective-permute-start | bytes 786440 | tf_op jit(solution)/shard_map/ppermute | solution.py:342
  119.0 4.6 %far_sum.2 = f32[768,512]{1,0:T(8,128)} custom-call(s32[6]{0:T(128)} %slice.58.refs_0_, s32[6]{0:T(128)} %slice.59.refs_1_, s32[1]{0:T(128)} %constant.65.clone.1.refs_2_, f32[4096,512]{1,0:T(8,128)} %bitcast.45, f32[4096,512]{1,0:T(8,128)} %bitcast.46, f32[8,512]{1,0:T(8,128)} %get-tuple-element.64.refs_5_.refs_7_.mask_ref, ...), custom_call_target="tpu_custom_call" | custom-call | tf_op jit(solution)/shard_map/far_sum/pallas_call | solution.py:214
  123.7 1.2 pad_maximum_fusion.pack_ref
  124.9 4.8 %collective-permute-done.23.refs_8_ = f32[256,512]{1,0:T(8,128)} collective-permute-done((f32[256,512]{1,0:T(8,128)}, f32[256,512]{1,0:T(8,128)}, u32[]{:S(2)}, u32[]{:S(2)}) %collective-permute-start.23) | collective-permute-done | bytes 524320 | tf_op jit(solution)/shard_map/ppermute | solution.py:43
  129.7 1.3 collective-permute-start.28
  131.0 4.0 %collective-permute-start.11 = (f32[1024,512]{1,0:T(8,128)}, f32[1024,512]{1,0:T(8,128)}, u32[]{:S(2)}, u32[]{:S(2)}) collective-permute-start(f32[1024,512]{1,0:T(8,128)} %near_rows.1), channel_id=1, source_target_pairs={{0,8},{8,0},{16,24},{24,16},{1,9},{9,1},{17,25},{25,17},{2,10},{10... | collective-permute-start | bytes 6291464 | tf_op jit(solution)/shard_map/ppermute | solution.py:43
  135.8 9.0 %root_step.1 = (bf16[256,512]{1,0:T(8,128)(2,1)S(1)}, f32[128,128]{1,0:T(8,128)S(1)}, f32[128,128]{1,0:T(8,128)S(1)}, bf16[128,128]{1,0:T(8,128)(2,1)S(1)}, f32[8,128]{1,0:T(8,128)S(1)}) custom-call(s32[4]{0:T(128)S(1)} %pad_add_fusion.1.leaf_ref, f32[256,256]{1,0:T(8,128)S(1)} %broadcast_select_fusion.11.corner_ref, f32[256,512]{1,0:T(8,128)S(1)} %add.162.first_ref, ...), custom_call_target="tpu_custom_call" | custom-call | tf_op jit(solution)/shard_map/root_step/pallas_call | solution.py:515
  146.0 1.6 collective-permute-start.31
  148.6 1.3 broadcast_select_fusion.1.refs_3_
  150.0 1.3 collective-permute-start.32
  151.3 1.3 collective-permute-start.30
  152.6 1.9 collective-permute-start.29
  154.6 17.4 %collective-permute-done.30 = bf16[256,512]{1,0:T(8,128)(2,1)} collective-permute-done((bf16[256,512]{1,0:T(8,128)(2,1)S(1)}, bf16[256,512]{1,0:T(8,128)(2,1)}, u32[]{:S(2)}, u32[]{:S(2)}) %collective-permute-start.30) | collective-permute-done | bytes 262176 | tf_op jit(solution)/shard_map/ppermute | solution.py:466
  172.0 1.4 collective-permute-start.34
  173.5 2.1 %collective-permute-start.33 = (bf16[512,512]{1,0:T(8,128)(2,1)}, bf16[512,512]{1,0:T(8,128)(2,1)}, u32[]{:S(2)}, u32[]{:S(2)}) collective-permute-start(bf16[512,512]{1,0:T(8,128)(2,1)} %collective-permute-done.32), channel_id=1, source_target_pairs={{2,3},{3,2},{6,7},{7,6},{8,9},{9,8},{12,13},{13,12},{22,23},{23,22... | collective-permute-start | bytes 1572872 | tf_op jit(solution)/shard_map/ppermute | solution.py:478
  177.1 1.5 collective-permute-start.35
  178.7 6.2 %base_rows.1.refs_1_ = f32[1024,512]{1,0:T(8,128)} custom-call(s32[8]{0:T(128)} %get-tuple-element.119.refs_0_, s32[8]{0:T(128)} %get-tuple-element.116.refs_1_, s32[1]{0:T(128)} %constant.65.clone.1.refs_2_, f32[4096,512]{1,0:T(8,128)} %bitcast.47, f32[4096,512]{1,0:T(8,128)} %bitcast.48, f32[8,512]{1,0:T(8,128)} %get-tuple-element.64.refs_5_.refs_7_.mask_ref, ...), custom_call_target="tpu_custom_call" | custom-call | tf_op jit(solution)/shard_map/base_rows/pallas_call | solution.py:214
  186.0 3.5 %collective-permute-done.33 = bf16[512,512]{1,0:T(8,128)(2,1)} collective-permute-done((bf16[512,512]{1,0:T(8,128)(2,1)}, bf16[512,512]{1,0:T(8,128)(2,1)}, u32[]{:S(2)}, u32[]{:S(2)}) %collective-permute-start.33) | collective-permute-done | bytes 524320 | tf_op jit(solution)/shard_map/ppermute | solution.py:478
  190.6 1.3 broadcast_select_fusion.refs_4_
  191.9 2.1 %update.1.refs_2_ = f32[1024,512]{1,0:T(8,128)S(1)} custom-call(s32[2]{0:T(128)S(1)} %iota_xor_fusion.refs_0_, f32[1024,512]{1,0:T(8,128)S(1)} %copy-done, bf16[1024,512]{1,0:T(8,128)(2,1)S(1)} %pad_maximum_fusion.1.d01_ref.refs_2_, bf16[1024,512]{1,0:T(8,128)(2,1)S(1)} %broadcast_select_fusion.1.refs_3_, bf16[1024,512]{1,0:T(8,128)(2,1)S(1)} %broadcast_select_fusion.refs_4_), custom_call_target="tpu_custom_call" | custom-call | tf_op jit(solution)/shard_map/update/pallas_call | solution.py:545
  194.5 4.9 %finish.1 = f32[1024,512]{1,0:T(8,128)} custom-call(s32[2]{0:T(128)S(1)} %iota_xor_fusion.refs_0_, s32[3]{0:T(128)S(1)} %pad_add_fusion.refs_1_, f32[1024,512]{1,0:T(8,128)S(1)} %update.1.refs_2_, bf16[512,512]{1,0:T(8,128)(2,1)S(1)} %bitcast.28, bf16[256,512]{1,0:T(8,128)(2,1)S(1)} %get-tuple-element.96.refs_4_, f32[128,128]{1,0:T(8,128)S(1)} %get-tuple-element.102.refs_5_, ...), custom_call_target="tpu_custom_call" | custom-call | tf_op jit(solution)/shard_map/finish/pallas_call | solution.py:570
  (110 shorter events, 25.5 us)
Async XLA Ops:
  2.7 25.0 %copy-start.7 = (f32[384,256]{1,0:T(8,128)S(1)}, f32[384,256]{1,0:T(8,128)}, u32[]{:S(2)}) copy-start(f32[384,256]{1,0:T(8,128)} %get-tuple-element.62) | copy-start | bytes 1179652
  2.8 3.3 %collective-permute-start = (f32[8,128]{1,0:T(8,128)}, f32[8,128]{1,0:T(8,128)S(1)}, u32[]{:S(2)}, u32[]{:S(2)}) collective-permute-start(f32[8,128]{1,0:T(8,128)} %get-tuple-element.55), channel_id=1, source_target_pairs={{0,1},{1,0},{2,3},{3,2},{4,5},{5,4},{6,7},{7,6},{8,9},{9,8},{10,11... | collective-permute-start | bytes 12296 | tf_op jit(solution)/shard_map/ppermute | solution.py:43
  4.8 5.7 %collective-permute-start.2 = (f32[384,128]{1,0:T(8,128)}, f32[384,128]{1,0:T(8,128)S(1)}, u32[]{:S(2)}, u32[]{:S(2)}) collective-permute-start(f32[384,128]{1,0:T(8,128)} %get-tuple-element.56), channel_id=1, source_target_pairs={{0,1},{1,0},{2,3},{3,2},{4,5},{5,4},{6,7},{7,6},{8,9},{9,8},{10,11... | collective-permute-start | bytes 589832 | tf_op jit(solution)/shard_map/ppermute | solution.py:43
  6.7 2.8 %collective-permute-start.1 = (f32[8,128]{1,0:T(8,128)S(1)}, f32[8,128]{1,0:T(8,128)S(1)}, u32[]{:S(2)}, u32[]{:S(2)}) collective-permute-start(f32[8,128]{1,0:T(8,128)S(1)} %add.150), channel_id=1, source_target_pairs={{0,2},{1,3},{2,0},{3,1},{4,6},{5,7},{6,4},{7,5},{8,10},{9,11},{10,... | collective-permute-start | bytes 12296 | tf_op jit(solution)/shard_map/ppermute | solution.py:43
  11.4 16.3 %collective-permute-start.6 = (f32[384,256]{1,0:T(8,128)}, f32[384,256]{1,0:T(8,128)S(1)}, u32[]{:S(2)}, u32[]{:S(2)}) collective-permute-start(f32[384,256]{1,0:T(8,128)} %get-tuple-element.62), channel_id=1, source_target_pairs={{0,4},{8,12},{16,20},{24,28}} | collective-permute-start | bytes 1179656 | tf_op jit(solution)/shard_map/ppermute | solution.py:342
  15.7 11.0 %collective-permute-start.4 = (f32[384,128]{1,0:T(8,128)S(1)}, f32[384,128]{1,0:T(8,128)S(1)}, u32[]{:S(2)}, u32[]{:S(2)}) collective-permute-start(f32[384,128]{1,0:T(8,128)S(1)} %add.152), channel_id=1, source_target_pairs={{0,2},{1,3},{2,0},{3,1},{4,6},{5,7},{6,4},{7,5},{8,10},{9,11},{10,... | collective-permute-start | bytes 589832 | tf_op jit(solution)/shard_map/ppermute | solution.py:43
  15.8 11.0 %collective-permute-start.5 = (f32[384,128]{1,0:T(8,128)}, f32[384,128]{1,0:T(8,128)S(1)}, u32[]{:S(2)}, u32[]{:S(2)}) collective-permute-start(f32[384,128]{1,0:T(8,128)} %get-tuple-element.61), channel_id=1, source_target_pairs={{0,1},{1,0},{2,3},{3,2},{4,5},{5,4},{6,7},{7,6},{8,9},{9,8},{10,11... | collective-permute-start | bytes 589832 | tf_op jit(solution)/shard_map/ppermute | solution.py:43
  15.9 10.8 %collective-permute-start.3 = (f32[8,128]{1,0:T(8,128)S(1)}, f32[8,128]{1,0:T(8,128)S(1)}, u32[]{:S(2)}, u32[]{:S(2)}) collective-permute-start(f32[8,128]{1,0:T(8,128)S(1)} %add.151), channel_id=1, source_target_pairs={{0,4},{1,5},{2,6},{3,7},{4,0},{5,1},{6,2},{7,3},{8,12},{9,13},{10,... | collective-permute-start | bytes 12296 | tf_op jit(solution)/shard_map/ppermute | solution.py:43
  26.7 7.2 %copy-start.8 = (f32[8,128]{1,0:T(8,128)}, f32[8,128]{1,0:T(8,128)S(1)}, u32[]{:S(2)}) copy-start(f32[8,128]{1,0:T(8,128)S(1)} %add.153.table_ref) | copy-start | bytes 12292
  27.8 22.9 %collective-permute-start.9 = (f32[384,256]{1,0:T(8,128)S(1)}, f32[384,256]{1,0:T(8,128)S(1)}, u32[]{:S(2)}, u32[]{:S(2)}) collective-permute-start(f32[384,256]{1,0:T(8,128)S(1)} %broadcast_select_fusion.10), channel_id=1, source_target_pairs={{0,1},{4,5},{8,9},{12,13},{16,17},{20,21},{24,25},{28,29}} | collective-permute-start | bytes 1179656 | tf_op jit(solution)/shard_map/ppermute | solution.py:342
  33.9 16.9 %collective-permute-start.10 = (f32[256,512]{1,0:T(8,128)}, f32[256,512]{1,0:T(8,128)S(1)}, u32[]{:S(2)}, u32[]{:S(2)}) collective-permute-start(f32[256,512]{1,0:T(8,128)} %first_rows.1), channel_id=1, source_target_pairs={{0,8},{8,0},{16,24},{24,16},{1,9},{9,1},{17,25},{25,17},{2,10},{10... | collective-permute-start | bytes 1572872 | tf_op jit(solution)/shard_map/ppermute | solution.py:43
  37.3 12.6 %collective-permute-start.7 = (f32[384,128]{1,0:T(8,128)S(1)}, f32[384,128]{1,0:T(8,128)S(1)}, u32[]{:S(2)}, u32[]{:S(2)}) collective-permute-start(f32[384,128]{1,0:T(8,128)S(1)} %add.154), channel_id=1, source_target_pairs={{0,4},{1,5},{2,6},{3,7},{4,0},{5,1},{6,2},{7,3},{8,12},{9,13},{10,... | collective-permute-start | bytes 589832 | tf_op jit(solution)/shard_map/ppermute | solution.py:43
  40.4 10.3 %collective-permute-start.8 = (f32[384,128]{1,0:T(8,128)S(1)}, f32[384,128]{1,0:T(8,128)S(1)}, u32[]{:S(2)}, u32[]{:S(2)}) collective-permute-start(f32[384,128]{1,0:T(8,128)S(1)} %add.155), channel_id=1, source_target_pairs={{0,2},{1,3},{2,0},{3,1},{4,6},{5,7},{6,4},{7,5},{8,10},{9,11},{10,... | collective-permute-start | bytes 589832 | tf_op jit(solution)/shard_map/ppermute | solution.py:43
  47.6 3.2 %copy-start.5 = (f32[256,512]{1,0:T(8,128)S(1)}, f32[256,512]{1,0:T(8,128)}, u32[]{:S(2)}) copy-start(f32[256,512]{1,0:T(8,128)} %first_rows.1) | copy-start | bytes 1572868
  50.9 16.3 %collective-permute-start.13 = (f32[384,256]{1,0:T(8,128)S(1)}, f32[384,256]{1,0:T(8,128)S(1)}, u32[]{:S(2)}, u32[]{:S(2)}) collective-permute-start(f32[384,256]{1,0:T(8,128)S(1)} %broadcast_select_fusion.9), channel_id=1, source_target_pairs={{0,2},{1,3},{4,6},{5,7},{8,10},{9,11},{12,14},{13,15},{16,18},{17,... | collective-permute-start | bytes 1179656 | tf_op jit(solution)/shard_map/ppermute | solution.py:342
  53.4 43.6 %collective-permute-start.18 = (f32[1024,512]{1,0:T(8,128)}, f32[1024,512]{1,0:T(8,128)}, u32[]{:S(2)}, u32[]{:S(2)}) collective-permute-start(f32[1024,512]{1,0:T(8,128)} %far_rows.1), channel_id=1, source_target_pairs={{0,8},{8,0},{16,24},{24,16},{1,9},{9,1},{17,25},{25,17},{2,10},{10... | collective-permute-start | bytes 6291464 | tf_op jit(solution)/shard_map/ppermute | solution.py:43
  54.5 13.5 %collective-permute-start.14 = (f32[256,512]{1,0:T(8,128)S(1)}, f32[256,512]{1,0:T(8,128)S(1)}, u32[]{:S(2)}, u32[]{:S(2)}) collective-permute-start(f32[256,512]{1,0:T(8,128)S(1)} %add.160), channel_id=1, source_target_pairs={{0,16},{8,24},{16,0},{24,8},{1,17},{9,25},{17,1},{25,9},{2,18},{10... | collective-permute-start | bytes 1572872 | tf_op jit(solution)/shard_map/ppermute | solution.py:43
  55.7 10.8 %collective-permute-start.12 = (f32[384,128]{1,0:T(8,128)S(1)}, f32[384,128]{1,0:T(8,128)S(1)}, u32[]{:S(2)}, u32[]{:S(2)}) collective-permute-start(f32[384,128]{1,0:T(8,128)S(1)} %add.159), channel_id=1, source_target_pairs={{0,4},{1,5},{2,6},{3,7},{4,0},{5,1},{6,2},{7,3},{8,12},{9,13},{10,... | collective-permute-start | bytes 589832 | tf_op jit(solution)/shard_map/ppermute | solution.py:43
  65.1 2.9 %copy-start.4 = (bf16[256,512]{1,0:T(8,128)(2,1)S(1)}, bf16[256,512]{1,0:T(8,128)(2,1)}, u32[]{:S(2)}) copy-start(bf16[256,512]{1,0:T(8,128)(2,1)} %get-tuple-element.75.p_ref) | copy-start | bytes 786436
  68.1 7.0 %collective-permute-start.15 = (bf16[256,512]{1,0:T(8,128)(2,1)S(1)}, bf16[256,512]{1,0:T(8,128)(2,1)S(1)}, u32[]{:S(2)}, u32[]{:S(2)}) collective-permute-start(bf16[256,512]{1,0:T(8,128)(2,1)S(1)} %copy-done.4), channel_id=1, source_target_pairs={{0,16},{8,24},{16,0},{24,8},{1,17},{9,25},{17,1},{25,9},{2,18},{10... | collective-permute-start | bytes 786440 | tf_op jit(solution)/shard_map/ppermute | solution.py:43
  75.2 11.3 %collective-permute-start.16 = (bf16[512,512]{1,0:T(8,128)(2,1)S(1)}, bf16[512,512]{1,0:T(8,128)(2,1)S(1)}, u32[]{:S(2)}, u32[]{:S(2)}) collective-permute-start(bf16[512,512]{1,0:T(8,128)(2,1)S(1)} %pad_maximum_fusion.3), channel_id=1, source_target_pairs={{0,8},{8,0},{16,24},{24,16},{1,9},{9,1},{17,25},{25,17},{2,10},{10... | collective-permute-start | bytes 1572872 | tf_op jit(solution)/shard_map/ppermute | solution.py:43
  77.0 9.5 %collective-permute-start.17 = (f32[256,256]{1,0:T(8,128)S(1)}, f32[256,256]{1,0:T(8,128)S(1)}, u32[]{:S(2)}, u32[]{:S(2)}) collective-permute-start(f32[256,256]{1,0:T(8,128)S(1)} %slice.57), channel_id=1, source_target_pairs={{0,4},{8,12},{16,20},{24,28}} | collective-permute-start | bytes 786440 | tf_op jit(solution)/shard_map/ppermute | solution.py:342
  86.6 31.2 %collective-permute-start.22 = (bf16[1024,512]{1,0:T(8,128)(2,1)S(1)}, bf16[1024,512]{1,0:T(8,128)(2,1)S(1)}, u32[]{:S(2)}, u32[]{:S(2)}) collective-permute-start(bf16[1024,512]{1,0:T(8,128)(2,1)S(1)} %pad_maximum_fusion.1.d01_ref.refs_2_), channel_id=1, source_target_pairs={{0,4},{1,5},{10,14},{11,15},{20,16},{21,17},{30,26},{31,27}} | collective-permute-start | bytes 3145736 | tf_op jit(solution)/shard_map/ppermute | solution.py:466
  87.3 10.8 %collective-permute-start.20 = (f32[256,256]{1,0:T(8,128)S(1)}, f32[256,256]{1,0:T(8,128)}, u32[]{:S(2)}, u32[]{:S(2)}) collective-permute-start(f32[256,256]{1,0:T(8,128)S(1)} %broadcast_select_fusion.13), channel_id=1, source_target_pairs={{0,2},{4,6},{8,10},{12,14},{16,18},{20,22},{24,26},{28,30}} | collective-permute-start | bytes 786440 | tf_op jit(solution)/shard_map/ppermute | solution.py:342
  97.0 6.3 %collective-permute-start.19 = (bf16[336,512]{1,0:T(8,128)(2,1)}, bf16[336,512]{1,0:T(8,128)(2,1)S(1)}, u32[]{:S(2)}, u32[]{:S(2)}) collective-permute-start(bf16[336,512]{1,0:T(8,128)(2,1)} %leaf_last.1), channel_id=1, source_target_pairs={{0,16},{8,24},{16,0},{24,8},{1,17},{9,25},{17,1},{25,9},{2,18},{10... | collective-permute-start | bytes 1032200 | tf_op jit(solution)/shard_map/ppermute | solution.py:43
  105.2 18.5 %collective-permute-start.21 = (bf16[672,512]{1,0:T(8,128)(2,1)}, bf16[672,512]{1,0:T(8,128)(2,1)}, u32[]{:S(2)}, u32[]{:S(2)}) collective-permute-start(bf16[672,512]{1,0:T(8,128)(2,1)} %pad_maximum_fusion.2), channel_id=1, source_target_pairs={{0,8},{8,0},{16,24},{24,16},{1,9},{9,1},{17,25},{25,17},{2,10},{10... | collective-permute-start | bytes 2064392 | tf_op jit(solution)/shard_map/ppermute | solution.py:43
  115.8 13.9 %collective-permute-start.23 = (f32[256,512]{1,0:T(8,128)}, f32[256,512]{1,0:T(8,128)}, u32[]{:S(2)}, u32[]{:S(2)}) collective-permute-start(f32[256,512]{1,0:T(8,128)} %far_sum.3), channel_id=1, source_target_pairs={{0,16},{8,24},{16,0},{24,8},{1,17},{9,25},{17,1},{25,9},{2,18},{10... | collective-permute-start | bytes 1572872 | tf_op jit(solution)/shard_map/ppermute | solution.py:43
  115.8 7.8 %collective-permute-start.24 = (f32[256,256]{1,0:T(8,128)S(1)}, f32[256,256]{1,0:T(8,128)}, u32[]{:S(2)}, u32[]{:S(2)}) collective-permute-start(f32[256,256]{1,0:T(8,128)S(1)} %broadcast_select_fusion.12), channel_id=1, source_target_pairs={{0,1},{2,3},{4,5},{6,7},{8,9},{10,11},{12,13},{14,15},{16,17},{18,... | collective-permute-start | bytes 786440 | tf_op jit(solution)/shard_map/ppermute | solution.py:342
  119.0 4.7 %copy-start.3 = (bf16[336,512]{1,0:T(8,128)(2,1)S(1)}, bf16[336,512]{1,0:T(8,128)(2,1)}, u32[]{:S(2)}) copy-start(bf16[336,512]{1,0:T(8,128)(2,1)} %leaf_last.1) | copy-start | bytes 1032196
  129.7 18.9 %collective-permute-start.28 = (bf16[1024,512]{1,0:T(8,128)(2,1)}, bf16[1024,512]{1,0:T(8,128)(2,1)}, u32[]{:S(2)}, u32[]{:S(2)}) collective-permute-start(bf16[1024,512]{1,0:T(8,128)(2,1)} %broadcast_select_fusion.2), channel_id=1, source_target_pairs={{0,2},{1,3},{4,6},{5,7},{10,8},{11,9},{14,12},{15,13},{20,22},{21,... | collective-permute-start | bytes 3145736 | tf_op jit(solution)/shard_map/ppermute | solution.py:466
  131.0 46.2 %collective-permute-start.11 = (f32[1024,512]{1,0:T(8,128)}, f32[1024,512]{1,0:T(8,128)}, u32[]{:S(2)}, u32[]{:S(2)}) collective-permute-start(f32[1024,512]{1,0:T(8,128)} %near_rows.1), channel_id=1, source_target_pairs={{0,8},{8,0},{16,24},{24,16},{1,9},{9,1},{17,25},{25,17},{2,10},{10... | collective-permute-start | bytes 6291464 | tf_op jit(solution)/shard_map/ppermute | solution.py:43
  135.0 12.8 %collective-permute-start.27 = (bf16[512,512]{1,0:T(8,128)(2,1)S(1)}, bf16[512,512]{1,0:T(8,128)(2,1)S(1)}, u32[]{:S(2)}, u32[]{:S(2)}) collective-permute-start(bf16[512,512]{1,0:T(8,128)(2,1)S(1)} %bitcast.27), channel_id=1, source_target_pairs={{0,4},{1,5},{10,14},{11,15},{20,16},{21,17},{30,26},{31,27}} | collective-permute-start | bytes 1572872 | tf_op jit(solution)/shard_map/ppermute | solution.py:466
  144.7 0.6 copy-start.1
  145.3 2.3 %collective-permute-start.26 = (bf16[256,512]{1,0:T(8,128)(2,1)S(1)}, bf16[256,512]{1,0:T(8,128)(2,1)S(1)}, u32[]{:S(2)}, u32[]{:S(2)}) collective-permute-start(bf16[256,512]{1,0:T(8,128)(2,1)S(1)} %get-tuple-element.96.refs_4_), channel_id=1, source_target_pairs={{0,4},{1,5},{10,14},{11,15},{20,16},{21,17},{30,26},{31,27}} | collective-permute-start | bytes 786440 | tf_op jit(solution)/shard_map/ppermute | solution.py:466
  146.0 6.6 %collective-permute-start.31 = (bf16[1024,512]{1,0:T(8,128)(2,1)}, bf16[1024,512]{1,0:T(8,128)(2,1)}, u32[]{:S(2)}, u32[]{:S(2)}) collective-permute-start(bf16[1024,512]{1,0:T(8,128)(2,1)} %broadcast_select_fusion.2), channel_id=1, source_target_pairs={{0,1},{1,0},{4,5},{5,4},{10,11},{11,10},{14,15},{15,14},{20,21},{2... | collective-permute-start | bytes 3145736 | tf_op jit(solution)/shard_map/ppermute | solution.py:478
  147.7 31.0 %collective-permute-start.25 = (f32[768,512]{1,0:T(8,128)}, f32[768,512]{1,0:T(8,128)}, u32[]{:S(2)}, u32[]{:S(2)}) collective-permute-start(f32[768,512]{1,0:T(8,128)} %far_sum.2), channel_id=1, source_target_pairs={{0,16},{8,24},{16,0},{24,8},{1,17},{9,25},{17,1},{25,9},{2,18},{10... | collective-permute-start | bytes 4718600 | tf_op jit(solution)/shard_map/ppermute | solution.py:43
  147.7 3.6 %copy-start.6 = (bf16[256,512]{1,0:T(8,128)(2,1)}, bf16[256,512]{1,0:T(8,128)(2,1)S(1)}, u32[]{:S(2)}) copy-start(bf16[256,512]{1,0:T(8,128)(2,1)S(1)} %broadcast_select_fusion.7) | copy-start | bytes 786436
  150.0 23.5 %collective-permute-start.32 = (bf16[512,512]{1,0:T(8,128)(2,1)}, bf16[512,512]{1,0:T(8,128)(2,1)}, u32[]{:S(2)}, u32[]{:S(2)}) collective-permute-start(bf16[512,512]{1,0:T(8,128)(2,1)} %broadcast_select_fusion.5), channel_id=1, source_target_pairs={{0,2},{1,3},{4,6},{5,7},{10,8},{11,9},{14,12},{15,13},{20,22},{21,... | collective-permute-start | bytes 1572872 | tf_op jit(solution)/shard_map/ppermute | solution.py:466
  151.3 20.8 %collective-permute-start.30 = (bf16[256,512]{1,0:T(8,128)(2,1)S(1)}, bf16[256,512]{1,0:T(8,128)(2,1)}, u32[]{:S(2)}, u32[]{:S(2)}) collective-permute-start(bf16[256,512]{1,0:T(8,128)(2,1)S(1)} %broadcast_select_fusion.7), channel_id=1, source_target_pairs={{0,2},{1,3},{4,6},{5,7},{10,8},{11,9},{14,12},{15,13},{20,22},{21,... | collective-permute-start | bytes 786440 | tf_op jit(solution)/shard_map/ppermute | solution.py:466
  152.6 37.9 %collective-permute-start.29 = (bf16[1024,512]{1,0:T(8,128)(2,1)}, bf16[1024,512]{1,0:T(8,128)(2,1)}, u32[]{:S(2)}, u32[]{:S(2)}) collective-permute-start(bf16[1024,512]{1,0:T(8,128)(2,1)} %collective-permute-done.28), channel_id=1, source_target_pairs={{2,3},{3,2},{6,7},{7,6},{8,9},{9,8},{12,13},{13,12},{22,23},{23,22... | collective-permute-start | bytes 3145736 | tf_op jit(solution)/shard_map/ppermute | solution.py:478
  172.0 13.9 %collective-permute-start.34 = (bf16[512,512]{1,0:T(8,128)(2,1)}, bf16[512,512]{1,0:T(8,128)(2,1)}, u32[]{:S(2)}, u32[]{:S(2)}) collective-permute-start(bf16[512,512]{1,0:T(8,128)(2,1)} %broadcast_select_fusion.5), channel_id=1, source_target_pairs={{0,1},{1,0},{4,5},{5,4},{10,11},{11,10},{14,15},{15,14},{20,21},{2... | collective-permute-start | bytes 1572872 | tf_op jit(solution)/shard_map/ppermute | solution.py:478
  173.5 15.9 %collective-permute-start.33 = (bf16[512,512]{1,0:T(8,128)(2,1)}, bf16[512,512]{1,0:T(8,128)(2,1)}, u32[]{:S(2)}, u32[]{:S(2)}) collective-permute-start(bf16[512,512]{1,0:T(8,128)(2,1)} %collective-permute-done.32), channel_id=1, source_target_pairs={{2,3},{3,2},{6,7},{7,6},{8,9},{9,8},{12,13},{13,12},{22,23},{23,22... | collective-permute-start | bytes 1572872 | tf_op jit(solution)/shard_map/ppermute | solution.py:478
  177.1 17.3 %collective-permute-start.35 = (bf16[256,512]{1,0:T(8,128)(2,1)S(1)}, bf16[256,512]{1,0:T(8,128)(2,1)S(1)}, u32[]{:S(2)}, u32[]{:S(2)}) collective-permute-start(bf16[256,512]{1,0:T(8,128)(2,1)S(1)} %broadcast_select_fusion.6.refs_11_), channel_id=1, source_target_pairs={{0,1},{1,0},{4,5},{5,4},{2,3},{3,2},{6,7},{7,6},{10,11},{11,10},{1... | collective-permute-start | bytes 786440 | tf_op jit(solution)/shard_map/ppermute | solution.py:478
  186.0 5.9 %copy-start = (f32[1024,512]{1,0:T(8,128)S(1)}, f32[1024,512]{1,0:T(8,128)}, u32[]{:S(2)}) copy-start(f32[1024,512]{1,0:T(8,128)} %base_rows.1.refs_1_) | copy-start | bytes 6291460
  191.9 2.6 %copy-start.2 = (bf16[128,128]{1,0:T(8,128)(2,1)S(1)}, bf16[128,128]{1,0:T(8,128)(2,1)}, u32[]{:S(2)}) copy-start(bf16[128,128]{1,0:T(8,128)(2,1)} %copy-done.1) | copy-start | bytes 98308

commit v12 on v7

--- a/solution.py
+++ b/solution.py
@@ -522,12 +522,11 @@
     s01 = (s01[0], s01_held, (s01[2][0], s01_got))
     s2 = (s2[0], held, None)
     sq_hop = zone_hop((sq_hop[0], q_held, None))
-    early2 = early_hops(s2)
     s2 = zone_hop(s2)
     q_held, far_last, *early01 = tie((sq_hop[1], far_last, *early01))
     rq = inner_hops((sq_hop[0], q_held, None))
     r01 = inner_hops(s01, early01)
-    r2 = inner_hops(s2, early2)
+    r2 = inner_hops(s2)
 
     adds = [(root_front, 0, 0), (near, 0, 0), (far_near, 0, 0), (far_last, 1, 0)]
     base = rows_at(3 * n, n, adds, "base_rows")

time: 202 us -> 203 us (level)
  other arithmetic: 16.6 us -> 13.9 us
    ppermute x19, starting transfers between devices: 23.1 us -> 28.9 us  [flip(): return lax.ppermute(value, axis, [(i, i ^ bit) for i in range(size)])]
    ppermute x5 -> x4, waiting for transfers between devices: 11.4 us -> 6.51 us  [inner_hop(): return lax.ppermute(value, ('grp', 'mem'), pairs)]
    ppermute x6, waiting for transfers between devices: 11.9 us -> 14.9 us  [zone_hop(): got = lax.ppermute(held, ('grp', 'mem'), pairs)]
    select_n x6, other arithmetic: 5.49 us -> 2.67 us  [zone_hop(): return (have + new, jnp.where(among(new), got, held), (new, got))]
    ppermute x5 -> x4, starting transfers between devices: 7.92 us -> 5.1 us  [inner_hop(): return lax.ppermute(value, ('grp', 'mem'), pairs)]
  transfers between devices with their start and end apart: 36 -> 35, of which waited for: 12 -> 12; matrix products, arithmetic and copies ran while one was open for 9% -> 7% of each run, Pallas kernels for 25% -> 25%
where the time goes in v12:
time: 203 us; the launch traced here: 199 us
  waiting for transfers between devices  60.7 us (30%)
  starting transfers between devices  58.3 us (29%)
  Pallas kernels  57.7 us (28%)
  other arithmetic  13.9 us (7%)
  local copies, waits for them, and re-layouts  7.42 us (4%)
    ppermute x19, waiting for transfers between devices, flip(): return lax.ppermute(value, axis, [(i, i ^ bit) for i in range(size)])  37 us
    ppermute x19, starting transfers between devices, flip(): return lax.ppermute(value, axis, [(i, i ^ bit) for i in range(size)])  28.9 us
    pallas_call x6, Pallas kernels, take_rows(): pl.pallas_call(body, grid_spec=pltpu.PrefetchScalarGridSpec(num_scalar_pr...  21.5 us
    ppermute x6, starting transfers between devices, lead_hop(): got = lax.ppermute(held, 'mem', [(src, src ^ bit) for src in sources])  17.2 us
    ppermute x6, waiting for transfers between devices, zone_hop(): got = lax.ppermute(held, ('grp', 'mem'), pairs)  14.9 us
    pallas_call x1, Pallas kernels, local(): pl.pallas_call(leaf_two, grid=(1,), in_specs=[vmem, w_spec(0), w_spec(1),...  9.43 us
    pallas_call x1, Pallas kernels, local(): pl.pallas_call(root_step, in_specs=[smem] + [vmem] * 4, out_shape=(shape(...  8.96 us
    pallas_call x1, Pallas kernels, local(): pl.pallas_call(leaf_last, grid=(1,), in_specs=[vmem, w_spec(2)] + [vmem]...  7.58 us
  transfers between devices with their start and end apart: 35, of which 12 were waited for; matrix products, arithmetic and copies ran while one was open for 7% of the time, Pallas kernels for 25%

profile of v12, /device:TPU:1, one launch (start us, length us, event | category | flops | bytes accessed | tf_op | source)
XLA Modules:
  0.0 199.3 jit_solution(568709759249687695)
XLA Ops:
  0.6 2.1 %pick_pivots.1 = (f32[8,128]{1,0:T(8,128)}, f32[384,128]{1,0:T(8,128)}, f32[384,128]{1,0:T(8,128)}, f32[8,512]{1,0:T(8,128)}, f32[384,256]{1,0:T(8,128)}) custom-call(s32[4]{0:T(128)} %bitcast.55, s32[1]{0:T(128)} %bitcast.2.at_ref, f32[4096,512]{1,0:T(8,128)} %bitcast.29), custom_call_target="tpu_custom_call" | custom-call | tf_op jit(solution)/shard_map/pick_pivots/pallas_call | solution.py:346
  2.8 2.1 %collective-permute-start = (f32[8,128]{1,0:T(8,128)}, f32[8,128]{1,0:T(8,128)S(1)}, u32[]{:S(2)}, u32[]{:S(2)}) collective-permute-start(f32[8,128]{1,0:T(8,128)} %get-tuple-element.56), channel_id=1, source_target_pairs={{0,1},{1,0},{2,3},{3,2},{4,5},{5,4},{6,7},{7,6},{8,9},{9,8},{10,11... | collective-permute-start | bytes 12296 | tf_op jit(solution)/shard_map/ppermute | solution.py:43
  4.8 4.2 %collective-permute-start.4 = (f32[384,256]{1,0:T(8,128)}, f32[384,256]{1,0:T(8,128)S(1)}, u32[]{:S(2)}, u32[]{:S(2)}) collective-permute-start(f32[384,256]{1,0:T(8,128)} %get-tuple-element.59), channel_id=1, source_target_pairs={{0,4},{8,12},{16,20},{24,28}} | collective-permute-start | bytes 1179656 | tf_op jit(solution)/shard_map/ppermute | solution.py:342
  10.0 6.8 %collective-permute-done.1 = f32[8,128]{1,0:T(8,128)S(1)} collective-permute-done((f32[8,128]{1,0:T(8,128)S(1)}, f32[8,128]{1,0:T(8,128)S(1)}, u32[]{:S(2)}, u32[]{:S(2)}) %collective-permute-start.1) | collective-permute-done | bytes 4128 | tf_op jit(solution)/shard_map/ppermute | solution.py:43
  16.9 3.2 %collective-permute-done.2 = f32[8,128]{1,0:T(8,128)S(1)} collective-permute-done((f32[8,128]{1,0:T(8,128)S(1)}, f32[8,128]{1,0:T(8,128)S(1)}, u32[]{:S(2)}, u32[]{:S(2)}) %collective-permute-start.2) | collective-permute-done | bytes 4128 | tf_op jit(solution)/shard_map/ppermute | solution.py:43
  24.9 1.9 collective-permute-start.5
  27.5 3.3 %far_rows.1 = f32[1024,512]{1,0:T(8,128)} custom-call(s32[8]{0:T(128)} %get-tuple-element.120.refs_0_, s32[8]{0:T(128)} %get-tuple-element.117.refs_1_, s32[1]{0:T(128)} %constant.64.clone.1.refs_2_, f32[4096,512]{1,0:T(8,128)} %bitcast.30, f32[4096,512]{1,0:T(8,128)} %bitcast.31, f32[4096,512]{1,0:T(8,128)} %bitcast.32, f32[4096,512]{1,0:T(8,128)} %bitcast.33, ...), custom_call_target="tpu_custom_call" | custom-call | tf_op jit(solution)/shard_map/far_rows/pallas_call | solution.py:214
  30.8 2.8 %first_rows.1 = f32[256,512]{1,0:T(8,128)} custom-call(s32[2]{0:T(128)} %slice.53.refs_0_, s32[2]{0:T(128)} %slice.54.refs_1_, s32[1]{0:T(128)} %bitcast.10.refs_2_, f32[4096,512]{1,0:T(8,128)} %bitcast.34, f32[4096,512]{1,0:T(8,128)} %bitcast.35, f32[8,512]{1,0:T(8,128)} %get-tuple-element.61.refs_7_.refs_5_.mask_ref, f32[1024,512]{1,0:T(8,128)} %refs_8_.1), custom_call_target="tpu_custom_call" | custom-call | tf_op jit(solution)/shard_map/first_rows/pallas_call | solution.py:214
  33.6 3.4 %collective-permute-start.9 = (f32[384,256]{1,0:T(8,128)S(1)}, f32[384,256]{1,0:T(8,128)S(1)}, u32[]{:S(2)}, u32[]{:S(2)}) collective-permute-start(f32[384,256]{1,0:T(8,128)S(1)} %broadcast_select_fusion.9), channel_id=1, source_target_pairs={{0,1},{4,5},{8,9},{12,13},{16,17},{20,21},{24,25},{28,29}} | collective-permute-start | bytes 1179656 | tf_op jit(solution)/shard_map/ppermute | solution.py:342
  37.0 4.3 %collective-permute-start.10 = (f32[256,512]{1,0:T(8,128)}, f32[256,512]{1,0:T(8,128)S(1)}, u32[]{:S(2)}, u32[]{:S(2)}) collective-permute-start(f32[256,512]{1,0:T(8,128)} %first_rows.1), channel_id=1, source_target_pairs={{0,8},{8,0},{16,24},{24,16},{1,9},{9,1},{17,25},{25,17},{2,10},{10... | collective-permute-start | bytes 1572872 | tf_op jit(solution)/shard_map/ppermute | solution.py:43
  41.3 3.3 %near_rows.1 = f32[1024,512]{1,0:T(8,128)} custom-call(s32[8]{0:T(128)} %get-tuple-element.119.refs_0_, s32[8]{0:T(128)} %get-tuple-element.116.refs_1_, s32[1]{0:T(128)} %constant.64.clone.1.refs_2_, f32[4096,512]{1,0:T(8,128)} %bitcast.36, f32[4096,512]{1,0:T(8,128)} %bitcast.37, f32[4096,512]{1,0:T(8,128)} %bitcast.38, f32[4096,512]{1,0:T(8,128)} %bitcast.39, ...), custom_call_target="tpu_custom_call" | custom-call | tf_op jit(solution)/shard_map/near_rows/pallas_call | solution.py:214
  44.6 6.0 %collective-permute-done.8 = f32[384,128]{1,0:T(8,128)S(1)} collective-permute-done((f32[384,128]{1,0:T(8,128)S(1)}, f32[384,128]{1,0:T(8,128)S(1)}, u32[]{:S(2)}, u32[]{:S(2)}) %collective-permute-start.8) | collective-permute-done | bytes 196640 | tf_op jit(solution)/shard_map/ppermute | solution.py:43
  50.6 2.2 %collective-permute-done.7 = f32[384,128]{1,0:T(8,128)S(1)} collective-permute-done((f32[384,128]{1,0:T(8,128)S(1)}, f32[384,128]{1,0:T(8,128)S(1)}, u32[]{:S(2)}, u32[]{:S(2)}) %collective-permute-start.7) | collective-permute-done | bytes 196640 | tf_op jit(solution)/shard_map/ppermute | solution.py:43
  54.7 1.3 collective-permute-start.13
  56.0 1.3 collective-permute-start.14
  57.3 2.1 %collective-permute-start.12 = (f32[384,128]{1,0:T(8,128)S(1)}, f32[384,128]{1,0:T(8,128)S(1)}, u32[]{:S(2)}, u32[]{:S(2)}) collective-permute-start(f32[384,128]{1,0:T(8,128)S(1)} %add.159), channel_id=1, source_target_pairs={{0,4},{1,5},{2,6},{3,7},{4,0},{5,1},{6,2},{7,3},{8,12},{9,13},{10,... | collective-permute-start | bytes 589832 | tf_op jit(solution)/shard_map/ppermute | solution.py:43
  59.4 9.4 %leaf_two.1 = (bf16[256,512]{1,0:T(8,128)(2,1)}, f32[128,128]{1,0:T(8,128)}, f32[128,128]{1,0:T(8,128)}, bf16[128,128]{1,0:T(8,128)(2,1)}, f32[8,128]{1,0:T(8,128)}) custom-call(f32[384,128]{1,0:T(8,128)} %add.158.head_ref, f32[4096,512]{1,0:T(8,128)} %bitcast.41, f32[4096,512]{1,0:T(8,128)} %bitcast.40, f32[8,512]{1,0:T(8,128)} %get-tuple-element.61.refs_7_.refs_5_.mask_ref), custom_call_target="tpu_custom_call" | custom-call | tf_op jit(solution)/shard_map/leaf_two/pallas_call | solution.py:415
  70.6 1.3 collective-permute-start.16
  72.5 5.0 %collective-permute-start.18 = (f32[256,256]{1,0:T(8,128)S(1)}, f32[256,256]{1,0:T(8,128)S(1)}, u32[]{:S(2)}, u32[]{:S(2)}) collective-permute-start(f32[256,256]{1,0:T(8,128)S(1)} %slice.57), channel_id=1, source_target_pairs={{0,4},{8,12},{16,20},{24,28}} | collective-permute-start | bytes 786440 | tf_op jit(solution)/shard_map/ppermute | solution.py:342
  77.8 1.7 collective-permute-start.17
  80.1 3.3 %far_sum.2 = f32[512,512]{1,0:T(8,128)} custom-call(s32[4]{0:T(128)} %get-tuple-element.115.refs_0_, s32[4]{0:T(128)} %get-tuple-element.113.refs_1_, s32[1]{0:T(128)} %constant.64.clone.1.refs_2_, f32[4096,512]{1,0:T(8,128)} %bitcast.42, f32[4096,512]{1,0:T(8,128)} %bitcast.43, f32[4096,512]{1,0:T(8,128)} %bitcast.44, f32[4096,512]{1,0:T(8,128)} %bitcast.45, ...), custom_call_target="tpu_custom_call" | custom-call | tf_op jit(solution)/shard_map/far_sum/pallas_call | solution.py:214
  83.5 1.2 collective-permute-start.21
  85.8 2.0 %collective-permute-start.20 = (f32[256,256]{1,0:T(8,128)S(1)}, f32[256,256]{1,0:T(8,128)}, u32[]{:S(2)}, u32[]{:S(2)}) collective-permute-start(f32[256,256]{1,0:T(8,128)S(1)} %broadcast_select_fusion.12), channel_id=1, source_target_pairs={{0,1},{4,5},{8,9},{12,13},{16,17},{20,21},{24,25},{28,29}} | collective-permute-start | bytes 786440 | tf_op jit(solution)/shard_map/ppermute | solution.py:342
  87.8 7.6 %leaf_last.1 = bf16[336,512]{1,0:T(8,128)(2,1)} custom-call(f32[384,128]{1,0:T(8,128)} %add.161.rest_ref, f32[4096,512]{1,0:T(8,128)} %bitcast.46, f32[384,256]{1,0:T(8,128)} %broadcast_select_fusion.7.w_lead_ref, f32[8,128]{1,0:T(8,128)} %copy-done.9, f32[8,512]{1,0:T(8,128)} %get-tuple-element.61.refs_7_.refs_5_.mask_ref, ...), custom_call_target="tpu_custom_call" | custom-call | tf_op jit(solution)/shard_map/leaf_last/pallas_call | solution.py:439
  95.7 1.7 collective-permute-start.23
  97.4 11.1 %collective-permute-done.21.refs_10_ = f32[512,512]{1,0:T(8,128)S(1)} collective-permute-done((f32[512,512]{1,0:T(8,128)}, f32[512,512]{1,0:T(8,128)S(1)}, u32[]{:S(2)}, u32[]{:S(2)}) %collective-permute-start.21) | collective-permute-done | bytes 1048608 | tf_op jit(solution)/shard_map/ppermute | solution.py:43
  108.5 7.4 %collective-permute-done.19 = bf16[336,512]{1,0:T(8,128)(2,1)S(1)} collective-permute-done((bf16[336,512]{1,0:T(8,128)(2,1)}, bf16[336,512]{1,0:T(8,128)(2,1)S(1)}, u32[]{:S(2)}, u32[]{:S(2)}) %collective-permute-start.19) | collective-permute-done | bytes 344096 | tf_op jit(solution)/shard_map/ppermute | solution.py:43
  115.8 1.9 pad_maximum_fusion.2
  118.5 1.3 collective-permute-start.24
  119.9 3.5 %far_sum.3 = f32[512,512]{1,0:T(8,128)} custom-call(s32[4]{0:T(128)} %get-tuple-element.114.refs_0_, s32[4]{0:T(128)} %get-tuple-element.112.refs_1_, s32[1]{0:T(128)} %constant.64.clone.1.refs_2_, f32[4096,512]{1,0:T(8,128)} %bitcast.47, f32[4096,512]{1,0:T(8,128)} %bitcast.48, f32[4096,512]{1,0:T(8,128)} %bitcast.49, f32[4096,512]{1,0:T(8,128)} %bitcast.50, ...), custom_call_target="tpu_custom_call" | custom-call | tf_op jit(solution)/shard_map/far_sum/pallas_call | solution.py:214
  123.3 2.3 %collective-permute-done.24 = f32[256,256]{1,0:T(8,128)S(1)} collective-permute-done((f32[256,256]{1,0:T(8,128)S(1)}, f32[256,256]{1,0:T(8,128)S(1)}, u32[]{:S(2)}, u32[]{:S(2)}) %collective-permute-start.24) | collective-permute-done | bytes 262176 | tf_op jit(solution)/shard_map/ppermute | solution.py:342
  125.7 1.2 pad_maximum_fusion.pack_ref
  128.0 1.3 collective-permute-start.27
  130.1 9.0 %root_step.1 = (bf16[256,512]{1,0:T(8,128)(2,1)S(1)}, f32[128,128]{1,0:T(8,128)S(1)}, f32[128,128]{1,0:T(8,128)S(1)}, bf16[128,128]{1,0:T(8,128)(2,1)S(1)}, f32[8,128]{1,0:T(8,128)S(1)}) custom-call(s32[4]{0:T(128)S(1)} %pad_add_fusion.1.leaf_ref, f32[256,256]{1,0:T(8,128)S(1)} %broadcast_select_fusion.10.corner_ref, f32[256,512]{1,0:T(8,128)S(1)} %add.162.first_ref, ...), custom_call_target="tpu_custom_call" | custom-call | tf_op jit(solution)/shard_map/root_step/pallas_call | solution.py:512
  140.3 11.0 %collective-permute-start.11 = (f32[1024,512]{1,0:T(8,128)}, f32[1024,512]{1,0:T(8,128)}, u32[]{:S(2)}, u32[]{:S(2)}) collective-permute-start(f32[1024,512]{1,0:T(8,128)} %near_rows.1), channel_id=1, source_target_pairs={{0,8},{8,0},{16,24},{24,16},{1,9},{9,1},{17,25},{25,17},{2,10},{10... | collective-permute-start | bytes 6291464 | tf_op jit(solution)/shard_map/ppermute | solution.py:43
  151.3 1.7 collective-permute-start.30
  153.2 1.3 broadcast_select_fusion.1.refs_3_
  154.6 1.3 collective-permute-start.32
  155.9 1.9 collective-permute-start.31
  158.4 9.0 %collective-permute-done.32 = bf16[512,512]{1,0:T(8,128)(2,1)S(1)} collective-permute-done((bf16[512,512]{1,0:T(8,128)(2,1)S(1)}, bf16[512,512]{1,0:T(8,128)(2,1)S(1)}, u32[]{:S(2)}, u32[]{:S(2)}) %collective-permute-start.32) | collective-permute-done | bytes 524320 | tf_op jit(solution)/shard_map/ppermute | solution.py:465
  167.4 1.5 collective-permute-start.28
  169.0 5.9 %collective-permute-done.28 = bf16[256,512]{1,0:T(8,128)(2,1)S(1)} collective-permute-done((bf16[256,512]{1,0:T(8,128)(2,1)S(1)}, bf16[256,512]{1,0:T(8,128)(2,1)S(1)}, u32[]{:S(2)}, u32[]{:S(2)}) %collective-permute-start.28) | collective-permute-done | bytes 262176 | tf_op jit(solution)/shard_map/ppermute | solution.py:465
  175.9 1.5 collective-permute-start.34
  177.4 5.3 %base_rows.1.refs_1_ = f32[1024,512]{1,0:T(8,128)} custom-call(s32[8]{0:T(128)} %get-tuple-element.121.refs_0_, s32[8]{0:T(128)} %get-tuple-element.118.refs_1_, s32[1]{0:T(128)} %constant.64.clone.1.refs_2_, f32[4096,512]{1,0:T(8,128)} %bitcast.51, f32[4096,512]{1,0:T(8,128)} %bitcast.52, f32[4096,512]{1,0:T(8,128)} %bitcast.53, f32[4096,512]{1,0:T(8,128)} %bitcast.54, ...), custom_call_target="tpu_custom_call" | custom-call | tf_op jit(solution)/shard_map/base_rows/pallas_call | solution.py:214
  182.8 1.5 broadcast_select_fusion.refs_4_
  184.7 2.1 %update.1.refs_2_ = f32[1024,512]{1,0:T(8,128)S(1)} custom-call(s32[2]{0:T(128)S(1)} %iota_xor_fusion.refs_0_, f32[1024,512]{1,0:T(8,128)S(1)} %copy-done, bf16[1024,512]{1,0:T(8,128)(2,1)S(1)} %pad_maximum_fusion.1.d01_ref.refs_2_, bf16[1024,512]{1,0:T(8,128)(2,1)S(1)} %broadcast_select_fusion.1.refs_3_, bf16[1024,512]{1,0:T(8,128)(2,1)S(1)} %broadcast_select_fusion.refs_4_), custom_call_target="tpu_custom_call" | custom-call | tf_op jit(solution)/shard_map/update/pallas_call | solution.py:541
  186.7 6.5 %collective-permute-done.34.refs_12_ = bf16[256,512]{1,0:T(8,128)(2,1)S(1)} collective-permute-done((bf16[256,512]{1,0:T(8,128)(2,1)S(1)}, bf16[256,512]{1,0:T(8,128)(2,1)S(1)}, u32[]{:S(2)}, u32[]{:S(2)}) %collective-permute-start.34) | collective-permute-done | bytes 262176 | tf_op jit(solution)/shard_map/ppermute | solution.py:477
  193.3 6.0 %finish.1 = f32[1024,512]{1,0:T(8,128)} custom-call(s32[2]{0:T(128)S(1)} %iota_xor_fusion.refs_0_, s32[3]{0:T(128)S(1)} %pad_add_fusion.refs_1_, f32[1024,512]{1,0:T(8,128)S(1)} %update.1.refs_2_, bf16[512,512]{1,0:T(8,128)(2,1)S(1)} %bitcast.28, bf16[256,512]{1,0:T(8,128)(2,1)S(1)} %get-tuple-element.96.refs_4_, f32[128,128]{1,0:T(8,128)S(1)} %get-tuple-element.104.refs_5_, ...), custom_call_target="tpu_custom_call" | custom-call | tf_op jit(solution)/shard_map/finish/pallas_call | solution.py:566
  (109 shorter events, 19.4 us)
Async XLA Ops:
  2.7 22.2 %copy-start.8 = (f32[384,128]{1,0:T(8,128)S(1)}, f32[384,128]{1,0:T(8,128)}, u32[]{:S(2)}) copy-start(f32[384,128]{1,0:T(8,128)} %get-tuple-element.63) | copy-start | bytes 589828
  2.8 6.5 %collective-permute-start = (f32[8,128]{1,0:T(8,128)}, f32[8,128]{1,0:T(8,128)S(1)}, u32[]{:S(2)}, u32[]{:S(2)}) collective-permute-start(f32[8,128]{1,0:T(8,128)} %get-tuple-element.56), channel_id=1, source_target_pairs={{0,1},{1,0},{2,3},{3,2},{4,5},{5,4},{6,7},{7,6},{8,9},{9,8},{10,11... | collective-permute-start | bytes 12296 | tf_op jit(solution)/shard_map/ppermute | solution.py:43
  4.8 16.3 %collective-permute-start.4 = (f32[384,256]{1,0:T(8,128)}, f32[384,256]{1,0:T(8,128)S(1)}, u32[]{:S(2)}, u32[]{:S(2)}) collective-permute-start(f32[384,256]{1,0:T(8,128)} %get-tuple-element.59), channel_id=1, source_target_pairs={{0,4},{8,12},{16,20},{24,28}} | collective-permute-start | bytes 1179656 | tf_op jit(solution)/shard_map/ppermute | solution.py:342
  9.1 11.1 %collective-permute-start.3 = (f32[384,128]{1,0:T(8,128)}, f32[384,128]{1,0:T(8,128)S(1)}, u32[]{:S(2)}, u32[]{:S(2)}) collective-permute-start(f32[384,128]{1,0:T(8,128)} %get-tuple-element.57), channel_id=1, source_target_pairs={{0,1},{1,0},{2,3},{3,2},{4,5},{5,4},{6,7},{7,6},{8,9},{9,8},{10,11... | collective-permute-start | bytes 589832 | tf_op jit(solution)/shard_map/ppermute | solution.py:43
  10.0 6.8 %collective-permute-start.1 = (f32[8,128]{1,0:T(8,128)S(1)}, f32[8,128]{1,0:T(8,128)S(1)}, u32[]{:S(2)}, u32[]{:S(2)}) collective-permute-start(f32[8,128]{1,0:T(8,128)S(1)} %add.150), channel_id=1, source_target_pairs={{0,2},{1,3},{2,0},{3,1},{4,6},{5,7},{6,4},{7,5},{8,10},{9,11},{10,... | collective-permute-start | bytes 12296 | tf_op jit(solution)/shard_map/ppermute | solution.py:43
  16.8 3.4 %collective-permute-start.2 = (f32[8,128]{1,0:T(8,128)S(1)}, f32[8,128]{1,0:T(8,128)S(1)}, u32[]{:S(2)}, u32[]{:S(2)}) collective-permute-start(f32[8,128]{1,0:T(8,128)S(1)} %add.151), channel_id=1, source_target_pairs={{0,4},{1,5},{2,6},{3,7},{4,0},{5,1},{6,2},{7,3},{8,12},{9,13},{10,... | collective-permute-start | bytes 12296 | tf_op jit(solution)/shard_map/ppermute | solution.py:43
  20.2 10.6 %copy-start.9 = (f32[8,128]{1,0:T(8,128)}, f32[8,128]{1,0:T(8,128)S(1)}, u32[]{:S(2)}) copy-start(f32[8,128]{1,0:T(8,128)S(1)} %add.152.table_ref) | copy-start | bytes 12292
  24.9 8.6 %collective-permute-start.6 = (f32[384,128]{1,0:T(8,128)S(1)}, f32[384,128]{1,0:T(8,128)S(1)}, u32[]{:S(2)}, u32[]{:S(2)}) collective-permute-start(f32[384,128]{1,0:T(8,128)S(1)} %copy-done.8), channel_id=1, source_target_pairs={{0,1},{1,0},{2,3},{3,2},{4,5},{5,4},{6,7},{7,6},{8,9},{9,8},{10,11... | collective-permute-start | bytes 589832 | tf_op jit(solution)/shard_map/ppermute | solution.py:43
  24.9 8.7 %collective-permute-start.5 = (f32[384,128]{1,0:T(8,128)S(1)}, f32[384,128]{1,0:T(8,128)S(1)}, u32[]{:S(2)}, u32[]{:S(2)}) collective-permute-start(f32[384,128]{1,0:T(8,128)S(1)} %add.153), channel_id=1, source_target_pairs={{0,2},{1,3},{2,0},{3,1},{4,6},{5,7},{6,4},{7,5},{8,10},{9,11},{10,... | collective-permute-start | bytes 589832 | tf_op jit(solution)/shard_map/ppermute | solution.py:43
  33.6 19.9 %collective-permute-start.9 = (f32[384,256]{1,0:T(8,128)S(1)}, f32[384,256]{1,0:T(8,128)S(1)}, u32[]{:S(2)}, u32[]{:S(2)}) collective-permute-start(f32[384,256]{1,0:T(8,128)S(1)} %broadcast_select_fusion.9), channel_id=1, source_target_pairs={{0,1},{4,5},{8,9},{12,13},{16,17},{20,21},{24,25},{28,29}} | collective-permute-start | bytes 1179656 | tf_op jit(solution)/shard_map/ppermute | solution.py:342
  37.0 16.6 %collective-permute-start.10 = (f32[256,512]{1,0:T(8,128)}, f32[256,512]{1,0:T(8,128)S(1)}, u32[]{:S(2)}, u32[]{:S(2)}) collective-permute-start(f32[256,512]{1,0:T(8,128)} %first_rows.1), channel_id=1, source_target_pairs={{0,8},{8,0},{16,24},{24,16},{1,9},{9,1},{17,25},{25,17},{2,10},{10... | collective-permute-start | bytes 1572872 | tf_op jit(solution)/shard_map/ppermute | solution.py:43
  41.3 9.3 %collective-permute-start.8 = (f32[384,128]{1,0:T(8,128)S(1)}, f32[384,128]{1,0:T(8,128)S(1)}, u32[]{:S(2)}, u32[]{:S(2)}) collective-permute-start(f32[384,128]{1,0:T(8,128)S(1)} %add.157), channel_id=1, source_target_pairs={{0,2},{1,3},{2,0},{3,1},{4,6},{5,7},{6,4},{7,5},{8,10},{9,11},{10,... | collective-permute-start | bytes 589832 | tf_op jit(solution)/shard_map/ppermute | solution.py:43
  41.3 11.5 %collective-permute-start.7 = (f32[384,128]{1,0:T(8,128)S(1)}, f32[384,128]{1,0:T(8,128)S(1)}, u32[]{:S(2)}, u32[]{:S(2)}) collective-permute-start(f32[384,128]{1,0:T(8,128)S(1)} %add.156), channel_id=1, source_target_pairs={{0,4},{1,5},{2,6},{3,7},{4,0},{5,1},{6,2},{7,3},{8,12},{9,13},{10,... | collective-permute-start | bytes 589832 | tf_op jit(solution)/shard_map/ppermute | solution.py:43
  44.6 9.0 %copy-start.5 = (f32[256,512]{1,0:T(8,128)S(1)}, f32[256,512]{1,0:T(8,128)}, u32[]{:S(2)}) copy-start(f32[256,512]{1,0:T(8,128)} %first_rows.1) | copy-start | bytes 1572868
  53.7 16.9 %collective-permute-start.15 = (f32[1024,512]{1,0:T(8,128)}, f32[1024,512]{1,0:T(8,128)}, u32[]{:S(2)}, u32[]{:S(2)}) collective-permute-start(f32[1024,512]{1,0:T(8,128)} %far_rows.1), channel_id=1, source_target_pairs={{0,8},{8,0},{16,24},{24,16},{1,9},{9,1},{17,25},{25,17},{2,10},{10... | collective-permute-start | bytes 6291464 | tf_op jit(solution)/shard_map/ppermute | solution.py:43
  54.7 14.9 %collective-permute-start.13 = (f32[384,256]{1,0:T(8,128)S(1)}, f32[384,256]{1,0:T(8,128)S(1)}, u32[]{:S(2)}, u32[]{:S(2)}) collective-permute-start(f32[384,256]{1,0:T(8,128)S(1)} %broadcast_select_fusion.8), channel_id=1, source_target_pairs={{0,2},{1,3},{4,6},{5,7},{8,10},{9,11},{12,14},{13,15},{16,18},{17,... | collective-permute-start | bytes 1179656 | tf_op jit(solution)/shard_map/ppermute | solution.py:342
  56.0 14.4 %collective-permute-start.14 = (f32[256,512]{1,0:T(8,128)S(1)}, f32[256,512]{1,0:T(8,128)S(1)}, u32[]{:S(2)}, u32[]{:S(2)}) collective-permute-start(f32[256,512]{1,0:T(8,128)S(1)} %add.160), channel_id=1, source_target_pairs={{0,16},{8,24},{16,0},{24,8},{1,17},{9,25},{17,1},{25,9},{2,18},{10... | collective-permute-start | bytes 1572872 | tf_op jit(solution)/shard_map/ppermute | solution.py:43
  57.3 11.6 %collective-permute-start.12 = (f32[384,128]{1,0:T(8,128)S(1)}, f32[384,128]{1,0:T(8,128)S(1)}, u32[]{:S(2)}, u32[]{:S(2)}) collective-permute-start(f32[384,128]{1,0:T(8,128)S(1)} %add.159), channel_id=1, source_target_pairs={{0,4},{1,5},{2,6},{3,7},{4,0},{5,1},{6,2},{7,3},{8,12},{9,13},{10,... | collective-permute-start | bytes 589832 | tf_op jit(solution)/shard_map/ppermute | solution.py:43
  68.8 1.8 copy-start.4
  70.6 7.2 %collective-permute-start.16 = (bf16[256,512]{1,0:T(8,128)(2,1)S(1)}, bf16[256,512]{1,0:T(8,128)(2,1)S(1)}, u32[]{:S(2)}, u32[]{:S(2)}) collective-permute-start(bf16[256,512]{1,0:T(8,128)(2,1)S(1)} %copy-done.4), channel_id=1, source_target_pairs={{0,16},{8,24},{16,0},{24,8},{1,17},{9,25},{17,1},{25,9},{2,18},{10... | collective-permute-start | bytes 786440 | tf_op jit(solution)/shard_map/ppermute | solution.py:43
  72.5 12.2 %collective-permute-start.18 = (f32[256,256]{1,0:T(8,128)S(1)}, f32[256,256]{1,0:T(8,128)S(1)}, u32[]{:S(2)}, u32[]{:S(2)}) collective-permute-start(f32[256,256]{1,0:T(8,128)S(1)} %slice.57), channel_id=1, source_target_pairs={{0,4},{8,12},{16,20},{24,28}} | collective-permute-start | bytes 786440 | tf_op jit(solution)/shard_map/ppermute | solution.py:342
  77.8 6.9 %collective-permute-start.17 = (bf16[512,512]{1,0:T(8,128)(2,1)S(1)}, bf16[512,512]{1,0:T(8,128)(2,1)}, u32[]{:S(2)}, u32[]{:S(2)}) collective-permute-start(bf16[512,512]{1,0:T(8,128)(2,1)S(1)} %pad_maximum_fusion.3), channel_id=1, source_target_pairs={{0,8},{8,0},{16,24},{24,16},{1,9},{9,1},{17,25},{25,17},{2,10},{10... | collective-permute-start | bytes 1572872 | tf_op jit(solution)/shard_map/ppermute | solution.py:43
  83.5 25.0 %collective-permute-start.21 = (f32[512,512]{1,0:T(8,128)}, f32[512,512]{1,0:T(8,128)S(1)}, u32[]{:S(2)}, u32[]{:S(2)}) collective-permute-start(f32[512,512]{1,0:T(8,128)} %far_sum.2), channel_id=1, source_target_pairs={{0,16},{8,24},{16,0},{24,8},{1,17},{9,25},{17,1},{25,9},{2,18},{10... | collective-permute-start | bytes 3145736 | tf_op jit(solution)/shard_map/ppermute | solution.py:43
  85.8 11.5 %collective-permute-start.20 = (f32[256,256]{1,0:T(8,128)S(1)}, f32[256,256]{1,0:T(8,128)}, u32[]{:S(2)}, u32[]{:S(2)}) collective-permute-start(f32[256,256]{1,0:T(8,128)S(1)} %broadcast_select_fusion.12), channel_id=1, source_target_pairs={{0,1},{4,5},{8,9},{12,13},{16,17},{20,21},{24,25},{28,29}} | collective-permute-start | bytes 786440 | tf_op jit(solution)/shard_map/ppermute | solution.py:342
  95.4 20.4 %collective-permute-start.19 = (bf16[336,512]{1,0:T(8,128)(2,1)}, bf16[336,512]{1,0:T(8,128)(2,1)S(1)}, u32[]{:S(2)}, u32[]{:S(2)}) collective-permute-start(bf16[336,512]{1,0:T(8,128)(2,1)} %leaf_last.1), channel_id=1, source_target_pairs={{0,16},{8,24},{16,0},{24,8},{1,17},{9,25},{17,1},{25,9},{2,18},{10... | collective-permute-start | bytes 1032200 | tf_op jit(solution)/shard_map/ppermute | solution.py:43
  95.7 31.2 %collective-permute-start.23 = (bf16[1024,512]{1,0:T(8,128)(2,1)S(1)}, bf16[1024,512]{1,0:T(8,128)(2,1)}, u32[]{:S(2)}, u32[]{:S(2)}) collective-permute-start(bf16[1024,512]{1,0:T(8,128)(2,1)S(1)} %pad_maximum_fusion.1.d01_ref.refs_2_), channel_id=1, source_target_pairs={{0,4},{1,5},{10,14},{11,15},{20,16},{21,17},{30,26},{31,27}} | collective-permute-start | bytes 3145736 | tf_op jit(solution)/shard_map/ppermute | solution.py:465
  108.5 14.9 %copy-start.6 = (f32[512,512]{1,0:T(8,128)}, f32[512,512]{1,0:T(8,128)S(1)}, u32[]{:S(2)}) copy-start(f32[512,512]{1,0:T(8,128)S(1)} %collective-permute-done.21.refs_10_) | copy-start | bytes 3145732
  117.7 7.9 %collective-permute-start.22 = (bf16[672,512]{1,0:T(8,128)(2,1)}, bf16[672,512]{1,0:T(8,128)(2,1)}, u32[]{:S(2)}, u32[]{:S(2)}) collective-permute-start(bf16[672,512]{1,0:T(8,128)(2,1)} %pad_maximum_fusion.2), channel_id=1, source_target_pairs={{0,8},{8,0},{16,24},{24,16},{1,9},{9,1},{17,25},{25,17},{2,10},{10... | collective-permute-start | bytes 2064392 | tf_op jit(solution)/shard_map/ppermute | solution.py:43
  118.5 7.1 %collective-permute-start.24 = (f32[256,256]{1,0:T(8,128)S(1)}, f32[256,256]{1,0:T(8,128)S(1)}, u32[]{:S(2)}, u32[]{:S(2)}) collective-permute-start(f32[256,256]{1,0:T(8,128)S(1)} %broadcast_select_fusion.11), channel_id=1, source_target_pairs={{0,2},{1,3},{4,6},{5,7},{8,10},{9,11},{12,14},{13,15},{16,18},{17,... | collective-permute-start | bytes 786440 | tf_op jit(solution)/shard_map/ppermute | solution.py:342
  119.8 5.8 %copy-start.3 = (bf16[336,512]{1,0:T(8,128)(2,1)S(1)}, bf16[336,512]{1,0:T(8,128)(2,1)}, u32[]{:S(2)}) copy-start(bf16[336,512]{1,0:T(8,128)(2,1)} %leaf_last.1) | copy-start | bytes 1032196
  128.0 25.3 %collective-permute-start.27 = (bf16[1024,512]{1,0:T(8,128)(2,1)}, bf16[1024,512]{1,0:T(8,128)(2,1)}, u32[]{:S(2)}, u32[]{:S(2)}) collective-permute-start(bf16[1024,512]{1,0:T(8,128)(2,1)} %broadcast_select_fusion.2), channel_id=1, source_target_pairs={{0,2},{1,3},{4,6},{5,7},{10,8},{11,9},{14,12},{15,13},{20,22},{21,... | collective-permute-start | bytes 3145736 | tf_op jit(solution)/shard_map/ppermute | solution.py:465
  129.3 23.8 %collective-permute-start.26 = (bf16[512,512]{1,0:T(8,128)(2,1)S(1)}, bf16[512,512]{1,0:T(8,128)(2,1)S(1)}, u32[]{:S(2)}, u32[]{:S(2)}) collective-permute-start(bf16[512,512]{1,0:T(8,128)(2,1)S(1)} %bitcast.27), channel_id=1, source_target_pairs={{0,4},{1,5},{10,14},{11,15},{20,16},{21,17},{30,26},{31,27}} | collective-permute-start | bytes 1572872 | tf_op jit(solution)/shard_map/ppermute | solution.py:465
  139.0 0.6 copy-start.1
  139.7 13.4 %collective-permute-start.25 = (bf16[256,512]{1,0:T(8,128)(2,1)S(1)}, bf16[256,512]{1,0:T(8,128)(2,1)S(1)}, u32[]{:S(2)}, u32[]{:S(2)}) collective-permute-start(bf16[256,512]{1,0:T(8,128)(2,1)S(1)} %get-tuple-element.96.refs_4_), channel_id=1, source_target_pairs={{0,4},{1,5},{10,14},{11,15},{20,16},{21,17},{30,26},{31,27}} | collective-permute-start | bytes 786440 | tf_op jit(solution)/shard_map/ppermute | solution.py:465
  140.3 37.1 %collective-permute-start.11 = (f32[1024,512]{1,0:T(8,128)}, f32[1024,512]{1,0:T(8,128)}, u32[]{:S(2)}, u32[]{:S(2)}) collective-permute-start(f32[1024,512]{1,0:T(8,128)} %near_rows.1), channel_id=1, source_target_pairs={{0,8},{8,0},{16,24},{24,16},{1,9},{9,1},{17,25},{25,17},{2,10},{10... | collective-permute-start | bytes 6291464 | tf_op jit(solution)/shard_map/ppermute | solution.py:43
  151.3 24.6 %collective-permute-start.30 = (bf16[1024,512]{1,0:T(8,128)(2,1)}, bf16[1024,512]{1,0:T(8,128)(2,1)}, u32[]{:S(2)}, u32[]{:S(2)}) collective-permute-start(bf16[1024,512]{1,0:T(8,128)(2,1)} %broadcast_select_fusion.2), channel_id=1, source_target_pairs={{0,1},{1,0},{4,5},{5,4},{10,11},{11,10},{14,15},{15,14},{20,21},{2... | collective-permute-start | bytes 3145736 | tf_op jit(solution)/shard_map/ppermute | solution.py:477
  153.0 21.9 %collective-permute-start.29 = (f32[512,512]{1,0:T(8,128)}, f32[512,512]{1,0:T(8,128)S(1)}, u32[]{:S(2)}, u32[]{:S(2)}) collective-permute-start(f32[512,512]{1,0:T(8,128)} %far_sum.3), channel_id=1, source_target_pairs={{0,16},{8,24},{16,0},{24,8},{1,17},{9,25},{17,1},{25,9},{2,18},{10... | collective-permute-start | bytes 3145736 | tf_op jit(solution)/shard_map/ppermute | solution.py:43
  154.6 12.8 %collective-permute-start.32 = (bf16[512,512]{1,0:T(8,128)(2,1)S(1)}, bf16[512,512]{1,0:T(8,128)(2,1)S(1)}, u32[]{:S(2)}, u32[]{:S(2)}) collective-permute-start(bf16[512,512]{1,0:T(8,128)(2,1)S(1)} %broadcast_select_fusion.4), channel_id=1, source_target_pairs={{0,2},{1,3},{4,6},{5,7},{10,8},{11,9},{14,12},{15,13},{20,22},{21,... | collective-permute-start | bytes 1572872 | tf_op jit(solution)/shard_map/ppermute | solution.py:465
  155.9 26.9 %collective-permute-start.31 = (bf16[1024,512]{1,0:T(8,128)(2,1)}, bf16[1024,512]{1,0:T(8,128)(2,1)}, u32[]{:S(2)}, u32[]{:S(2)}) collective-permute-start(bf16[1024,512]{1,0:T(8,128)(2,1)} %collective-permute-done.27), channel_id=1, source_target_pairs={{2,3},{3,2},{6,7},{7,6},{8,9},{9,8},{12,13},{13,12},{22,23},{23,22... | collective-permute-start | bytes 3145736 | tf_op jit(solution)/shard_map/ppermute | solution.py:477
  167.4 7.5 %collective-permute-start.28 = (bf16[256,512]{1,0:T(8,128)(2,1)S(1)}, bf16[256,512]{1,0:T(8,128)(2,1)S(1)}, u32[]{:S(2)}, u32[]{:S(2)}) collective-permute-start(bf16[256,512]{1,0:T(8,128)(2,1)S(1)} %broadcast_select_fusion.5), channel_id=1, source_target_pairs={{0,2},{1,3},{4,6},{5,7},{10,8},{11,9},{14,12},{15,13},{20,22},{21,... | collective-permute-start | bytes 786440 | tf_op jit(solution)/shard_map/ppermute | solution.py:465
  174.9 18.3 %collective-permute-start.33 = (bf16[512,512]{1,0:T(8,128)(2,1)S(1)}, bf16[512,512]{1,0:T(8,128)(2,1)}, u32[]{:S(2)}, u32[]{:S(2)}) collective-permute-start(bf16[512,512]{1,0:T(8,128)(2,1)S(1)} %broadcast_select_fusion.3.refs_9_), channel_id=1, source_target_pairs={{0,1},{1,0},{4,5},{5,4},{2,3},{3,2},{6,7},{7,6},{10,11},{11,10},{1... | collective-permute-start | bytes 1572872 | tf_op jit(solution)/shard_map/ppermute | solution.py:477
  175.0 1.0 copy-start.7
  175.9 17.3 %collective-permute-start.34 = (bf16[256,512]{1,0:T(8,128)(2,1)S(1)}, bf16[256,512]{1,0:T(8,128)(2,1)S(1)}, u32[]{:S(2)}, u32[]{:S(2)}) collective-permute-start(bf16[256,512]{1,0:T(8,128)(2,1)S(1)} %broadcast_select_fusion.6.refs_11_), channel_id=1, source_target_pairs={{0,1},{1,0},{4,5},{5,4},{2,3},{3,2},{6,7},{7,6},{10,11},{11,10},{1... | collective-permute-start | bytes 786440 | tf_op jit(solution)/shard_map/ppermute | solution.py:477
  182.8 1.9 copy-start
  184.7 8.6 %copy-start.2 = (bf16[128,128]{1,0:T(8,128)(2,1)S(1)}, bf16[128,128]{1,0:T(8,128)(2,1)}, u32[]{:S(2)}) copy-start(bf16[128,128]{1,0:T(8,128)(2,1)} %copy-done.1) | copy-start | bytes 98308
